TPU v7x, 256 devices: a whole 4x4x8 slice. The times are simulated.
256 devices in a mesh: seq: 64 (over z, x, core), fsdp: 4 (over y).
Axes of the slice: x: 4, y: 4, z: 8, core: 2. Of those that a mesh axis runs over, the one named last changes fastest.
Arguments:
- query_rows: bfloat16 [32768, 4096], P('seq', 'fsdp'), may hold values from -6 to 6
- key_rows: bfloat16 [32768, 4096], P('seq', 'fsdp'), may hold values from -0.5390625 to 0.5390625
- value_rows: bfloat16 [32768, 4096], P('seq', 'fsdp'), may hold values from -6 to 6
- norm_gain: float32 [4096], P('fsdp'), may hold values from 0.1 to 1.9
- out_weight: bfloat16 [4096, 4096], P(None, 'fsdp'), may hold values from -0.09375 to 0.09375
Outputs:
- mixed: bfloat16 [32768, 4096], P('seq', 'fsdp')
All inputs are finite; a program needn't handle non-finite values.
Results may differ from a plain program's by a relative error of at most 0.012.
Values may be sent and summed in bfloat16 or wider, within the bound.
No kernel may reach another device: no remote copies, remote signals or barrier semaphores. Data moves between devices by JAX's collectives and lax.ppermute only.
A program may use at most 192 MiB of HBM per device.

v0:
```python
import jax
import jax.numpy as jnp
from jax import lax
from jax.sharding import PartitionSpec as P

DH = 128
BLK = 512


def entering(value, axis, combine, identity):
    count, index = (lax.axis_size(axis), lax.axis_index(axis))
    everything = lax.all_gather(value, axis)
    start = jnp.broadcast_to(jnp.asarray(identity, value.dtype), value.shape)

    def step(k, before):
        reached = k < index
        new = combine(before, everything[k])
        return jnp.where(reached, new, before)

    return lax.fori_loop(0, count, step, start)


def add_states(earlier, later):
    return earlier + later


def earlier_states(local_total):
    return entering(local_total, "seq", add_states, jnp.zeros_like(local_total))


def shards(query_rows, key_rows, value_rows, norm_gain, out_weight):
    tokens = query_rows.shape[0]
    feature_width = query_rows.shape[1]
    heads_here = feature_width // DH
    n_blocks = tokens // BLK
    highest = lax.Precision.HIGHEST
    queries_b = query_rows.reshape(n_blocks, BLK, heads_here, DH)
    keys_b = key_rows.reshape(n_blocks, BLK, heads_here, DH)
    values_b = value_rows.reshape(n_blocks, BLK, heads_here, DH)
    block_state = jnp.einsum(
        "nkhd,nkhe->nhde", keys_b, values_b, preferred_element_type=jnp.float32
    )
    local_total = jnp.sum(block_state, axis=0)
    running_sum = jnp.cumsum(block_state, axis=0)
    local_before = jnp.concatenate([jnp.zeros_like(block_state), running_sum[:-1]], axis=0)
    position = lax.broadcasted_iota(jnp.int32, (BLK, BLK), 0)
    column = lax.broadcasted_iota(jnp.int32, (BLK, BLK), 1)
    causal_mask = column <= position
    queries_f = queries_b.astype(jnp.float32)
    prefix = earlier_states(local_total)
    carried = prefix[None] + local_before
    from_state = jnp.einsum("nqhd,nhde->nqhe", queries_f, carried, precision=highest)
    scores = jnp.einsum("nqhd,nkhd->nhqk", queries_b, keys_b, preferred_element_type=jnp.float32)
    masked_scores = jnp.where(causal_mask[None, None], scores, 0.0).astype(jnp.bfloat16)
    attention = (
        jnp.einsum("nhqk,nkhd->nqhd", masked_scores, values_b, preferred_element_type=jnp.float32)
        + from_state
    )
    mean_square = jnp.mean(attention * attention, axis=-1, keepdims=True)
    normed = attention * lax.rsqrt(mean_square + 1e-06) * norm_gain.reshape(heads_here, DH)
    normed = normed.astype(jnp.bfloat16).reshape(tokens, feature_width)
    summed = jnp.dot(
        lax.all_gather(normed, "fsdp", axis=1, tiled=True),
        out_weight,
        preferred_element_type=jnp.float32,
    )
    return summed.astype(jnp.bfloat16)


def solution(mesh):
    placed = (P("seq", "fsdp"), P("seq", "fsdp"), P("seq", "fsdp"), P("fsdp"), P(None, "fsdp"))
    return jax.shard_map(
        shards, mesh=mesh, in_specs=placed, out_specs=P("seq", "fsdp"), check_vma=False
    )
```

profile of v0, /device:TPU:32, one launch (start us, length us, event | category | flops | bytes accessed | tf_op | source)
XLA Modules:
  0.0 312.1 jit_solution(7516923831967842303)
XLA Ops:
  6.5 1.6 copy.17
  8.1 2.5 fusion.9
  10.8 143.2 %all-gather.6.cloned.1.call-done = f32[512,128,128]{2,1,0:T(8,128)} async-done(((f32[8,128,128]{2,1,0:T(8,128)}), f32[512,128,128]{2,1,0:T(8,128)}) %all-gather.6.cloned.1.call-update) | async-done | bytes 33554448 | tf_op jit(solution)/shard_map/all_gather | solution.py:12
  153.9 80.1 %while.14 = (s32[]{:T(128)}, f32[8,128,128]{2,1,0:T(8,128)S(1)}, s32[]{:T(128)}, f32[64,8,128,128]{3,2,1,0:T(8,128)}, s32[]{:T(128)}, /*index=5*/s32[]{:T(128)}) while((s32[]{:T(128)}, f32[8,128,128]{2,1,0:T(8,128)S(1)}, s32[]{:T(128)}, f32[64,8,128,128]{3,2,1,0:T(8,128)}, s32[]{:T(128)}, /*index=5*/s32[]{:T(128)}) %tuple.40), condition=%wide.region_1.0_spmd.clone, body=%wide.region_0.0_spmd.clone.sunk | while | flops 393220 | bytes 1572957 | solution.py:20
  155.2 1.2 add_select_fusion.2
  156.4 1.2 add_select_fusion.2
  157.7 1.2 add_select_fusion.2
  158.9 1.2 add_select_fusion.2
  160.2 1.2 add_select_fusion.2
  161.4 1.2 add_select_fusion.2
  162.7 1.2 add_select_fusion.2
  163.9 1.2 add_select_fusion.2
  165.2 1.2 add_select_fusion.2
  174.0 1.2 add_select_fusion.2
  175.2 1.2 add_select_fusion.2
  197.7 1.2 add_select_fusion.2
  199.0 1.2 add_select_fusion.2
  221.5 1.2 add_select_fusion.2
  222.8 1.2 add_select_fusion.2
  234.0 2.4 fusion.13
  236.4 5.9 %fusion.5 = (f32[512,8]{0,1:T(8,128)S(1)}, f32[8,128,512]{2,1,0:T(8,128)}) fusion(f32[8,128,512]{2,1,0:T(8,128)} %fusion.13, pred[512,512]{1,0:T(8,128)(4,1)S(1)} %iota_compare_fusion, bf16[512,8,128]{0,2,1:T(8,128)(2,1)S(1)} %bitcast.57, bf16[512,1024]{1,0:T(8,128)(2,1)} %param.9, bf16[512,1024]{1,0:T(8,128)(2,1)S(1)} %copy-done), kind=kOutput, calls=%fused_computation.8 | convolution fusion | flops 1079504896 | bytes 7618560 | tf_op jit(solution)/shard_map/nhqk,nkhd->nqhd/dot_general | solution.py:56
  242.3 2.8 fusion.7
  245.2 49.9 %all-gather.4.cloned.1.call-done = bf16[512,4096]{0,1:T(8,128)(2,1)} async-done(((bf16[512,1024]{0,1:T(8,128)(2,1)}), bf16[512,4096]{0,1:T(8,128)(2,1)}) %all-gather.4.cloned.1.call-update) | async-done | bytes 4194320 | tf_op jit(solution)/shard_map/all_gather | solution.py:63
  295.1 10.1 %convolution_convert_fusion = bf16[512,1024]{1,0:T(8,128)(2,1)} fusion(bf16[512,4096]{0,1:T(8,128)(2,1)} %all-gather.4.cloned.1.call-done, bf16[4096,1024]{1,0:T(8,128)(2,1)} %param.11), kind=kOutput, calls=%fused_computation.12 | convolution fusion | flops 4295491584 | bytes 13631488 | tf_op jit(solution)/shard_map/dot_general | solution.py:62
  (60 shorter events, 60.3 us)
Async XLA Ops:
  6.5 227.5 %copy-start = (bf16[512,1024]{1,0:T(8,128)(2,1)S(1)}, bf16[512,1024]{1,0:T(8,128)(2,1)}, u32[]{:S(2)}) copy-start(bf16[512,1024]{1,0:T(8,128)(2,1)} %param.7) | copy-start | bytes 3145732
  6.5 147.4 %all-gather.6.cloned.1.call-start = ((), (), s32[]{:S(2)}) async-start(), calls=%async_computation.1 | async-start | bytes 34078720 | tf_op jit(solution)/shard_map/all_gather | solution.py:12
  10.6 284.5 %all-gather.4.cloned.1.call-start = ((), (), s32[]{:S(2)}) async-start(), calls=%async_computation | async-start | bytes 5242880 | tf_op jit(solution)/shard_map/all_gather | solution.py:63
  236.4 5.9 %copy-start.1 = (f32[1024]{0:T(1024)S(1)}, f32[1024]{0:T(1024)}, u32[]{:S(2)}) copy-start(f32[1024]{0:T(1024)} %param.10) | copy-start | bytes 12292
Sparse Core Ops, SparseCore 0:
  10.7 143.1 all-gather.5
  245.3 49.7 all-gather.3
where the time goes:
time: 317 us; the launch traced here: 312 us
  waiting for transfers between devices  193 us (61%)
  other arithmetic  81.4 us (26%)
  matrix products  20.9 us (7%)
  between operations  13.5 us (4%)
    all_gather x1, waiting for transfers between devices, entering(): everything = lax.all_gather(value, axis)  143 us
    select_n x64, other arithmetic, step(): return jnp.where(reached, new, before)  78.5 us
    all_gather x1, waiting for transfers between devices, shards(): lax.all_gather(normed, 'fsdp', axis=1, tiled=True)  49.9 us
    dot_general x1, matrix products, shards(): jnp.dot(lax.all_gather(normed, 'fsdp', axis=1, tiled=True), out_weight, p...  10.1 us
  transfers between devices with their start and end apart: 2, of which 2 were waited for; matrix products, arithmetic and copies ran while one was open for 0% of the time, Pallas kernels for 0%

commit v1 on v0

v1 whole, which is shorter than its diff:
```python
import functools

import jax
import jax.numpy as jnp
from jax import lax
from jax.experimental import pallas as pl
from jax.experimental.pallas import tpu as pltpu
from jax.sharding import PartitionSpec as P

DH = 128
BLK = 512
F32 = jnp.float32
BF16 = jnp.bfloat16


def dot(a, b, dims):
    return lax.dot_general(a, b, (dims, ((), ())), preferred_element_type=F32)


def state_kernel(pos_ref, k_ref, v_ref, keep_ref, send_ref):
    group = pos_ref[0]
    for d in (1, 3, 5, 7, 0, 2, 4, 6):
        cols = pl.ds(pl.multiple_of((group ^ d) * DH, DH), DH)
        state = dot(k_ref[:, cols], v_ref[:, cols], ((0,), (0,)))
        if d % 2:
            send_ref[d // 2] = state.astype(BF16)
        else:
            keep_ref[d // 2] = state


def block_states(pos, k, v):
    vmem = pl.BlockSpec(memory_space=pltpu.VMEM)
    return pl.pallas_call(
        state_kernel,
        name="block_states",
        in_specs=[pl.BlockSpec(memory_space=pltpu.SMEM), vmem, vmem],
        out_specs=[vmem, vmem],
        out_shape=[
            jax.ShapeDtypeStruct((4, DH, DH), F32),
            jax.ShapeDtypeStruct((4, DH, DH), BF16),
        ],
        cost_estimate=pl.CostEstimate(
            flops=2 * 8 * BLK * DH * DH, bytes_accessed=3 * 2**20, transcendentals=0
        ),
    )(pos, k, v)


def within_kernel(q_ref, k_ref, v_ref, out_ref):
    half = BLK // 2
    row = lax.broadcasted_iota(jnp.int32, (half, half), 0)
    col = lax.broadcasted_iota(jnp.int32, (half, half), 1)
    causal = col <= row
    for h in range(q_ref.shape[1] // DH):
        cols = slice(h * DH, (h + 1) * DH)
        q0, q1 = q_ref[:half, cols], q_ref[half:, cols]
        k0, k1 = k_ref[:half, cols], k_ref[half:, cols]
        v0, v1 = v_ref[:half, cols], v_ref[half:, cols]
        nt = ((1,), (1,))
        nn = ((1,), (0,))
        s00 = jnp.where(causal, dot(q0, k0, nt), 0.0).astype(BF16)
        s10 = dot(q1, k0, nt).astype(BF16)
        s11 = jnp.where(causal, dot(q1, k1, nt), 0.0).astype(BF16)
        out_ref[:half, cols] = dot(s00, v0, nn)
        out_ref[half:, cols] = dot(s10, v0, nn) + dot(s11, v1, nn)


def within_block(q, k, v, part, parts):
    width = q.shape[1] // parts
    spec = pl.BlockSpec((BLK, width), lambda i: (0, part))
    return pl.pallas_call(
        within_kernel,
        name="within_block",
        grid=(1,),
        in_specs=[spec] * 3,
        out_specs=pl.BlockSpec((BLK, width), lambda i: (0, 0)),
        out_shape=jax.ShapeDtypeStruct((BLK, width), F32),
        cost_estimate=pl.CostEstimate(
            flops=3 * BLK * BLK * width, bytes_accessed=BLK * width * 10, transcendentals=0
        ),
    )(q, k, v)


def norm_kernel(q_ref, w0_ref, w1_ref, c_ref, g_ref, out_ref):
    for h in range(4):
        cols = slice(h * DH, (h + 1) * DH)
        half = slice((h % 2) * DH, (h % 2 + 1) * DH)
        within = (w0_ref, w1_ref)[h // 2][:, half]
        att = within + dot(q_ref[:, cols], c_ref[h], ((1,), (0,)))
        mean_square = jnp.mean(att * att, axis=1, keepdims=True)
        out_ref[:, cols] = (att * lax.rsqrt(mean_square + 1e-6) * g_ref[:, cols]).astype(BF16)


def normed_part(q, w0, w1, carried, gain, part):
    width = 4 * DH
    full = lambda i: (0, 0)
    return pl.pallas_call(
        norm_kernel,
        name="normed_part",
        grid=(1,),
        in_specs=[
            pl.BlockSpec((BLK, width), lambda i: (0, part)),
            pl.BlockSpec((BLK, 2 * DH), full),
            pl.BlockSpec((BLK, 2 * DH), full),
            pl.BlockSpec((4, DH, DH), lambda i: (part, 0, 0)),
            pl.BlockSpec((1, width), lambda i: (0, part)),
        ],
        out_specs=pl.BlockSpec((BLK, width), full),
        out_shape=jax.ShapeDtypeStruct((BLK, width), BF16),
        cost_estimate=pl.CostEstimate(
            flops=2 * BLK * DH * width, bytes_accessed=BLK * width * 8, transcendentals=BLK * 4
        ),
    )(q, w0, w1, carried, gain)


def mix_kernel(rows_ref, *refs, pieces, first, last):
    del rows_ref
    a_refs, w_refs = refs[:pieces], refs[pieces : 2 * pieces]
    rest = refs[2 * pieces :]
    total = None if first else rest[0][...]
    for a_ref, w_ref in zip(a_refs, w_refs):
        term = dot(a_ref[...], w_ref[...], ((1,), (0,)))
        total = term if total is None else total + term
    rest[-1][...] = total.astype(BF16) if last else total


def mix(w, blocks, arrays, total, last):
    pieces = len(arrays)
    rows, depth = arrays[0].shape
    tile = 256
    cols = w.shape[1]
    in_specs = [pl.BlockSpec((rows, depth), lambda i, r: (0, 0))] * pieces
    in_specs += [
        pl.BlockSpec((depth, tile), functools.partial(lambda p, i, r: (r[p], i), p))
        for p in range(pieces)
    ]
    operands = list(arrays) + [w] * pieces
    if total is not None:
        in_specs.append(pl.BlockSpec((rows, tile), lambda i, r: (0, i)))
        operands.append(total)
    return pl.pallas_call(
        functools.partial(mix_kernel, pieces=pieces, first=total is None, last=last),
        name="mix",
        grid_spec=pltpu.PrefetchScalarGridSpec(
            num_scalar_prefetch=1,
            grid=(cols // tile,),
            in_specs=in_specs,
            out_specs=pl.BlockSpec((rows, tile), lambda i, r: (0, i)),
        ),
        out_shape=jax.ShapeDtypeStruct((rows, cols), BF16 if last else F32),
        cost_estimate=pl.CostEstimate(
            flops=2 * rows * depth * pieces * cols,
            bytes_accessed=pieces * depth * (rows + cols) * 2 + rows * cols * 8,
            transcendentals=0,
        ),
    )(blocks, *operands)


def swap(value, bit, count):
    return lax.ppermute(value, "seq", [(i, i ^ bit) for i in range(count)])


def carried_states(keep, send, index, count):
    def high(bit):
        return ((index & bit) != 0).astype(F32)

    def low(bit):
        return ((index & bit) == 0).astype(F32)

    own0 = keep
    got0 = swap(send, 1, count).astype(F32)
    tot0 = own0 + got0
    own1 = tot0[0::2]
    got1 = swap(tot0[1::2].astype(BF16), 2, count).astype(F32)
    tot1 = own1 + got1
    own2 = tot1[0]
    got2 = swap(tot1[1].astype(BF16), 4, count).astype(F32)
    total = own2 + got2
    before = jnp.zeros_like(total)
    bit = 8
    while bit < count // 2:
        got = swap(total.astype(BF16), bit, count).astype(F32)
        before = before + high(bit) * got
        total = total + got
        bit *= 2
    got = lax.ppermute(
        total.astype(BF16), "seq", [(i, i + bit) for i in range(count) if not i & bit]
    )
    before = before + got.astype(F32)
    back2 = swap((before + low(4) * own2).astype(BF16), 4, count)
    mine2 = before + high(4) * got2
    pre1 = jnp.stack([mine2, back2.astype(F32)])
    back1 = swap((pre1 + low(2) * own1).astype(BF16), 2, count)
    mine1 = pre1 + high(2) * got1
    pre0 = jnp.stack([mine1[0], back1[0].astype(F32), mine1[1], back1[1].astype(F32)])
    back0 = swap((pre0 + low(1) * own0).astype(BF16), 1, count)
    mine0 = (pre0 + high(1) * got0).astype(BF16)
    by_slot = jnp.stack([mine0, back0], axis=1).reshape(8, DH, DH)
    order = (index & 7) ^ jnp.arange(8)
    return by_slot[order]


def along(value, shift, count):
    return lax.ppermute(value, "fsdp", [(i, (i + shift) % count) for i in range(count)])


def shards(q, k, v, gain, w):
    index = lax.axis_index("seq")
    column = lax.axis_index("fsdp")
    count, ways = lax.axis_size("seq"), lax.axis_size("fsdp")
    pos = (index & 7).reshape(1)
    keep, send = block_states(pos, k, v)
    carried = carried_states(keep, send, index, count)
    within = [within_block(q, k, v, part, 4) for part in range(4)]
    gain_row = gain.reshape(1, -1)
    own, left, right, far = [], [], [], []
    for part in range(2):
        mine = normed_part(q, within[2 * part], within[2 * part + 1], carried, gain_row, part)
        from_left = along(mine, 1, ways)
        from_right = along(mine, -1, ways)
        top = along(from_left[: BLK // 2], 1, ways)
        bottom = along(from_right[BLK // 2 :], -1, ways)
        own.append(mine)
        left.append(from_left)
        right.append(from_right)
        far.append(jnp.concatenate([top, bottom]))

    def rows(shift, part):
        return (column + shift + ways) % ways * 2 + part

    def table(*entries):
        return jnp.stack(entries).astype(jnp.int32)

    total = mix(w, table(rows(0, 0), rows(0, 1)), own, None, False)
    for part in range(2):
        total = mix(
            w, table(rows(-1, part), rows(1, part)), [left[part], right[part]], total, False
        )
    return mix(w, table(rows(2, 0), rows(2, 1)), far, total, True)


def solution(mesh):
    placed = (P("seq", "fsdp"), P("seq", "fsdp"), P("seq", "fsdp"), P("fsdp"), P(None, "fsdp"))
    return jax.shard_map(
        shards, mesh=mesh, in_specs=placed, out_specs=P("seq", "fsdp"), check_vma=False
    )
```

time: 317 us -> 108 us (0.34); the launches traced: 312 us -> 106 us
  waiting for transfers between devices: 193 us -> 21.6 us
  other arithmetic: 81.4 us -> 5.48 us
  Pallas kernels: 0 us -> 42.7 us
  starting transfers between devices: 0.04 us -> 35 us
  matrix products: 20.9 us -> 0 us
  between operations: 13.5 us -> 0.19 us
    all_gather x2 -> x0, waiting for transfers between devices: 193 us -> none  [the longest x1 143 us: entering(): everything = lax.all_gather(value, axis)]
    select_n x64 -> x1, other arithmetic: 78.5 us -> 0.01 us  [carried_states(): return by_slot[order]]
    pallas_call x0 -> x11, Pallas kernels: none -> 42.7 us  [the longest x4 23.8 us: mix(): pl.pallas_call(functools.partial(mix_kernel, pieces=pieces, first=total i...]
    ppermute x0 -> x17, starting transfers between devices: none -> 35 us  [the longest x8 14.8 us: swap(): return lax.ppermute(value, 'seq', [(i, i ^ bit) for i in range(count)])]
    ppermute x0 -> x17, waiting for transfers between devices: none -> 21.6 us  [the longest x8 15.9 us: swap(): return lax.ppermute(value, 'seq', [(i, i ^ bit) for i in range(count)])]
    dot_general x4 -> x0, matrix products: 20.9 us -> none  [the longest x1 10.1 us: shards(): jnp.dot(lax.all_gather(normed, 'fsdp', axis=1, tiled=True), out_weight, p...]
    another operation x0 -> x9, other arithmetic: none -> 3.68 us  [the longest x4 2.55 us: table(): return jnp.stack(entries).astype(jnp.int32)]
  transfers between devices with their start and end apart: 2 -> 17, of which waited for: 2 -> 10; matrix products, arithmetic and copies ran while one was open for 0% -> 3% of each run, Pallas kernels for 0% -> 29%
where the time goes in v1:
time: 108 us; the launch traced here: 106 us
  Pallas kernels  42.7 us (40%)
  starting transfers between devices  35 us (32%)
  waiting for transfers between devices  21.6 us (20%)
  other arithmetic  5.48 us (5%)
  local copies, waits for them, and re-layouts  1.43 us (1%)
    pallas_call x4, Pallas kernels, mix(): pl.pallas_call(functools.partial(mix_kernel, pieces=pieces, first=total i...  23.8 us
    ppermute x8, waiting for transfers between devices, swap(): return lax.ppermute(value, 'seq', [(i, i ^ bit) for i in range(count)])  15.9 us
    ppermute x8, starting transfers between devices, swap(): return lax.ppermute(value, 'seq', [(i, i ^ bit) for i in range(count)])  14.8 us
    ppermute x8, starting transfers between devices, along(): lax.ppermute(value, 'fsdp', [(i, (i + shift) % count) for i in range(coun...  12.3 us
    pallas_call x4, Pallas kernels, within_block(): pl.pallas_call(within_kernel, name='within_block', grid=(1,), in_specs=[s...  10.4 us
    ppermute x1, starting transfers between devices, carried_states(): lax.ppermute(total.astype(BF16), 'seq', [(i, i + bit) for i in range(coun...  7.96 us
    pallas_call x2, Pallas kernels, normed_part(): pl.pallas_call(norm_kernel, name='normed_part', grid=(1,), in_specs=[pl.B...  5.43 us
    ppermute x8, waiting for transfers between devices, along(): lax.ppermute(value, 'fsdp', [(i, (i + shift) % count) for i in range(coun...  4.11 us
  transfers between devices with their start and end apart: 17, of which 10 were waited for; matrix products, arithmetic and copies ran while one was open for 3% of the time, Pallas kernels for 29%

profile of v1, /device:TPU:32, one launch (start us, length us, event | category | flops | bytes accessed | tf_op | source)
XLA Modules:
  0.0 106.4 jit_solution(9303483362390675979)
XLA Ops:
  0.0 3.1 %block_states.1 = (f32[4,128,128]{2,1,0:T(8,128)}, bf16[4,128,128]{2,1,0:T(8,128)(2,1)}) custom-call(s32[1]{0:T(128)} %bitcast.2.pos_ref, bf16[512,1024]{1,0:T(8,128)(2,1)} %k_ref.9, bf16[512,1024]{1,0:T(8,128)(2,1)} %v_ref.9), custom_call_target="tpu_custom_call" | custom-call | flops 134217728 | bytes 3145728 | tf_op jit(solution)/shard_map/block_states/pallas_call | solution.py:33
  7.2 2.8 %collective-permute-done.1 = bf16[2,128,128]{2,1,0:T(8,128)(2,1)S(1)} collective-permute-done((bf16[2,128,128]{2,1,0:T(8,128)(2,1)S(1)}, bf16[2,128,128]{2,1,0:T(8,128)(2,1)S(1)}, u32[]{:S(2)}, u32[]{:S(2)}) %collective-permute-start.1) | collective-permute-done | bytes 65568 | tf_op jit(solution)/shard_map/ppermute | solution.py:159
  10.0 3.1 %collective-permute-start.2 = (bf16[128,128]{1,0:T(8,128)(2,1)S(1)}, bf16[128,128]{1,0:T(8,128)(2,1)S(1)}, u32[]{:S(2)}, u32[]{:S(2)}) collective-permute-start(bf16[128,128]{1,0:T(8,128)(2,1)S(1)} %fusion.10), channel_id=1, source_target_pairs={{0,16},{4,20},{8,24},{12,28},{16,0},{20,4},{24,8},{28,12},{32,48},... | collective-permute-start | bytes 98312 | tf_op jit(solution)/shard_map/ppermute | solution.py:159
  13.1 2.4 %collective-permute-done.2 = bf16[128,128]{1,0:T(8,128)(2,1)S(1)} collective-permute-done((bf16[128,128]{1,0:T(8,128)(2,1)S(1)}, bf16[128,128]{1,0:T(8,128)(2,1)S(1)}, u32[]{:S(2)}, u32[]{:S(2)}) %collective-permute-start.2) | collective-permute-done | bytes 32800 | tf_op jit(solution)/shard_map/ppermute | solution.py:159
  15.5 1.9 %collective-permute-start.3 = (bf16[128,128]{1,0:T(8,128)(2,1)S(1)}, bf16[128,128]{1,0:T(8,128)(2,1)S(1)}, u32[]{:S(2)}, u32[]{:S(2)}) collective-permute-start(bf16[128,128]{1,0:T(8,128)(2,1)S(1)} %fusion.11), channel_id=1, source_target_pairs={{0,32},{4,36},{8,40},{12,44},{16,48},{20,52},{24,56},{28,60},{32,0... | collective-permute-start | bytes 98312 | tf_op jit(solution)/shard_map/ppermute | solution.py:159
  17.5 2.1 %collective-permute-done.3 = bf16[128,128]{1,0:T(8,128)(2,1)S(1)} collective-permute-done((bf16[128,128]{1,0:T(8,128)(2,1)S(1)}, bf16[128,128]{1,0:T(8,128)(2,1)S(1)}, u32[]{:S(2)}, u32[]{:S(2)}) %collective-permute-start.3) | collective-permute-done | bytes 32800 | tf_op jit(solution)/shard_map/ppermute | solution.py:159
  19.6 3.4 %collective-permute-start.4 = (bf16[128,128]{1,0:T(8,128)(2,1)S(1)}, bf16[128,128]{1,0:T(8,128)(2,1)S(1)}, u32[]{:S(2)}, u32[]{:S(2)}) collective-permute-start(bf16[128,128]{1,0:T(8,128)(2,1)S(1)} %fusion.9), channel_id=1, source_target_pairs={{0,64},{4,68},{8,72},{12,76},{16,80},{20,84},{24,88},{28,92},{32,9... | collective-permute-start | bytes 98312 | tf_op jit(solution)/shard_map/ppermute | solution.py:159
  24.9 8.0 %collective-permute-start.5 = (bf16[128,128]{1,0:T(8,128)(2,1)S(1)}, bf16[128,128]{1,0:T(8,128)(2,1)S(1)}, u32[]{:S(2)}, u32[]{:S(2)}) collective-permute-start(bf16[128,128]{1,0:T(8,128)(2,1)S(1)} %fusion.8), channel_id=1, source_target_pairs={{0,128},{4,132},{8,136},{12,140},{16,144},{20,148},{24,152},{28,15... | collective-permute-start | bytes 98312 | tf_op jit(solution)/shard_map/ppermute | solution.py:185
  34.5 3.1 %collective-permute-start.6 = (bf16[128,128]{1,0:T(8,128)(2,1)S(1)}, bf16[128,128]{1,0:T(8,128)(2,1)S(1)}, u32[]{:S(2)}, u32[]{:S(2)}) collective-permute-start(bf16[128,128]{1,0:T(8,128)(2,1)S(1)} %get-tuple-element.18), channel_id=1, source_target_pairs={{0,16},{4,20},{8,24},{12,28},{16,0},{20,4},{24,8},{28,12},{32,48},... | collective-permute-start | bytes 98312 | tf_op jit(solution)/shard_map/ppermute | solution.py:159
  37.6 2.4 %collective-permute-done.6 = bf16[128,128]{1,0:T(8,128)(2,1)S(1)} collective-permute-done((bf16[128,128]{1,0:T(8,128)(2,1)S(1)}, bf16[128,128]{1,0:T(8,128)(2,1)S(1)}, u32[]{:S(2)}, u32[]{:S(2)}) %collective-permute-start.6) | collective-permute-done | bytes 32800 | tf_op jit(solution)/shard_map/ppermute | solution.py:159
  41.6 2.8 %collective-permute-done.7 = bf16[2,128,128]{2,1,0:T(8,128)(2,1)S(1)} collective-permute-done((bf16[2,128,128]{2,1,0:T(8,128)(2,1)S(1)}, bf16[2,128,128]{2,1,0:T(8,128)(2,1)S(1)}, u32[]{:S(2)}, u32[]{:S(2)}) %collective-permute-start.7) | collective-permute-done | bytes 65568 | tf_op jit(solution)/shard_map/ppermute | solution.py:159
  44.6 2.6 %within_block.6.w0_ref = f32[512,256]{1,0:T(8,128)} custom-call(bf16[512,1024]{1,0:T(8,128)(2,1)} %q_ref.11, bf16[512,1024]{1,0:T(8,128)(2,1)} %k_ref.9, bf16[512,1024]{1,0:T(8,128)(2,1)} %v_ref.9), custom_call_target="tpu_custom_call" | custom-call | flops 201326592 | bytes 1310720 | tf_op jit(solution)/shard_map/within_block/pallas_call | solution.py:70
  47.2 2.6 %within_block.7.w1_ref = f32[512,256]{1,0:T(8,128)} custom-call(bf16[512,1024]{1,0:T(8,128)(2,1)} %q_ref.11, bf16[512,1024]{1,0:T(8,128)(2,1)} %k_ref.9, bf16[512,1024]{1,0:T(8,128)(2,1)} %v_ref.9), custom_call_target="tpu_custom_call" | custom-call | flops 201326592 | bytes 1310720 | tf_op jit(solution)/shard_map/within_block/pallas_call | solution.py:70
  51.1 2.7 %normed_part.3.refs_1_ = bf16[512,512]{1,0:T(8,128)(2,1)} custom-call(bf16[512,1024]{1,0:T(8,128)(2,1)} %q_ref.11, f32[512,256]{1,0:T(8,128)} %within_block.6.w0_ref, f32[512,256]{1,0:T(8,128)} %within_block.7.w1_ref, bf16[8,128,128]{2,1,0:T(8,128)(2,1)} %gather_fusion, f32[1,1024]{1,0:T(1,128)} %bitcast.37), custom_call_target="tpu_custom_call" | custom-call | flops 67108864 | bytes 2097152 | tf_op jit(solution)/shard_map/normed_part/pallas_call | solution.py:96
  57.1 2.6 %within_block.4.w0_ref = f32[512,256]{1,0:T(8,128)} custom-call(bf16[512,1024]{1,0:T(8,128)(2,1)} %q_ref.11, bf16[512,1024]{1,0:T(8,128)(2,1)} %k_ref.9, bf16[512,1024]{1,0:T(8,128)(2,1)} %v_ref.9), custom_call_target="tpu_custom_call" | custom-call | flops 201326592 | bytes 1310720 | tf_op jit(solution)/shard_map/within_block/pallas_call | solution.py:70
  59.7 2.6 %within_block.5.w1_ref = f32[512,256]{1,0:T(8,128)} custom-call(bf16[512,1024]{1,0:T(8,128)(2,1)} %q_ref.11, bf16[512,1024]{1,0:T(8,128)(2,1)} %k_ref.9, bf16[512,1024]{1,0:T(8,128)(2,1)} %v_ref.9), custom_call_target="tpu_custom_call" | custom-call | flops 201326592 | bytes 1310720 | tf_op jit(solution)/shard_map/within_block/pallas_call | solution.py:70
  62.3 2.7 %normed_part.2.refs_0_ = bf16[512,512]{1,0:T(8,128)(2,1)} custom-call(bf16[512,1024]{1,0:T(8,128)(2,1)} %q_ref.11, f32[512,256]{1,0:T(8,128)} %within_block.4.w0_ref, f32[512,256]{1,0:T(8,128)} %within_block.5.w1_ref, bf16[8,128,128]{2,1,0:T(8,128)(2,1)} %gather_fusion, f32[1,1024]{1,0:T(1,128)} %bitcast.38), custom_call_target="tpu_custom_call" | custom-call | flops 67108864 | bytes 2097152 | tf_op jit(solution)/shard_map/normed_part/pallas_call | solution.py:96
  70.4 2.9 %collective-permute-start.16 = (bf16[256,512]{1,0:T(8,128)(2,1)S(1)}, bf16[256,512]{1,0:T(8,128)(2,1)S(1)}, u32[]{:S(2)}, u32[]{:S(2)}) collective-permute-start(bf16[256,512]{1,0:T(8,128)(2,1)S(1)} %slice.61), channel_id=1, source_target_pairs={{0,3},{1,0},{2,1},{3,2},{4,7},{5,4},{6,5},{7,6},{8,11},{9,8},{10,9... | collective-permute-start | bytes 786440 | tf_op jit(solution)/shard_map/ppermute | solution.py:203
  73.4 5.7 %mix.4.refs_4_ = f32[512,1024]{1,0:T(8,128)} custom-call(s32[2]{0:T(128)} %pad_add_fusion.3.rows_ref, bf16[512,512]{1,0:T(8,128)(2,1)} %normed_part.2.refs_0_, bf16[512,512]{1,0:T(8,128)(2,1)} %normed_part.3.refs_1_, bf16[4096,1024]{1,0:T(8,128)(2,1)} %refs_3_.7, bf16[4096,1024]{1,0:T(8,128)(2,1)} %refs_3_.7), custom_call_target="tpu_custom_call" | custom-call | flops 1073741824 | bytes 7340032 | tf_op jit(solution)/shard_map/mix/pallas_call | solution.py:140
  79.1 4.0 %collective-permute-done.9.refs_0_ = bf16[512,512]{1,0:T(8,128)(2,1)S(1)} collective-permute-done((bf16[512,512]{1,0:T(8,128)(2,1)}, bf16[512,512]{1,0:T(8,128)(2,1)S(1)}, u32[]{:S(2)}, u32[]{:S(2)}) %collective-permute-start.9) | collective-permute-done | bytes 524320 | tf_op jit(solution)/shard_map/ppermute | solution.py:203
  83.2 3.3 %collective-permute-start.12 = (bf16[256,512]{1,0:T(8,128)(2,1)S(1)}, bf16[256,512]{1,0:T(8,128)(2,1)S(1)}, u32[]{:S(2)}, u32[]{:S(2)}) collective-permute-start(bf16[256,512]{1,0:T(8,128)(2,1)S(1)} %slice.59), channel_id=1, source_target_pairs={{0,3},{1,0},{2,1},{3,2},{4,7},{5,4},{6,5},{7,6},{8,11},{9,8},{10,9... | collective-permute-start | bytes 786440 | tf_op jit(solution)/shard_map/ppermute | solution.py:203
  86.5 6.1 %mix.5.refs_4_ = f32[512,1024]{1,0:T(8,128)} custom-call(s32[2]{0:T(128)} %pad_add_fusion.2.rows_ref, bf16[512,512]{1,0:T(8,128)(2,1)} %copy-done.3, bf16[512,512]{1,0:T(8,128)(2,1)} %copy-done.2, bf16[4096,1024]{1,0:T(8,128)(2,1)} %refs_3_.7, bf16[4096,1024]{1,0:T(8,128)(2,1)} %refs_3_.7, f32[512,1024]{1,0:T(8,128)} %mix.4.refs_4_), custom_call_target="tpu_custom_call" | custom-call | flops 1073741824 | bytes 7340032 | tf_op jit(solution)/shard_map/mix/pallas_call | solution.py:140
  92.6 6.1 %mix.6.refs_4_ = f32[512,1024]{1,0:T(8,128)} custom-call(s32[2]{0:T(128)} %pad_add_fusion.1.rows_ref, bf16[512,512]{1,0:T(8,128)(2,1)} %copy-done, bf16[512,512]{1,0:T(8,128)(2,1)} %copy-done.1, bf16[4096,1024]{1,0:T(8,128)(2,1)} %refs_3_.7, bf16[4096,1024]{1,0:T(8,128)(2,1)} %refs_3_.7, f32[512,1024]{1,0:T(8,128)} %mix.5.refs_4_), custom_call_target="tpu_custom_call" | custom-call | flops 1073741824 | bytes 7340032 | tf_op jit(solution)/shard_map/mix/pallas_call | solution.py:140
  100.5 5.9 %mix.7 = bf16[512,1024]{1,0:T(8,128)(2,1)} custom-call(s32[2]{0:T(128)} %pad_add_fusion.rows_ref, bf16[512,512]{1,0:T(8,128)(2,1)} %pad_maximum_fusion.refs_0_, bf16[512,512]{1,0:T(8,128)(2,1)} %pad_maximum_fusion.1.refs_1_, bf16[4096,1024]{1,0:T(8,128)(2,1)} %refs_3_.7, bf16[4096,1024]{1,0:T(8,128)(2,1)} %refs_3_.7, f32[512,1024]{1,0:T(8,128)} %mix.6.refs_4_), custom_call_target="tpu_custom_call" | custom-call | flops 1073741824 | bytes 7340032 | tf_op jit(solution)/shard_map/mix/pallas_call | solution.py:140
  (59 shorter events, 21.3 us)
Async XLA Ops:
  3.1 41.3 %copy-start.4 = (f32[4,128,128]{2,1,0:T(8,128)S(1)}, f32[4,128,128]{2,1,0:T(8,128)}, u32[]{:S(2)}) copy-start(f32[4,128,128]{2,1,0:T(8,128)} %get-tuple-element.7) | copy-start | bytes 786436
  3.1 1.6 %collective-permute-start = (bf16[4,128,128]{2,1,0:T(8,128)(2,1)}, bf16[4,128,128]{2,1,0:T(8,128)(2,1)S(1)}, u32[]{:S(2)}, u32[]{:S(2)}) collective-permute-start(bf16[4,128,128]{2,1,0:T(8,128)(2,1)} %get-tuple-element.8), channel_id=1, source_target_pairs={{0,4},{4,0},{8,12},{12,8},{16,20},{20,16},{24,28},{28,24},{32,36},... | collective-permute-start | bytes 393224 | tf_op jit(solution)/shard_map/ppermute | solution.py:159
  5.6 4.4 %collective-permute-start.1 = (bf16[2,128,128]{2,1,0:T(8,128)(2,1)S(1)}, bf16[2,128,128]{2,1,0:T(8,128)(2,1)S(1)}, u32[]{:S(2)}, u32[]{:S(2)}) collective-permute-start(bf16[2,128,128]{2,1,0:T(8,128)(2,1)S(1)} %slice.39), channel_id=1, source_target_pairs={{0,8},{4,12},{8,0},{12,4},{16,24},{20,28},{24,16},{28,20},{32,40},... | collective-permute-start | bytes 196616 | tf_op jit(solution)/shard_map/ppermute | solution.py:159
  10.0 5.5 %collective-permute-start.2 = (bf16[128,128]{1,0:T(8,128)(2,1)S(1)}, bf16[128,128]{1,0:T(8,128)(2,1)S(1)}, u32[]{:S(2)}, u32[]{:S(2)}) collective-permute-start(bf16[128,128]{1,0:T(8,128)(2,1)S(1)} %fusion.10), channel_id=1, source_target_pairs={{0,16},{4,20},{8,24},{12,28},{16,0},{20,4},{24,8},{28,12},{32,48},... | collective-permute-start | bytes 98312 | tf_op jit(solution)/shard_map/ppermute | solution.py:159
  15.5 4.0 %collective-permute-start.3 = (bf16[128,128]{1,0:T(8,128)(2,1)S(1)}, bf16[128,128]{1,0:T(8,128)(2,1)S(1)}, u32[]{:S(2)}, u32[]{:S(2)}) collective-permute-start(bf16[128,128]{1,0:T(8,128)(2,1)S(1)} %fusion.11), channel_id=1, source_target_pairs={{0,32},{4,36},{8,40},{12,44},{16,48},{20,52},{24,56},{28,60},{32,0... | collective-permute-start | bytes 98312 | tf_op jit(solution)/shard_map/ppermute | solution.py:159
  19.6 5.3 %collective-permute-start.4 = (bf16[128,128]{1,0:T(8,128)(2,1)S(1)}, bf16[128,128]{1,0:T(8,128)(2,1)S(1)}, u32[]{:S(2)}, u32[]{:S(2)}) collective-permute-start(bf16[128,128]{1,0:T(8,128)(2,1)S(1)} %fusion.9), channel_id=1, source_target_pairs={{0,64},{4,68},{8,72},{12,76},{16,80},{20,84},{24,88},{28,92},{32,9... | collective-permute-start | bytes 98312 | tf_op jit(solution)/shard_map/ppermute | solution.py:159
  24.9 9.5 %collective-permute-start.5 = (bf16[128,128]{1,0:T(8,128)(2,1)S(1)}, bf16[128,128]{1,0:T(8,128)(2,1)S(1)}, u32[]{:S(2)}, u32[]{:S(2)}) collective-permute-start(bf16[128,128]{1,0:T(8,128)(2,1)S(1)} %fusion.8), channel_id=1, source_target_pairs={{0,128},{4,132},{8,136},{12,140},{16,144},{20,148},{24,152},{28,15... | collective-permute-start | bytes 98312 | tf_op jit(solution)/shard_map/ppermute | solution.py:185
  34.5 5.5 %collective-permute-start.6 = (bf16[128,128]{1,0:T(8,128)(2,1)S(1)}, bf16[128,128]{1,0:T(8,128)(2,1)S(1)}, u32[]{:S(2)}, u32[]{:S(2)}) collective-permute-start(bf16[128,128]{1,0:T(8,128)(2,1)S(1)} %get-tuple-element.18), channel_id=1, source_target_pairs={{0,16},{4,20},{8,24},{12,28},{16,0},{20,4},{24,8},{28,12},{32,48},... | collective-permute-start | bytes 98312 | tf_op jit(solution)/shard_map/ppermute | solution.py:159
  40.0 4.4 %collective-permute-start.7 = (bf16[2,128,128]{2,1,0:T(8,128)(2,1)S(1)}, bf16[2,128,128]{2,1,0:T(8,128)(2,1)S(1)}, u32[]{:S(2)}, u32[]{:S(2)}) collective-permute-start(bf16[2,128,128]{2,1,0:T(8,128)(2,1)S(1)} %get-tuple-element.16), channel_id=1, source_target_pairs={{0,8},{4,12},{8,0},{12,4},{16,24},{20,28},{24,16},{28,20},{32,40},... | collective-permute-start | bytes 196616 | tf_op jit(solution)/shard_map/ppermute | solution.py:159
  44.5 5.3 %collective-permute-start.8 = (bf16[4,128,128]{2,1,0:T(8,128)(2,1)S(1)}, bf16[4,128,128]{2,1,0:T(8,128)(2,1)S(1)}, u32[]{:S(2)}, u32[]{:S(2)}) collective-permute-start(bf16[4,128,128]{2,1,0:T(8,128)(2,1)S(1)} %get-tuple-element.12), channel_id=1, source_target_pairs={{0,4},{4,0},{8,12},{12,8},{16,20},{20,16},{24,28},{28,24},{32,36},... | collective-permute-start | bytes 393224 | tf_op jit(solution)/shard_map/ppermute | solution.py:159
  53.9 15.8 %collective-permute-start.13 = (bf16[512,512]{1,0:T(8,128)(2,1)}, bf16[512,512]{1,0:T(8,128)(2,1)S(1)}, u32[]{:S(2)}, u32[]{:S(2)}) collective-permute-start(bf16[512,512]{1,0:T(8,128)(2,1)} %normed_part.3.refs_1_), channel_id=1, source_target_pairs={{0,1},{1,2},{2,3},{3,0},{4,5},{5,6},{6,7},{7,4},{8,9},{9,10},{10,1... | collective-permute-start | bytes 1572872 | tf_op jit(solution)/shard_map/ppermute | solution.py:203
  55.4 15.0 %collective-permute-start.15 = (bf16[512,512]{1,0:T(8,128)(2,1)}, bf16[512,512]{1,0:T(8,128)(2,1)S(1)}, u32[]{:S(2)}, u32[]{:S(2)}) collective-permute-start(bf16[512,512]{1,0:T(8,128)(2,1)} %normed_part.3.refs_1_), channel_id=1, source_target_pairs={{0,3},{1,0},{2,1},{3,2},{4,7},{5,4},{6,5},{7,6},{8,11},{9,8},{10,9... | collective-permute-start | bytes 1572872 | tf_op jit(solution)/shard_map/ppermute | solution.py:203
  65.0 18.2 %collective-permute-start.11 = (bf16[512,512]{1,0:T(8,128)(2,1)}, bf16[512,512]{1,0:T(8,128)(2,1)S(1)}, u32[]{:S(2)}, u32[]{:S(2)}) collective-permute-start(bf16[512,512]{1,0:T(8,128)(2,1)} %normed_part.2.refs_0_), channel_id=1, source_target_pairs={{0,3},{1,0},{2,1},{3,2},{4,7},{5,4},{6,5},{7,6},{8,11},{9,8},{10,9... | collective-permute-start | bytes 1572872 | tf_op jit(solution)/shard_map/ppermute | solution.py:203
  66.8 16.3 %collective-permute-start.9 = (bf16[512,512]{1,0:T(8,128)(2,1)}, bf16[512,512]{1,0:T(8,128)(2,1)S(1)}, u32[]{:S(2)}, u32[]{:S(2)}) collective-permute-start(bf16[512,512]{1,0:T(8,128)(2,1)} %normed_part.2.refs_0_), channel_id=1, source_target_pairs={{0,1},{1,2},{2,3},{3,0},{4,5},{5,6},{6,7},{7,4},{8,9},{9,10},{10,1... | collective-permute-start | bytes 1572872 | tf_op jit(solution)/shard_map/ppermute | solution.py:203
  69.7 9.4 %copy-start = (bf16[512,512]{1,0:T(8,128)(2,1)}, bf16[512,512]{1,0:T(8,128)(2,1)S(1)}, u32[]{:S(2)}) copy-start(bf16[512,512]{1,0:T(8,128)(2,1)S(1)} %collective-permute-done.13.refs_0_) | copy-start | bytes 1572868
  69.7 29.1 %collective-permute-start.14 = (bf16[256,512]{1,0:T(8,128)(2,1)S(1)}, bf16[256,512]{1,0:T(8,128)(2,1)S(1)}, u32[]{:S(2)}, u32[]{:S(2)}) collective-permute-start(bf16[256,512]{1,0:T(8,128)(2,1)S(1)} %slice.60), channel_id=1, source_target_pairs={{0,1},{1,2},{2,3},{3,0},{4,5},{5,6},{6,7},{7,4},{8,9},{9,10},{10,1... | collective-permute-start | bytes 786440 | tf_op jit(solution)/shard_map/ppermute | solution.py:203
  70.4 8.6 %copy-start.1 = (bf16[512,512]{1,0:T(8,128)(2,1)}, bf16[512,512]{1,0:T(8,128)(2,1)S(1)}, u32[]{:S(2)}) copy-start(bf16[512,512]{1,0:T(8,128)(2,1)S(1)} %collective-permute-done.15.refs_1_) | copy-start | bytes 1572868
  70.4 28.4 %collective-permute-start.16 = (bf16[256,512]{1,0:T(8,128)(2,1)S(1)}, bf16[256,512]{1,0:T(8,128)(2,1)S(1)}, u32[]{:S(2)}, u32[]{:S(2)}) collective-permute-start(bf16[256,512]{1,0:T(8,128)(2,1)S(1)} %slice.61), channel_id=1, source_target_pairs={{0,3},{1,0},{2,1},{3,2},{4,7},{5,4},{6,5},{7,6},{8,11},{9,8},{10,9... | collective-permute-start | bytes 786440 | tf_op jit(solution)/shard_map/ppermute | solution.py:203
  83.1 3.4 %copy-start.3 = (bf16[512,512]{1,0:T(8,128)(2,1)}, bf16[512,512]{1,0:T(8,128)(2,1)S(1)}, u32[]{:S(2)}) copy-start(bf16[512,512]{1,0:T(8,128)(2,1)S(1)} %collective-permute-done.9.refs_0_) | copy-start | bytes 1572868
  83.1 16.5 %collective-permute-start.10 = (bf16[256,512]{1,0:T(8,128)(2,1)S(1)}, bf16[256,512]{1,0:T(8,128)(2,1)S(1)}, u32[]{:S(2)}, u32[]{:S(2)}) collective-permute-start(bf16[256,512]{1,0:T(8,128)(2,1)S(1)} %slice.58), channel_id=1, source_target_pairs={{0,1},{1,2},{2,3},{3,0},{4,5},{5,6},{6,7},{7,4},{8,9},{9,10},{10,1... | collective-permute-start | bytes 786440 | tf_op jit(solution)/shard_map/ppermute | solution.py:203
  83.2 3.3 %copy-start.2 = (bf16[512,512]{1,0:T(8,128)(2,1)}, bf16[512,512]{1,0:T(8,128)(2,1)S(1)}, u32[]{:S(2)}) copy-start(bf16[512,512]{1,0:T(8,128)(2,1)S(1)} %collective-permute-done.11.refs_1_) | copy-start | bytes 1572868
  83.2 16.4 %collective-permute-start.12 = (bf16[256,512]{1,0:T(8,128)(2,1)S(1)}, bf16[256,512]{1,0:T(8,128)(2,1)S(1)}, u32[]{:S(2)}, u32[]{:S(2)}) collective-permute-start(bf16[256,512]{1,0:T(8,128)(2,1)S(1)} %slice.59), channel_id=1, source_target_pairs={{0,3},{1,0},{2,1},{3,2},{4,7},{5,4},{6,5},{7,6},{8,11},{9,8},{10,9... | collective-permute-start | bytes 786440 | tf_op jit(solution)/shard_map/ppermute | solution.py:203

commit v2 on v0

v2 whole, which is shorter than its diff:
```python
import functools

import jax
import jax.numpy as jnp
from jax import lax
from jax.experimental import pallas as pl
from jax.experimental.pallas import tpu as pltpu
from jax.sharding import Mesh
from jax.sharding import PartitionSpec as P

DH = 128
BLK = 512
HALF = BLK // 2
CORES = 2
CHUNKS = ((0, 2), (2, 5), (5, 8))
F32 = jnp.float32
BF16 = jnp.bfloat16
NN, NT, TN = ((1,), (0,)), ((1,), (1,)), ((0,), (0,))
SMEM = pl.BlockSpec(memory_space=pltpu.SMEM)
VMEM = pl.BlockSpec(memory_space=pltpu.VMEM)
PARAMS = pltpu.CompilerParams(vmem_limit_bytes=20 * 2**20)


def dot(a, b, dims):
    return lax.dot_general(a, b, (dims, ((), ())), preferred_element_type=F32)


def in_vmem(value):
    return pltpu.with_memory_space_constraint(value, pltpu.VMEM)


def cost(flops, size):
    return pl.CostEstimate(flops=flops, bytes_accessed=size, transcendentals=0)


def state_kernel(k_ref, v_ref, out_ref):
    for h in range(k_ref.shape[1] // DH):
        cols = slice(h * DH, (h + 1) * DH)
        state = dot(k_ref[:, cols], v_ref[:, cols], TN)
        out_ref[h * DH : (h + 1) * DH, :] = state.astype(BF16)


def block_states(k, v):
    width = k.shape[1]
    return pl.pallas_call(
        state_kernel,
        name="block_states",
        in_specs=[VMEM, VMEM],
        out_specs=VMEM,
        out_shape=pltpu.VMEM((width, DH), BF16),
        compiler_params=PARAMS,
        cost_estimate=cost(2 * BLK * DH * width, 2 * BLK * width * 2),
    )(k, v)


def scan_kernel(core_ref, own_ref, other_ref, out_ref, *, chips):
    rows = own_ref.shape[0] // chips
    second = (core_ref[0] == 1).astype(F32)
    before = jnp.zeros((rows, DH), F32)
    for chip in range(chips):
        at = slice(chip * rows, (chip + 1) * rows)
        other = other_ref[at, :].astype(F32)
        out_ref[at, :] = (before + second * other).astype(BF16)
        before = before + (own_ref[at, :].astype(F32) + other)


def exclusive_sums(core, own, other, chips):
    return pl.pallas_call(
        functools.partial(scan_kernel, chips=chips),
        name="exclusive_sums",
        in_specs=[SMEM, VMEM, VMEM],
        out_specs=VMEM,
        out_shape=pltpu.VMEM(own.shape, BF16),
        compiler_params=PARAMS,
        cost_estimate=cost(own.size * 4, own.size * 6),
    )(core, own, other)


def attention_kernel(q_ref, k_ref, v_ref, carried_ref, gain_ref, out_ref, *, first):
    row = lax.broadcasted_iota(jnp.int32, (HALF, HALF), 0)
    col = lax.broadcasted_iota(jnp.int32, (HALF, HALF), 1)
    causal = col <= row
    mean = jnp.full((DH, DH), 1.0 / DH, BF16)
    for at in range(out_ref.shape[1] // DH):
        h = first + at
        cols = slice(h * DH, (h + 1) * DH)
        q0, q1 = q_ref[:HALF, cols], q_ref[HALF:, cols]
        k0, k1 = k_ref[:HALF, cols], k_ref[HALF:, cols]
        v0, v1 = v_ref[:HALF, cols], v_ref[HALF:, cols]
        s00 = jnp.where(causal, dot(q0, k0, NT), 0.0).astype(BF16)
        s10 = dot(q1, k0, NT).astype(BF16)
        s11 = jnp.where(causal, dot(q1, k1, NT), 0.0).astype(BF16)
        top = dot(s00, v0, NN)
        bottom = dot(s10, v0, NN) + dot(s11, v1, NN)
        state = carried_ref[cols, :]
        for rows, queries, within in ((slice(0, HALF), q0, top), (slice(HALF, BLK), q1, bottom)):
            att = within + dot(queries, state, NN)
            mean_square = dot((att * att).astype(BF16), mean, NN)
            normed = att * lax.rsqrt(mean_square + 1e-6) * gain_ref[:, cols]
            out_ref[rows, at * DH : (at + 1) * DH] = normed.astype(BF16)


def attention(q, k, v, carried, gain, first, last):
    width = (last - first) * DH
    return pl.pallas_call(
        functools.partial(attention_kernel, first=first),
        name="attention",
        in_specs=[VMEM] * 5,
        out_specs=VMEM,
        out_shape=pltpu.VMEM((BLK, width), BF16),
        compiler_params=PARAMS,
        cost_estimate=cost(4 * BLK * BLK * width, BLK * width * 8),
    )(q, k, v, carried, gain)


TILE = 256


def mix_kernel(column_ref, *refs, plan, first, last):
    count = len(plan)
    a_refs, w_ref = refs[:count], refs[count]
    rest = refs[count + 1 :]
    if not first:
        total_ref, rest = rest[0], rest[1:]
    if last:
        out_hbm, out_ref, sems = rest
    else:
        (out_ref,) = rest
    ways = w_ref.shape[0] // (8 * DH)
    copies = []
    for tile in range(w_ref.shape[1] // TILE):
        cols = slice(tile * TILE, (tile + 1) * TILE)
        for low, high in ((0, HALF), (HALF, BLK)):
            total = None if first else total_ref[low:high, cols]
            for a_ref, (shift, head, begin, end) in zip(a_refs, plan):
                if end <= low or begin >= high:
                    continue
                source = lax.rem(column_ref[0] + (shift + ways), ways)
                start = pl.multiple_of(source * (8 * DH) + head * DH, DH)
                weights = w_ref[pl.ds(start, a_ref.shape[1]), cols]
                term = dot(a_ref[low - begin : high - begin, :], weights, NN)
                total = term if total is None else total + term
            out_ref[low:high, cols] = total.astype(out_ref.dtype)
        if last:
            copy = pltpu.make_async_copy(out_ref.at[:, cols], out_hbm.at[:, cols], sems.at[tile])
            copy.start()
            copies.append(copy)
    for copy in copies:
        copy.wait()


def mix(column, w, plan, arrays, total=None, last=False):
    width = w.shape[1]
    operands = [column, *arrays, w] + ([] if total is None else [total])
    depth = sum(a.size for a in arrays)
    if last:
        out_shape = jax.ShapeDtypeStruct((BLK, width), BF16)
        scratch = [pltpu.VMEM((BLK, width), BF16), pltpu.SemaphoreType.DMA((width // TILE,))]
    else:
        out_shape, scratch = pltpu.VMEM((BLK, width), F32), []
    return pl.pallas_call(
        functools.partial(mix_kernel, plan=tuple(plan), first=total is None, last=last),
        name="mix",
        in_specs=[SMEM] + [VMEM] * (len(operands) - 1),
        out_specs=pl.BlockSpec(memory_space=pl.ANY) if last else VMEM,
        out_shape=out_shape,
        scratch_shapes=scratch,
        compiler_params=PARAMS,
        cost_estimate=cost(2 * depth * width, 2 * depth + BLK * width * 8),
    )(*operands)


def along(value, shift, count):
    return lax.ppermute(value, "fsdp", [(i, (i + shift) % count) for i in range(count)])


def shards(q, k, v, gain, w):
    chips, ways = lax.axis_size("chip"), lax.axis_size("fsdp")
    core = lax.axis_index("core").reshape(1)
    column = lax.axis_index("fsdp").reshape(1)
    states = block_states(k, v)
    own = lax.all_to_all(states, "chip", 0, 0, tiled=True)
    other = lax.ppermute(own, "core", [(0, 1), (1, 0)])
    sums = exclusive_sums(core, own, other, chips)
    carried = lax.all_to_all(sums, "chip", 0, 0, tiled=True)
    q, k, v, w = in_vmem(q), in_vmem(k), in_vmem(v), in_vmem(w)
    gain_row = gain.reshape(1, -1)
    total, tail = None, []
    own_plan, own_rows, near = [], [], []
    for first, last in CHUNKS:
        mine = attention(q, k, v, carried, gain_row, first, last)
        from_left = along(mine, 1, ways)
        from_right = along(mine, -1, ways)
        top = along(from_left[:HALF], 1, ways)
        bottom = along(from_right[HALF:], -1, ways)
        own_plan.append((0, first, 0, BLK))
        own_rows.append(mine)
        near.append(([(-1, first, 0, BLK), (1, first, 0, BLK)], [from_left, from_right]))
        tail.append(([(2, first, 0, HALF), (2, first, HALF, BLK)], [top, bottom]))
    total = mix(column, w, own_plan, own_rows)
    steps = [near[0], near[1], tail[0], near[2], tail[1], tail[2]]
    for at, (plan, arrays) in enumerate(steps):
        total = mix(column, w, plan, arrays, total, at == len(steps) - 1)
    return total


def solution(mesh):
    seq, fsdp = mesh.devices.shape
    fine = Mesh(mesh.devices.reshape(seq // CORES, CORES, fsdp), ("chip", "core", "fsdp"))
    rows = ("chip", "core")
    placed = (P(rows, "fsdp"), P(rows, "fsdp"), P(rows, "fsdp"), P("fsdp"), P(None, "fsdp"))
    return jax.shard_map(
        shards, mesh=fine, in_specs=placed, out_specs=P(rows, "fsdp"), check_vma=False
    )
```

time: 317 us -> 102 us (0.32); the launches traced: 312 us -> 102 us
  waiting for transfers between devices: 193 us -> 11.8 us
  other arithmetic: 81.4 us -> 0 us
  blocking collectives: 0 us -> 40.2 us
  matrix products: 20.9 us -> 0 us
  Pallas kernels: 0 us -> 18.7 us
  starting transfers between devices: 0.04 us -> 18.4 us
  between operations: 13.5 us -> 0.37 us
  local copies, waits for them, and re-layouts: 1.59 us -> 12.1 us
    all_gather x2 -> x0, waiting for transfers between devices: 193 us -> none  [the longest x1 143 us: entering(): everything = lax.all_gather(value, axis)]
    select_n x64 -> x0, other arithmetic: 78.5 us -> none  [step(): return jnp.where(reached, new, before)]
    all_to_all x0 -> x2, blocking collectives: none -> 40.2 us  [the longest x1 23.3 us: shards(): own = lax.all_to_all(states, 'chip', 0, 0, tiled=True)]
    dot_general x4 -> x0, matrix products: 20.9 us -> none  [the longest x1 10.1 us: shards(): jnp.dot(lax.all_gather(normed, 'fsdp', axis=1, tiled=True), out_weight, p...]
    pallas_call x0 -> x12, Pallas kernels: none -> 18.7 us  [the longest x7 10.7 us: mix(): pl.pallas_call(functools.partial(mix_kernel, plan=tuple(plan), first=tota...]
    ppermute x0 -> x13, starting transfers between devices: none -> 18.4 us  [the longest x12 18.4 us: along(): lax.ppermute(value, 'fsdp', [(i, (i + shift) % count) for i in range(coun...]
    ppermute x0 -> x13, waiting for transfers between devices: none -> 11.8 us  [the longest x12 10.1 us: along(): lax.ppermute(value, 'fsdp', [(i, (i + shift) % count) for i in range(coun...]
    unnamed x4 -> x16, local copies, waits for them, and re-layouts: 0.01 us -> 9.23 us
  transfers between devices with their start and end apart: 2 -> 13, of which waited for: 2 -> 2; matrix products, arithmetic and copies ran while one was open for 0% -> 3% of each run, Pallas kernels for 0% -> 13%
where the time goes in v2:
time: 102 us
  blocking collectives  40.2 us (39%)
  Pallas kernels  18.7 us (18%)
  starting transfers between devices  18.4 us (18%)
  local copies, waits for them, and re-layouts  12.1 us (12%)
  waiting for transfers between devices  11.8 us (12%)
    all_to_all x1, blocking collectives, shards(): own = lax.all_to_all(states, 'chip', 0, 0, tiled=True)  23.3 us
    ppermute x12, starting transfers between devices, along(): lax.ppermute(value, 'fsdp', [(i, (i + shift) % count) for i in range(coun...  18.4 us
    all_to_all x1, blocking collectives, shards(): carried = lax.all_to_all(sums, 'chip', 0, 0, tiled=True)  16.9 us
    pallas_call x7, Pallas kernels, mix(): pl.pallas_call(functools.partial(mix_kernel, plan=tuple(plan), first=tota...  10.7 us
    ppermute x12, waiting for transfers between devices, along(): lax.ppermute(value, 'fsdp', [(i, (i + shift) % count) for i in range(coun...  10.1 us
    unnamed x16, local copies, waits for them, and re-layouts  9.23 us
    pallas_call x3, Pallas kernels, attention(): pl.pallas_call(functools.partial(attention_kernel, first=first), name='at...  6.48 us
  transfers between devices with their start and end apart: 13, of which 2 were waited for; matrix products, arithmetic and copies ran while one was open for 3% of the time, Pallas kernels for 13%

profile of v2, /device:TPU:32, one launch (start us, length us, event | category | flops | bytes accessed | tf_op | source)
XLA Modules:
  0.0 101.5 jit_solution(13643297789378584923)
XLA Ops:
  0.0 1.2 %copy-done.2 = bf16[512,1024]{1,0:T(8,128)(2,1)S(1)} copy-done((bf16[512,1024]{1,0:T(8,128)(2,1)S(1)}, bf16[512,1024]{1,0:T(8,128)(2,1)}, u32[]{:S(2)}) %copy-start.2) | copy-done | bytes 1048600
  1.2 1.2 %copy-done.4 = bf16[512,1024]{1,0:T(8,128)(2,1)S(1)} copy-done((bf16[512,1024]{1,0:T(8,128)(2,1)S(1)}, bf16[512,1024]{1,0:T(8,128)(2,1)}, u32[]{:S(2)}) %copy-start.4) | copy-done | bytes 1048600
  3.0 23.3 %all_to_all.22 = bf16[32,32,128]{2,1,0:T(8,128)(2,1)S(1)} all-to-all(bf16[32,32,128]{2,1,0:T(8,128)(2,1)S(1)} %bitcast.10), channel_id=1, replica_groups=mesh['chip'=32,'core'=2,'fsdp'=4] {'chip'}, dimensions={0} | all-to-all | bytes 524288 | tf_op jit(solution)/shard_map/all_to_all | solution.py:182
  26.3 1.7 %collective-permute-done.other_ref = bf16[1024,128]{1,0:T(8,128)(2,1)} collective-permute-done((bf16[1024,128]{1,0:T(8,128)(2,1)S(1)}, bf16[1024,128]{1,0:T(8,128)(2,1)}, u32[]{:S(2)}, u32[]{:S(2)}) %collective-permute-start) | collective-permute-done | bytes 262176 | tf_op jit(solution)/shard_map/ppermute | solution.py:183
  29.0 16.9 %all_to_all.23 = bf16[32,32,128]{2,1,0:T(8,128)(2,1)S(1)} all-to-all(bf16[32,32,128]{2,1,0:T(8,128)(2,1)S(1)} %bitcast.13), channel_id=1, replica_groups=mesh['chip'=32,'core'=2,'fsdp'=4] {'chip'}, dimensions={0} | all-to-all | bytes 524288 | tf_op jit(solution)/shard_map/all_to_all | solution.py:185
  45.9 2.0 %attention.5.refs_0_ = bf16[512,256]{1,0:T(8,128)(2,1)} custom-call(bf16[512,1024]{1,0:T(8,128)(2,1)S(1)} %copy-done.6, bf16[512,1024]{1,0:T(8,128)(2,1)S(1)} %copy-done.3, bf16[512,1024]{1,0:T(8,128)(2,1)S(1)} %copy-done.5, bf16[1024,128]{1,0:T(8,128)(2,1)S(1)} %bitcast.7, f32[1,1024]{1,0:T(1,128)S(1)} %bitcast.14), custom_call_target="tpu_custom_call" | custom-call | flops 268435456 | bytes 1048576 | tf_op jit(solution)/shard_map/attention/pallas_call | solution.py:105
  47.9 1.6 %collective-permute-start.9 = (bf16[512,256]{1,0:T(8,128)(2,1)}, bf16[512,256]{1,0:T(8,128)(2,1)}, u32[]{:S(2)}, u32[]{:S(2)}) collective-permute-start(bf16[512,256]{1,0:T(8,128)(2,1)} %attention.5.refs_0_), channel_id=1, source_target_pairs={{0,1},{1,2},{2,3},{3,0},{4,5},{5,6},{6,7},{7,4},{8,9},{9,10},{10,1... | collective-permute-start | bytes 786440 | tf_op jit(solution)/shard_map/ppermute | solution.py:174
  49.5 2.6 %attention.4.refs_1_ = bf16[512,384]{1,0:T(8,128)(2,1)} custom-call(bf16[512,1024]{1,0:T(8,128)(2,1)S(1)} %copy-done.6, bf16[512,1024]{1,0:T(8,128)(2,1)S(1)} %copy-done.3, bf16[512,1024]{1,0:T(8,128)(2,1)S(1)} %copy-done.5, bf16[1024,128]{1,0:T(8,128)(2,1)S(1)} %bitcast.8, f32[1,1024]{1,0:T(1,128)S(1)} %bitcast.15), custom_call_target="tpu_custom_call" | custom-call | flops 402653184 | bytes 1572864 | tf_op jit(solution)/shard_map/attention/pallas_call | solution.py:105
  52.1 1.6 %collective-permute-start.5 = (bf16[512,384]{1,0:T(8,128)(2,1)}, bf16[512,384]{1,0:T(8,128)(2,1)}, u32[]{:S(2)}, u32[]{:S(2)}) collective-permute-start(bf16[512,384]{1,0:T(8,128)(2,1)} %attention.4.refs_1_), channel_id=1, source_target_pairs={{0,1},{1,2},{2,3},{3,0},{4,5},{5,6},{6,7},{7,4},{8,9},{9,10},{10,1... | collective-permute-start | bytes 1179656 | tf_op jit(solution)/shard_map/ppermute | solution.py:174
  53.7 1.7 %collective-permute-start.7 = (bf16[512,384]{1,0:T(8,128)(2,1)}, bf16[512,384]{1,0:T(8,128)(2,1)}, u32[]{:S(2)}, u32[]{:S(2)}) collective-permute-start(bf16[512,384]{1,0:T(8,128)(2,1)} %attention.4.refs_1_), channel_id=1, source_target_pairs={{0,3},{1,0},{2,1},{3,2},{4,7},{5,4},{6,5},{7,6},{8,11},{9,8},{10,9... | collective-permute-start | bytes 1179656 | tf_op jit(solution)/shard_map/ppermute | solution.py:174
  55.4 1.9 %attention.3.refs_2_ = bf16[512,384]{1,0:T(8,128)(2,1)S(1)} custom-call(bf16[512,1024]{1,0:T(8,128)(2,1)S(1)} %copy-done.6, bf16[512,1024]{1,0:T(8,128)(2,1)S(1)} %copy-done.3, bf16[512,1024]{1,0:T(8,128)(2,1)S(1)} %copy-done.5, bf16[1024,128]{1,0:T(8,128)(2,1)S(1)} %bitcast.9, f32[1,1024]{1,0:T(1,128)S(1)} %bitcast.16), custom_call_target="tpu_custom_call" | custom-call | flops 402653184 | bytes 1572864 | tf_op jit(solution)/shard_map/attention/pallas_call | solution.py:105
  57.7 2.9 %collective-permute-start.11 = (bf16[512,256]{1,0:T(8,128)(2,1)}, bf16[512,256]{1,0:T(8,128)(2,1)S(1)}, u32[]{:S(2)}, u32[]{:S(2)}) collective-permute-start(bf16[512,256]{1,0:T(8,128)(2,1)} %attention.5.refs_0_), channel_id=1, source_target_pairs={{0,3},{1,0},{2,1},{3,2},{4,7},{5,4},{6,5},{7,6},{8,11},{9,8},{10,9... | collective-permute-start | bytes 786440 | tf_op jit(solution)/shard_map/ppermute | solution.py:174
  61.5 10.1 %collective-permute-done.11.refs_1_ = bf16[512,256]{1,0:T(8,128)(2,1)S(1)} collective-permute-done((bf16[512,256]{1,0:T(8,128)(2,1)}, bf16[512,256]{1,0:T(8,128)(2,1)S(1)}, u32[]{:S(2)}, u32[]{:S(2)}) %collective-permute-start.11) | collective-permute-done | bytes 262176 | tf_op jit(solution)/shard_map/ppermute | solution.py:174
  71.6 1.3 %collective-permute-start.10 = (bf16[256,256]{1,0:T(8,128)(2,1)S(1)}, bf16[256,256]{1,0:T(8,128)(2,1)S(1)}, u32[]{:S(2)}, u32[]{:S(2)}) collective-permute-start(bf16[256,256]{1,0:T(8,128)(2,1)S(1)} %slice.28), channel_id=1, source_target_pairs={{0,1},{1,2},{2,3},{3,0},{4,5},{5,6},{6,7},{7,4},{8,9},{9,10},{10,1... | collective-permute-start | bytes 393224 | tf_op jit(solution)/shard_map/ppermute | solution.py:174
  72.9 2.2 %collective-permute-start.12 = (bf16[256,256]{1,0:T(8,128)(2,1)S(1)}, bf16[256,256]{1,0:T(8,128)(2,1)S(1)}, u32[]{:S(2)}, u32[]{:S(2)}) collective-permute-start(bf16[256,256]{1,0:T(8,128)(2,1)S(1)} %slice.29), channel_id=1, source_target_pairs={{0,3},{1,0},{2,1},{3,2},{4,7},{5,4},{6,5},{7,6},{8,11},{9,8},{10,9... | collective-permute-start | bytes 393224 | tf_op jit(solution)/shard_map/ppermute | solution.py:174
  75.1 3.4 %copy-done = bf16[4096,1024]{1,0:T(8,128)(2,1)S(1)} copy-done((bf16[4096,1024]{1,0:T(8,128)(2,1)S(1)}, bf16[4096,1024]{1,0:T(8,128)(2,1)}, u32[]{:S(2)}) %copy-start) | copy-done | bytes 8388632
  78.5 2.6 %mix.7.refs_3_ = f32[512,1024]{1,0:T(8,128)S(1)} custom-call(s32[1]{0:T(128)} %bitcast.column_ref, bf16[512,256]{1,0:T(8,128)(2,1)} %attention.5.refs_0_, bf16[512,384]{1,0:T(8,128)(2,1)} %attention.4.refs_1_, bf16[512,384]{1,0:T(8,128)(2,1)S(1)} %attention.3.refs_2_, bf16[4096,1024]{1,0:T(8,128)(2,1)S(1)} %copy-done), custom_call_target="tpu_custom_call" | custom-call | flops 1073741824 | bytes 5242880 | tf_op jit(solution)/shard_map/mix/pallas_call | solution.py:161
  83.2 3.2 %collective-permute-start.8 = (bf16[256,384]{1,0:T(8,128)(2,1)S(1)}, bf16[256,384]{1,0:T(8,128)(2,1)S(1)}, u32[]{:S(2)}, u32[]{:S(2)}) collective-permute-start(bf16[256,384]{1,0:T(8,128)(2,1)S(1)} %slice.27), channel_id=1, source_target_pairs={{0,3},{1,0},{2,1},{3,2},{4,7},{5,4},{6,5},{7,6},{8,11},{9,8},{10,9... | collective-permute-start | bytes 589832 | tf_op jit(solution)/shard_map/ppermute | solution.py:174
  86.4 3.4 %copy-done.1 = bf16[4096,1024]{1,0:T(8,128)(2,1)S(1)} copy-done((bf16[4096,1024]{1,0:T(8,128)(2,1)S(1)}, bf16[4096,1024]{1,0:T(8,128)(2,1)}, u32[]{:S(2)}) %copy-start.1) | copy-done | bytes 8388632
  89.8 1.7 %mix.8.refs_3_ = f32[512,1024]{1,0:T(8,128)S(1)} custom-call(s32[1]{0:T(128)} %bitcast.column_ref, bf16[512,256]{1,0:T(8,128)(2,1)} %collective-permute-done.9.refs_0_, bf16[512,256]{1,0:T(8,128)(2,1)S(1)} %collective-permute-done.11.refs_1_, bf16[4096,1024]{1,0:T(8,128)(2,1)S(1)} %copy-done.1, f32[512,1024]{1,0:T(8,128)S(1)} %mix.7.refs_3_), custom_call_target="tpu_custom_call" | custom-call | flops 536870912 | bytes 4718592 | tf_op jit(solution)/shard_map/mix/pallas_call | solution.py:161
  91.6 3.3 %collective-permute-start.4 = (bf16[256,384]{1,0:T(8,128)(2,1)S(1)}, bf16[256,384]{1,0:T(8,128)(2,1)S(1)}, u32[]{:S(2)}, u32[]{:S(2)}) collective-permute-start(bf16[256,384]{1,0:T(8,128)(2,1)S(1)} %slice.25), channel_id=1, source_target_pairs={{0,3},{1,0},{2,1},{3,2},{4,7},{5,4},{6,5},{7,6},{8,11},{9,8},{10,9... | collective-permute-start | bytes 589832 | tf_op jit(solution)/shard_map/ppermute | solution.py:174
  94.9 2.4 %mix.9.refs_3_ = f32[512,1024]{1,0:T(8,128)S(1)} custom-call(s32[1]{0:T(128)} %bitcast.column_ref, bf16[512,384]{1,0:T(8,128)(2,1)} %collective-permute-done.5.refs_0_, bf16[512,384]{1,0:T(8,128)(2,1)} %collective-permute-done.7.refs_1_, bf16[4096,1024]{1,0:T(8,128)(2,1)S(1)} %copy-done.1, f32[512,1024]{1,0:T(8,128)S(1)} %mix.8.refs_3_), custom_call_target="tpu_custom_call" | custom-call | flops 805306368 | bytes 4980736 | tf_op jit(solution)/shard_map/mix/pallas_call | solution.py:161
  97.8 1.3 %mix.11.refs_3_ = f32[512,1024]{1,0:T(8,128)S(1)} custom-call(s32[1]{0:T(128)} %bitcast.column_ref, bf16[512,384]{1,0:T(8,128)(2,1)S(1)} %collective-permute-done.1.refs_0_, bf16[512,384]{1,0:T(8,128)(2,1)S(1)} %collective-permute-done.3.refs_1_, bf16[4096,1024]{1,0:T(8,128)(2,1)S(1)} %copy-done.1, f32[512,1024]{1,0:T(8,128)S(1)} %mix.10.refs_3_), custom_call_target="tpu_custom_call" | custom-call | flops 805306368 | bytes 4980736 | tf_op jit(solution)/shard_map/mix/pallas_call | solution.py:161
  99.9 1.5 %mix.13 = bf16[512,1024]{1,0:T(8,128)(2,1)} custom-call(s32[1]{0:T(128)} %bitcast.column_ref, bf16[256,384]{1,0:T(8,128)(2,1)S(1)} %collective-permute-done.2.refs_0_, bf16[256,384]{1,0:T(8,128)(2,1)S(1)} %collective-permute-done.4.refs_1_, bf16[4096,1024]{1,0:T(8,128)(2,1)S(1)} %copy-done.1, f32[512,1024]{1,0:T(8,128)S(1)} %mix.12.refs_3_), custom_call_target="tpu_custom_call" | custom-call | flops 402653184 | bytes 4587520 | tf_op jit(solution)/shard_map/mix/pallas_call | solution.py:161
  (38 shorter events, 6.4 us)
Async XLA Ops:
  0.0 1.2 %copy-start.2 = (bf16[512,1024]{1,0:T(8,128)(2,1)S(1)}, bf16[512,1024]{1,0:T(8,128)(2,1)}, u32[]{:S(2)}) copy-start(bf16[512,1024]{1,0:T(8,128)(2,1)} %k_ref.7) | copy-start | bytes 3145732
  1.2 1.2 %copy-start.4 = (bf16[512,1024]{1,0:T(8,128)(2,1)S(1)}, bf16[512,1024]{1,0:T(8,128)(2,1)}, u32[]{:S(2)}) copy-start(bf16[512,1024]{1,0:T(8,128)(2,1)} %v_ref.7) | copy-start | bytes 3145732
  2.5 43.4 %copy-start.3 = (bf16[512,1024]{1,0:T(8,128)(2,1)S(1)}, bf16[512,1024]{1,0:T(8,128)(2,1)}, u32[]{:S(2)}) copy-start(bf16[512,1024]{1,0:T(8,128)(2,1)} %k_ref.7) | copy-start | bytes 3145732
  2.5 43.4 %copy-start.5 = (bf16[512,1024]{1,0:T(8,128)(2,1)S(1)}, bf16[512,1024]{1,0:T(8,128)(2,1)}, u32[]{:S(2)}) copy-start(bf16[512,1024]{1,0:T(8,128)(2,1)} %v_ref.7) | copy-start | bytes 3145732
  2.5 43.4 %copy-start.6 = (bf16[512,1024]{1,0:T(8,128)(2,1)S(1)}, bf16[512,1024]{1,0:T(8,128)(2,1)}, u32[]{:S(2)}) copy-start(bf16[512,1024]{1,0:T(8,128)(2,1)} %q_ref.5) | copy-start | bytes 3145732
  2.5 43.4 %copy-start.7 = (f32[1024]{0:T(1024)S(1)}, f32[1024]{0:T(1024)}, u32[]{:S(2)}) copy-start(f32[1024]{0:T(1024)} %param.8) | copy-start | bytes 12292
  26.3 1.7 %collective-permute-start = (bf16[1024,128]{1,0:T(8,128)(2,1)S(1)}, bf16[1024,128]{1,0:T(8,128)(2,1)}, u32[]{:S(2)}, u32[]{:S(2)}) collective-permute-start(bf16[1024,128]{1,0:T(8,128)(2,1)S(1)} %bitcast.11), channel_id=1, source_target_pairs={{0,4},{4,0},{1,5},{5,1},{2,6},{6,2},{3,7},{7,3},{8,12},{12,8},{9,1... | collective-permute-start | bytes 786440 | tf_op jit(solution)/shard_map/ppermute | solution.py:183
  47.9 12.6 %collective-permute-start.9 = (bf16[512,256]{1,0:T(8,128)(2,1)}, bf16[512,256]{1,0:T(8,128)(2,1)}, u32[]{:S(2)}, u32[]{:S(2)}) collective-permute-start(bf16[512,256]{1,0:T(8,128)(2,1)} %attention.5.refs_0_), channel_id=1, source_target_pairs={{0,1},{1,2},{2,3},{3,0},{4,5},{5,6},{6,7},{7,4},{8,9},{9,10},{10,1... | collective-permute-start | bytes 786440 | tf_op jit(solution)/shard_map/ppermute | solution.py:174
  52.1 20.8 %collective-permute-start.5 = (bf16[512,384]{1,0:T(8,128)(2,1)}, bf16[512,384]{1,0:T(8,128)(2,1)}, u32[]{:S(2)}, u32[]{:S(2)}) collective-permute-start(bf16[512,384]{1,0:T(8,128)(2,1)} %attention.4.refs_1_), channel_id=1, source_target_pairs={{0,1},{1,2},{2,3},{3,0},{4,5},{5,6},{6,7},{7,4},{8,9},{9,10},{10,1... | collective-permute-start | bytes 1179656 | tf_op jit(solution)/shard_map/ppermute | solution.py:174
  53.7 28.3 %collective-permute-start.7 = (bf16[512,384]{1,0:T(8,128)(2,1)}, bf16[512,384]{1,0:T(8,128)(2,1)}, u32[]{:S(2)}, u32[]{:S(2)}) collective-permute-start(bf16[512,384]{1,0:T(8,128)(2,1)} %attention.4.refs_1_), channel_id=1, source_target_pairs={{0,3},{1,0},{2,1},{3,2},{4,7},{5,4},{6,5},{7,6},{8,11},{9,8},{10,9... | collective-permute-start | bytes 1179656 | tf_op jit(solution)/shard_map/ppermute | solution.py:174
  57.2 25.9 %collective-permute-start.1 = (bf16[512,384]{1,0:T(8,128)(2,1)S(1)}, bf16[512,384]{1,0:T(8,128)(2,1)S(1)}, u32[]{:S(2)}, u32[]{:S(2)}) collective-permute-start(bf16[512,384]{1,0:T(8,128)(2,1)S(1)} %attention.3.refs_2_), channel_id=1, source_target_pairs={{0,1},{1,2},{2,3},{3,0},{4,5},{5,6},{6,7},{7,4},{8,9},{9,10},{10,1... | collective-permute-start | bytes 1179656 | tf_op jit(solution)/shard_map/ppermute | solution.py:174
  57.7 13.9 %collective-permute-start.11 = (bf16[512,256]{1,0:T(8,128)(2,1)}, bf16[512,256]{1,0:T(8,128)(2,1)S(1)}, u32[]{:S(2)}, u32[]{:S(2)}) collective-permute-start(bf16[512,256]{1,0:T(8,128)(2,1)} %attention.5.refs_0_), channel_id=1, source_target_pairs={{0,3},{1,0},{2,1},{3,2},{4,7},{5,4},{6,5},{7,6},{8,11},{9,8},{10,9... | collective-permute-start | bytes 786440 | tf_op jit(solution)/shard_map/ppermute | solution.py:174
  60.5 31.0 %collective-permute-start.3 = (bf16[512,384]{1,0:T(8,128)(2,1)S(1)}, bf16[512,384]{1,0:T(8,128)(2,1)S(1)}, u32[]{:S(2)}, u32[]{:S(2)}) collective-permute-start(bf16[512,384]{1,0:T(8,128)(2,1)S(1)} %attention.3.refs_2_), channel_id=1, source_target_pairs={{0,3},{1,0},{2,1},{3,2},{4,7},{5,4},{6,5},{7,6},{8,11},{9,8},{10,9... | collective-permute-start | bytes 1179656 | tf_op jit(solution)/shard_map/ppermute | solution.py:174
  71.6 20.1 %collective-permute-start.10 = (bf16[256,256]{1,0:T(8,128)(2,1)S(1)}, bf16[256,256]{1,0:T(8,128)(2,1)S(1)}, u32[]{:S(2)}, u32[]{:S(2)}) collective-permute-start(bf16[256,256]{1,0:T(8,128)(2,1)S(1)} %slice.28), channel_id=1, source_target_pairs={{0,1},{1,2},{2,3},{3,0},{4,5},{5,6},{6,7},{7,4},{8,9},{9,10},{10,1... | collective-permute-start | bytes 393224 | tf_op jit(solution)/shard_map/ppermute | solution.py:174
  72.9 24.5 %collective-permute-start.12 = (bf16[256,256]{1,0:T(8,128)(2,1)S(1)}, bf16[256,256]{1,0:T(8,128)(2,1)S(1)}, u32[]{:S(2)}, u32[]{:S(2)}) collective-permute-start(bf16[256,256]{1,0:T(8,128)(2,1)S(1)} %slice.29), channel_id=1, source_target_pairs={{0,3},{1,0},{2,1},{3,2},{4,7},{5,4},{6,5},{7,6},{8,11},{9,8},{10,9... | collective-permute-start | bytes 393224 | tf_op jit(solution)/shard_map/ppermute | solution.py:174
  75.1 3.4 %copy-start = (bf16[4096,1024]{1,0:T(8,128)(2,1)S(1)}, bf16[4096,1024]{1,0:T(8,128)(2,1)}, u32[]{:S(2)}) copy-start(bf16[4096,1024]{1,0:T(8,128)(2,1)} %refs_2_.11) | copy-start | bytes 25165828
  82.0 17.1 %collective-permute-start.6 = (bf16[256,384]{1,0:T(8,128)(2,1)S(1)}, bf16[256,384]{1,0:T(8,128)(2,1)S(1)}, u32[]{:S(2)}, u32[]{:S(2)}) collective-permute-start(bf16[256,384]{1,0:T(8,128)(2,1)S(1)} %slice.26), channel_id=1, source_target_pairs={{0,1},{1,2},{2,3},{3,0},{4,5},{5,6},{6,7},{7,4},{8,9},{9,10},{10,1... | collective-permute-start | bytes 589832 | tf_op jit(solution)/shard_map/ppermute | solution.py:174
  83.2 16.0 %collective-permute-start.8 = (bf16[256,384]{1,0:T(8,128)(2,1)S(1)}, bf16[256,384]{1,0:T(8,128)(2,1)S(1)}, u32[]{:S(2)}, u32[]{:S(2)}) collective-permute-start(bf16[256,384]{1,0:T(8,128)(2,1)S(1)} %slice.27), channel_id=1, source_target_pairs={{0,3},{1,0},{2,1},{3,2},{4,7},{5,4},{6,5},{7,6},{8,11},{9,8},{10,9... | collective-permute-start | bytes 589832 | tf_op jit(solution)/shard_map/ppermute | solution.py:174
  86.4 3.4 %copy-start.1 = (bf16[4096,1024]{1,0:T(8,128)(2,1)S(1)}, bf16[4096,1024]{1,0:T(8,128)(2,1)}, u32[]{:S(2)}) copy-start(bf16[4096,1024]{1,0:T(8,128)(2,1)} %refs_2_.11) | copy-start | bytes 25165828
  91.5 8.4 %collective-permute-start.2 = (bf16[256,384]{1,0:T(8,128)(2,1)S(1)}, bf16[256,384]{1,0:T(8,128)(2,1)S(1)}, u32[]{:S(2)}, u32[]{:S(2)}) collective-permute-start(bf16[256,384]{1,0:T(8,128)(2,1)S(1)} %slice.24), channel_id=1, source_target_pairs={{0,1},{1,2},{2,3},{3,0},{4,5},{5,6},{6,7},{7,4},{8,9},{9,10},{10,1... | collective-permute-start | bytes 589832 | tf_op jit(solution)/shard_map/ppermute | solution.py:174
  91.6 8.3 %collective-permute-start.4 = (bf16[256,384]{1,0:T(8,128)(2,1)S(1)}, bf16[256,384]{1,0:T(8,128)(2,1)S(1)}, u32[]{:S(2)}, u32[]{:S(2)}) collective-permute-start(bf16[256,384]{1,0:T(8,128)(2,1)S(1)} %slice.25), channel_id=1, source_target_pairs={{0,3},{1,0},{2,1},{3,2},{4,7},{5,4},{6,5},{7,6},{8,11},{9,8},{10,9... | collective-permute-start | bytes 589832 | tf_op jit(solution)/shard_map/ppermute | solution.py:174

commit v3 on v2

--- a/solution.py
+++ b/solution.py
@@ -12,12 +12,13 @@
 BLK = 512
 HALF = BLK // 2
 CORES = 2
-CHUNKS = ((0, 2), (2, 5), (5, 8))
+CHUNKS = ((0, 4), (4, 8))
 F32 = jnp.float32
 BF16 = jnp.bfloat16
 NN, NT, TN = ((1,), (0,)), ((1,), (1,)), ((0,), (0,))
 SMEM = pl.BlockSpec(memory_space=pltpu.SMEM)
 VMEM = pl.BlockSpec(memory_space=pltpu.VMEM)
+HBM = pl.BlockSpec(memory_space=pltpu.HBM)
 PARAMS = pltpu.CompilerParams(vmem_limit_bytes=20 * 2**20)
 
 
@@ -33,11 +34,24 @@
     return pl.CostEstimate(flops=flops, bytes_accessed=size, transcendentals=0)
 
 
-def state_kernel(k_ref, v_ref, out_ref):
-    for h in range(k_ref.shape[1] // DH):
-        cols = slice(h * DH, (h + 1) * DH)
-        state = dot(k_ref[:, cols], v_ref[:, cols], TN)
-        out_ref[h * DH : (h + 1) * DH, :] = state.astype(BF16)
+PARTS = 2
+
+
+def state_kernel(k_hbm, v_hbm, out_ref, k_ref, v_ref, sems):
+    width = k_ref.shape[1] // PARTS
+    copies = []
+    for part in range(PARTS):
+        cols = slice(part * width, (part + 1) * width)
+        for at, (hbm, ref) in enumerate(((k_hbm, k_ref), (v_hbm, v_ref))):
+            copy = pltpu.make_async_copy(hbm.at[:, cols], ref.at[:, cols], sems.at[part, at])
+            copy.start()
+            copies.append(copy)
+    for part in range(PARTS):
+        copies[2 * part].wait()
+        copies[2 * part + 1].wait()
+        for h in range(part * width // DH, (part + 1) * width // DH):
+            cols = slice(h * DH, (h + 1) * DH)
+            out_ref[cols, :] = dot(k_ref[:, cols], v_ref[:, cols], TN).astype(BF16)
 
 
 def block_states(k, v):
@@ -45,9 +59,14 @@
     return pl.pallas_call(
         state_kernel,
         name="block_states",
-        in_specs=[VMEM, VMEM],
+        in_specs=[HBM, HBM],
         out_specs=VMEM,
         out_shape=pltpu.VMEM((width, DH), BF16),
+        scratch_shapes=[
+            pltpu.VMEM(k.shape, BF16),
+            pltpu.VMEM(v.shape, BF16),
+            pltpu.SemaphoreType.DMA((PARTS, 2)),
+        ],
         compiler_params=PARAMS,
         cost_estimate=cost(2 * BLK * DH * width, 2 * BLK * width * 2),
     )(k, v)
@@ -116,58 +135,86 @@
 TILE = 256
 
 
-def mix_kernel(column_ref, *refs, plan, first, last):
+def mix_kernel(column_ref, *refs, plan, first):
     count = len(plan)
-    a_refs, w_ref = refs[:count], refs[count]
-    rest = refs[count + 1 :]
+    a_refs, w_hbm, rest = refs[:count], refs[count], refs[count + 1 :]
     if not first:
         total_ref, rest = rest[0], rest[1:]
-    if last:
-        out_hbm, out_ref, sems = rest
-    else:
-        (out_ref,) = rest
-    ways = w_ref.shape[0] // (8 * DH)
+    out_ref, w_ref, sems = rest
+    ways = w_hbm.shape[0] // (8 * DH)
+    copies, at = [], 0
+    for piece, (a_ref, (shift, head)) in enumerate(zip(a_refs, plan)):
+        depth = a_ref.shape[1]
+        source = lax.rem(column_ref[0] + (shift + ways), ways)
+        start = pl.multiple_of(source * (8 * DH) + head * DH, DH)
+        rows = slice(at, at + depth)
+        copies.append(
+            pltpu.make_async_copy(w_hbm.at[pl.ds(start, depth)], w_ref.at[rows], sems.at[piece])
+        )
+        copies[-1].start()
+        at += depth
+    for copy in copies:
+        copy.wait()
+    for tile in range(out_ref.shape[1] // TILE):
+        cols = slice(tile * TILE, (tile + 1) * TILE)
+        total, at = None if first else total_ref[:, cols], 0
+        for a_ref in a_refs:
+            depth = a_ref.shape[1]
+            term = dot(a_ref[...], w_ref[at : at + depth, cols], NN)
+            total = term if total is None else total + term
+            at += depth
+        out_ref[:, cols] = total
+
+
+def mix(column, w, plan, arrays, total=None):
+    width = w.shape[1]
+    operands = [column, *arrays, w] + ([] if total is None else [total])
+    depth = sum(a.shape[1] for a in arrays)
+    specs = [SMEM] + [VMEM] * (len(operands) - 1)
+    specs[1 + len(arrays)] = HBM
+    return pl.pallas_call(
+        functools.partial(mix_kernel, plan=tuple(plan), first=total is None),
+        name="mix",
+        in_specs=specs,
+        out_specs=VMEM,
+        out_shape=pltpu.VMEM((BLK, width), F32),
+        scratch_shapes=[
+            pltpu.VMEM((depth, width), BF16),
+            pltpu.SemaphoreType.DMA((len(arrays),)),
+        ],
+        compiler_params=PARAMS,
+        cost_estimate=cost(2 * BLK * depth * width, 2 * depth * width),
+    )(*operands)
+
+
+def last_kernel(a_ref, w_ref, total_ref, out_hbm, out_ref, sems):
     copies = []
     for tile in range(w_ref.shape[1] // TILE):
         cols = slice(tile * TILE, (tile + 1) * TILE)
-        for low, high in ((0, HALF), (HALF, BLK)):
-            total = None if first else total_ref[low:high, cols]
-            for a_ref, (shift, head, begin, end) in zip(a_refs, plan):
-                if end <= low or begin >= high:
-                    continue
-                source = lax.rem(column_ref[0] + (shift + ways), ways)
-                start = pl.multiple_of(source * (8 * DH) + head * DH, DH)
-                weights = w_ref[pl.ds(start, a_ref.shape[1]), cols]
-                term = dot(a_ref[low - begin : high - begin, :], weights, NN)
-                total = term if total is None else total + term
-            out_ref[low:high, cols] = total.astype(out_ref.dtype)
-        if last:
-            copy = pltpu.make_async_copy(out_ref.at[:, cols], out_hbm.at[:, cols], sems.at[tile])
-            copy.start()
-            copies.append(copy)
+        total = total_ref[:, cols] + dot(a_ref[...], w_ref[:, cols], NN)
+        out_ref[:, cols] = total.astype(BF16)
+        copy = pltpu.make_async_copy(out_ref.at[:, cols], out_hbm.at[:, cols], sems.at[tile])
+        copy.start()
+        copies.append(copy)
     for copy in copies:
         copy.wait()
 
 
-def mix(column, w, plan, arrays, total=None, last=False):
-    width = w.shape[1]
-    operands = [column, *arrays, w] + ([] if total is None else [total])
-    depth = sum(a.size for a in arrays)
-    if last:
-        out_shape = jax.ShapeDtypeStruct((BLK, width), BF16)
-        scratch = [pltpu.VMEM((BLK, width), BF16), pltpu.SemaphoreType.DMA((width // TILE,))]
-    else:
-        out_shape, scratch = pltpu.VMEM((BLK, width), F32), []
-    return pl.pallas_call(
-        functools.partial(mix_kernel, plan=tuple(plan), first=total is None, last=last),
-        name="mix",
-        in_specs=[SMEM] + [VMEM] * (len(operands) - 1),
-        out_specs=pl.BlockSpec(memory_space=pl.ANY) if last else VMEM,
-        out_shape=out_shape,
-        scratch_shapes=scratch,
-        compiler_params=PARAMS,
-        cost_estimate=cost(2 * depth * width, 2 * depth + BLK * width * 8),
-    )(*operands)
+def last_mix(array, w, total):
+    depth, width = w.shape
+    return pl.pallas_call(
+        last_kernel,
+        name="last_mix",
+        in_specs=[VMEM] * 3,
+        out_specs=HBM,
+        out_shape=jax.ShapeDtypeStruct((BLK, width), BF16),
+        scratch_shapes=[
+            pltpu.VMEM((BLK, width), BF16),
+            pltpu.SemaphoreType.DMA((width // TILE,)),
+        ],
+        compiler_params=PARAMS,
+        cost_estimate=cost(2 * BLK * depth * width, BLK * width * 4),
+    )(array, w, total)
 
 
 def along(value, shift, count):
@@ -183,25 +230,24 @@
     other = lax.ppermute(own, "core", [(0, 1), (1, 0)])
     sums = exclusive_sums(core, own, other, chips)
     carried = lax.all_to_all(sums, "chip", 0, 0, tiled=True)
-    q, k, v, w = in_vmem(q), in_vmem(k), in_vmem(v), in_vmem(w)
+    q, k, v = in_vmem(q), in_vmem(k), in_vmem(v)
     gain_row = gain.reshape(1, -1)
-    total, tail = None, []
-    own_plan, own_rows, near = [], [], []
-    for first, last in CHUNKS:
+    own, near, far = [], [], []
+    for at, (first, last) in enumerate(CHUNKS):
         mine = attention(q, k, v, carried, gain_row, first, last)
-        from_left = along(mine, 1, ways)
-        from_right = along(mine, -1, ways)
-        top = along(from_left[:HALF], 1, ways)
-        bottom = along(from_right[HALF:], -1, ways)
-        own_plan.append((0, first, 0, BLK))
-        own_rows.append(mine)
-        near.append(([(-1, first, 0, BLK), (1, first, 0, BLK)], [from_left, from_right]))
-        tail.append(([(2, first, 0, HALF), (2, first, HALF, BLK)], [top, bottom]))
-    total = mix(column, w, own_plan, own_rows)
-    steps = [near[0], near[1], tail[0], near[2], tail[1], tail[2]]
-    for at, (plan, arrays) in enumerate(steps):
-        total = mix(column, w, plan, arrays, total, at == len(steps) - 1)
-    return total
+        left = along(mine, 1, ways)
+        right = along(mine, -1, ways)
+        far.append(along(right, -1, ways) if at % 2 else along(left, 1, ways))
+        own.append(mine)
+        near.append([left, right])
+    heads = [first for first, _ in CHUNKS]
+    total = mix(column, w, [(0, head) for head in heads], own)
+    for head, pair in zip(heads, near):
+        total = mix(column, w, [(-1, head), (1, head)], pair, total)
+    total = mix(column, w, [(2, heads[0])], far[:1], total)
+    row = lax.rem(column[0] + ways // 2, ways) * (8 * DH) + heads[1] * DH
+    tail = in_vmem(lax.dynamic_slice_in_dim(w, row, far[1].shape[1]))
+    return last_mix(far[1], tail, total)
 
 
 def solution(mesh):

time: 102 us -> 91.7 us (0.90); the launches traced: 102 us -> 90.2 us
  starting transfers between devices: 18.4 us -> 8.51 us
  waiting for transfers between devices: 11.8 us -> 16.9 us
  local copies, waits for them, and re-layouts: 12.1 us -> 7.13 us
  Pallas kernels: 18.7 us -> 17.4 us
    ppermute x12 -> x6, starting transfers between devices: 18.4 us -> 8.5 us  [along(): lax.ppermute(value, 'fsdp', [(i, (i + shift) % count) for i in range(coun...]
    ppermute x12 -> x6, waiting for transfers between devices: 10.1 us -> 15.2 us  [along(): lax.ppermute(value, 'fsdp', [(i, (i + shift) % count) for i in range(coun...]
    unnamed x16 -> x14, local copies, waits for them, and re-layouts: 9.23 us -> 5.84 us
    pallas_call x7 -> x4, Pallas kernels: 10.7 us -> 7.32 us  [mix(): pl.pallas_call(functools.partial(mix_kernel, plan=tuple(plan), first=tota...]
    slice x6 -> x0, local copies, waits for them, and re-layouts: 2.86 us -> none  [the longest x3 1.88 us: shards(): top = along(from_left[:HALF], 1, ways)]
    pallas_call x1 -> x2, Pallas kernels: 0.52 us -> 2.68 us  [the longest x1 1.6 us: last_mix(): pl.pallas_call(last_kernel, name='last_mix', in_specs=[VMEM] * 3, out_spe...]
    dynamic_slice x0 -> x1, local copies, waits for them, and re-layouts: none -> 1.29 us  [shards(): tail = in_vmem(lax.dynamic_slice_in_dim(w, row, far[1].shape[1]))]
    pallas_call x3 -> x2, Pallas kernels: 6.48 us -> 6.33 us  [attention(): pl.pallas_call(functools.partial(attention_kernel, first=first), name='at...]
  transfers between devices with their start and end apart: 13 -> 7, of which waited for: 2 -> 6; matrix products, arithmetic and copies ran while one was open for 3% -> 1% of each run, Pallas kernels for 13% -> 12%
where the time goes in v3:
time: 91.7 us; the launch traced here: 90.2 us
  blocking collectives  40 us (44%)
  Pallas kernels  17.4 us (19%)
  waiting for transfers between devices  16.9 us (18%)
  starting transfers between devices  8.51 us (9%)
  local copies, waits for them, and re-layouts  7.13 us (8%)
    all_to_all x1, blocking collectives, shards(): own = lax.all_to_all(states, 'chip', 0, 0, tiled=True)  23.1 us
    all_to_all x1, blocking collectives, shards(): carried = lax.all_to_all(sums, 'chip', 0, 0, tiled=True)  16.9 us
    ppermute x6, waiting for transfers between devices, along(): lax.ppermute(value, 'fsdp', [(i, (i + shift) % count) for i in range(coun...  15.2 us
    ppermute x6, starting transfers between devices, along(): lax.ppermute(value, 'fsdp', [(i, (i + shift) % count) for i in range(coun...  8.5 us
    pallas_call x4, Pallas kernels, mix(): pl.pallas_call(functools.partial(mix_kernel, plan=tuple(plan), first=tota...  7.32 us
    pallas_call x2, Pallas kernels, attention(): pl.pallas_call(functools.partial(attention_kernel, first=first), name='at...  6.33 us
    unnamed x14, local copies, waits for them, and re-layouts  5.84 us
  transfers between devices with their start and end apart: 7, of which 6 were waited for; matrix products, arithmetic and copies ran while one was open for 1% of the time, Pallas kernels for 12%

profile of v3, /device:TPU:32, one launch (start us, length us, event | category | flops | bytes accessed | tf_op | source)
XLA Modules:
  0.0 90.2 jit_solution(12267068396723367123)
XLA Ops:
  0.0 1.2 %copy-done.1 = bf16[512,1024]{1,0:T(8,128)(2,1)S(1)} copy-done((bf16[512,1024]{1,0:T(8,128)(2,1)S(1)}, bf16[512,1024]{1,0:T(8,128)(2,1)}, u32[]{:S(2)}) %copy-start.1) | copy-done | bytes 1048600
  1.2 1.2 %copy-done.3 = bf16[512,1024]{1,0:T(8,128)(2,1)S(1)} copy-done((bf16[512,1024]{1,0:T(8,128)(2,1)S(1)}, bf16[512,1024]{1,0:T(8,128)(2,1)}, u32[]{:S(2)}) %copy-start.3) | copy-done | bytes 1048600
  2.5 1.1 %block_states.1 = bf16[1024,128]{1,0:T(8,128)(2,1)S(1)} custom-call(bf16[512,1024]{1,0:T(8,128)(2,1)S(1)} %copy-done.1, bf16[512,1024]{1,0:T(8,128)(2,1)S(1)} %copy-done.3), custom_call_target="tpu_custom_call" | custom-call | flops 134217728 | bytes 2097152 | tf_op jit(solution)/shard_map/block_states/pallas_call | solution.py:59
  3.5 23.1 %all_to_all.22 = bf16[32,32,128]{2,1,0:T(8,128)(2,1)S(1)} all-to-all(bf16[32,32,128]{2,1,0:T(8,128)(2,1)S(1)} %bitcast.9), channel_id=1, replica_groups=mesh['chip'=32,'core'=2,'fsdp'=4] {'chip'}, dimensions={0} | all-to-all | bytes 524288 | tf_op jit(solution)/shard_map/all_to_all | solution.py:229
  26.7 1.7 %collective-permute-done.other_ref = bf16[1024,128]{1,0:T(8,128)(2,1)} collective-permute-done((bf16[1024,128]{1,0:T(8,128)(2,1)S(1)}, bf16[1024,128]{1,0:T(8,128)(2,1)}, u32[]{:S(2)}, u32[]{:S(2)}) %collective-permute-start) | collective-permute-done | bytes 262176 | tf_op jit(solution)/shard_map/ppermute | solution.py:230
  28.4 1.1 %exclusive_sums.1 = bf16[1024,128]{1,0:T(8,128)(2,1)S(1)} custom-call(s32[1]{0:T(128)} %bitcast.core_ref, bf16[1024,128]{1,0:T(8,128)(2,1)S(1)} %bitcast.11, bf16[1024,128]{1,0:T(8,128)(2,1)} %collective-permute-done.other_ref), custom_call_target="tpu_custom_call" | custom-call | flops 524288 | bytes 786432 | tf_op jit(solution)/shard_map/exclusive_sums/pallas_call | solution.py:87
  29.4 16.9 %all_to_all.23 = bf16[32,32,128]{2,1,0:T(8,128)(2,1)S(1)} all-to-all(bf16[32,32,128]{2,1,0:T(8,128)(2,1)S(1)} %bitcast.12), channel_id=1, replica_groups=mesh['chip'=32,'core'=2,'fsdp'=4] {'chip'}, dimensions={0} | all-to-all | bytes 524288 | tf_op jit(solution)/shard_map/all_to_all | solution.py:232
  46.3 3.2 %attention.3.refs_0_ = bf16[512,512]{1,0:T(8,128)(2,1)} custom-call(bf16[512,1024]{1,0:T(8,128)(2,1)S(1)} %copy-done.5, bf16[512,1024]{1,0:T(8,128)(2,1)S(1)} %copy-done.2, bf16[512,1024]{1,0:T(8,128)(2,1)S(1)} %copy-done.4, bf16[1024,128]{1,0:T(8,128)(2,1)S(1)} %bitcast.7, f32[1,1024]{1,0:T(1,128)S(1)} %bitcast.13), custom_call_target="tpu_custom_call" | custom-call | flops 536870912 | bytes 2097152 | tf_op jit(solution)/shard_map/attention/pallas_call | solution.py:124
  49.5 1.6 %collective-permute-start.3 = (bf16[512,512]{1,0:T(8,128)(2,1)}, bf16[512,512]{1,0:T(8,128)(2,1)}, u32[]{:S(2)}, u32[]{:S(2)}) collective-permute-start(bf16[512,512]{1,0:T(8,128)(2,1)} %attention.3.refs_0_), channel_id=1, source_target_pairs={{0,1},{1,2},{2,3},{3,0},{4,5},{5,6},{6,7},{7,4},{8,9},{9,10},{10,1... | collective-permute-start | bytes 1572872 | tf_op jit(solution)/shard_map/ppermute | solution.py:221
  51.1 3.2 %attention.2.refs_1_ = bf16[512,512]{1,0:T(8,128)(2,1)} custom-call(bf16[512,1024]{1,0:T(8,128)(2,1)S(1)} %copy-done.5, bf16[512,1024]{1,0:T(8,128)(2,1)S(1)} %copy-done.2, bf16[512,1024]{1,0:T(8,128)(2,1)S(1)} %copy-done.4, bf16[1024,128]{1,0:T(8,128)(2,1)S(1)} %bitcast.8, f32[1,1024]{1,0:T(1,128)S(1)} %bitcast.14), custom_call_target="tpu_custom_call" | custom-call | flops 536870912 | bytes 2097152 | tf_op jit(solution)/shard_map/attention/pallas_call | solution.py:124
  54.2 1.7 %collective-permute-start.1 = (bf16[512,512]{1,0:T(8,128)(2,1)}, bf16[512,512]{1,0:T(8,128)(2,1)S(1)}, u32[]{:S(2)}, u32[]{:S(2)}) collective-permute-start(bf16[512,512]{1,0:T(8,128)(2,1)} %attention.2.refs_1_), channel_id=1, source_target_pairs={{0,3},{1,0},{2,1},{3,2},{4,7},{5,4},{6,5},{7,6},{8,11},{9,8},{10,9... | collective-permute-start | bytes 1572872 | tf_op jit(solution)/shard_map/ppermute | solution.py:221
  55.9 1.8 %collective-permute-start.6 = (bf16[512,512]{1,0:T(8,128)(2,1)}, bf16[512,512]{1,0:T(8,128)(2,1)S(1)}, u32[]{:S(2)}, u32[]{:S(2)}) collective-permute-start(bf16[512,512]{1,0:T(8,128)(2,1)} %attention.3.refs_0_), channel_id=1, source_target_pairs={{0,3},{1,0},{2,1},{3,2},{4,7},{5,4},{6,5},{7,6},{8,11},{9,8},{10,9... | collective-permute-start | bytes 1572872 | tf_op jit(solution)/shard_map/ppermute | solution.py:221
  57.9 8.0 %collective-permute-done.3.refs_0_ = bf16[512,512]{1,0:T(8,128)(2,1)} collective-permute-done((bf16[512,512]{1,0:T(8,128)(2,1)}, bf16[512,512]{1,0:T(8,128)(2,1)}, u32[]{:S(2)}, u32[]{:S(2)}) %collective-permute-start.3) | collective-permute-done | bytes 524320 | tf_op jit(solution)/shard_map/ppermute | solution.py:221
  66.3 3.1 %collective-permute-done.1.refs_1_ = bf16[512,512]{1,0:T(8,128)(2,1)S(1)} collective-permute-done((bf16[512,512]{1,0:T(8,128)(2,1)}, bf16[512,512]{1,0:T(8,128)(2,1)S(1)}, u32[]{:S(2)}, u32[]{:S(2)}) %collective-permute-start.1) | collective-permute-done | bytes 524320 | tf_op jit(solution)/shard_map/ppermute | solution.py:221
  69.3 2.9 %collective-permute-start.2 = (bf16[512,512]{1,0:T(8,128)(2,1)S(1)}, bf16[512,512]{1,0:T(8,128)(2,1)S(1)}, u32[]{:S(2)}, u32[]{:S(2)}) collective-permute-start(bf16[512,512]{1,0:T(8,128)(2,1)S(1)} %collective-permute-done.1.refs_1_), channel_id=1, source_target_pairs={{0,3},{1,0},{2,1},{3,2},{4,7},{5,4},{6,5},{7,6},{8,11},{9,8},{10,9... | collective-permute-start | bytes 1572872 | tf_op jit(solution)/shard_map/ppermute | solution.py:221
  72.2 1.3 %constant_dynamic-slice_fusion.w_ref = bf16[512,1024]{1,0:T(8,128)(2,1)S(1)} fusion(bf16[4096,1024]{1,0:T(8,128)(2,1)} %refs_1_.1, s32[]{:T(128)S(6)} %select_n.3), kind=kLoop, calls=%fused_computation | loop fusion | bytes 2097156 | tf_op jit(solution)/shard_map/dynamic_slice | solution.py:249
  73.5 3.4 %copy-done = bf16[4096,1024]{1,0:T(8,128)(2,1)S(1)} copy-done((bf16[4096,1024]{1,0:T(8,128)(2,1)S(1)}, bf16[4096,1024]{1,0:T(8,128)(2,1)}, u32[]{:S(2)}) %copy-start) | copy-done | bytes 8388632
  76.9 2.6 %mix.4.refs_3_ = f32[512,1024]{1,0:T(8,128)S(1)} custom-call(s32[1]{0:T(128)} %bitcast.6.column_ref, bf16[512,512]{1,0:T(8,128)(2,1)} %attention.3.refs_0_, bf16[512,512]{1,0:T(8,128)(2,1)} %attention.2.refs_1_, bf16[4096,1024]{1,0:T(8,128)(2,1)S(1)} %copy-done), custom_call_target="tpu_custom_call" | custom-call | flops 1073741824 | bytes 2097152 | tf_op jit(solution)/shard_map/mix/pallas_call | solution.py:175
  79.5 1.1 %collective-permute-done.6.refs_1_ = bf16[512,512]{1,0:T(8,128)(2,1)S(1)} collective-permute-done((bf16[512,512]{1,0:T(8,128)(2,1)}, bf16[512,512]{1,0:T(8,128)(2,1)S(1)}, u32[]{:S(2)}, u32[]{:S(2)}) %collective-permute-start.6) | collective-permute-done | bytes 524320 | tf_op jit(solution)/shard_map/ppermute | solution.py:221
  80.5 2.5 %mix.5.refs_3_ = f32[512,1024]{1,0:T(8,128)S(1)} custom-call(s32[1]{0:T(128)} %bitcast.6.column_ref, bf16[512,512]{1,0:T(8,128)(2,1)} %collective-permute-done.3.refs_0_, bf16[512,512]{1,0:T(8,128)(2,1)S(1)} %collective-permute-done.6.refs_1_, bf16[4096,1024]{1,0:T(8,128)(2,1)S(1)} %copy-done, f32[512,1024]{1,0:T(8,128)S(1)} %mix.4.refs_3_), custom_call_target="tpu_custom_call" | custom-call | flops 1073741824 | bytes 2097152 | tf_op jit(solution)/shard_map/mix/pallas_call | solution.py:175
  83.0 1.4 %mix.6.refs_2_ = f32[512,1024]{1,0:T(8,128)S(1)} custom-call(s32[1]{0:T(128)} %bitcast.6.column_ref, bf16[512,512]{1,0:T(8,128)(2,1)S(1)} %collective-permute-done.5.refs_0_, bf16[512,512]{1,0:T(8,128)(2,1)S(1)} %collective-permute-done.1.refs_1_, bf16[4096,1024]{1,0:T(8,128)(2,1)S(1)} %copy-done, f32[512,1024]{1,0:T(8,128)S(1)} %mix.5.refs_3_), custom_call_target="tpu_custom_call" | custom-call | flops 1073741824 | bytes 2097152 | tf_op jit(solution)/shard_map/mix/pallas_call | solution.py:175
  85.2 0.8 mix.7.total_ref
  86.0 2.4 %collective-permute-done.2.a_ref = bf16[512,512]{1,0:T(8,128)(2,1)S(1)} collective-permute-done((bf16[512,512]{1,0:T(8,128)(2,1)S(1)}, bf16[512,512]{1,0:T(8,128)(2,1)S(1)}, u32[]{:S(2)}, u32[]{:S(2)}) %collective-permute-start.2) | collective-permute-done | bytes 524320 | tf_op jit(solution)/shard_map/ppermute | solution.py:221
  88.4 1.6 %last_mix.1 = bf16[512,1024]{1,0:T(8,128)(2,1)} custom-call(bf16[512,512]{1,0:T(8,128)(2,1)S(1)} %collective-permute-done.2.a_ref, bf16[512,1024]{1,0:T(8,128)(2,1)S(1)} %constant_dynamic-slice_fusion.w_ref, f32[512,1024]{1,0:T(8,128)S(1)} %mix.7.total_ref), custom_call_target="tpu_custom_call" | custom-call | flops 536870912 | bytes 2097152 | tf_op jit(solution)/shard_map/last_mix/pallas_call | solution.py:205
  (16 shorter events, 1.4 us)
Async XLA Ops:
  0.0 1.2 %copy-start.1 = (bf16[512,1024]{1,0:T(8,128)(2,1)S(1)}, bf16[512,1024]{1,0:T(8,128)(2,1)}, u32[]{:S(2)}) copy-start(bf16[512,1024]{1,0:T(8,128)(2,1)} %k_ref.3) | copy-start | bytes 3145732
  1.2 1.2 %copy-start.3 = (bf16[512,1024]{1,0:T(8,128)(2,1)S(1)}, bf16[512,1024]{1,0:T(8,128)(2,1)}, u32[]{:S(2)}) copy-start(bf16[512,1024]{1,0:T(8,128)(2,1)} %v_ref.3) | copy-start | bytes 3145732
  2.5 43.9 %copy-start.2 = (bf16[512,1024]{1,0:T(8,128)(2,1)S(1)}, bf16[512,1024]{1,0:T(8,128)(2,1)}, u32[]{:S(2)}) copy-start(bf16[512,1024]{1,0:T(8,128)(2,1)} %k_ref.3) | copy-start | bytes 3145732
  2.5 43.9 %copy-start.4 = (bf16[512,1024]{1,0:T(8,128)(2,1)S(1)}, bf16[512,1024]{1,0:T(8,128)(2,1)}, u32[]{:S(2)}) copy-start(bf16[512,1024]{1,0:T(8,128)(2,1)} %v_ref.3) | copy-start | bytes 3145732
  2.5 43.9 %copy-start.5 = (bf16[512,1024]{1,0:T(8,128)(2,1)S(1)}, bf16[512,1024]{1,0:T(8,128)(2,1)}, u32[]{:S(2)}) copy-start(bf16[512,1024]{1,0:T(8,128)(2,1)} %q_ref.3) | copy-start | bytes 3145732
  2.5 43.9 %copy-start.6 = (f32[1024]{0:T(1024)S(1)}, f32[1024]{0:T(1024)}, u32[]{:S(2)}) copy-start(f32[1024]{0:T(1024)} %param.8) | copy-start | bytes 12292
  26.7 1.7 %collective-permute-start = (bf16[1024,128]{1,0:T(8,128)(2,1)S(1)}, bf16[1024,128]{1,0:T(8,128)(2,1)}, u32[]{:S(2)}, u32[]{:S(2)}) collective-permute-start(bf16[1024,128]{1,0:T(8,128)(2,1)S(1)} %bitcast.10), channel_id=1, source_target_pairs={{0,4},{4,0},{1,5},{5,1},{2,6},{6,2},{3,7},{7,3},{8,12},{12,8},{9,1... | collective-permute-start | bytes 786440 | tf_op jit(solution)/shard_map/ppermute | solution.py:230
  49.5 16.4 %collective-permute-start.3 = (bf16[512,512]{1,0:T(8,128)(2,1)}, bf16[512,512]{1,0:T(8,128)(2,1)}, u32[]{:S(2)}, u32[]{:S(2)}) collective-permute-start(bf16[512,512]{1,0:T(8,128)(2,1)} %attention.3.refs_0_), channel_id=1, source_target_pairs={{0,1},{1,2},{2,3},{3,0},{4,5},{5,6},{6,7},{7,4},{8,9},{9,10},{10,1... | collective-permute-start | bytes 1572872 | tf_op jit(solution)/shard_map/ppermute | solution.py:221
  54.2 15.1 %collective-permute-start.1 = (bf16[512,512]{1,0:T(8,128)(2,1)}, bf16[512,512]{1,0:T(8,128)(2,1)S(1)}, u32[]{:S(2)}, u32[]{:S(2)}) collective-permute-start(bf16[512,512]{1,0:T(8,128)(2,1)} %attention.2.refs_1_), channel_id=1, source_target_pairs={{0,3},{1,0},{2,1},{3,2},{4,7},{5,4},{6,5},{7,6},{8,11},{9,8},{10,9... | collective-permute-start | bytes 1572872 | tf_op jit(solution)/shard_map/ppermute | solution.py:221
  55.9 24.6 %collective-permute-start.6 = (bf16[512,512]{1,0:T(8,128)(2,1)}, bf16[512,512]{1,0:T(8,128)(2,1)S(1)}, u32[]{:S(2)}, u32[]{:S(2)}) collective-permute-start(bf16[512,512]{1,0:T(8,128)(2,1)} %attention.3.refs_0_), channel_id=1, source_target_pairs={{0,3},{1,0},{2,1},{3,2},{4,7},{5,4},{6,5},{7,6},{8,11},{9,8},{10,9... | collective-permute-start | bytes 1572872 | tf_op jit(solution)/shard_map/ppermute | solution.py:221
  57.7 25.3 %collective-permute-start.5 = (bf16[512,512]{1,0:T(8,128)(2,1)}, bf16[512,512]{1,0:T(8,128)(2,1)S(1)}, u32[]{:S(2)}, u32[]{:S(2)}) collective-permute-start(bf16[512,512]{1,0:T(8,128)(2,1)} %attention.2.refs_1_), channel_id=1, source_target_pairs={{0,1},{1,2},{2,3},{3,0},{4,5},{5,6},{6,7},{7,4},{8,9},{9,10},{10,1... | collective-permute-start | bytes 1572872 | tf_op jit(solution)/shard_map/ppermute | solution.py:221
  65.9 19.3 %collective-permute-start.4 = (bf16[512,512]{1,0:T(8,128)(2,1)}, bf16[512,512]{1,0:T(8,128)(2,1)S(1)}, u32[]{:S(2)}, u32[]{:S(2)}) collective-permute-start(bf16[512,512]{1,0:T(8,128)(2,1)} %collective-permute-done.3.refs_0_), channel_id=1, source_target_pairs={{0,1},{1,2},{2,3},{3,0},{4,5},{5,6},{6,7},{7,4},{8,9},{9,10},{10,1... | collective-permute-start | bytes 1572872 | tf_op jit(solution)/shard_map/ppermute | solution.py:221
  69.3 19.1 %collective-permute-start.2 = (bf16[512,512]{1,0:T(8,128)(2,1)S(1)}, bf16[512,512]{1,0:T(8,128)(2,1)S(1)}, u32[]{:S(2)}, u32[]{:S(2)}) collective-permute-start(bf16[512,512]{1,0:T(8,128)(2,1)S(1)} %collective-permute-done.1.refs_1_), channel_id=1, source_target_pairs={{0,3},{1,0},{2,1},{3,2},{4,7},{5,4},{6,5},{7,6},{8,11},{9,8},{10,9... | collective-permute-start | bytes 1572872 | tf_op jit(solution)/shard_map/ppermute | solution.py:221
  73.5 3.4 %copy-start = (bf16[4096,1024]{1,0:T(8,128)(2,1)S(1)}, bf16[4096,1024]{1,0:T(8,128)(2,1)}, u32[]{:S(2)}) copy-start(bf16[4096,1024]{1,0:T(8,128)(2,1)} %refs_1_.1) | copy-start | bytes 25165828

commit v4 on v3

v4 whole, which is shorter than its diff:
```python
import functools

import jax
import jax.numpy as jnp
from jax import lax
from jax.experimental import pallas as pl
from jax.experimental.pallas import tpu as pltpu
from jax.sharding import Mesh
from jax.sharding import PartitionSpec as P

DH = 128
BLK = 512
HALF = BLK // 2
CORES = 2
HEADS = 8
LATE = 5
EARLY = HEADS - LATE
GAIN_ROWS = 16
CALLS = (((0, 1), (1, 2)), ((2, 3), (3, 5)))
F32 = jnp.float32
BF16 = jnp.bfloat16
NN, NT, TN = ((1,), (0,)), ((1,), (1,)), ((0,), (0,))
SMEM = pl.BlockSpec(memory_space=pltpu.SMEM)
VMEM = pl.BlockSpec(memory_space=pltpu.VMEM)
HBM = pl.BlockSpec(memory_space=pltpu.HBM)
PARAMS = pltpu.CompilerParams(vmem_limit_bytes=20 * 2**20)


def dot(a, b, dims):
    return lax.dot_general(a, b, (dims, ((), ())), preferred_element_type=F32)


def in_vmem(value):
    return pltpu.with_memory_space_constraint(value, pltpu.VMEM)


def in_hbm(value):
    return pltpu.with_memory_space_constraint(value, pltpu.HBM)


def cost(flops, size):
    return pl.CostEstimate(flops=flops, bytes_accessed=size, transcendentals=0)


def within_block(q_ref, k_ref, v_ref, h, causal, shift=0):
    cols, query_cols = slice(h * DH, (h + 1) * DH), slice((h - shift) * DH, (h - shift + 1) * DH)
    q0, q1 = q_ref[:HALF, query_cols], q_ref[HALF:, query_cols]
    k0, k1 = k_ref[:HALF, cols], k_ref[HALF:, cols]
    v0, v1 = v_ref[:HALF, cols], v_ref[HALF:, cols]
    s00 = jnp.where(causal, dot(q0, k0, NT), 0.0).astype(BF16)
    s10 = dot(q1, k0, NT).astype(BF16)
    s11 = jnp.where(causal, dot(q1, k1, NT), 0.0).astype(BF16)
    return dot(s00, v0, NN), dot(s10, v0, NN) + dot(s11, v1, NN)


def causal_mask():
    row = lax.broadcasted_iota(jnp.int32, (HALF, HALF), 0)
    col = lax.broadcasted_iota(jnp.int32, (HALF, HALF), 1)
    return col <= row


def finish(queries, within, state, gain):
    att = within + dot(queries, state, NN)
    mean = jnp.full((DH, DH), 1.0 / DH, BF16)
    mean_square = dot((att * att).astype(BF16), mean, NN)
    return (att * lax.rsqrt(mean_square + 1e-6) * gain).astype(BF16)


def state_kernel(q_hbm, k_hbm, v_hbm, gain_ref, out_ref, early_ref, q_ref, k_ref, v_ref, sems):
    early = slice(LATE * DH, HEADS * DH)
    late = slice(0, LATE * DH)
    copies = [
        pltpu.make_async_copy(hbm.at[:, cols], ref.at[:, cols], sems.at[at])
        for at, (hbm, ref, cols) in enumerate(
            (
                (k_hbm, k_ref, early),
                (v_hbm, v_ref, early),
                (k_hbm, k_ref, late),
                (v_hbm, v_ref, late),
            )
        )
    ]
    copies.append(pltpu.make_async_copy(q_hbm.at[:, early], q_ref, sems.at[4]))
    for copy in copies:
        copy.start()
    gain = gain_ref[:, early]
    high = gain.astype(BF16)
    rest = gain - high.astype(F32)
    middle = rest.astype(BF16)
    low = (rest - middle.astype(F32)).astype(BF16)
    blank = jnp.zeros((GAIN_ROWS - 3, EARLY * DH), BF16)
    early_ref[BLK:, : EARLY * DH] = jnp.concatenate([high, middle, low, blank])
    early_ref[BLK:, EARLY * DH :] = jnp.zeros((GAIN_ROWS, EARLY * DH), BF16)
    causal = causal_mask()

    def state(h):
        cols = slice(h * DH, (h + 1) * DH)
        out_ref[cols, :] = dot(k_ref[:, cols], v_ref[:, cols], TN).astype(BF16)

    copies[0].wait()
    copies[1].wait()
    for h in range(LATE, HEADS):
        state(h)
    copies[4].wait()
    early_ref[:BLK, : EARLY * DH] = q_ref[...]
    for h in range(LATE, HEADS):
        top, bottom = within_block(q_ref, k_ref, v_ref, h, causal, LATE)
        cols = slice((EARLY + h - LATE) * DH, (EARLY + h - LATE + 1) * DH)
        early_ref[:HALF, cols] = top.astype(BF16)
        early_ref[HALF:BLK, cols] = bottom.astype(BF16)
    copies[2].wait()
    copies[3].wait()
    for h in range(LATE):
        state(h)


def block_states(q, k, v, gain):
    width = k.shape[1]
    return pl.pallas_call(
        state_kernel,
        name="block_states",
        in_specs=[HBM, HBM, HBM, VMEM],
        out_specs=[VMEM, VMEM],
        out_shape=[
            pltpu.VMEM((width, DH), BF16),
            jax.ShapeDtypeStruct((BLK + GAIN_ROWS, 2 * EARLY * DH), BF16),
        ],
        scratch_shapes=[
            pltpu.VMEM((BLK, EARLY * DH), BF16),
            pltpu.VMEM(k.shape, BF16),
            pltpu.VMEM(v.shape, BF16),
            pltpu.SemaphoreType.DMA((5,)),
        ],
        compiler_params=PARAMS,
        cost_estimate=cost(2 * BLK * DH * width, 2 * BLK * width * 2),
    )(in_hbm(q), in_hbm(k), in_hbm(v), gain)


def scan_kernel(core_ref, own_ref, other_ref, out_ref, *, chips):
    rows = own_ref.shape[0] // chips
    second = (core_ref[0] == 1).astype(F32)
    before = jnp.zeros((rows, DH), F32)
    for chip in range(chips):
        at = slice(chip * rows, (chip + 1) * rows)
        other = other_ref[at, :].astype(F32)
        out_ref[at, :] = (before + second * other).astype(BF16)
        before = before + (own_ref[at, :].astype(F32) + other)


def exclusive_sums(core, own, other, chips):
    return pl.pallas_call(
        functools.partial(scan_kernel, chips=chips),
        name="exclusive_sums",
        in_specs=[SMEM, VMEM, VMEM],
        out_specs=VMEM,
        out_shape=pltpu.VMEM(own.shape, BF16),
        compiler_params=PARAMS,
        cost_estimate=cost(own.size * 4, own.size * 6),
    )(core, own, other)


def attention_kernel(q_ref, k_ref, v_ref, carried_ref, gain_ref, *out_refs, groups, states):
    causal = causal_mask()
    for out_ref, (first, last) in zip(out_refs, groups):
        for h in range(first, last):
            cols = slice(h * DH, (h + 1) * DH)
            out_cols = slice((h - first) * DH, (h - first + 1) * DH)
            parts = within_block(q_ref, k_ref, v_ref, h, causal)
            for rows, within in zip((slice(0, HALF), slice(HALF, BLK)), parts):
                out_ref[rows, out_cols] = finish(
                    q_ref[rows, cols], within, carried_ref[cols, :], gain_ref[:, cols]
                )
    if states:
        out_refs[0][BLK:, :] = carried_ref[LATE * DH :, :]


def attention(q, k, v, carried, gain, groups, states=False):
    heads = sum(last - first for first, last in groups)
    shapes = [(BLK, (last - first) * DH) for first, last in groups]
    if states:
        shapes[0] = (BLK + EARLY * DH, DH)
    return pl.pallas_call(
        functools.partial(attention_kernel, groups=groups, states=states),
        name="attention",
        in_specs=[VMEM] * 5,
        out_specs=[VMEM] * len(shapes),
        out_shape=[pltpu.VMEM(shape, BF16) for shape in shapes],
        compiler_params=PARAMS,
        cost_estimate=cost(4 * BLK * BLK * DH * heads, BLK * DH * heads * 8),
    )(q, k, v, carried, gain)


TILE = 256


def mix_kernel(column_ref, *refs, plan, first, early):
    count = len(plan)
    a_refs, rest = refs[:count], refs[count:]
    if early:
        g_hbm, rest = rest[0], rest[1:]
    w_hbm, rest = rest[0], rest[1:]
    if not first:
        total_ref, rest = rest[0], rest[1:]
    out_ref, w_ref, sems, rest = rest[0], rest[1], rest[2], rest[3:]
    if early:
        g_ref, normed_ref, g_sems = rest
    ways = w_hbm.shape[0] // (HEADS * DH)
    copies, g_copies, at = [], [], 0
    for piece, (shift, head, heads) in enumerate(plan):
        depth = heads * DH
        source = lax.rem(column_ref[0] + (shift + ways), ways)
        start = pl.multiple_of(source * (HEADS * DH) + head * DH, DH)
        copies.append(
            pltpu.make_async_copy(
                w_hbm.at[pl.ds(start, depth)], w_ref.at[at : at + depth], sems.at[piece]
            )
        )
        at += depth
        if early:
            height = BLK + GAIN_ROWS
            g_rows = pl.ds(pl.multiple_of(source * height, GAIN_ROWS), height)
            g_copies.append(
                pltpu.make_async_copy(g_hbm.at[g_rows], g_ref.at[piece], g_sems.at[piece])
            )
    for copy in g_copies + copies:
        copy.start()
    if early:
        for piece, a_ref in enumerate(a_refs):
            g_copies[piece].wait()
            for h in range(EARLY):
                cols = slice(h * DH, (h + 1) * DH)
                terms = g_ref[piece, BLK:, cols].astype(F32)
                gain = terms[0:1] + terms[1:2] + terms[2:3]
                within = g_ref[piece, :BLK, (EARLY + h) * DH : (EARLY + h + 1) * DH]
                state = a_ref[BLK + h * DH : BLK + (h + 1) * DH, :]
                normed_ref[piece, :, cols] = finish(
                    g_ref[piece, :BLK, cols], within.astype(F32), state, gain
                )
    for copy in copies:
        copy.wait()
    for tile in range(out_ref.shape[1] // TILE):
        cols = slice(tile * TILE, (tile + 1) * TILE)
        total, at = None if first else total_ref[:, cols], 0
        for piece, (a_ref, (_, _, heads)) in enumerate(zip(a_refs, plan)):
            depth = heads * DH
            rows = normed_ref[piece] if early else a_ref[:BLK, :]
            term = dot(rows, w_ref[at : at + depth, cols], NN)
            total = term if total is None else total + term
            at += depth
        out_ref[:, cols] = total


def mix(column, w, plan, arrays, total=None, gathered=None):
    width, early = w.shape[1], gathered is not None
    operands = [column, *arrays]
    specs = [SMEM] + [VMEM] * len(arrays)
    for value in ([gathered] if early else []) + [w]:
        operands.append(value)
        specs.append(HBM)
    if total is not None:
        operands.append(total)
        specs.append(VMEM)
    depth = sum(heads for _, _, heads in plan) * DH
    scratch = [
        pltpu.VMEM((depth, width), BF16),
        pltpu.SemaphoreType.DMA((len(arrays),)),
    ]
    if early:
        scratch += [
            pltpu.VMEM((len(arrays), BLK + GAIN_ROWS, 2 * EARLY * DH), BF16),
            pltpu.VMEM((len(arrays), BLK, EARLY * DH), BF16),
            pltpu.SemaphoreType.DMA((len(arrays),)),
        ]
    return pl.pallas_call(
        functools.partial(mix_kernel, plan=tuple(plan), first=total is None, early=early),
        name="mix_early" if early else "mix",
        in_specs=specs,
        out_specs=VMEM,
        out_shape=pltpu.VMEM((BLK, width), F32),
        scratch_shapes=scratch,
        compiler_params=PARAMS,
        cost_estimate=cost(2 * BLK * depth * width, 2 * depth * width),
    )(*operands)


def last_kernel(*refs):
    *a_refs, w_ref, total_ref, out_hbm, out_ref, sems = refs
    copies = []
    for tile in range(w_ref.shape[1] // TILE):
        cols = slice(tile * TILE, (tile + 1) * TILE)
        total, at = total_ref[:, cols], 0
        for a_ref in a_refs:
            depth = a_ref.shape[1]
            total = total + dot(a_ref[...], w_ref[at : at + depth, cols], NN)
            at += depth
        out_ref[:, cols] = total.astype(BF16)
        copy = pltpu.make_async_copy(out_ref.at[:, cols], out_hbm.at[:, cols], sems.at[tile])
        copy.start()
        copies.append(copy)
    for copy in copies:
        copy.wait()


def last_mix(arrays, w, total):
    depth, width = w.shape
    return pl.pallas_call(
        last_kernel,
        name="last_mix",
        in_specs=[VMEM] * (len(arrays) + 2),
        out_specs=HBM,
        out_shape=jax.ShapeDtypeStruct((BLK, width), BF16),
        scratch_shapes=[
            pltpu.VMEM((BLK, width), BF16),
            pltpu.SemaphoreType.DMA((width // TILE,)),
        ],
        compiler_params=PARAMS,
        cost_estimate=cost(2 * BLK * depth * width, BLK * width * 4),
    )(*arrays, w, total)


def along(value, shift, count):
    return lax.ppermute(value, "fsdp", [(i, (i + shift) % count) for i in range(count)])


def shards(q, k, v, gain, w):
    chips, ways = lax.axis_size("chip"), lax.axis_size("fsdp")
    core = lax.axis_index("core").reshape(1)
    column = lax.axis_index("fsdp").reshape(1)
    gain_row = gain.reshape(1, -1)
    states, early = block_states(q, k, v, gain_row)
    gathered = in_hbm(lax.all_gather(early, "fsdp", axis=0, tiled=True))
    own = lax.all_to_all(states, "chip", 0, 0, tiled=True)
    other = lax.ppermute(own, "core", [(0, 1), (1, 0)])
    sums = exclusive_sums(core, own, other, chips)
    carried = lax.all_to_all(sums, "chip", 0, 0, tiled=True)
    q, k, v, weights = in_vmem(q), in_vmem(k), in_vmem(v), in_hbm(w)
    groups, mine, left, right, far = [], [], [], [], []
    for call, pair in enumerate(CALLS):
        groups += pair
        mine += attention(q, k, v, carried, gain_row, pair, call == 0)
    for at, value in enumerate(mine):
        left.append(along(value, 1, ways))
        right.append(along(value, -1, ways))
        far.append(along(right[at], -1, ways) if at % 2 else along(left[at], 1, ways))
    mine += attention(q, k, v, carried, gain_row, ((LATE, HEADS),))

    def plan(shift, groups):
        return [(shift, first, last - first) for first, last in groups]

    early_rows = ((LATE, HEADS),)
    total = mix(column, weights, plan(0, (*groups, *early_rows)), mine)
    sides = plan(-1, early_rows) + plan(1, early_rows)
    total = mix(column, weights, sides, [left[0], right[0]], total, gathered)
    for a, b in ((0, 2), (2, 4)):
        sides = plan(-1, groups[a:b]) + plan(1, groups[a:b])
        total = mix(column, weights, sides, left[a:b] + right[a:b], total)
    total = mix(column, weights, plan(2, early_rows), far[:1], total, gathered)
    total = mix(column, weights, plan(2, groups[:2]), far[:2], total)
    row = lax.rem(column[0] + ways // 2, ways) * (HEADS * DH) + groups[2][0] * DH
    depth = (groups[3][1] - groups[2][0]) * DH
    tail = in_vmem(lax.dynamic_slice_in_dim(w, row, depth))
    return last_mix(far[2:], tail, total)


def solution(mesh):
    seq, fsdp = mesh.devices.shape
    fine = Mesh(mesh.devices.reshape(seq // CORES, CORES, fsdp), ("chip", "core", "fsdp"))
    rows = ("chip", "core")
    placed = (P(rows, "fsdp"), P(rows, "fsdp"), P(rows, "fsdp"), P("fsdp"), P(None, "fsdp"))
    return jax.shard_map(
        shards, mesh=fine, in_specs=placed, out_specs=P(rows, "fsdp"), check_vma=False
    )
```

time: 91.7 us -> 112 us (1.22)
  waiting for transfers between devices: 16.9 us -> 1.71 us
  Pallas kernels: 17.4 us -> 32.4 us
  between operations: 0.25 us -> 13.6 us
  starting transfers between devices: 8.51 us -> 18.3 us
  local copies, waits for them, and re-layouts: 7.13 us -> 5.02 us
    ppermute x6 -> x12, waiting for transfers between devices: 15.2 us -> 0.03 us  [along(): lax.ppermute(value, 'fsdp', [(i, (i + shift) % count) for i in range(coun...]
    pallas_call x4 -> x6, Pallas kernels: 7.32 us -> 20.3 us  [mix(): pl.pallas_call(functools.partial(mix_kernel, plan=tuple(plan), first=tota...]
    ppermute x6 -> x12, starting transfers between devices: 8.5 us -> 18.3 us  [along(): lax.ppermute(value, 'fsdp', [(i, (i + shift) % count) for i in range(coun...]
    unnamed x14 -> x24, local copies, waits for them, and re-layouts: 5.84 us -> 2.96 us
    pallas_call x4 -> x5, Pallas kernels: 9.01 us -> 11.1 us  [the longest x3 6.34 us: attention(): pl.pallas_call(functools.partial(attention_kernel, groups=groups, states=...]
  transfers between devices with their start and end apart: 7 -> 14, of which waited for: 6 -> 1; matrix products, arithmetic and copies ran while one was open for 1% -> 2% of each run, Pallas kernels for 12% -> 25%
where the time goes in v4:
time: 112 us; the launch traced here: 111 us
  blocking collectives  40.4 us (36%)
  Pallas kernels  32.4 us (29%)
  starting transfers between devices  18.3 us (16%)
  between operations  13.6 us (12%)
  local copies, waits for them, and re-layouts  5.02 us (4%)
  waiting for transfers between devices  1.71 us (2%)
    all_to_all x1, blocking collectives, shards(): own = lax.all_to_all(states, 'chip', 0, 0, tiled=True)  23.5 us
    pallas_call x6, Pallas kernels, mix(): pl.pallas_call(functools.partial(mix_kernel, plan=tuple(plan), first=tota...  20.3 us
    ppermute x12, starting transfers between devices, along(): lax.ppermute(value, 'fsdp', [(i, (i + shift) % count) for i in range(coun...  18.3 us
    all_to_all x1, blocking collectives, shards(): carried = lax.all_to_all(sums, 'chip', 0, 0, tiled=True)  16.9 us
    pallas_call x3, Pallas kernels, attention(): pl.pallas_call(functools.partial(attention_kernel, groups=groups, states=...  6.34 us
    pallas_call x1, Pallas kernels, block_states(): pl.pallas_call(state_kernel, name='block_states', in_specs=[HBM, HBM, HBM...  3.17 us
    unnamed x24, local copies, waits for them, and re-layouts  2.96 us
  transfers between devices with their start and end apart: 14, of which 1 were waited for; matrix products, arithmetic and copies ran while one was open for 2% of the time, Pallas kernels for 25%

profile of v4, /device:TPU:32, one launch (start us, length us, event | category | flops | bytes accessed | tf_op | source)
XLA Modules:
  0.0 111.5 jit_solution(7365765766036976586)
XLA Ops:
  7.2 3.2 %block_states.1 = (bf16[1024,128]{1,0:T(8,128)(2,1)S(1)}, bf16[528,768]{1,0:T(8,128)(2,1)S(1)}) custom-call(bf16[512,1024]{1,0:T(8,128)(2,1)} %q_ref.5, bf16[512,1024]{1,0:T(8,128)(2,1)} %k_ref.5, bf16[512,1024]{1,0:T(8,128)(2,1)} %v_ref.5, f32[1,1024]{1,0:T(1,128)S(1)} %bitcast.14), custom_call_target="tpu_custom_call" | custom-call | flops 134217728 | bytes 2097152 | tf_op jit(solution)/shard_map/block_states/pallas_call | solution.py:119
  12.0 23.5 %all_to_all.22 = bf16[32,32,128]{2,1,0:T(8,128)(2,1)S(1)} all-to-all(bf16[32,32,128]{2,1,0:T(8,128)(2,1)} %bitcast.13), channel_id=1, replica_groups=mesh['chip'=32,'core'=2,'fsdp'=4] {'chip'}, dimensions={0} | all-to-all | bytes 524288 | tf_op jit(solution)/shard_map/all_to_all | solution.py:332
  35.5 1.7 %collective-permute-done.other_ref = bf16[1024,128]{1,0:T(8,128)(2,1)} collective-permute-done((bf16[1024,128]{1,0:T(8,128)(2,1)S(1)}, bf16[1024,128]{1,0:T(8,128)(2,1)}, u32[]{:S(2)}, u32[]{:S(2)}) %collective-permute-start) | collective-permute-done | bytes 262176 | tf_op jit(solution)/shard_map/ppermute | solution.py:333
  37.2 1.1 exclusive_sums.1
  38.3 16.9 %all_to_all.23 = bf16[32,32,128]{2,1,0:T(8,128)(2,1)S(1)} all-to-all(bf16[32,32,128]{2,1,0:T(8,128)(2,1)S(1)} %bitcast.12), channel_id=1, replica_groups=mesh['chip'=32,'core'=2,'fsdp'=4] {'chip'}, dimensions={0} | all-to-all | bytes 524288 | tf_op jit(solution)/shard_map/all_to_all | solution.py:335
  55.1 1.9 %attention.4 = (bf16[896,128]{1,0:T(8,128)(2,1)}, bf16[512,128]{1,0:T(8,128)(2,1)S(1)}) custom-call(bf16[512,1024]{1,0:T(8,128)(2,1)S(1)} %copy-done, bf16[512,1024]{1,0:T(8,128)(2,1)S(1)} %copy-done.1, bf16[512,1024]{1,0:T(8,128)(2,1)S(1)} %copy-done.2, bf16[1024,128]{1,0:T(8,128)(2,1)S(1)} %bitcast.7, f32[1,1024]{1,0:T(1,128)S(1)} %bitcast.15), custom_call_target="tpu_custom_call" | custom-call | flops 268435456 | bytes 1048576 | tf_op jit(solution)/shard_map/attention/pallas_call | solution.py:182
  57.7 1.6 %collective-permute-start.5 = (bf16[896,128]{1,0:T(8,128)(2,1)}, bf16[896,128]{1,0:T(8,128)(2,1)}, u32[]{:S(2)}, u32[]{:S(2)}) collective-permute-start(bf16[896,128]{1,0:T(8,128)(2,1)} %get-tuple-element.14.refs_0_), channel_id=1, source_target_pairs={{0,1},{1,2},{2,3},{3,0},{4,5},{5,6},{6,7},{7,4},{8,9},{9,10},{10,1... | collective-permute-start | bytes 688136 | tf_op jit(solution)/shard_map/ppermute | solution.py:322
  59.3 1.7 %collective-permute-start.12 = (bf16[896,128]{1,0:T(8,128)(2,1)}, bf16[896,128]{1,0:T(8,128)(2,1)}, u32[]{:S(2)}, u32[]{:S(2)}) collective-permute-start(bf16[896,128]{1,0:T(8,128)(2,1)} %get-tuple-element.14.refs_0_), channel_id=1, source_target_pairs={{0,3},{1,0},{2,1},{3,2},{4,7},{5,4},{6,5},{7,6},{8,11},{9,8},{10,9... | collective-permute-start | bytes 688136 | tf_op jit(solution)/shard_map/ppermute | solution.py:322
  61.0 1.8 %collective-permute-start.7 = (bf16[512,128]{1,0:T(8,128)(2,1)}, bf16[512,128]{1,0:T(8,128)(2,1)S(1)}, u32[]{:S(2)}, u32[]{:S(2)}) collective-permute-start(bf16[512,128]{1,0:T(8,128)(2,1)} %copy-done.6), channel_id=1, source_target_pairs={{0,3},{1,0},{2,1},{3,2},{4,7},{5,4},{6,5},{7,6},{8,11},{9,8},{10,9... | collective-permute-start | bytes 393224 | tf_op jit(solution)/shard_map/ppermute | solution.py:322
  63.0 2.6 %attention.3 = (bf16[512,128]{1,0:T(8,128)(2,1)}, bf16[512,256]{1,0:T(8,128)(2,1)}) custom-call(bf16[512,1024]{1,0:T(8,128)(2,1)S(1)} %copy-done, bf16[512,1024]{1,0:T(8,128)(2,1)S(1)} %copy-done.1, bf16[512,1024]{1,0:T(8,128)(2,1)S(1)} %copy-done.2, bf16[1024,128]{1,0:T(8,128)(2,1)S(1)} %bitcast.8, f32[1,1024]{1,0:T(1,128)S(1)} %bitcast.16), custom_call_target="tpu_custom_call" | custom-call | flops 402653184 | bytes 1572864 | tf_op jit(solution)/shard_map/attention/pallas_call | solution.py:182
  65.6 3.0 %collective-permute-start.3 = (bf16[512,256]{1,0:T(8,128)(2,1)}, bf16[512,256]{1,0:T(8,128)(2,1)}, u32[]{:S(2)}, u32[]{:S(2)}) collective-permute-start(bf16[512,256]{1,0:T(8,128)(2,1)} %get-tuple-element.13.refs_3_), channel_id=1, source_target_pairs={{0,3},{1,0},{2,1},{3,2},{4,7},{5,4},{6,5},{7,6},{8,11},{9,8},{10,9... | collective-permute-start | bytes 786440 | tf_op jit(solution)/shard_map/ppermute | solution.py:322
  68.6 2.1 %constant_dynamic-slice_fusion.refs_2_ = bf16[384,1024]{1,0:T(8,128)(2,1)} fusion(bf16[4096,1024]{1,0:T(8,128)(2,1)} %refs_2_.3, s32[]{:T(128)S(6)} %select_n.3), kind=kLoop, calls=%fused_computation | loop fusion | bytes 1572868 | tf_op jit(solution)/shard_map/dynamic_slice | solution.py:361
  70.6 1.2 %collective-permute-start.9 = (bf16[512,256]{1,0:T(8,128)(2,1)}, bf16[512,256]{1,0:T(8,128)(2,1)}, u32[]{:S(2)}, u32[]{:S(2)}) collective-permute-start(bf16[512,256]{1,0:T(8,128)(2,1)} %get-tuple-element.13.refs_3_), channel_id=1, source_target_pairs={{0,1},{1,2},{2,3},{3,0},{4,5},{5,6},{6,7},{7,4},{8,9},{9,10},{10,1... | collective-permute-start | bytes 786440 | tf_op jit(solution)/shard_map/ppermute | solution.py:322
  71.9 1.8 %attention.5.refs_4_ = bf16[512,384]{1,0:T(8,128)(2,1)S(1)} custom-call(bf16[512,1024]{1,0:T(8,128)(2,1)S(1)} %copy-done, bf16[512,1024]{1,0:T(8,128)(2,1)S(1)} %copy-done.1, bf16[512,1024]{1,0:T(8,128)(2,1)S(1)} %copy-done.2, bf16[1024,128]{1,0:T(8,128)(2,1)S(1)} %bitcast.9, f32[1,1024]{1,0:T(1,128)S(1)} %bitcast.17), custom_call_target="tpu_custom_call" | custom-call | flops 402653184 | bytes 1572864 | tf_op jit(solution)/shard_map/attention/pallas_call | solution.py:182
  74.7 2.4 %collective-permute-start.10 = (bf16[512,128]{1,0:T(8,128)(2,1)}, bf16[512,128]{1,0:T(8,128)(2,1)}, u32[]{:S(2)}, u32[]{:S(2)}) collective-permute-start(bf16[512,128]{1,0:T(8,128)(2,1)} %get-tuple-element.12.refs_2_), channel_id=1, source_target_pairs={{0,3},{1,0},{2,1},{3,2},{4,7},{5,4},{6,5},{7,6},{8,11},{9,8},{10,9... | collective-permute-start | bytes 393224 | tf_op jit(solution)/shard_map/ppermute | solution.py:322
  77.1 4.5 %mix.4.refs_4_ = f32[512,1024]{1,0:T(8,128)S(1)} custom-call(s32[1]{0:T(128)} %bitcast.6.column_ref, bf16[896,128]{1,0:T(8,128)(2,1)} %get-tuple-element.14.refs_0_, bf16[512,128]{1,0:T(8,128)(2,1)S(1)} %copy-done.7, bf16[512,128]{1,0:T(8,128)(2,1)} %get-tuple-element.12.refs_2_, bf16[512,256]{1,0:T(8,128)(2,1)} %get-tuple-element.13.refs_3_, ...), custom_call_target="tpu_custom_call" | custom-call | flops 1073741824 | bytes 2097152 | tf_op jit(solution)/shard_map/mix/pallas_call | solution.py:274
  81.6 3.3 %collective-permute-start.4 = (bf16[512,256]{1,0:T(8,128)(2,1)}, bf16[512,256]{1,0:T(8,128)(2,1)S(1)}, u32[]{:S(2)}, u32[]{:S(2)}) collective-permute-start(bf16[512,256]{1,0:T(8,128)(2,1)} %collective-permute-done.3.refs_3_), channel_id=1, source_target_pairs={{0,3},{1,0},{2,1},{3,2},{4,7},{5,4},{6,5},{7,6},{8,11},{9,8},{10,9... | collective-permute-start | bytes 786440 | tf_op jit(solution)/shard_map/ppermute | solution.py:322
  84.9 4.4 %mix_early.2.refs_5_ = f32[512,1024]{1,0:T(8,128)S(1)} custom-call(s32[1]{0:T(128)} %bitcast.6.column_ref, bf16[896,128]{1,0:T(8,128)(2,1)} %collective-permute-done.5.refs_0_, bf16[896,128]{1,0:T(8,128)(2,1)} %collective-permute-done.12.refs_1_.refs_2_, bf16[2112,768]{1,0:T(8,128)(2,1)} %all-gather.2.cloned.1.call-done.refs_2_.refs_1_, ...), custom_call_target="tpu_custom_call" | custom-call | flops 805306368 | bytes 1572864 | tf_op jit(solution)/shard_map/mix_early/pallas_call | solution.py:274
  89.5 3.5 %mix.5.refs_5_ = f32[512,1024]{1,0:T(8,128)S(1)} custom-call(s32[1]{0:T(128)} %bitcast.6.column_ref, bf16[896,128]{1,0:T(8,128)(2,1)} %collective-permute-done.5.refs_0_, bf16[512,128]{1,0:T(8,128)(2,1)S(1)} %copy-done.9, bf16[896,128]{1,0:T(8,128)(2,1)} %collective-permute-done.12.refs_1_.refs_2_, bf16[512,128]{1,0:T(8,128)(2,1)S(1)} %collective-permute-done.7.refs_3_, ...), custom_call_target="tpu_custom_call" | custom-call | flops 536870912 | bytes 1048576 | tf_op jit(solution)/shard_map/mix/pallas_call | solution.py:274
  93.0 2.1 %collective-permute-start.2 = (bf16[512,128]{1,0:T(8,128)(2,1)S(1)}, bf16[512,128]{1,0:T(8,128)(2,1)S(1)}, u32[]{:S(2)}, u32[]{:S(2)}) collective-permute-start(bf16[512,128]{1,0:T(8,128)(2,1)S(1)} %collective-permute-done.1.refs_0_), channel_id=1, source_target_pairs={{0,1},{1,2},{2,3},{3,0},{4,5},{5,6},{6,7},{7,4},{8,9},{9,10},{10,1... | collective-permute-start | bytes 393224 | tf_op jit(solution)/shard_map/ppermute | solution.py:322
  95.0 3.7 %mix.6.refs_3_ = f32[512,1024]{1,0:T(8,128)S(1)} custom-call(s32[1]{0:T(128)} %bitcast.6.column_ref, bf16[512,128]{1,0:T(8,128)(2,1)S(1)} %collective-permute-done.1.refs_0_, bf16[512,256]{1,0:T(8,128)(2,1)} %collective-permute-done.9.refs_1_, bf16[512,128]{1,0:T(8,128)(2,1)} %collective-permute-done.10.refs_2_, ...), custom_call_target="tpu_custom_call" | custom-call | flops 805306368 | bytes 1572864 | tf_op jit(solution)/shard_map/mix/pallas_call | solution.py:274
  98.8 2.3 %mix_early.3.refs_3_ = f32[512,1024]{1,0:T(8,128)S(1)} custom-call(s32[1]{0:T(128)} %bitcast.6.column_ref, bf16[896,128]{1,0:T(8,128)(2,1)S(1)} %collective-permute-done.6.refs_0_, bf16[2112,768]{1,0:T(8,128)(2,1)} %all-gather.2.cloned.1.call-done.refs_2_.refs_1_, bf16[4096,1024]{1,0:T(8,128)(2,1)} %refs_2_.3, f32[512,1024]{1,0:T(8,128)S(1)} %mix.6.refs_3_), custom_call_target="tpu_custom_call" | custom-call | flops 402653184 | bytes 786432 | tf_op jit(solution)/shard_map/mix_early/pallas_call | solution.py:274
  101.2 1.8 %mix.7.refs_3_ = f32[512,1024]{1,0:T(8,128)S(1)} custom-call(s32[1]{0:T(128)} %bitcast.6.column_ref, bf16[896,128]{1,0:T(8,128)(2,1)S(1)} %collective-permute-done.6.refs_0_, bf16[512,128]{1,0:T(8,128)(2,1)S(1)} %collective-permute-done.8.refs_1_, bf16[4096,1024]{1,0:T(8,128)(2,1)} %refs_2_.3, f32[512,1024]{1,0:T(8,128)S(1)} %mix_early.3.refs_3_), custom_call_target="tpu_custom_call" | custom-call | flops 268435456 | bytes 524288 | tf_op jit(solution)/shard_map/mix/pallas_call | solution.py:274
  103.0 1.6 %last_mix.1 = bf16[512,1024]{1,0:T(8,128)(2,1)} custom-call(bf16[512,128]{1,0:T(8,128)(2,1)S(1)} %collective-permute-done.2.refs_0_, bf16[512,256]{1,0:T(8,128)(2,1)S(1)} %collective-permute-done.4.refs_1_, bf16[384,1024]{1,0:T(8,128)(2,1)S(1)} %copy-done.3, f32[512,1024]{1,0:T(8,128)S(1)} %mix.7.refs_3_), custom_call_target="tpu_custom_call" | custom-call | flops 402653184 | bytes 2097152 | tf_op jit(solution)/shard_map/last_mix/pallas_call | solution.py:306
  (44 shorter events, 4.3 us)
Async XLA Ops:
  6.5 78.4 %all-gather.2.cloned.1.call-start = ((), (), s32[]{:S(2)}) async-start(), calls=%async_computation.2 | async-start | bytes 4055040 | tf_op jit(solution)/shard_map/all_gather | solution.py:331
  7.2 47.9 %copy-start.2 = (bf16[512,1024]{1,0:T(8,128)(2,1)S(1)}, bf16[512,1024]{1,0:T(8,128)(2,1)}, u32[]{:S(2)}) copy-start(bf16[512,1024]{1,0:T(8,128)(2,1)} %v_ref.5) | copy-start | bytes 3145732
  10.4 0.9 copy-start.4
  11.3 0.7 copy-start.5
  12.0 43.1 %copy-start = (bf16[512,1024]{1,0:T(8,128)(2,1)S(1)}, bf16[512,1024]{1,0:T(8,128)(2,1)}, u32[]{:S(2)}) copy-start(bf16[512,1024]{1,0:T(8,128)(2,1)} %q_ref.5) | copy-start | bytes 3145732
  12.0 43.1 %copy-start.1 = (bf16[512,1024]{1,0:T(8,128)(2,1)S(1)}, bf16[512,1024]{1,0:T(8,128)(2,1)}, u32[]{:S(2)}) copy-start(bf16[512,1024]{1,0:T(8,128)(2,1)} %k_ref.5) | copy-start | bytes 3145732
  12.0 43.1 %copy-start.11 = (f32[1024]{0:T(1024)S(1)}, f32[1024]{0:T(1024)}, u32[]{:S(2)}) copy-start(f32[1024]{0:T(1024)} %param.8) | copy-start | bytes 12292
  35.5 1.7 %collective-permute-start = (bf16[1024,128]{1,0:T(8,128)(2,1)S(1)}, bf16[1024,128]{1,0:T(8,128)(2,1)}, u32[]{:S(2)}, u32[]{:S(2)}) collective-permute-start(bf16[1024,128]{1,0:T(8,128)(2,1)S(1)} %bitcast.10), channel_id=1, source_target_pairs={{0,4},{4,0},{1,5},{5,1},{2,6},{6,2},{3,7},{7,3},{8,12},{12,8},{9,1... | collective-permute-start | bytes 786440 | tf_op jit(solution)/shard_map/ppermute | solution.py:333
  57.7 17.0 %collective-permute-start.5 = (bf16[896,128]{1,0:T(8,128)(2,1)}, bf16[896,128]{1,0:T(8,128)(2,1)}, u32[]{:S(2)}, u32[]{:S(2)}) collective-permute-start(bf16[896,128]{1,0:T(8,128)(2,1)} %get-tuple-element.14.refs_0_), channel_id=1, source_target_pairs={{0,1},{1,2},{2,3},{3,0},{4,5},{5,6},{6,7},{7,4},{8,9},{9,10},{10,1... | collective-permute-start | bytes 688136 | tf_op jit(solution)/shard_map/ppermute | solution.py:322
  59.3 17.8 %collective-permute-start.12 = (bf16[896,128]{1,0:T(8,128)(2,1)}, bf16[896,128]{1,0:T(8,128)(2,1)}, u32[]{:S(2)}, u32[]{:S(2)}) collective-permute-start(bf16[896,128]{1,0:T(8,128)(2,1)} %get-tuple-element.14.refs_0_), channel_id=1, source_target_pairs={{0,3},{1,0},{2,1},{3,2},{4,7},{5,4},{6,5},{7,6},{8,11},{9,8},{10,9... | collective-permute-start | bytes 688136 | tf_op jit(solution)/shard_map/ppermute | solution.py:322
  61.0 9.7 %collective-permute-start.7 = (bf16[512,128]{1,0:T(8,128)(2,1)}, bf16[512,128]{1,0:T(8,128)(2,1)S(1)}, u32[]{:S(2)}, u32[]{:S(2)}) collective-permute-start(bf16[512,128]{1,0:T(8,128)(2,1)} %copy-done.6), channel_id=1, source_target_pairs={{0,3},{1,0},{2,1},{3,2},{4,7},{5,4},{6,5},{7,6},{8,11},{9,8},{10,9... | collective-permute-start | bytes 393224 | tf_op jit(solution)/shard_map/ppermute | solution.py:322
  62.8 11.0 %collective-permute-start.11 = (bf16[512,128]{1,0:T(8,128)(2,1)}, bf16[512,128]{1,0:T(8,128)(2,1)S(1)}, u32[]{:S(2)}, u32[]{:S(2)}) collective-permute-start(bf16[512,128]{1,0:T(8,128)(2,1)} %copy-done.6), channel_id=1, source_target_pairs={{0,1},{1,2},{2,3},{3,0},{4,5},{5,6},{6,7},{7,4},{8,9},{9,10},{10,1... | collective-permute-start | bytes 393224 | tf_op jit(solution)/shard_map/ppermute | solution.py:322
  65.6 16.0 %collective-permute-start.3 = (bf16[512,256]{1,0:T(8,128)(2,1)}, bf16[512,256]{1,0:T(8,128)(2,1)}, u32[]{:S(2)}, u32[]{:S(2)}) collective-permute-start(bf16[512,256]{1,0:T(8,128)(2,1)} %get-tuple-element.13.refs_3_), channel_id=1, source_target_pairs={{0,3},{1,0},{2,1},{3,2},{4,7},{5,4},{6,5},{7,6},{8,11},{9,8},{10,9... | collective-permute-start | bytes 786440 | tf_op jit(solution)/shard_map/ppermute | solution.py:322
  70.6 6.4 %copy-start.7 = (bf16[512,128]{1,0:T(8,128)(2,1)S(1)}, bf16[512,128]{1,0:T(8,128)(2,1)}, u32[]{:S(2)}) copy-start(bf16[512,128]{1,0:T(8,128)(2,1)} %copy-done.6) | copy-start | bytes 393220
  70.6 24.4 %collective-permute-start.9 = (bf16[512,256]{1,0:T(8,128)(2,1)}, bf16[512,256]{1,0:T(8,128)(2,1)}, u32[]{:S(2)}, u32[]{:S(2)}) collective-permute-start(bf16[512,256]{1,0:T(8,128)(2,1)} %get-tuple-element.13.refs_3_), channel_id=1, source_target_pairs={{0,1},{1,2},{2,3},{3,0},{4,5},{5,6},{6,7},{7,4},{8,9},{9,10},{10,1... | collective-permute-start | bytes 786440 | tf_op jit(solution)/shard_map/ppermute | solution.py:322
  73.7 7.8 %copy-start.8 = (bf16[512,128]{1,0:T(8,128)(2,1)}, bf16[512,128]{1,0:T(8,128)(2,1)S(1)}, u32[]{:S(2)}) copy-start(bf16[512,128]{1,0:T(8,128)(2,1)S(1)} %collective-permute-done.11.refs_1_) | copy-start | bytes 393220
  73.7 15.6 %collective-permute-start.1 = (bf16[512,128]{1,0:T(8,128)(2,1)}, bf16[512,128]{1,0:T(8,128)(2,1)S(1)}, u32[]{:S(2)}, u32[]{:S(2)}) collective-permute-start(bf16[512,128]{1,0:T(8,128)(2,1)} %get-tuple-element.12.refs_2_), channel_id=1, source_target_pairs={{0,1},{1,2},{2,3},{3,0},{4,5},{5,6},{6,7},{7,4},{8,9},{9,10},{10,1... | collective-permute-start | bytes 393224 | tf_op jit(solution)/shard_map/ppermute | solution.py:322
  74.7 18.3 %collective-permute-start.10 = (bf16[512,128]{1,0:T(8,128)(2,1)}, bf16[512,128]{1,0:T(8,128)(2,1)}, u32[]{:S(2)}, u32[]{:S(2)}) collective-permute-start(bf16[512,128]{1,0:T(8,128)(2,1)} %get-tuple-element.12.refs_2_), channel_id=1, source_target_pairs={{0,3},{1,0},{2,1},{3,2},{4,7},{5,4},{6,5},{7,6},{8,11},{9,8},{10,9... | collective-permute-start | bytes 393224 | tf_op jit(solution)/shard_map/ppermute | solution.py:322
  77.1 21.7 %collective-permute-start.6 = (bf16[896,128]{1,0:T(8,128)(2,1)}, bf16[896,128]{1,0:T(8,128)(2,1)S(1)}, u32[]{:S(2)}, u32[]{:S(2)}) collective-permute-start(bf16[896,128]{1,0:T(8,128)(2,1)} %collective-permute-done.5.refs_0_), channel_id=1, source_target_pairs={{0,1},{1,2},{2,3},{3,0},{4,5},{5,6},{6,7},{7,4},{8,9},{9,10},{10,1... | collective-permute-start | bytes 688136 | tf_op jit(solution)/shard_map/ppermute | solution.py:322
  81.6 7.9 %copy-start.9 = (bf16[512,128]{1,0:T(8,128)(2,1)S(1)}, bf16[512,128]{1,0:T(8,128)(2,1)}, u32[]{:S(2)}) copy-start(bf16[512,128]{1,0:T(8,128)(2,1)} %copy-done.8) | copy-start | bytes 393220
  81.6 21.4 %collective-permute-start.4 = (bf16[512,256]{1,0:T(8,128)(2,1)}, bf16[512,256]{1,0:T(8,128)(2,1)S(1)}, u32[]{:S(2)}, u32[]{:S(2)}) collective-permute-start(bf16[512,256]{1,0:T(8,128)(2,1)} %collective-permute-done.3.refs_3_), channel_id=1, source_target_pairs={{0,3},{1,0},{2,1},{3,2},{4,7},{5,4},{6,5},{7,6},{8,11},{9,8},{10,9... | collective-permute-start | bytes 786440 | tf_op jit(solution)/shard_map/ppermute | solution.py:322
  89.3 11.8 %collective-permute-start.8 = (bf16[512,128]{1,0:T(8,128)(2,1)S(1)}, bf16[512,128]{1,0:T(8,128)(2,1)S(1)}, u32[]{:S(2)}, u32[]{:S(2)}) collective-permute-start(bf16[512,128]{1,0:T(8,128)(2,1)S(1)} %collective-permute-done.7.refs_3_), channel_id=1, source_target_pairs={{0,3},{1,0},{2,1},{3,2},{4,7},{5,4},{6,5},{7,6},{8,11},{9,8},{10,9... | collective-permute-start | bytes 393224 | tf_op jit(solution)/shard_map/ppermute | solution.py:322
  93.0 10.0 %collective-permute-start.2 = (bf16[512,128]{1,0:T(8,128)(2,1)S(1)}, bf16[512,128]{1,0:T(8,128)(2,1)S(1)}, u32[]{:S(2)}, u32[]{:S(2)}) collective-permute-start(bf16[512,128]{1,0:T(8,128)(2,1)S(1)} %collective-permute-done.1.refs_0_), channel_id=1, source_target_pairs={{0,1},{1,2},{2,3},{3,0},{4,5},{5,6},{6,7},{7,4},{8,9},{9,10},{10,1... | collective-permute-start | bytes 393224 | tf_op jit(solution)/shard_map/ppermute | solution.py:322
  101.1 1.9 %copy-start.3 = (bf16[384,1024]{1,0:T(8,128)(2,1)S(1)}, bf16[384,1024]{1,0:T(8,128)(2,1)}, u32[]{:S(2)}) copy-start(bf16[384,1024]{1,0:T(8,128)(2,1)} %constant_dynamic-slice_fusion.refs_2_) | copy-start | bytes 2359300
  (2 other events, 1.3 us)
Sparse Core Ops, SparseCore 0:
  12.1 45.5 all-gather.1

commit v5 on v3

--- a/solution.py
+++ b/solution.py
@@ -12,7 +12,8 @@
 BLK = 512
 HALF = BLK // 2
 CORES = 2
-CHUNKS = ((0, 4), (4, 8))
+HEADS = 8
+CALLS = (((0, 2), (2, 4)), ((4, 6), (6, 8)))
 F32 = jnp.float32
 BF16 = jnp.bfloat16
 NN, NT, TN = ((1,), (0,)), ((1,), (1,)), ((0,), (0,))
@@ -30,8 +31,36 @@
     return pltpu.with_memory_space_constraint(value, pltpu.VMEM)
 
 
+def in_hbm(value):
+    return pltpu.with_memory_space_constraint(value, pltpu.HBM)
+
+
 def cost(flops, size):
     return pl.CostEstimate(flops=flops, bytes_accessed=size, transcendentals=0)
+
+
+def within_block(q_ref, k_ref, v_ref, h, causal):
+    cols = slice(h * DH, (h + 1) * DH)
+    q0, q1 = q_ref[:HALF, cols], q_ref[HALF:, cols]
+    k0, k1 = k_ref[:HALF, cols], k_ref[HALF:, cols]
+    v0, v1 = v_ref[:HALF, cols], v_ref[HALF:, cols]
+    s00 = jnp.where(causal, dot(q0, k0, NT), 0.0).astype(BF16)
+    s10 = dot(q1, k0, NT).astype(BF16)
+    s11 = jnp.where(causal, dot(q1, k1, NT), 0.0).astype(BF16)
+    return dot(s00, v0, NN), dot(s10, v0, NN) + dot(s11, v1, NN)
+
+
+def causal_mask():
+    row = lax.broadcasted_iota(jnp.int32, (HALF, HALF), 0)
+    col = lax.broadcasted_iota(jnp.int32, (HALF, HALF), 1)
+    return col <= row
+
+
+def finish(queries, within, state, gain):
+    att = within + dot(queries, state, NN)
+    mean = jnp.full((DH, DH), 1.0 / DH, BF16)
+    mean_square = dot((att * att).astype(BF16), mean, NN)
+    return (att * lax.rsqrt(mean_square + 1e-6) * gain).astype(BF16)
 
 
 PARTS = 2
@@ -69,7 +98,7 @@
         ],
         compiler_params=PARAMS,
         cost_estimate=cost(2 * BLK * DH * width, 2 * BLK * width * 2),
-    )(k, v)
+    )(in_hbm(k), in_hbm(v))
 
 
 def scan_kernel(core_ref, own_ref, other_ref, out_ref, *, chips):
@@ -95,40 +124,29 @@
     )(core, own, other)
 
 
-def attention_kernel(q_ref, k_ref, v_ref, carried_ref, gain_ref, out_ref, *, first):
-    row = lax.broadcasted_iota(jnp.int32, (HALF, HALF), 0)
-    col = lax.broadcasted_iota(jnp.int32, (HALF, HALF), 1)
-    causal = col <= row
-    mean = jnp.full((DH, DH), 1.0 / DH, BF16)
-    for at in range(out_ref.shape[1] // DH):
-        h = first + at
-        cols = slice(h * DH, (h + 1) * DH)
-        q0, q1 = q_ref[:HALF, cols], q_ref[HALF:, cols]
-        k0, k1 = k_ref[:HALF, cols], k_ref[HALF:, cols]
-        v0, v1 = v_ref[:HALF, cols], v_ref[HALF:, cols]
-        s00 = jnp.where(causal, dot(q0, k0, NT), 0.0).astype(BF16)
-        s10 = dot(q1, k0, NT).astype(BF16)
-        s11 = jnp.where(causal, dot(q1, k1, NT), 0.0).astype(BF16)
-        top = dot(s00, v0, NN)
-        bottom = dot(s10, v0, NN) + dot(s11, v1, NN)
-        state = carried_ref[cols, :]
-        for rows, queries, within in ((slice(0, HALF), q0, top), (slice(HALF, BLK), q1, bottom)):
-            att = within + dot(queries, state, NN)
-            mean_square = dot((att * att).astype(BF16), mean, NN)
-            normed = att * lax.rsqrt(mean_square + 1e-6) * gain_ref[:, cols]
-            out_ref[rows, at * DH : (at + 1) * DH] = normed.astype(BF16)
-
-
-def attention(q, k, v, carried, gain, first, last):
-    width = (last - first) * DH
-    return pl.pallas_call(
-        functools.partial(attention_kernel, first=first),
+def attention_kernel(q_ref, k_ref, v_ref, carried_ref, gain_ref, *out_refs, groups):
+    causal = causal_mask()
+    for out_ref, (first, last) in zip(out_refs, groups):
+        for h in range(first, last):
+            cols = slice(h * DH, (h + 1) * DH)
+            out_cols = slice((h - first) * DH, (h - first + 1) * DH)
+            parts = within_block(q_ref, k_ref, v_ref, h, causal)
+            for rows, within in zip((slice(0, HALF), slice(HALF, BLK)), parts):
+                out_ref[rows, out_cols] = finish(
+                    q_ref[rows, cols], within, carried_ref[cols, :], gain_ref[:, cols]
+                )
+
+
+def attention(q, k, v, carried, gain, groups):
+    heads = sum(last - first for first, last in groups)
+    return pl.pallas_call(
+        functools.partial(attention_kernel, groups=groups),
         name="attention",
         in_specs=[VMEM] * 5,
-        out_specs=VMEM,
-        out_shape=pltpu.VMEM((BLK, width), BF16),
-        compiler_params=PARAMS,
-        cost_estimate=cost(4 * BLK * BLK * width, BLK * width * 8),
+        out_specs=[VMEM] * len(groups),
+        out_shape=[pltpu.VMEM((BLK, (last - first) * DH), BF16) for first, last in groups],
+        compiler_params=PARAMS,
+        cost_estimate=cost(4 * BLK * BLK * DH * heads, BLK * DH * heads * 8),
     )(q, k, v, carried, gain)
 
 
@@ -141,24 +159,27 @@
     if not first:
         total_ref, rest = rest[0], rest[1:]
     out_ref, w_ref, sems = rest
-    ways = w_hbm.shape[0] // (8 * DH)
-    copies, at = [], 0
-    for piece, (a_ref, (shift, head)) in enumerate(zip(a_refs, plan)):
-        depth = a_ref.shape[1]
-        source = lax.rem(column_ref[0] + (shift + ways), ways)
-        start = pl.multiple_of(source * (8 * DH) + head * DH, DH)
-        rows = slice(at, at + depth)
-        copies.append(
-            pltpu.make_async_copy(w_hbm.at[pl.ds(start, depth)], w_ref.at[rows], sems.at[piece])
-        )
-        copies[-1].start()
-        at += depth
-    for copy in copies:
-        copy.wait()
-    for tile in range(out_ref.shape[1] // TILE):
-        cols = slice(tile * TILE, (tile + 1) * TILE)
+    ways = w_hbm.shape[0] // (HEADS * DH)
+    tiles = [slice(at, at + TILE) for at in range(0, out_ref.shape[1], TILE)]
+    copies = {}
+    for tile, cols in enumerate(tiles):
+        at = 0
+        for piece, (a_ref, (shift, head)) in enumerate(zip(a_refs, plan)):
+            depth = a_ref.shape[1]
+            source = lax.rem(column_ref[0] + (shift + ways), ways)
+            start = pl.multiple_of(source * (HEADS * DH) + head * DH, DH)
+            copy = pltpu.make_async_copy(
+                w_hbm.at[pl.ds(start, depth), cols],
+                w_ref.at[at : at + depth, cols],
+                sems.at[tile, piece],
+            )
+            copy.start()
+            copies[tile, piece] = copy
+            at += depth
+    for tile, cols in enumerate(tiles):
         total, at = None if first else total_ref[:, cols], 0
-        for a_ref in a_refs:
+        for piece, a_ref in enumerate(a_refs):
+            copies[tile, piece].wait()
             depth = a_ref.shape[1]
             term = dot(a_ref[...], w_ref[at : at + depth, cols], NN)
             total = term if total is None else total + term
@@ -180,18 +201,23 @@
         out_shape=pltpu.VMEM((BLK, width), F32),
         scratch_shapes=[
             pltpu.VMEM((depth, width), BF16),
-            pltpu.SemaphoreType.DMA((len(arrays),)),
+            pltpu.SemaphoreType.DMA((width // TILE, len(arrays))),
         ],
         compiler_params=PARAMS,
         cost_estimate=cost(2 * BLK * depth * width, 2 * depth * width),
     )(*operands)
 
 
-def last_kernel(a_ref, w_ref, total_ref, out_hbm, out_ref, sems):
+def last_kernel(*refs):
+    *a_refs, w_ref, total_ref, out_hbm, out_ref, sems = refs
     copies = []
     for tile in range(w_ref.shape[1] // TILE):
         cols = slice(tile * TILE, (tile + 1) * TILE)
-        total = total_ref[:, cols] + dot(a_ref[...], w_ref[:, cols], NN)
+        total, at = total_ref[:, cols], 0
+        for a_ref in a_refs:
+            depth = a_ref.shape[1]
+            total = total + dot(a_ref[...], w_ref[at : at + depth, cols], NN)
+            at += depth
         out_ref[:, cols] = total.astype(BF16)
         copy = pltpu.make_async_copy(out_ref.at[:, cols], out_hbm.at[:, cols], sems.at[tile])
         copy.start()
@@ -200,12 +226,12 @@
         copy.wait()
 
 
-def last_mix(array, w, total):
+def last_mix(arrays, w, total):
     depth, width = w.shape
     return pl.pallas_call(
         last_kernel,
         name="last_mix",
-        in_specs=[VMEM] * 3,
+        in_specs=[VMEM] * (len(arrays) + 2),
         out_specs=HBM,
         out_shape=jax.ShapeDtypeStruct((BLK, width), BF16),
         scratch_shapes=[
@@ -214,7 +240,7 @@
         ],
         compiler_params=PARAMS,
         cost_estimate=cost(2 * BLK * depth * width, BLK * width * 4),
-    )(array, w, total)
+    )(*arrays, w, total)
 
 
 def along(value, shift, count):
@@ -230,24 +256,30 @@
     other = lax.ppermute(own, "core", [(0, 1), (1, 0)])
     sums = exclusive_sums(core, own, other, chips)
     carried = lax.all_to_all(sums, "chip", 0, 0, tiled=True)
-    q, k, v = in_vmem(q), in_vmem(k), in_vmem(v)
+    q, k, v, weights = in_vmem(q), in_vmem(k), in_vmem(v), in_hbm(w)
     gain_row = gain.reshape(1, -1)
-    own, near, far = [], [], []
-    for at, (first, last) in enumerate(CHUNKS):
-        mine = attention(q, k, v, carried, gain_row, first, last)
-        left = along(mine, 1, ways)
-        right = along(mine, -1, ways)
-        far.append(along(right, -1, ways) if at % 2 else along(left, 1, ways))
-        own.append(mine)
-        near.append([left, right])
-    heads = [first for first, _ in CHUNKS]
-    total = mix(column, w, [(0, head) for head in heads], own)
-    for head, pair in zip(heads, near):
-        total = mix(column, w, [(-1, head), (1, head)], pair, total)
-    total = mix(column, w, [(2, heads[0])], far[:1], total)
-    row = lax.rem(column[0] + ways // 2, ways) * (8 * DH) + heads[1] * DH
-    tail = in_vmem(lax.dynamic_slice_in_dim(w, row, far[1].shape[1]))
-    return last_mix(far[1], tail, total)
+    heads, mine, left, right, far = [], [], [], [], []
+    for groups in CALLS:
+        heads += [first for first, _ in groups]
+        mine += attention(q, k, v, carried, gain_row, groups)
+    for value in mine:
+        left.append(along(value, 1, ways))
+        right.append(along(value, -1, ways))
+
+    def plan(shift, begin, end):
+        return [(shift, head) for head in heads[begin:end]]
+
+    total = mix(column, weights, plan(0, 0, 4), mine)
+    left[0], right[1], total = lax.optimization_barrier((left[0], right[1], total))
+    for at in range(4):
+        far.append(along(right[at], -1, ways) if at % 2 else along(left[at], 1, ways))
+    for a, b in ((0, 2), (2, 4)):
+        sides = plan(-1, a, b) + plan(1, a, b)
+        total = mix(column, weights, sides, left[a:b] + right[a:b], total)
+    total = mix(column, weights, plan(2, 0, 2), far[:2], total)
+    row = lax.rem(column[0] + ways // 2, ways) * (HEADS * DH) + heads[2] * DH
+    tail = in_vmem(lax.dynamic_slice_in_dim(w, row, (HEADS - heads[2]) * DH))
+    return last_mix(far[2:], tail, total)
 
 
 def solution(mesh):

time: 91.7 us -> 94.5 us (1.031); the launches traced: 90.2 us -> 94.1 us
  Pallas kernels: 17.4 us -> 29.1 us
  waiting for transfers between devices: 16.9 us -> 7.12 us
  starting transfers between devices: 8.51 us -> 16.2 us
  local copies, waits for them, and re-layouts: 7.13 us -> 1.31 us
    pallas_call x4, Pallas kernels: 7.32 us -> 18.2 us  [mix(): pl.pallas_call(functools.partial(mix_kernel, plan=tuple(plan), first=tota...]
    ppermute x6 -> x12, waiting for transfers between devices: 15.2 us -> 5.46 us  [along(): lax.ppermute(value, 'fsdp', [(i, (i + shift) % count) for i in range(coun...]
    ppermute x6 -> x12, starting transfers between devices: 8.5 us -> 16.2 us  [along(): lax.ppermute(value, 'fsdp', [(i, (i + shift) % count) for i in range(coun...]
    unnamed x14 -> x8, local copies, waits for them, and re-layouts: 5.84 us -> 0.02 us
    pallas_call x1, Pallas kernels: 1.07 us -> 2.14 us  [block_states(): pl.pallas_call(state_kernel, name='block_states', in_specs=[HBM, HBM], ou...]
  transfers between devices with their start and end apart: 7 -> 13, of which waited for: 6 -> 4; matrix products, arithmetic and copies ran while one was open for 1% -> 1% of each run, Pallas kernels for 12% -> 23%
where the time goes in v5:
time: 94.5 us; the launch traced here: 94.1 us
  blocking collectives  40 us (42%)
  Pallas kernels  29.1 us (31%)
  starting transfers between devices  16.2 us (17%)
  waiting for transfers between devices  7.12 us (8%)
  local copies, waits for them, and re-layouts  1.31 us (1%)
    all_to_all x1, blocking collectives, shards(): own = lax.all_to_all(states, 'chip', 0, 0, tiled=True)  23.1 us
    pallas_call x4, Pallas kernels, mix(): pl.pallas_call(functools.partial(mix_kernel, plan=tuple(plan), first=tota...  18.2 us
    all_to_all x1, blocking collectives, shards(): carried = lax.all_to_all(sums, 'chip', 0, 0, tiled=True)  16.9 us
    ppermute x12, starting transfers between devices, along(): lax.ppermute(value, 'fsdp', [(i, (i + shift) % count) for i in range(coun...  16.2 us
    pallas_call x2, Pallas kernels, attention(): pl.pallas_call(functools.partial(attention_kernel, groups=groups), name='...  6.16 us
    ppermute x12, waiting for transfers between devices, along(): lax.ppermute(value, 'fsdp', [(i, (i + shift) % count) for i in range(coun...  5.46 us
    pallas_call x1, Pallas kernels, block_states(): pl.pallas_call(state_kernel, name='block_states', in_specs=[HBM, HBM], ou...  2.14 us
  transfers between devices with their start and end apart: 13, of which 4 were waited for; matrix products, arithmetic and copies ran while one was open for 1% of the time, Pallas kernels for 23%

profile of v5, /device:TPU:32, one launch (start us, length us, event | category | flops | bytes accessed | tf_op | source)
XLA Modules:
  0.0 94.1 jit_solution(9777447495155643998)
XLA Ops:
  0.0 2.1 %block_states.1 = bf16[1024,128]{1,0:T(8,128)(2,1)S(1)} custom-call(bf16[512,1024]{1,0:T(8,128)(2,1)} %k_ref.3, bf16[512,1024]{1,0:T(8,128)(2,1)} %v_ref.3), custom_call_target="tpu_custom_call" | custom-call | flops 134217728 | bytes 2097152 | tf_op jit(solution)/shard_map/block_states/pallas_call | solution.py:88
  2.2 23.1 %all_to_all.22 = bf16[32,32,128]{2,1,0:T(8,128)(2,1)S(1)} all-to-all(bf16[32,32,128]{2,1,0:T(8,128)(2,1)S(1)} %bitcast.9), channel_id=1, replica_groups=mesh['chip'=32,'core'=2,'fsdp'=4] {'chip'}, dimensions={0} | all-to-all | bytes 524288 | tf_op jit(solution)/shard_map/all_to_all | solution.py:255
  25.3 1.7 %collective-permute-done.other_ref = bf16[1024,128]{1,0:T(8,128)(2,1)} collective-permute-done((bf16[1024,128]{1,0:T(8,128)(2,1)S(1)}, bf16[1024,128]{1,0:T(8,128)(2,1)}, u32[]{:S(2)}, u32[]{:S(2)}) %collective-permute-start) | collective-permute-done | bytes 262176 | tf_op jit(solution)/shard_map/ppermute | solution.py:256
  27.0 1.1 %exclusive_sums.1 = bf16[1024,128]{1,0:T(8,128)(2,1)S(1)} custom-call(s32[1]{0:T(128)} %bitcast.core_ref, bf16[1024,128]{1,0:T(8,128)(2,1)S(1)} %bitcast.11, bf16[1024,128]{1,0:T(8,128)(2,1)} %collective-permute-done.other_ref), custom_call_target="tpu_custom_call" | custom-call | flops 524288 | bytes 786432 | tf_op jit(solution)/shard_map/exclusive_sums/pallas_call | solution.py:116
  28.1 16.9 %all_to_all.23 = bf16[32,32,128]{2,1,0:T(8,128)(2,1)S(1)} all-to-all(bf16[32,32,128]{2,1,0:T(8,128)(2,1)S(1)} %bitcast.12), channel_id=1, replica_groups=mesh['chip'=32,'core'=2,'fsdp'=4] {'chip'}, dimensions={0} | all-to-all | bytes 524288 | tf_op jit(solution)/shard_map/all_to_all | solution.py:258
  45.0 3.1 %attention.3 = (bf16[512,256]{1,0:T(8,128)(2,1)}, bf16[512,256]{1,0:T(8,128)(2,1)}) custom-call(bf16[512,1024]{1,0:T(8,128)(2,1)S(1)} %copy-done.2, bf16[512,1024]{1,0:T(8,128)(2,1)S(1)} %copy-done, bf16[512,1024]{1,0:T(8,128)(2,1)S(1)} %copy-done.1, bf16[1024,128]{1,0:T(8,128)(2,1)S(1)} %bitcast.7, f32[1,1024]{1,0:T(1,128)S(1)} %bitcast.13), custom_call_target="tpu_custom_call" | custom-call | flops 536870912 | bytes 2097152 | tf_op jit(solution)/shard_map/attention/pallas_call | solution.py:142
  48.0 1.6 %collective-permute-start.5 = (bf16[512,256]{1,0:T(8,128)(2,1)}, bf16[512,256]{1,0:T(8,128)(2,1)S(1)}, u32[]{:S(2)}, u32[]{:S(2)}) collective-permute-start(bf16[512,256]{1,0:T(8,128)(2,1)} %get-tuple-element.14.refs_0_), channel_id=1, source_target_pairs={{0,1},{1,2},{2,3},{3,0},{4,5},{5,6},{6,7},{7,4},{8,9},{9,10},{10,1... | collective-permute-start | bytes 786440 | tf_op jit(solution)/shard_map/ppermute | solution.py:247
  49.6 1.7 %collective-permute-start.6 = (bf16[512,256]{1,0:T(8,128)(2,1)}, bf16[512,256]{1,0:T(8,128)(2,1)}, u32[]{:S(2)}, u32[]{:S(2)}) collective-permute-start(bf16[512,256]{1,0:T(8,128)(2,1)} %get-tuple-element.15.refs_1_), channel_id=1, source_target_pairs={{0,3},{1,0},{2,1},{3,2},{4,7},{5,4},{6,5},{7,6},{8,11},{9,8},{10,9... | collective-permute-start | bytes 786440 | tf_op jit(solution)/shard_map/ppermute | solution.py:247
  51.6 2.9 %collective-permute-start.12 = (bf16[512,256]{1,0:T(8,128)(2,1)}, bf16[512,256]{1,0:T(8,128)(2,1)}, u32[]{:S(2)}, u32[]{:S(2)}) collective-permute-start(bf16[512,256]{1,0:T(8,128)(2,1)} %get-tuple-element.14.refs_0_), channel_id=1, source_target_pairs={{0,3},{1,0},{2,1},{3,2},{4,7},{5,4},{6,5},{7,6},{8,11},{9,8},{10,9... | collective-permute-start | bytes 786440 | tf_op jit(solution)/shard_map/ppermute | solution.py:247
  54.5 3.1 %attention.2 = (bf16[512,256]{1,0:T(8,128)(2,1)}, bf16[512,256]{1,0:T(8,128)(2,1)}) custom-call(bf16[512,1024]{1,0:T(8,128)(2,1)S(1)} %copy-done.2, bf16[512,1024]{1,0:T(8,128)(2,1)S(1)} %copy-done, bf16[512,1024]{1,0:T(8,128)(2,1)S(1)} %copy-done.1, bf16[1024,128]{1,0:T(8,128)(2,1)S(1)} %bitcast.8, f32[1,1024]{1,0:T(1,128)S(1)} %bitcast.14), custom_call_target="tpu_custom_call" | custom-call | flops 536870912 | bytes 2097152 | tf_op jit(solution)/shard_map/attention/pallas_call | solution.py:142
  57.6 0.9 collective-permute-done.5.refs_0_
  58.5 2.3 %collective-permute-start.3 = (bf16[512,256]{1,0:T(8,128)(2,1)}, bf16[512,256]{1,0:T(8,128)(2,1)S(1)}, u32[]{:S(2)}, u32[]{:S(2)}) collective-permute-start(bf16[512,256]{1,0:T(8,128)(2,1)} %get-tuple-element.13.refs_3_), channel_id=1, source_target_pairs={{0,3},{1,0},{2,1},{3,2},{4,7},{5,4},{6,5},{7,6},{8,11},{9,8},{10,9... | collective-permute-start | bytes 786440 | tf_op jit(solution)/shard_map/ppermute | solution.py:247
  60.8 0.7 collective-permute-start.10
  61.5 2.6 %collective-permute-done.11.refs_1_ = bf16[512,256]{1,0:T(8,128)(2,1)} collective-permute-done((bf16[512,256]{1,0:T(8,128)(2,1)}, bf16[512,256]{1,0:T(8,128)(2,1)}, u32[]{:S(2)}, u32[]{:S(2)}) %collective-permute-start.11) | collective-permute-done | bytes 262176 | tf_op jit(solution)/shard_map/ppermute | solution.py:247
  64.8 5.4 %mix.4.refs_5_ = f32[512,1024]{1,0:T(8,128)S(1)} custom-call(s32[1]{0:T(128)} %bitcast.6.column_ref, bf16[512,256]{1,0:T(8,128)(2,1)} %get-tuple-element.14.refs_0_, bf16[512,256]{1,0:T(8,128)(2,1)} %get-tuple-element.15.refs_1_, bf16[512,256]{1,0:T(8,128)(2,1)} %get-tuple-element.12.refs_2_, bf16[512,256]{1,0:T(8,128)(2,1)} %get-tuple-element.13.refs_3_, ...), custom_call_target="tpu_custom_call" | custom-call | flops 1073741824 | bytes 2097152 | tf_op jit(solution)/shard_map/mix/pallas_call | solution.py:196
  70.2 1.7 %collective-permute-start.7 = (bf16[512,256]{1,0:T(8,128)(2,1)S(1)}, bf16[512,256]{1,0:T(8,128)(2,1)S(1)}, u32[]{:S(2)}, u32[]{:S(2)}) collective-permute-start(bf16[512,256]{1,0:T(8,128)(2,1)S(1)} %collective-permute-done.5.refs_0_), channel_id=1, source_target_pairs={{0,1},{1,2},{2,3},{3,0},{4,5},{5,6},{6,7},{7,4},{8,9},{9,10},{10,1... | collective-permute-start | bytes 786440 | tf_op jit(solution)/shard_map/ppermute | solution.py:247
  71.9 1.7 %collective-permute-start.8 = (bf16[512,256]{1,0:T(8,128)(2,1)}, bf16[512,256]{1,0:T(8,128)(2,1)S(1)}, u32[]{:S(2)}, u32[]{:S(2)}) collective-permute-start(bf16[512,256]{1,0:T(8,128)(2,1)} %collective-permute-done.6.refs_3_), channel_id=1, source_target_pairs={{0,3},{1,0},{2,1},{3,2},{4,7},{5,4},{6,5},{7,6},{8,11},{9,8},{10,9... | collective-permute-start | bytes 786440 | tf_op jit(solution)/shard_map/ppermute | solution.py:247
  73.9 2.0 %collective-permute-done.10.refs_2_ = bf16[512,256]{1,0:T(8,128)(2,1)S(1)} collective-permute-done((bf16[512,256]{1,0:T(8,128)(2,1)}, bf16[512,256]{1,0:T(8,128)(2,1)S(1)}, u32[]{:S(2)}, u32[]{:S(2)}) %collective-permute-start.10) | collective-permute-done | bytes 262176 | tf_op jit(solution)/shard_map/ppermute | solution.py:247
  75.9 2.3 %collective-permute-start.4 = (bf16[512,256]{1,0:T(8,128)(2,1)S(1)}, bf16[512,256]{1,0:T(8,128)(2,1)S(1)}, u32[]{:S(2)}, u32[]{:S(2)}) collective-permute-start(bf16[512,256]{1,0:T(8,128)(2,1)S(1)} %collective-permute-done.3.refs_3_), channel_id=1, source_target_pairs={{0,3},{1,0},{2,1},{3,2},{4,7},{5,4},{6,5},{7,6},{8,11},{9,8},{10,9... | collective-permute-start | bytes 786440 | tf_op jit(solution)/shard_map/ppermute | solution.py:247
  78.2 1.3 %constant_dynamic-slice_fusion.refs_2_ = bf16[512,1024]{1,0:T(8,128)(2,1)S(1)} fusion(bf16[4096,1024]{1,0:T(8,128)(2,1)} %refs_2_.1, s32[]{:T(128)S(6)} %select_n.3), kind=kLoop, calls=%fused_computation | loop fusion | bytes 2097156 | tf_op jit(solution)/shard_map/dynamic_slice | solution.py:281
  79.5 5.5 %mix.5.refs_5_ = f32[512,1024]{1,0:T(8,128)S(1)} custom-call(s32[1]{0:T(128)} %bitcast.6.column_ref, bf16[512,256]{1,0:T(8,128)(2,1)S(1)} %collective-permute-done.5.refs_0_, bf16[512,256]{1,0:T(8,128)(2,1)} %collective-permute-done.11.refs_1_, bf16[512,256]{1,0:T(8,128)(2,1)} %collective-permute-done.12.refs_2_, ...), custom_call_target="tpu_custom_call" | custom-call | flops 1073741824 | bytes 2097152 | tf_op jit(solution)/shard_map/mix/pallas_call | solution.py:196
  85.0 4.4 %mix.6.refs_3_ = f32[512,1024]{1,0:T(8,128)S(1)} custom-call(s32[1]{0:T(128)} %bitcast.6.column_ref, bf16[512,256]{1,0:T(8,128)(2,1)S(1)} %collective-permute-done.1.refs_0_, bf16[512,256]{1,0:T(8,128)(2,1)S(1)} %collective-permute-done.9.refs_1_, bf16[512,256]{1,0:T(8,128)(2,1)S(1)} %collective-permute-done.10.refs_2_, ...), custom_call_target="tpu_custom_call" | custom-call | flops 1073741824 | bytes 2097152 | tf_op jit(solution)/shard_map/mix/pallas_call | solution.py:196
  89.4 2.9 %mix.7.refs_3_ = f32[512,1024]{1,0:T(8,128)S(1)} custom-call(s32[1]{0:T(128)} %bitcast.6.column_ref, bf16[512,256]{1,0:T(8,128)(2,1)S(1)} %collective-permute-done.7.refs_0_, bf16[512,256]{1,0:T(8,128)(2,1)S(1)} %collective-permute-done.8.refs_1_, bf16[4096,1024]{1,0:T(8,128)(2,1)} %refs_2_.1, f32[512,1024]{1,0:T(8,128)S(1)} %mix.6.refs_3_), custom_call_target="tpu_custom_call" | custom-call | flops 536870912 | bytes 1048576 | tf_op jit(solution)/shard_map/mix/pallas_call | solution.py:196
  92.3 1.6 %last_mix.1 = bf16[512,1024]{1,0:T(8,128)(2,1)} custom-call(bf16[512,256]{1,0:T(8,128)(2,1)S(1)} %collective-permute-done.2.refs_0_, bf16[512,256]{1,0:T(8,128)(2,1)S(1)} %collective-permute-done.4.refs_1_, bf16[512,1024]{1,0:T(8,128)(2,1)S(1)} %constant_dynamic-slice_fusion.refs_2_, f32[512,1024]{1,0:T(8,128)S(1)} %mix.7.refs_3_), custom_call_target="tpu_custom_call" | custom-call | flops 536870912 | bytes 2097152 | tf_op jit(solution)/shard_map/last_mix/pallas_call | solution.py:231
  (22 shorter events, 1.5 us)
Async XLA Ops:
  0.0 44.9 %copy-start = (bf16[512,1024]{1,0:T(8,128)(2,1)S(1)}, bf16[512,1024]{1,0:T(8,128)(2,1)}, u32[]{:S(2)}) copy-start(bf16[512,1024]{1,0:T(8,128)(2,1)} %k_ref.3) | copy-start | bytes 3145732
  0.0 44.9 %copy-start.1 = (bf16[512,1024]{1,0:T(8,128)(2,1)S(1)}, bf16[512,1024]{1,0:T(8,128)(2,1)}, u32[]{:S(2)}) copy-start(bf16[512,1024]{1,0:T(8,128)(2,1)} %v_ref.3) | copy-start | bytes 3145732
  0.0 44.9 %copy-start.3 = (f32[1024]{0:T(1024)S(1)}, f32[1024]{0:T(1024)}, u32[]{:S(2)}) copy-start(f32[1024]{0:T(1024)} %param.8) | copy-start | bytes 12292
  0.0 44.9 %copy-start.2 = (bf16[512,1024]{1,0:T(8,128)(2,1)S(1)}, bf16[512,1024]{1,0:T(8,128)(2,1)}, u32[]{:S(2)}) copy-start(bf16[512,1024]{1,0:T(8,128)(2,1)} %q_ref.3) | copy-start | bytes 3145732
  25.3 1.7 %collective-permute-start = (bf16[1024,128]{1,0:T(8,128)(2,1)S(1)}, bf16[1024,128]{1,0:T(8,128)(2,1)}, u32[]{:S(2)}, u32[]{:S(2)}) collective-permute-start(bf16[1024,128]{1,0:T(8,128)(2,1)S(1)} %bitcast.10), channel_id=1, source_target_pairs={{0,4},{4,0},{1,5},{5,1},{2,6},{6,2},{3,7},{7,3},{8,12},{12,8},{9,1... | collective-permute-start | bytes 786440 | tf_op jit(solution)/shard_map/ppermute | solution.py:256
  48.0 10.4 %collective-permute-start.5 = (bf16[512,256]{1,0:T(8,128)(2,1)}, bf16[512,256]{1,0:T(8,128)(2,1)S(1)}, u32[]{:S(2)}, u32[]{:S(2)}) collective-permute-start(bf16[512,256]{1,0:T(8,128)(2,1)} %get-tuple-element.14.refs_0_), channel_id=1, source_target_pairs={{0,1},{1,2},{2,3},{3,0},{4,5},{5,6},{6,7},{7,4},{8,9},{9,10},{10,1... | collective-permute-start | bytes 786440 | tf_op jit(solution)/shard_map/ppermute | solution.py:247
  49.6 11.2 %collective-permute-start.6 = (bf16[512,256]{1,0:T(8,128)(2,1)}, bf16[512,256]{1,0:T(8,128)(2,1)}, u32[]{:S(2)}, u32[]{:S(2)}) collective-permute-start(bf16[512,256]{1,0:T(8,128)(2,1)} %get-tuple-element.15.refs_1_), channel_id=1, source_target_pairs={{0,3},{1,0},{2,1},{3,2},{4,7},{5,4},{6,5},{7,6},{8,11},{9,8},{10,9... | collective-permute-start | bytes 786440 | tf_op jit(solution)/shard_map/ppermute | solution.py:247
  51.3 12.8 %collective-permute-start.11 = (bf16[512,256]{1,0:T(8,128)(2,1)}, bf16[512,256]{1,0:T(8,128)(2,1)}, u32[]{:S(2)}, u32[]{:S(2)}) collective-permute-start(bf16[512,256]{1,0:T(8,128)(2,1)} %get-tuple-element.15.refs_1_), channel_id=1, source_target_pairs={{0,1},{1,2},{2,3},{3,0},{4,5},{5,6},{6,7},{7,4},{8,9},{9,10},{10,1... | collective-permute-start | bytes 786440 | tf_op jit(solution)/shard_map/ppermute | solution.py:247
  51.6 18.6 %collective-permute-start.12 = (bf16[512,256]{1,0:T(8,128)(2,1)}, bf16[512,256]{1,0:T(8,128)(2,1)}, u32[]{:S(2)}, u32[]{:S(2)}) collective-permute-start(bf16[512,256]{1,0:T(8,128)(2,1)} %get-tuple-element.14.refs_0_), channel_id=1, source_target_pairs={{0,3},{1,0},{2,1},{3,2},{4,7},{5,4},{6,5},{7,6},{8,11},{9,8},{10,9... | collective-permute-start | bytes 786440 | tf_op jit(solution)/shard_map/ppermute | solution.py:247
  57.6 14.3 %collective-permute-start.1 = (bf16[512,256]{1,0:T(8,128)(2,1)}, bf16[512,256]{1,0:T(8,128)(2,1)S(1)}, u32[]{:S(2)}, u32[]{:S(2)}) collective-permute-start(bf16[512,256]{1,0:T(8,128)(2,1)} %get-tuple-element.12.refs_2_), channel_id=1, source_target_pairs={{0,1},{1,2},{2,3},{3,0},{4,5},{5,6},{6,7},{7,4},{8,9},{9,10},{10,1... | collective-permute-start | bytes 786440 | tf_op jit(solution)/shard_map/ppermute | solution.py:247
  58.5 15.1 %collective-permute-start.3 = (bf16[512,256]{1,0:T(8,128)(2,1)}, bf16[512,256]{1,0:T(8,128)(2,1)S(1)}, u32[]{:S(2)}, u32[]{:S(2)}) collective-permute-start(bf16[512,256]{1,0:T(8,128)(2,1)} %get-tuple-element.13.refs_3_), channel_id=1, source_target_pairs={{0,3},{1,0},{2,1},{3,2},{4,7},{5,4},{6,5},{7,6},{8,11},{9,8},{10,9... | collective-permute-start | bytes 786440 | tf_op jit(solution)/shard_map/ppermute | solution.py:247
  60.8 15.1 %collective-permute-start.10 = (bf16[512,256]{1,0:T(8,128)(2,1)}, bf16[512,256]{1,0:T(8,128)(2,1)S(1)}, u32[]{:S(2)}, u32[]{:S(2)}) collective-permute-start(bf16[512,256]{1,0:T(8,128)(2,1)} %get-tuple-element.12.refs_2_), channel_id=1, source_target_pairs={{0,3},{1,0},{2,1},{3,2},{4,7},{5,4},{6,5},{7,6},{8,11},{9,8},{10,9... | collective-permute-start | bytes 786440 | tf_op jit(solution)/shard_map/ppermute | solution.py:247
  64.1 20.9 %collective-permute-start.9 = (bf16[512,256]{1,0:T(8,128)(2,1)}, bf16[512,256]{1,0:T(8,128)(2,1)S(1)}, u32[]{:S(2)}, u32[]{:S(2)}) collective-permute-start(bf16[512,256]{1,0:T(8,128)(2,1)} %get-tuple-element.13.refs_3_), channel_id=1, source_target_pairs={{0,1},{1,2},{2,3},{3,0},{4,5},{5,6},{6,7},{7,4},{8,9},{9,10},{10,1... | collective-permute-start | bytes 786440 | tf_op jit(solution)/shard_map/ppermute | solution.py:247
  70.2 19.1 %collective-permute-start.7 = (bf16[512,256]{1,0:T(8,128)(2,1)S(1)}, bf16[512,256]{1,0:T(8,128)(2,1)S(1)}, u32[]{:S(2)}, u32[]{:S(2)}) collective-permute-start(bf16[512,256]{1,0:T(8,128)(2,1)S(1)} %collective-permute-done.5.refs_0_), channel_id=1, source_target_pairs={{0,1},{1,2},{2,3},{3,0},{4,5},{5,6},{6,7},{7,4},{8,9},{9,10},{10,1... | collective-permute-start | bytes 786440 | tf_op jit(solution)/shard_map/ppermute | solution.py:247
  71.9 17.5 %collective-permute-start.8 = (bf16[512,256]{1,0:T(8,128)(2,1)}, bf16[512,256]{1,0:T(8,128)(2,1)S(1)}, u32[]{:S(2)}, u32[]{:S(2)}) collective-permute-start(bf16[512,256]{1,0:T(8,128)(2,1)} %collective-permute-done.6.refs_3_), channel_id=1, source_target_pairs={{0,3},{1,0},{2,1},{3,2},{4,7},{5,4},{6,5},{7,6},{8,11},{9,8},{10,9... | collective-permute-start | bytes 786440 | tf_op jit(solution)/shard_map/ppermute | solution.py:247
  73.6 18.7 %collective-permute-start.2 = (bf16[512,256]{1,0:T(8,128)(2,1)S(1)}, bf16[512,256]{1,0:T(8,128)(2,1)S(1)}, u32[]{:S(2)}, u32[]{:S(2)}) collective-permute-start(bf16[512,256]{1,0:T(8,128)(2,1)S(1)} %collective-permute-done.1.refs_0_), channel_id=1, source_target_pairs={{0,1},{1,2},{2,3},{3,0},{4,5},{5,6},{6,7},{7,4},{8,9},{9,10},{10,1... | collective-permute-start | bytes 786440 | tf_op jit(solution)/shard_map/ppermute | solution.py:247
  75.9 16.4 %collective-permute-start.4 = (bf16[512,256]{1,0:T(8,128)(2,1)S(1)}, bf16[512,256]{1,0:T(8,128)(2,1)S(1)}, u32[]{:S(2)}, u32[]{:S(2)}) collective-permute-start(bf16[512,256]{1,0:T(8,128)(2,1)S(1)} %collective-permute-done.3.refs_3_), channel_id=1, source_target_pairs={{0,3},{1,0},{2,1},{3,2},{4,7},{5,4},{6,5},{7,6},{8,11},{9,8},{10,9... | collective-permute-start | bytes 786440 | tf_op jit(solution)/shard_map/ppermute | solution.py:247

commit v6 on v5

--- a/solution.py
+++ b/solution.py
@@ -13,7 +13,7 @@
 HALF = BLK // 2
 CORES = 2
 HEADS = 8
-CALLS = (((0, 2), (2, 4)), ((4, 6), (6, 8)))
+CALLS = (((0, 4),), ((4, 8),))
 F32 = jnp.float32
 BF16 = jnp.bfloat16
 NN, NT, TN = ((1,), (0,)), ((1,), (1,)), ((0,), (0,))
@@ -153,94 +153,93 @@
 TILE = 256
 
 
-def mix_kernel(column_ref, *refs, plan, first):
+def own_kernel(column_ref, *refs):
+    *a_refs, w_hbm, total_ref, w_ref, sems = refs
+    depth = HEADS * DH
+    ways = w_hbm.shape[0] // depth
+    copies, starts = [], []
+    for shift in range(ways):
+        start = pl.multiple_of(lax.rem(column_ref[0] + shift, ways) * depth, depth)
+        rows = pl.ds(start, depth)
+        copies.append(pltpu.make_async_copy(w_hbm.at[rows], w_ref.at[rows], sems.at[shift]))
+        copies[-1].start()
+        starts.append(start)
+    copies[0].wait()
+    for tile in range(total_ref.shape[1] // TILE):
+        cols = slice(tile * TILE, (tile + 1) * TILE)
+        total, at = None, 0
+        for a_ref in a_refs:
+            width = a_ref.shape[1]
+            rows = pl.ds(pl.multiple_of(starts[0] + at, DH), width)
+            term = dot(a_ref[...], w_ref[rows, cols], NN)
+            total = term if total is None else total + term
+            at += width
+        total_ref[:, cols] = total
+    for copy in copies[1:]:
+        copy.wait()
+
+
+def own_mix(column, w, arrays):
+    width, ways = w.shape[1], w.shape[0] // (HEADS * DH)
+    return pl.pallas_call(
+        own_kernel,
+        name="own_mix",
+        in_specs=[SMEM] + [VMEM] * len(arrays) + [HBM],
+        out_specs=[VMEM, VMEM],
+        out_shape=[pltpu.VMEM((BLK, width), F32), pltpu.VMEM(w.shape, BF16)],
+        scratch_shapes=[pltpu.SemaphoreType.DMA((ways,))],
+        compiler_params=PARAMS,
+        cost_estimate=cost(2 * BLK * HEADS * DH * width, 2 * w.size),
+    )(column, *arrays, in_hbm(w))
+
+
+def mix_kernel(column_ref, *refs, plan, first, last):
     count = len(plan)
-    a_refs, w_hbm, rest = refs[:count], refs[count], refs[count + 1 :]
+    a_refs, w_ref, rest = refs[:count], refs[count], refs[count + 1 :]
     if not first:
         total_ref, rest = rest[0], rest[1:]
-    out_ref, w_ref, sems = rest
-    ways = w_hbm.shape[0] // (HEADS * DH)
-    tiles = [slice(at, at + TILE) for at in range(0, out_ref.shape[1], TILE)]
-    copies = {}
-    for tile, cols in enumerate(tiles):
-        at = 0
-        for piece, (a_ref, (shift, head)) in enumerate(zip(a_refs, plan)):
-            depth = a_ref.shape[1]
+    if last:
+        out_hbm, out_ref, sems = rest
+    else:
+        (out_ref,) = rest
+    ways = w_ref.shape[0] // (HEADS * DH)
+    copies = []
+    for tile in range(out_ref.shape[1] // TILE):
+        cols = slice(tile * TILE, (tile + 1) * TILE)
+        total = None if first else total_ref[:, cols]
+        for a_ref, (shift, head) in zip(a_refs, plan):
             source = lax.rem(column_ref[0] + (shift + ways), ways)
             start = pl.multiple_of(source * (HEADS * DH) + head * DH, DH)
-            copy = pltpu.make_async_copy(
-                w_hbm.at[pl.ds(start, depth), cols],
-                w_ref.at[at : at + depth, cols],
-                sems.at[tile, piece],
-            )
+            term = dot(a_ref[...], w_ref[pl.ds(start, a_ref.shape[1]), cols], NN)
+            total = term if total is None else total + term
+        out_ref[:, cols] = total.astype(out_ref.dtype)
+        if last:
+            copy = pltpu.make_async_copy(out_ref.at[:, cols], out_hbm.at[:, cols], sems.at[tile])
             copy.start()
-            copies[tile, piece] = copy
-            at += depth
-    for tile, cols in enumerate(tiles):
-        total, at = None if first else total_ref[:, cols], 0
-        for piece, a_ref in enumerate(a_refs):
-            copies[tile, piece].wait()
-            depth = a_ref.shape[1]
-            term = dot(a_ref[...], w_ref[at : at + depth, cols], NN)
-            total = term if total is None else total + term
-            at += depth
-        out_ref[:, cols] = total
-
-
-def mix(column, w, plan, arrays, total=None):
+            copies.append(copy)
+    for copy in copies:
+        copy.wait()
+
+
+def mix(column, w, plan, arrays, total=None, last=False):
     width = w.shape[1]
     operands = [column, *arrays, w] + ([] if total is None else [total])
     depth = sum(a.shape[1] for a in arrays)
-    specs = [SMEM] + [VMEM] * (len(operands) - 1)
-    specs[1 + len(arrays)] = HBM
-    return pl.pallas_call(
-        functools.partial(mix_kernel, plan=tuple(plan), first=total is None),
+    if last:
+        out_shape = jax.ShapeDtypeStruct((BLK, width), BF16)
+        scratch = [pltpu.VMEM((BLK, width), BF16), pltpu.SemaphoreType.DMA((width // TILE,))]
+    else:
+        out_shape, scratch = pltpu.VMEM((BLK, width), F32), []
+    return pl.pallas_call(
+        functools.partial(mix_kernel, plan=tuple(plan), first=total is None, last=last),
         name="mix",
-        in_specs=specs,
-        out_specs=VMEM,
-        out_shape=pltpu.VMEM((BLK, width), F32),
-        scratch_shapes=[
-            pltpu.VMEM((depth, width), BF16),
-            pltpu.SemaphoreType.DMA((width // TILE, len(arrays))),
-        ],
+        in_specs=[SMEM] + [VMEM] * (len(operands) - 1),
+        out_specs=HBM if last else VMEM,
+        out_shape=out_shape,
+        scratch_shapes=scratch,
         compiler_params=PARAMS,
         cost_estimate=cost(2 * BLK * depth * width, 2 * depth * width),
     )(*operands)
-
-
-def last_kernel(*refs):
-    *a_refs, w_ref, total_ref, out_hbm, out_ref, sems = refs
-    copies = []
-    for tile in range(w_ref.shape[1] // TILE):
-        cols = slice(tile * TILE, (tile + 1) * TILE)
-        total, at = total_ref[:, cols], 0
-        for a_ref in a_refs:
-            depth = a_ref.shape[1]
-            total = total + dot(a_ref[...], w_ref[at : at + depth, cols], NN)
-            at += depth
-        out_ref[:, cols] = total.astype(BF16)
-        copy = pltpu.make_async_copy(out_ref.at[:, cols], out_hbm.at[:, cols], sems.at[tile])
-        copy.start()
-        copies.append(copy)
-    for copy in copies:
-        copy.wait()
-
-
-def last_mix(arrays, w, total):
-    depth, width = w.shape
-    return pl.pallas_call(
-        last_kernel,
-        name="last_mix",
-        in_specs=[VMEM] * (len(arrays) + 2),
-        out_specs=HBM,
-        out_shape=jax.ShapeDtypeStruct((BLK, width), BF16),
-        scratch_shapes=[
-            pltpu.VMEM((BLK, width), BF16),
-            pltpu.SemaphoreType.DMA((width // TILE,)),
-        ],
-        compiler_params=PARAMS,
-        cost_estimate=cost(2 * BLK * depth * width, BLK * width * 4),
-    )(*arrays, w, total)
 
 
 def along(value, shift, count):
@@ -256,30 +255,28 @@
     other = lax.ppermute(own, "core", [(0, 1), (1, 0)])
     sums = exclusive_sums(core, own, other, chips)
     carried = lax.all_to_all(sums, "chip", 0, 0, tiled=True)
-    q, k, v, weights = in_vmem(q), in_vmem(k), in_vmem(v), in_hbm(w)
+    q, k, v = in_vmem(q), in_vmem(k), in_vmem(v)
     gain_row = gain.reshape(1, -1)
     heads, mine, left, right, far = [], [], [], [], []
     for groups in CALLS:
         heads += [first for first, _ in groups]
         mine += attention(q, k, v, carried, gain_row, groups)
-    for value in mine:
-        left.append(along(value, 1, ways))
-        right.append(along(value, -1, ways))
+    for at, value in enumerate(mine):
+        sides = along(value, 1, ways), along(value, -1, ways)
+        sides = lax.optimization_barrier(sides)
+        left.append(sides[0])
+        right.append(sides[1])
+        far.append(along(sides[1], -1, ways) if at % 2 else along(sides[0], 1, ways))
 
     def plan(shift, begin, end):
         return [(shift, head) for head in heads[begin:end]]
 
-    total = mix(column, weights, plan(0, 0, 4), mine)
-    left[0], right[1], total = lax.optimization_barrier((left[0], right[1], total))
-    for at in range(4):
-        far.append(along(right[at], -1, ways) if at % 2 else along(left[at], 1, ways))
-    for a, b in ((0, 2), (2, 4)):
-        sides = plan(-1, a, b) + plan(1, a, b)
-        total = mix(column, weights, sides, left[a:b] + right[a:b], total)
-    total = mix(column, weights, plan(2, 0, 2), far[:2], total)
-    row = lax.rem(column[0] + ways // 2, ways) * (HEADS * DH) + heads[2] * DH
-    tail = in_vmem(lax.dynamic_slice_in_dim(w, row, (HEADS - heads[2]) * DH))
-    return last_mix(far[2:], tail, total)
+    total, w = own_mix(column, w, mine)
+    for at in range(2):
+        sides = plan(-1, at, at + 1) + plan(1, at, at + 1)
+        total = mix(column, w, sides, [left[at], right[at]], total)
+    total = mix(column, w, plan(2, 0, 1), far[:1], total)
+    return mix(column, w, plan(2, 1, 2), far[1:], total, True)
 
 
 def solution(mesh):

time: 94.5 us -> 88.7 us (0.939)
  Pallas kernels: 29.1 us -> 17.4 us
  waiting for transfers between devices: 7.12 us -> 16.8 us
  starting transfers between devices: 16.2 us -> 10 us
  local copies, waits for them, and re-layouts: 1.31 us -> 3.73 us
    pallas_call x4, Pallas kernels: 18.2 us -> 5.95 us  [mix(): pl.pallas_call(functools.partial(mix_kernel, plan=tuple(plan), first=tota...]
    ppermute x12 -> x6, waiting for transfers between devices: 5.46 us -> 15.2 us  [along(): lax.ppermute(value, 'fsdp', [(i, (i + shift) % count) for i in range(coun...]
    ppermute x12 -> x6, starting transfers between devices: 16.2 us -> 10 us  [along(): lax.ppermute(value, 'fsdp', [(i, (i + shift) % count) for i in range(coun...]
    unnamed x8 -> x20, local copies, waits for them, and re-layouts: 0.02 us -> 3.73 us
    pallas_call x1, Pallas kernels: 1.59 us -> 3.55 us  [own_mix(): pl.pallas_call(own_kernel, name='own_mix', in_specs=[SMEM] + [VMEM] * len...]
    pallas_call x2, Pallas kernels: 6.16 us -> 4.73 us  [attention(): pl.pallas_call(functools.partial(attention_kernel, groups=groups), name='...]
    dynamic_slice x1 -> x0, local copies, waits for them, and re-layouts: 1.29 us -> none  [shards(): tail = in_vmem(lax.dynamic_slice_in_dim(w, row, (HEADS - heads[2]) * DH))]
  transfers between devices with their start and end apart: 13 -> 7, of which waited for: 4 -> 4; matrix products, arithmetic and copies ran while one was open for 1% -> 0% of each run, Pallas kernels for 23% -> 12%
where the time goes in v6:
time: 88.7 us; the launch traced here: 88.3 us
  blocking collectives  40 us (45%)
  Pallas kernels  17.4 us (20%)
  waiting for transfers between devices  16.8 us (19%)
  starting transfers between devices  10 us (11%)
  local copies, waits for them, and re-layouts  3.73 us (4%)
    all_to_all x1, blocking collectives, shards(): own = lax.all_to_all(states, 'chip', 0, 0, tiled=True)  23.1 us
    all_to_all x1, blocking collectives, shards(): carried = lax.all_to_all(sums, 'chip', 0, 0, tiled=True)  16.9 us
    ppermute x6, waiting for transfers between devices, along(): lax.ppermute(value, 'fsdp', [(i, (i + shift) % count) for i in range(coun...  15.2 us
    ppermute x6, starting transfers between devices, along(): lax.ppermute(value, 'fsdp', [(i, (i + shift) % count) for i in range(coun...  10 us
    pallas_call x4, Pallas kernels, mix(): pl.pallas_call(functools.partial(mix_kernel, plan=tuple(plan), first=tota...  5.95 us
    pallas_call x2, Pallas kernels, attention(): pl.pallas_call(functools.partial(attention_kernel, groups=groups), name='...  4.73 us
    unnamed x20, local copies, waits for them, and re-layouts  3.73 us
    pallas_call x1, Pallas kernels, own_mix(): pl.pallas_call(own_kernel, name='own_mix', in_specs=[SMEM] + [VMEM] * len...  3.55 us
  transfers between devices with their start and end apart: 7, of which 4 were waited for; matrix products, arithmetic and copies ran while one was open for 0% of the time, Pallas kernels for 12%

profile of v6, /device:TPU:32, one launch (start us, length us, event | category | flops | bytes accessed | tf_op | source)
XLA Modules:
  0.0 88.3 jit_solution(12961579864987303116)
XLA Ops:
  0.0 2.1 %block_states.1 = bf16[1024,128]{1,0:T(8,128)(2,1)S(1)} custom-call(bf16[512,1024]{1,0:T(8,128)(2,1)} %k_ref.3, bf16[512,1024]{1,0:T(8,128)(2,1)} %v_ref.3), custom_call_target="tpu_custom_call" | custom-call | flops 134217728 | bytes 2097152 | tf_op jit(solution)/shard_map/block_states/pallas_call | solution.py:88
  2.2 23.1 %all_to_all.22 = bf16[32,32,128]{2,1,0:T(8,128)(2,1)S(1)} all-to-all(bf16[32,32,128]{2,1,0:T(8,128)(2,1)S(1)} %bitcast.9), channel_id=1, replica_groups=mesh['chip'=32,'core'=2,'fsdp'=4] {'chip'}, dimensions={0} | all-to-all | bytes 524288 | tf_op jit(solution)/shard_map/all_to_all | solution.py:254
  25.3 1.7 %collective-permute-done.other_ref = bf16[1024,128]{1,0:T(8,128)(2,1)} collective-permute-done((bf16[1024,128]{1,0:T(8,128)(2,1)S(1)}, bf16[1024,128]{1,0:T(8,128)(2,1)}, u32[]{:S(2)}, u32[]{:S(2)}) %collective-permute-start) | collective-permute-done | bytes 262176 | tf_op jit(solution)/shard_map/ppermute | solution.py:255
  27.0 1.1 %exclusive_sums.1 = bf16[1024,128]{1,0:T(8,128)(2,1)S(1)} custom-call(s32[1]{0:T(128)} %bitcast.1.core_ref, bf16[1024,128]{1,0:T(8,128)(2,1)S(1)} %bitcast.11, bf16[1024,128]{1,0:T(8,128)(2,1)} %collective-permute-done.other_ref), custom_call_target="tpu_custom_call" | custom-call | flops 524288 | bytes 786432 | tf_op jit(solution)/shard_map/exclusive_sums/pallas_call | solution.py:116
  28.1 16.9 %all_to_all.23 = bf16[32,32,128]{2,1,0:T(8,128)(2,1)S(1)} all-to-all(bf16[32,32,128]{2,1,0:T(8,128)(2,1)S(1)} %bitcast.12), channel_id=1, replica_groups=mesh['chip'=32,'core'=2,'fsdp'=4] {'chip'}, dimensions={0} | all-to-all | bytes 524288 | tf_op jit(solution)/shard_map/all_to_all | solution.py:257
  45.0 2.4 %attention.3.refs_0_ = bf16[512,512]{1,0:T(8,128)(2,1)S(1)} custom-call(bf16[512,1024]{1,0:T(8,128)(2,1)S(1)} %copy-done.2, bf16[512,1024]{1,0:T(8,128)(2,1)S(1)} %copy-done, bf16[512,1024]{1,0:T(8,128)(2,1)S(1)} %copy-done.1, bf16[1024,128]{1,0:T(8,128)(2,1)S(1)} %bitcast.7, f32[1,1024]{1,0:T(1,128)S(1)} %bitcast.13), custom_call_target="tpu_custom_call" | custom-call | flops 536870912 | bytes 2097152 | tf_op jit(solution)/shard_map/attention/pallas_call | solution.py:142
  47.3 1.7 %collective-permute-start.4 = (bf16[512,512]{1,0:T(8,128)(2,1)S(1)}, bf16[512,512]{1,0:T(8,128)(2,1)}, u32[]{:S(2)}, u32[]{:S(2)}) collective-permute-start(bf16[512,512]{1,0:T(8,128)(2,1)S(1)} %attention.3.refs_0_), channel_id=1, source_target_pairs={{0,1},{1,2},{2,3},{3,0},{4,5},{5,6},{6,7},{7,4},{8,9},{9,10},{10,1... | collective-permute-start | bytes 1572872 | tf_op jit(solution)/shard_map/ppermute | solution.py:246
  49.0 1.7 %collective-permute-start.5 = (bf16[512,512]{1,0:T(8,128)(2,1)S(1)}, bf16[512,512]{1,0:T(8,128)(2,1)S(1)}, u32[]{:S(2)}, u32[]{:S(2)}) collective-permute-start(bf16[512,512]{1,0:T(8,128)(2,1)S(1)} %attention.3.refs_0_), channel_id=1, source_target_pairs={{0,3},{1,0},{2,1},{3,2},{4,7},{5,4},{6,5},{7,6},{8,11},{9,8},{10,9... | collective-permute-start | bytes 1572872 | tf_op jit(solution)/shard_map/ppermute | solution.py:246
  50.7 2.4 %attention.2.refs_1_ = bf16[512,512]{1,0:T(8,128)(2,1)S(1)} custom-call(bf16[512,1024]{1,0:T(8,128)(2,1)S(1)} %copy-done.2, bf16[512,1024]{1,0:T(8,128)(2,1)S(1)} %copy-done, bf16[512,1024]{1,0:T(8,128)(2,1)S(1)} %copy-done.1, bf16[1024,128]{1,0:T(8,128)(2,1)S(1)} %bitcast.8, f32[1,1024]{1,0:T(1,128)S(1)} %bitcast.14), custom_call_target="tpu_custom_call" | custom-call | flops 536870912 | bytes 2097152 | tf_op jit(solution)/shard_map/attention/pallas_call | solution.py:142
  53.0 0.4 collective-permute-start.1
  53.5 2.9 %collective-permute-start.2 = (bf16[512,512]{1,0:T(8,128)(2,1)S(1)}, bf16[512,512]{1,0:T(8,128)(2,1)S(1)}, u32[]{:S(2)}, u32[]{:S(2)}) collective-permute-start(bf16[512,512]{1,0:T(8,128)(2,1)S(1)} %attention.2.refs_1_), channel_id=1, source_target_pairs={{0,3},{1,0},{2,1},{3,2},{4,7},{5,4},{6,5},{7,6},{8,11},{9,8},{10,9... | collective-permute-start | bytes 1572872 | tf_op jit(solution)/shard_map/ppermute | solution.py:246
  56.4 0.8 copy-done.5
  57.2 6.4 %collective-permute-done.4.refs_0_ = bf16[512,512]{1,0:T(8,128)(2,1)} collective-permute-done((bf16[512,512]{1,0:T(8,128)(2,1)S(1)}, bf16[512,512]{1,0:T(8,128)(2,1)}, u32[]{:S(2)}, u32[]{:S(2)}) %collective-permute-start.4) | collective-permute-done | bytes 524320 | tf_op jit(solution)/shard_map/ppermute | solution.py:246
  63.9 0.8 copy-done.7
  64.7 1.6 %collective-permute-start.6 = (bf16[512,512]{1,0:T(8,128)(2,1)}, bf16[512,512]{1,0:T(8,128)(2,1)S(1)}, u32[]{:S(2)}, u32[]{:S(2)}) collective-permute-start(bf16[512,512]{1,0:T(8,128)(2,1)} %collective-permute-done.4.refs_0_), channel_id=1, source_target_pairs={{0,1},{1,2},{2,3},{3,0},{4,5},{5,6},{6,7},{7,4},{8,9},{9,10},{10,1... | collective-permute-start | bytes 1572872 | tf_op jit(solution)/shard_map/ppermute | solution.py:246
  66.3 8.5 %collective-permute-done.1.refs_0_ = bf16[512,512]{1,0:T(8,128)(2,1)S(1)} collective-permute-done((bf16[512,512]{1,0:T(8,128)(2,1)S(1)}, bf16[512,512]{1,0:T(8,128)(2,1)S(1)}, u32[]{:S(2)}, u32[]{:S(2)}) %collective-permute-start.1) | collective-permute-done | bytes 524320 | tf_op jit(solution)/shard_map/ppermute | solution.py:246
  74.7 1.8 %collective-permute-start.3 = (bf16[512,512]{1,0:T(8,128)(2,1)S(1)}, bf16[512,512]{1,0:T(8,128)(2,1)S(1)}, u32[]{:S(2)}, u32[]{:S(2)}) collective-permute-start(bf16[512,512]{1,0:T(8,128)(2,1)S(1)} %collective-permute-done.2.refs_1_), channel_id=1, source_target_pairs={{0,3},{1,0},{2,1},{3,2},{4,7},{5,4},{6,5},{7,6},{8,11},{9,8},{10,9... | collective-permute-start | bytes 1572872 | tf_op jit(solution)/shard_map/ppermute | solution.py:246
  76.5 1.0 %copy-done.4 = bf16[512,512]{1,0:T(8,128)(2,1)S(1)} copy-done((bf16[512,512]{1,0:T(8,128)(2,1)S(1)}, bf16[512,512]{1,0:T(8,128)(2,1)}, u32[]{:S(2)}) %copy-start.4) | copy-done | bytes 524312
  77.6 1.0 %copy-done.6 = bf16[512,512]{1,0:T(8,128)(2,1)S(1)} copy-done((bf16[512,512]{1,0:T(8,128)(2,1)S(1)}, bf16[512,512]{1,0:T(8,128)(2,1)}, u32[]{:S(2)}) %copy-start.6) | copy-done | bytes 524312
  78.6 3.5 %own_mix.1 = (f32[512,1024]{1,0:T(8,128)S(1)}, bf16[4096,1024]{1,0:T(8,128)(2,1)S(1)}) custom-call(s32[1]{0:T(128)} %bitcast.column_ref, bf16[512,512]{1,0:T(8,128)(2,1)S(1)} %copy-done.4, bf16[512,512]{1,0:T(8,128)(2,1)S(1)} %copy-done.6, bf16[4096,1024]{1,0:T(8,128)(2,1)} %refs_2_.1), custom_call_target="tpu_custom_call" | custom-call | flops 1073741824 | bytes 8388608 | tf_op jit(solution)/shard_map/own_mix/pallas_call | solution.py:184
  82.2 2.3 %mix.4.refs_3_ = f32[512,1024]{1,0:T(8,128)S(1)} custom-call(s32[1]{0:T(128)} %bitcast.column_ref, bf16[512,512]{1,0:T(8,128)(2,1)} %collective-permute-done.4.refs_0_, bf16[512,512]{1,0:T(8,128)(2,1)S(1)} %copy-done.8, bf16[4096,1024]{1,0:T(8,128)(2,1)S(1)} %get-tuple-element.12.refs_2_.refs_1_, f32[512,1024]{1,0:T(8,128)S(1)} %get-tuple-element.16.refs_3_), custom_call_target="tpu_custom_call" | custom-call | flops 1073741824 | bytes 2097152 | tf_op jit(solution)/shard_map/mix/pallas_call | solution.py:233
  84.5 1.3 %mix.5.refs_2_ = f32[512,1024]{1,0:T(8,128)S(1)} custom-call(s32[1]{0:T(128)} %bitcast.column_ref, bf16[512,512]{1,0:T(8,128)(2,1)S(1)} %collective-permute-done.1.refs_0_, bf16[512,512]{1,0:T(8,128)(2,1)S(1)} %collective-permute-done.2.refs_1_, bf16[4096,1024]{1,0:T(8,128)(2,1)S(1)} %get-tuple-element.12.refs_2_.refs_1_, f32[512,1024]{1,0:T(8,128)S(1)} %mix.4.refs_3_), custom_call_target="tpu_custom_call" | custom-call | flops 1073741824 | bytes 2097152 | tf_op jit(solution)/shard_map/mix/pallas_call | solution.py:233
  85.8 0.7 mix.6.refs_2_
  86.6 1.6 %mix.7 = bf16[512,1024]{1,0:T(8,128)(2,1)} custom-call(s32[1]{0:T(128)} %bitcast.column_ref, bf16[512,512]{1,0:T(8,128)(2,1)S(1)} %collective-permute-done.3.refs_0_, bf16[4096,1024]{1,0:T(8,128)(2,1)S(1)} %get-tuple-element.12.refs_2_.refs_1_, f32[512,1024]{1,0:T(8,128)S(1)} %mix.6.refs_2_), custom_call_target="tpu_custom_call" | custom-call | flops 536870912 | bytes 1048576 | tf_op jit(solution)/shard_map/mix/pallas_call | solution.py:233
  (21 shorter events, 0.3 us)
Async XLA Ops:
  0.0 44.9 %copy-start = (bf16[512,1024]{1,0:T(8,128)(2,1)S(1)}, bf16[512,1024]{1,0:T(8,128)(2,1)}, u32[]{:S(2)}) copy-start(bf16[512,1024]{1,0:T(8,128)(2,1)} %k_ref.3) | copy-start | bytes 3145732
  0.0 44.9 %copy-start.1 = (bf16[512,1024]{1,0:T(8,128)(2,1)S(1)}, bf16[512,1024]{1,0:T(8,128)(2,1)}, u32[]{:S(2)}) copy-start(bf16[512,1024]{1,0:T(8,128)(2,1)} %v_ref.3) | copy-start | bytes 3145732
  0.0 44.9 %copy-start.9 = (f32[1024]{0:T(1024)S(1)}, f32[1024]{0:T(1024)}, u32[]{:S(2)}) copy-start(f32[1024]{0:T(1024)} %param.8) | copy-start | bytes 12292
  0.0 44.9 %copy-start.2 = (bf16[512,1024]{1,0:T(8,128)(2,1)S(1)}, bf16[512,1024]{1,0:T(8,128)(2,1)}, u32[]{:S(2)}) copy-start(bf16[512,1024]{1,0:T(8,128)(2,1)} %q_ref.3) | copy-start | bytes 3145732
  25.3 1.7 %collective-permute-start = (bf16[1024,128]{1,0:T(8,128)(2,1)S(1)}, bf16[1024,128]{1,0:T(8,128)(2,1)}, u32[]{:S(2)}, u32[]{:S(2)}) collective-permute-start(bf16[1024,128]{1,0:T(8,128)(2,1)S(1)} %bitcast.10), channel_id=1, source_target_pairs={{0,4},{4,0},{1,5},{5,1},{2,6},{6,2},{3,7},{7,3},{8,12},{12,8},{9,1... | collective-permute-start | bytes 786440 | tf_op jit(solution)/shard_map/ppermute | solution.py:255
  47.3 5.7 %copy-start.3 = (bf16[512,512]{1,0:T(8,128)(2,1)}, bf16[512,512]{1,0:T(8,128)(2,1)S(1)}, u32[]{:S(2)}) copy-start(bf16[512,512]{1,0:T(8,128)(2,1)S(1)} %attention.3.refs_0_) | copy-start | bytes 1572868
  47.3 16.3 %collective-permute-start.4 = (bf16[512,512]{1,0:T(8,128)(2,1)S(1)}, bf16[512,512]{1,0:T(8,128)(2,1)}, u32[]{:S(2)}, u32[]{:S(2)}) collective-permute-start(bf16[512,512]{1,0:T(8,128)(2,1)S(1)} %attention.3.refs_0_), channel_id=1, source_target_pairs={{0,1},{1,2},{2,3},{3,0},{4,5},{5,6},{6,7},{7,4},{8,9},{9,10},{10,1... | collective-permute-start | bytes 1572872 | tf_op jit(solution)/shard_map/ppermute | solution.py:246
  49.0 14.9 %collective-permute-start.5 = (bf16[512,512]{1,0:T(8,128)(2,1)S(1)}, bf16[512,512]{1,0:T(8,128)(2,1)S(1)}, u32[]{:S(2)}, u32[]{:S(2)}) collective-permute-start(bf16[512,512]{1,0:T(8,128)(2,1)S(1)} %attention.3.refs_0_), channel_id=1, source_target_pairs={{0,3},{1,0},{2,1},{3,2},{4,7},{5,4},{6,5},{7,6},{8,11},{9,8},{10,9... | collective-permute-start | bytes 1572872 | tf_op jit(solution)/shard_map/ppermute | solution.py:246
  53.0 21.7 %collective-permute-start.1 = (bf16[512,512]{1,0:T(8,128)(2,1)S(1)}, bf16[512,512]{1,0:T(8,128)(2,1)S(1)}, u32[]{:S(2)}, u32[]{:S(2)}) collective-permute-start(bf16[512,512]{1,0:T(8,128)(2,1)S(1)} %attention.2.refs_1_), channel_id=1, source_target_pairs={{0,1},{1,2},{2,3},{3,0},{4,5},{5,6},{6,7},{7,4},{8,9},{9,10},{10,1... | collective-permute-start | bytes 1572872 | tf_op jit(solution)/shard_map/ppermute | solution.py:246
  53.5 21.2 %collective-permute-start.2 = (bf16[512,512]{1,0:T(8,128)(2,1)S(1)}, bf16[512,512]{1,0:T(8,128)(2,1)S(1)}, u32[]{:S(2)}, u32[]{:S(2)}) collective-permute-start(bf16[512,512]{1,0:T(8,128)(2,1)S(1)} %attention.2.refs_1_), channel_id=1, source_target_pairs={{0,3},{1,0},{2,1},{3,2},{4,7},{5,4},{6,5},{7,6},{8,11},{9,8},{10,9... | collective-permute-start | bytes 1572872 | tf_op jit(solution)/shard_map/ppermute | solution.py:246
  56.4 0.8 copy-start.5
  63.9 0.8 copy-start.7
  64.7 21.1 %collective-permute-start.6 = (bf16[512,512]{1,0:T(8,128)(2,1)}, bf16[512,512]{1,0:T(8,128)(2,1)S(1)}, u32[]{:S(2)}, u32[]{:S(2)}) collective-permute-start(bf16[512,512]{1,0:T(8,128)(2,1)} %collective-permute-done.4.refs_0_), channel_id=1, source_target_pairs={{0,1},{1,2},{2,3},{3,0},{4,5},{5,6},{6,7},{7,4},{8,9},{9,10},{10,1... | collective-permute-start | bytes 1572872 | tf_op jit(solution)/shard_map/ppermute | solution.py:246
  74.7 11.8 %collective-permute-start.3 = (bf16[512,512]{1,0:T(8,128)(2,1)S(1)}, bf16[512,512]{1,0:T(8,128)(2,1)S(1)}, u32[]{:S(2)}, u32[]{:S(2)}) collective-permute-start(bf16[512,512]{1,0:T(8,128)(2,1)S(1)} %collective-permute-done.2.refs_1_), channel_id=1, source_target_pairs={{0,3},{1,0},{2,1},{3,2},{4,7},{5,4},{6,5},{7,6},{8,11},{9,8},{10,9... | collective-permute-start | bytes 1572872 | tf_op jit(solution)/shard_map/ppermute | solution.py:246
  76.5 1.0 %copy-start.4 = (bf16[512,512]{1,0:T(8,128)(2,1)S(1)}, bf16[512,512]{1,0:T(8,128)(2,1)}, u32[]{:S(2)}) copy-start(bf16[512,512]{1,0:T(8,128)(2,1)} %copy-done.3) | copy-start | bytes 1572868
  77.6 1.0 %copy-start.6 = (bf16[512,512]{1,0:T(8,128)(2,1)S(1)}, bf16[512,512]{1,0:T(8,128)(2,1)}, u32[]{:S(2)}) copy-start(bf16[512,512]{1,0:T(8,128)(2,1)} %copy-done.5) | copy-start | bytes 1572868
  78.6 3.6 %copy-start.8 = (bf16[512,512]{1,0:T(8,128)(2,1)S(1)}, bf16[512,512]{1,0:T(8,128)(2,1)}, u32[]{:S(2)}) copy-start(bf16[512,512]{1,0:T(8,128)(2,1)} %copy-done.7) | copy-start | bytes 1572868

commit v7 on v6

--- a/solution.py
+++ b/solution.py
@@ -13,7 +13,10 @@
 HALF = BLK // 2
 CORES = 2
 HEADS = 8
-CALLS = (((0, 4),), ((4, 8),))
+LATE = 6
+EARLY = HEADS - LATE
+GAIN_ROWS = 16
+CALLS = ((0, 3), (3, 6))
 F32 = jnp.float32
 BF16 = jnp.bfloat16
 NN, NT, TN = ((1,), (0,)), ((1,), (1,)), ((0,), (0,))
@@ -39,9 +42,9 @@
     return pl.CostEstimate(flops=flops, bytes_accessed=size, transcendentals=0)
 
 
-def within_block(q_ref, k_ref, v_ref, h, causal):
-    cols = slice(h * DH, (h + 1) * DH)
-    q0, q1 = q_ref[:HALF, cols], q_ref[HALF:, cols]
+def within_block(q_ref, k_ref, v_ref, h, causal, shift=0):
+    cols, query_cols = slice(h * DH, (h + 1) * DH), slice((h - shift) * DH, (h - shift + 1) * DH)
+    q0, q1 = q_ref[:HALF, query_cols], q_ref[HALF:, query_cols]
     k0, k1 = k_ref[:HALF, cols], k_ref[HALF:, cols]
     v0, v1 = v_ref[:HALF, cols], v_ref[HALF:, cols]
     s00 = jnp.where(causal, dot(q0, k0, NT), 0.0).astype(BF16)
@@ -63,42 +66,76 @@
     return (att * lax.rsqrt(mean_square + 1e-6) * gain).astype(BF16)
 
 
-PARTS = 2
-
-
-def state_kernel(k_hbm, v_hbm, out_ref, k_ref, v_ref, sems):
-    width = k_ref.shape[1] // PARTS
-    copies = []
-    for part in range(PARTS):
-        cols = slice(part * width, (part + 1) * width)
-        for at, (hbm, ref) in enumerate(((k_hbm, k_ref), (v_hbm, v_ref))):
-            copy = pltpu.make_async_copy(hbm.at[:, cols], ref.at[:, cols], sems.at[part, at])
-            copy.start()
-            copies.append(copy)
-    for part in range(PARTS):
-        copies[2 * part].wait()
-        copies[2 * part + 1].wait()
-        for h in range(part * width // DH, (part + 1) * width // DH):
-            cols = slice(h * DH, (h + 1) * DH)
-            out_ref[cols, :] = dot(k_ref[:, cols], v_ref[:, cols], TN).astype(BF16)
-
-
-def block_states(k, v):
+def state_kernel(q_hbm, k_hbm, v_hbm, gain_ref, out_ref, early_hbm, q_ref, k_ref, v_ref, early_ref, sems):
+    early = slice(LATE * DH, HEADS * DH)
+    late = slice(0, LATE * DH)
+    copies = [
+        pltpu.make_async_copy(hbm.at[:, cols], ref.at[:, cols], sems.at[at])
+        for at, (hbm, ref, cols) in enumerate(
+            (
+                (k_hbm, k_ref, early),
+                (v_hbm, v_ref, early),
+                (k_hbm, k_ref, late),
+                (v_hbm, v_ref, late),
+            )
+        )
+    ]
+    copies.append(pltpu.make_async_copy(q_hbm.at[:, early], q_ref, sems.at[4]))
+    for at in (4, 0, 1, 2, 3):
+        copies[at].start()
+    gain = gain_ref[:, early]
+    high = gain.astype(BF16)
+    rest = gain - high.astype(F32)
+    middle = rest.astype(BF16)
+    low = (rest - middle.astype(F32)).astype(BF16)
+    blank = jnp.zeros((GAIN_ROWS - 3, EARLY * DH), BF16)
+    early_ref[BLK:, : EARLY * DH] = jnp.concatenate([high, middle, low, blank])
+    early_ref[BLK:, EARLY * DH :] = jnp.zeros((GAIN_ROWS, EARLY * DH), BF16)
+    causal = causal_mask()
+
+    def state(h):
+        cols = slice(h * DH, (h + 1) * DH)
+        out_ref[cols, :] = dot(k_ref[:, cols], v_ref[:, cols], TN).astype(BF16)
+
+    copies[4].wait()
+    early_ref[:BLK, : EARLY * DH] = q_ref[...]
+    copies[0].wait()
+    copies[1].wait()
+    for h in range(LATE, HEADS):
+        top, bottom = within_block(q_ref, k_ref, v_ref, h, causal, LATE)
+        cols = slice((EARLY + h - LATE) * DH, (EARLY + h - LATE + 1) * DH)
+        early_ref[:HALF, cols] = top.astype(BF16)
+        early_ref[HALF:BLK, cols] = bottom.astype(BF16)
+    out = pltpu.make_async_copy(early_ref, early_hbm, sems.at[5])
+    out.start()
+    for h in range(LATE, HEADS):
+        state(h)
+    copies[2].wait()
+    copies[3].wait()
+    for h in range(LATE):
+        state(h)
+    out.wait()
+
+
+def block_states(q, k, v, gain):
     width = k.shape[1]
+    early = (BLK + GAIN_ROWS, 2 * EARLY * DH)
     return pl.pallas_call(
         state_kernel,
         name="block_states",
-        in_specs=[HBM, HBM],
-        out_specs=VMEM,
-        out_shape=pltpu.VMEM((width, DH), BF16),
+        in_specs=[HBM, HBM, HBM, VMEM],
+        out_specs=[VMEM, HBM],
+        out_shape=[pltpu.VMEM((width, DH), BF16), pltpu.HBM(early, BF16)],
         scratch_shapes=[
+            pltpu.VMEM((BLK, EARLY * DH), BF16),
             pltpu.VMEM(k.shape, BF16),
             pltpu.VMEM(v.shape, BF16),
-            pltpu.SemaphoreType.DMA((PARTS, 2)),
+            pltpu.VMEM(early, BF16),
+            pltpu.SemaphoreType.DMA((6,)),
         ],
         compiler_params=PARAMS,
         cost_estimate=cost(2 * BLK * DH * width, 2 * BLK * width * 2),
-    )(in_hbm(k), in_hbm(v))
+    )(in_hbm(q), in_hbm(k), in_hbm(v), gain)
 
 
 def scan_kernel(core_ref, own_ref, other_ref, out_ref, *, chips):
@@ -118,36 +155,110 @@
         name="exclusive_sums",
         in_specs=[SMEM, VMEM, VMEM],
         out_specs=VMEM,
-        out_shape=pltpu.VMEM(own.shape, BF16),
+        out_shape=jax.ShapeDtypeStruct(own.shape, BF16),
         compiler_params=PARAMS,
         cost_estimate=cost(own.size * 4, own.size * 6),
     )(core, own, other)
 
 
-def attention_kernel(q_ref, k_ref, v_ref, carried_ref, gain_ref, *out_refs, groups):
+def within_kernel(q_hbm, k_hbm, v_hbm, q_ref, out_ref, k_ref, v_ref, sems):
+    copies, split = [], CALLS[0][1] * DH
+    parts = (slice(0, split), slice(split, LATE * DH))
+    for part, cols in enumerate(parts):
+        for at, (hbm, ref) in enumerate(((q_hbm, q_ref), (k_hbm, k_ref), (v_hbm, v_ref))):
+            copies.append(
+                pltpu.make_async_copy(hbm.at[:, cols], ref.at[:, cols], sems.at[part, at])
+            )
+            copies[-1].start()
     causal = causal_mask()
-    for out_ref, (first, last) in zip(out_refs, groups):
+    for part, (first, last) in enumerate(CALLS):
+        for copy in copies[3 * part : 3 * part + 3]:
+            copy.wait()
         for h in range(first, last):
             cols = slice(h * DH, (h + 1) * DH)
-            out_cols = slice((h - first) * DH, (h - first + 1) * DH)
-            parts = within_block(q_ref, k_ref, v_ref, h, causal)
-            for rows, within in zip((slice(0, HALF), slice(HALF, BLK)), parts):
-                out_ref[rows, out_cols] = finish(
-                    q_ref[rows, cols], within, carried_ref[cols, :], gain_ref[:, cols]
-                )
-
-
-def attention(q, k, v, carried, gain, groups):
-    heads = sum(last - first for first, last in groups)
-    return pl.pallas_call(
-        functools.partial(attention_kernel, groups=groups),
-        name="attention",
-        in_specs=[VMEM] * 5,
-        out_specs=[VMEM] * len(groups),
-        out_shape=[pltpu.VMEM((BLK, (last - first) * DH), BF16) for first, last in groups],
-        compiler_params=PARAMS,
-        cost_estimate=cost(4 * BLK * BLK * DH * heads, BLK * DH * heads * 8),
-    )(q, k, v, carried, gain)
+            top, bottom = within_block(q_ref, k_ref, v_ref, h, causal)
+            out_ref[:HALF, cols] = top
+            out_ref[HALF:, cols] = bottom
+
+
+def within_late(q, k, v):
+    shape = (BLK, LATE * DH)
+    return pl.pallas_call(
+        within_kernel,
+        name="within_late",
+        in_specs=[HBM] * 3,
+        out_specs=[VMEM, VMEM],
+        out_shape=[pltpu.VMEM(shape, BF16), pltpu.VMEM(shape, F32)],
+        scratch_shapes=[
+            pltpu.VMEM(shape, BF16),
+            pltpu.VMEM(shape, BF16),
+            pltpu.SemaphoreType.DMA((2, 3)),
+        ],
+        compiler_params=PARAMS,
+        cost_estimate=cost(4 * BLK * BLK * DH * LATE, BLK * DH * LATE * 10),
+    )(in_hbm(q), in_hbm(k), in_hbm(v))
+
+
+def finish_kernel(q_ref, within_ref, carried_ref, gain_ref, out_ref, *, first, last):
+    for h in range(first, last):
+        cols = slice(h * DH, (h + 1) * DH)
+        out_cols = slice((h - first) * DH, (h - first + 1) * DH)
+        out_ref[:BLK, out_cols] = finish(
+            q_ref[:, cols], within_ref[:, cols], carried_ref[cols, :], gain_ref[:, cols]
+        )
+    if out_ref.shape[0] > BLK:
+        out_ref[BLK:, EARLY * DH :] = jnp.zeros((DH, out_ref.shape[1] - EARLY * DH), BF16)
+        for h in range(EARLY):
+            state = carried_ref[(LATE + h) * DH : (LATE + h + 1) * DH, :]
+            out_ref[BLK:, h * DH : (h + 1) * DH] = state
+
+
+def finish_heads(q, within, carried, gain, first, last, states=False):
+    heads = last - first
+    return pl.pallas_call(
+        functools.partial(finish_kernel, first=first, last=last),
+        name="finish_heads",
+        in_specs=[VMEM] * 4,
+        out_specs=VMEM,
+        out_shape=jax.ShapeDtypeStruct((BLK + DH if states else BLK, heads * DH), BF16),
+        compiler_params=PARAMS,
+        cost_estimate=cost(4 * BLK * DH * DH * heads, BLK * DH * heads * 8),
+    )(q, within, carried, gain)
+
+
+def early_kernel(*refs, count):
+    hbm_refs, a_refs, rest = refs[:count], refs[count : 2 * count], refs[2 * count :]
+    out_refs, e_ref, sems = rest[:count], rest[count], rest[count + 1]
+    copies = [
+        pltpu.make_async_copy(hbm, e_ref.at[at], sems.at[at]) for at, hbm in enumerate(hbm_refs)
+    ]
+    for copy in copies:
+        copy.start()
+    for at, (a_ref, out_ref) in enumerate(zip(a_refs, out_refs)):
+        copies[at].wait()
+        for h in range(EARLY):
+            cols = slice(h * DH, (h + 1) * DH)
+            terms = e_ref[at, BLK:, cols].astype(F32)
+            gain = terms[0:1] + terms[1:2] + terms[2:3]
+            within = e_ref[at, :BLK, (EARLY + h) * DH : (EARLY + h + 1) * DH].astype(F32)
+            out_ref[:, cols] = finish(e_ref[at, :BLK, cols], within, a_ref[BLK:, cols], gain)
+
+
+def early_heads(early, chunks):
+    count = len(early)
+    return pl.pallas_call(
+        functools.partial(early_kernel, count=count),
+        name="early_heads",
+        in_specs=[pl.BlockSpec(memory_space=pl.ANY)] * count + [VMEM] * count,
+        out_specs=[VMEM] * count,
+        out_shape=[jax.ShapeDtypeStruct((BLK, EARLY * DH), BF16)] * count,
+        scratch_shapes=[
+            pltpu.VMEM((count, *early[0].shape), BF16),
+            pltpu.SemaphoreType.DMA((count,)),
+        ],
+        compiler_params=PARAMS,
+        cost_estimate=cost(4 * BLK * DH * DH * EARLY * count, BLK * DH * EARLY * count * 6),
+    )(*early, *chunks)
 
 
 TILE = 256
@@ -171,7 +282,7 @@
         for a_ref in a_refs:
             width = a_ref.shape[1]
             rows = pl.ds(pl.multiple_of(starts[0] + at, DH), width)
-            term = dot(a_ref[...], w_ref[rows, cols], NN)
+            term = dot(a_ref[:BLK, :], w_ref[rows, cols], NN)
             total = term if total is None else total + term
             at += width
         total_ref[:, cols] = total
@@ -210,7 +321,7 @@
         for a_ref, (shift, head) in zip(a_refs, plan):
             source = lax.rem(column_ref[0] + (shift + ways), ways)
             start = pl.multiple_of(source * (HEADS * DH) + head * DH, DH)
-            term = dot(a_ref[...], w_ref[pl.ds(start, a_ref.shape[1]), cols], NN)
+            term = dot(a_ref[:BLK, :], w_ref[pl.ds(start, a_ref.shape[1]), cols], NN)
             total = term if total is None else total + term
         out_ref[:, cols] = total.astype(out_ref.dtype)
         if last:
@@ -250,33 +361,35 @@
     chips, ways = lax.axis_size("chip"), lax.axis_size("fsdp")
     core = lax.axis_index("core").reshape(1)
     column = lax.axis_index("fsdp").reshape(1)
-    states = block_states(k, v)
+    gain_row = gain.reshape(1, -1)
+    states, early = block_states(q, k, v, gain_row)
     own = lax.all_to_all(states, "chip", 0, 0, tiled=True)
+    own, *near_e = lax.optimization_barrier((own, along(early, 1, ways), along(early, -1, ways)))
+    across_e = along(early, ways // 2, ways)
     other = lax.ppermute(own, "core", [(0, 1), (1, 0)])
     sums = exclusive_sums(core, own, other, chips)
     carried = lax.all_to_all(sums, "chip", 0, 0, tiled=True)
-    q, k, v = in_vmem(q), in_vmem(k), in_vmem(v)
-    gain_row = gain.reshape(1, -1)
-    heads, mine, left, right, far = [], [], [], [], []
-    for groups in CALLS:
-        heads += [first for first, _ in groups]
-        mine += attention(q, k, v, carried, gain_row, groups)
-    for at, value in enumerate(mine):
-        sides = along(value, 1, ways), along(value, -1, ways)
-        sides = lax.optimization_barrier(sides)
-        left.append(sides[0])
-        right.append(sides[1])
-        far.append(along(sides[1], -1, ways) if at % 2 else along(sides[0], 1, ways))
-
-    def plan(shift, begin, end):
-        return [(shift, head) for head in heads[begin:end]]
-
-    total, w = own_mix(column, w, mine)
-    for at in range(2):
-        sides = plan(-1, at, at + 1) + plan(1, at, at + 1)
-        total = mix(column, w, sides, [left[at], right[at]], total)
-    total = mix(column, w, plan(2, 0, 1), far[:1], total)
-    return mix(column, w, plan(2, 1, 2), far[1:], total, True)
+    q_late, within = within_late(q, k, v)
+    carried, across_e, q_late, within = lax.optimization_barrier(
+        (carried, across_e, q_late, within)
+    )
+    (a0, a1), (b0, b1) = CALLS
+    mine_a = finish_heads(q_late, within, carried, gain_row, a0, a1, True)
+    left_a, right_a = lax.optimization_barrier((along(mine_a, 1, ways), along(mine_a, -1, ways)))
+    far_a = along(left_a, 1, ways)
+    mine_b = finish_heads(q_late, within, carried, gain_row, b0, b1)
+    mine_e, left_e, right_e = early_heads([early, *near_e], [mine_a, left_a, right_a])
+    left_b, right_b, mine_e, left_e, right_e = lax.optimization_barrier(
+        (along(mine_b, 1, ways), along(mine_b, -1, ways), mine_e, left_e, right_e)
+    )
+    far_b = along(right_b, -1, ways)
+    total, w = own_mix(column, w, [mine_a, mine_b, mine_e])
+    plan = [(-1, a0), (-1, LATE), (1, a0), (1, LATE)]
+    total = mix(column, w, plan, [left_a, left_e, right_a, right_e], total)
+    total = mix(column, w, [(-1, b0), (1, b0)], [left_b, right_b], total)
+    (far_e,) = early_heads([across_e], [far_a])
+    total = mix(column, w, [(2, a0), (2, LATE)], [far_a, far_e], total)
+    return mix(column, w, [(2, b0)], [far_b], total, True)
 
 
 def solution(mesh):

time: 88.7 us -> 89.2 us (level); the launches traced: 88.3 us -> 87.9 us
  blocking collectives: 40 us -> 22.7 us
  starting transfers between devices: 10 us -> 17.2 us
  waiting for transfers between devices: 16.8 us -> 22.9 us
  Pallas kernels: 17.4 us -> 21.7 us
    all_to_all x1 -> x0, blocking collectives: 16.9 us -> none  [shards(): carried = lax.all_to_all(sums, 'chip', 0, 0, tiled=True)]
    all_to_all x0 -> x1, starting transfers between devices: none -> 4.67 us  [shards(): carried = lax.all_to_all(sums, 'chip', 0, 0, tiled=True)]
    ppermute x6 -> x9, waiting for transfers between devices: 15.2 us -> 19.2 us  [along(): lax.ppermute(value, 'fsdp', [(i, (i + shift) % count) for i in range(coun...]
    pallas_call x3 -> x6, Pallas kernels: 6.88 us -> 10.7 us  [the longest x2 3.9 us: early_heads(): pl.pallas_call(functools.partial(early_kernel, count=count), name='early_...]
    all_to_all x0 -> x1, waiting for transfers between devices: none -> 3.67 us  [shards(): carried = lax.all_to_all(sums, 'chip', 0, 0, tiled=True)]
    ppermute x6 -> x9, starting transfers between devices: 10 us -> 12.5 us  [along(): lax.ppermute(value, 'fsdp', [(i, (i + shift) % count) for i in range(coun...]
    ppermute x1, waiting for transfers between devices: 1.66 us -> 0.01 us  [shards(): other = lax.ppermute(own, 'core', [(0, 1), (1, 0)])]
    unnamed x20 -> x18, local copies, waits for them, and re-layouts: 3.73 us -> 3.11 us
  transfers between devices with their start and end apart: 7 -> 11, of which waited for: 4 -> 4; matrix products, arithmetic and copies ran while one was open for 0% -> 0% of each run, Pallas kernels for 12% -> 19%
where the time goes in v7:
time: 89.2 us; the launch traced here: 87.9 us
  waiting for transfers between devices  22.9 us (26%)
  blocking collectives  22.7 us (25%)
  Pallas kernels  21.7 us (24%)
  starting transfers between devices  17.2 us (19%)
  local copies, waits for them, and re-layouts  3.11 us (3%)
    all_to_all x1, blocking collectives, shards(): own = lax.all_to_all(states, 'chip', 0, 0, tiled=True)  22.7 us
    ppermute x9, waiting for transfers between devices, along(): lax.ppermute(value, 'fsdp', [(i, (i + shift) % count) for i in range(coun...  19.2 us
    ppermute x9, starting transfers between devices, along(): lax.ppermute(value, 'fsdp', [(i, (i + shift) % count) for i in range(coun...  12.5 us
    pallas_call x4, Pallas kernels, mix(): pl.pallas_call(functools.partial(mix_kernel, plan=tuple(plan), first=tota...  6.71 us
    all_to_all x1, starting transfers between devices, shards(): carried = lax.all_to_all(sums, 'chip', 0, 0, tiled=True)  4.67 us
    pallas_call x2, Pallas kernels, early_heads(): pl.pallas_call(functools.partial(early_kernel, count=count), name='early_...  3.9 us
    all_to_all x1, waiting for transfers between devices, shards(): carried = lax.all_to_all(sums, 'chip', 0, 0, tiled=True)  3.67 us
    pallas_call x1, Pallas kernels, own_mix(): pl.pallas_call(own_kernel, name='own_mix', in_specs=[SMEM] + [VMEM] * len...  3.55 us
  transfers between devices with their start and end apart: 11, of which 4 were waited for; matrix products, arithmetic and copies ran while one was open for 0% of the time, Pallas kernels for 19%

profile of v7, /device:TPU:32, one launch (start us, length us, event | category | flops | bytes accessed | tf_op | source)
XLA Modules:
  0.0 87.9 jit_solution(9684140827086197998)
XLA Ops:
  0.7 2.7 %block_states.1 = (bf16[1024,128]{1,0:T(8,128)(2,1)S(1)}, bf16[528,512]{1,0:T(8,128)(2,1)}) custom-call(bf16[512,1024]{1,0:T(8,128)(2,1)} %q_hbm.3, bf16[512,1024]{1,0:T(8,128)(2,1)} %k_hbm.3, bf16[512,1024]{1,0:T(8,128)(2,1)} %v_hbm.3, f32[1,1024]{1,0:T(1,128)S(1)} %bitcast.12), custom_call_target="tpu_custom_call" | custom-call | flops 134217728 | bytes 2097152 | tf_op jit(solution)/shard_map/block_states/pallas_call | solution.py:123
  3.4 1.7 %collective-permute-start = (bf16[528,512]{1,0:T(8,128)(2,1)}, bf16[528,512]{1,0:T(8,128)(2,1)S(1)}, u32[]{:S(2)}, u32[]{:S(2)}) collective-permute-start(bf16[528,512]{1,0:T(8,128)(2,1)} %get-tuple-element.29.refs_0_), channel_id=1, source_target_pairs={{0,1},{1,2},{2,3},{3,0},{4,5},{5,6},{6,7},{7,4},{8,9},{9,10},{10,1... | collective-permute-start | bytes 1622024 | tf_op jit(solution)/shard_map/ppermute | solution.py:357
  5.0 1.7 %collective-permute-start.1 = (bf16[528,512]{1,0:T(8,128)(2,1)}, bf16[528,512]{1,0:T(8,128)(2,1)S(1)}, u32[]{:S(2)}, u32[]{:S(2)}) collective-permute-start(bf16[528,512]{1,0:T(8,128)(2,1)} %get-tuple-element.29.refs_0_), channel_id=1, source_target_pairs={{0,3},{1,0},{2,1},{3,2},{4,7},{5,4},{6,5},{7,6},{8,11},{9,8},{10,9... | collective-permute-start | bytes 1622024 | tf_op jit(solution)/shard_map/ppermute | solution.py:357
  6.7 22.7 %all_to_all.24 = bf16[32,32,128]{2,1,0:T(8,128)(2,1)S(1)} all-to-all(bf16[32,32,128]{2,1,0:T(8,128)(2,1)S(1)} %bitcast.11), channel_id=1, replica_groups=mesh['chip'=32,'core'=2,'fsdp'=4] {'chip'}, dimensions={0} | all-to-all | bytes 524288 | tf_op jit(solution)/shard_map/all_to_all | solution.py:366
  29.3 0.8 copy-done.3
  30.2 0.8 copy-done.5
  31.0 1.8 %collective-permute-start.3 = (bf16[528,512]{1,0:T(8,128)(2,1)}, bf16[528,512]{1,0:T(8,128)(2,1)}, u32[]{:S(2)}, u32[]{:S(2)}) collective-permute-start(bf16[528,512]{1,0:T(8,128)(2,1)} %get-tuple-element.29.refs_0_), channel_id=1, source_target_pairs={{0,2},{1,3},{2,0},{3,1},{4,6},{5,7},{6,4},{7,5},{8,10},{9,11},{10,... | collective-permute-start | bytes 1622024 | tf_op jit(solution)/shard_map/ppermute | solution.py:357
  32.8 0.8 exclusive_sums.1
  33.6 4.7 %all-to-all-start.1 = ((bf16[32,32,128]{2,1,0:T(8,128)(2,1)}), bf16[32,32,128]{2,1,0:T(8,128)(2,1)S(1)}, u32[]{:S(2)}, u32[]{:S(2)}) async-start(bf16[32,32,128]{2,1,0:T(8,128)(2,1)} %bitcast.5), calls=%async_computation.1 | async-start | bytes 524288 | tf_op jit(solution)/shard_map/all_to_all | solution.py:371
  38.3 3.2 %within_late.1 = (bf16[512,768]{1,0:T(8,128)(2,1)S(1)}, f32[512,768]{1,0:T(8,128)S(1)}) custom-call(bf16[512,1024]{1,0:T(8,128)(2,1)} %q_hbm.3, bf16[512,1024]{1,0:T(8,128)(2,1)} %k_hbm.3, bf16[512,1024]{1,0:T(8,128)(2,1)} %v_hbm.3), custom_call_target="tpu_custom_call" | custom-call | flops 805306368 | bytes 3932160 | tf_op jit(solution)/shard_map/within_late/pallas_call | solution.py:186
  41.5 6.0 %collective-permute-done.3.refs_0_ = bf16[528,512]{1,0:T(8,128)(2,1)} collective-permute-done((bf16[528,512]{1,0:T(8,128)(2,1)}, bf16[528,512]{1,0:T(8,128)(2,1)}, u32[]{:S(2)}, u32[]{:S(2)}) %collective-permute-start.3) | collective-permute-done | bytes 540704 | tf_op jit(solution)/shard_map/ppermute | solution.py:357
  47.5 3.7 %all-to-all-done.1 = bf16[32,32,128]{2,1,0:T(8,128)(2,1)S(1)} async-done(((bf16[32,32,128]{2,1,0:T(8,128)(2,1)}), bf16[32,32,128]{2,1,0:T(8,128)(2,1)S(1)}, u32[]{:S(2)}, u32[]{:S(2)}) %all-to-all-start.1) | async-done | bytes 262176 | tf_op jit(solution)/shard_map/all_to_all | solution.py:371
  52.4 2.6 %collective-permute-start.7 = (bf16[640,384]{1,0:T(8,128)(2,1)S(1)}, bf16[640,384]{1,0:T(8,128)(2,1)S(1)}, u32[]{:S(2)}, u32[]{:S(2)}) collective-permute-start(bf16[640,384]{1,0:T(8,128)(2,1)S(1)} %finish_heads.3.refs_3_.refs_0_), channel_id=1, source_target_pairs={{0,3},{1,0},{2,1},{3,2},{4,7},{5,4},{6,5},{7,6},{8,11},{9,8},{10,9... | collective-permute-start | bytes 1474568 | tf_op jit(solution)/shard_map/ppermute | solution.py:357
  55.5 3.2 %collective-permute-start.5 = (bf16[512,384]{1,0:T(8,128)(2,1)S(1)}, bf16[512,384]{1,0:T(8,128)(2,1)S(1)}, u32[]{:S(2)}, u32[]{:S(2)}) collective-permute-start(bf16[512,384]{1,0:T(8,128)(2,1)S(1)} %finish_heads.2.refs_1_), channel_id=1, source_target_pairs={{0,3},{1,0},{2,1},{3,2},{4,7},{5,4},{6,5},{7,6},{8,11},{9,8},{10,9... | collective-permute-start | bytes 1179656 | tf_op jit(solution)/shard_map/ppermute | solution.py:357
  58.8 8.5 %collective-permute-done.6.refs_4_.refs_0_ = bf16[640,384]{1,0:T(8,128)(2,1)} collective-permute-done((bf16[640,384]{1,0:T(8,128)(2,1)S(1)}, bf16[640,384]{1,0:T(8,128)(2,1)}, u32[]{:S(2)}, u32[]{:S(2)}) %collective-permute-start.6) | collective-permute-done | bytes 491552 | tf_op jit(solution)/shard_map/ppermute | solution.py:357
  67.6 2.4 %early_heads.2 = (bf16[512,256]{1,0:T(8,128)(2,1)S(1)}, bf16[512,256]{1,0:T(8,128)(2,1)S(1)}, bf16[512,256]{1,0:T(8,128)(2,1)S(1)}) custom-call(bf16[528,512]{1,0:T(8,128)(2,1)S(1)} %copy-done.2, bf16[528,512]{1,0:T(8,128)(2,1)S(1)} %copy-done.4, bf16[528,512]{1,0:T(8,128)(2,1)S(1)} %copy-done.6, bf16[640,384]{1,0:T(8,128)(2,1)S(1)} %finish_heads.3.refs_3_.refs_0_, ...), custom_call_target="tpu_custom_call" | custom-call | flops 201326592 | bytes 2359296 | tf_op jit(solution)/shard_map/early_heads/pallas_call | solution.py:249
  70.0 0.8 copy-done
  70.8 4.7 %collective-permute-done.4.refs_0_ = bf16[512,384]{1,0:T(8,128)(2,1)S(1)} collective-permute-done((bf16[512,384]{1,0:T(8,128)(2,1)S(1)}, bf16[512,384]{1,0:T(8,128)(2,1)S(1)}, u32[]{:S(2)}, u32[]{:S(2)}) %collective-permute-start.4) | collective-permute-done | bytes 393248 | tf_op jit(solution)/shard_map/ppermute | solution.py:357
  76.0 3.5 %own_mix.1 = (f32[512,1024]{1,0:T(8,128)S(1)}, bf16[4096,1024]{1,0:T(8,128)(2,1)S(1)}) custom-call(s32[1]{0:T(128)} %bitcast.column_ref, bf16[640,384]{1,0:T(8,128)(2,1)S(1)} %finish_heads.3.refs_3_.refs_0_, bf16[512,384]{1,0:T(8,128)(2,1)S(1)} %finish_heads.2.refs_1_, bf16[512,256]{1,0:T(8,128)(2,1)S(1)} %get-tuple-element.44.refs_2_, ...), custom_call_target="tpu_custom_call" | custom-call | flops 1073741824 | bytes 8388608 | tf_op jit(solution)/shard_map/own_mix/pallas_call | solution.py:295
  79.5 2.8 %mix.4.refs_3_ = f32[512,1024]{1,0:T(8,128)S(1)} custom-call(s32[1]{0:T(128)} %bitcast.column_ref, bf16[640,384]{1,0:T(8,128)(2,1)} %collective-permute-done.6.refs_4_.refs_0_, bf16[512,256]{1,0:T(8,128)(2,1)S(1)} %get-tuple-element.48.refs_1_, bf16[640,384]{1,0:T(8,128)(2,1)S(1)} %copy-done.1, bf16[512,256]{1,0:T(8,128)(2,1)S(1)} %get-tuple-element.49.refs_3_, ...), custom_call_target="tpu_custom_call" | custom-call | flops 1342177280 | bytes 2621440 | tf_op jit(solution)/shard_map/mix/pallas_call | solution.py:344
  82.4 1.3 %mix.5.refs_3_ = f32[512,1024]{1,0:T(8,128)S(1)} custom-call(s32[1]{0:T(128)} %bitcast.column_ref, bf16[512,384]{1,0:T(8,128)(2,1)S(1)} %collective-permute-done.4.refs_0_, bf16[512,384]{1,0:T(8,128)(2,1)S(1)} %collective-permute-done.5.refs_1_, bf16[4096,1024]{1,0:T(8,128)(2,1)S(1)} %get-tuple-element.45.refs_4_.refs_2_.refs_1_, f32[512,1024]{1,0:T(8,128)S(1)} %mix.4.refs_3_), custom_call_target="tpu_custom_call" | custom-call | flops 805306368 | bytes 1572864 | tf_op jit(solution)/shard_map/mix/pallas_call | solution.py:344
  83.7 1.5 %early_heads.3.refs_1_ = bf16[512,256]{1,0:T(8,128)(2,1)S(1)} custom-call(bf16[528,512]{1,0:T(8,128)(2,1)} %collective-permute-done.3.refs_0_, bf16[640,384]{1,0:T(8,128)(2,1)S(1)} %collective-permute-done.9.refs_1_.refs_0_), custom_call_target="tpu_custom_call" | custom-call | flops 67108864 | bytes 786432 | tf_op jit(solution)/shard_map/early_heads/pallas_call | solution.py:249
  85.1 1.0 %mix.6.refs_2_ = f32[512,1024]{1,0:T(8,128)S(1)} custom-call(s32[1]{0:T(128)} %bitcast.column_ref, bf16[640,384]{1,0:T(8,128)(2,1)S(1)} %collective-permute-done.9.refs_1_.refs_0_, bf16[512,256]{1,0:T(8,128)(2,1)S(1)} %early_heads.3.refs_1_, bf16[4096,1024]{1,0:T(8,128)(2,1)S(1)} %get-tuple-element.45.refs_4_.refs_2_.refs_1_, f32[512,1024]{1,0:T(8,128)S(1)} %mix.5.refs_3_), custom_call_target="tpu_custom_call" | custom-call | flops 671088640 | bytes 1310720 | tf_op jit(solution)/shard_map/mix/pallas_call | solution.py:344
  86.1 1.6 %mix.7 = bf16[512,1024]{1,0:T(8,128)(2,1)} custom-call(s32[1]{0:T(128)} %bitcast.column_ref, bf16[512,384]{1,0:T(8,128)(2,1)S(1)} %collective-permute-done.8.refs_0_, bf16[4096,1024]{1,0:T(8,128)(2,1)S(1)} %get-tuple-element.45.refs_4_.refs_2_.refs_1_, f32[512,1024]{1,0:T(8,128)S(1)} %mix.6.refs_2_), custom_call_target="tpu_custom_call" | custom-call | flops 402653184 | bytes 786432 | tf_op jit(solution)/shard_map/mix/pallas_call | solution.py:344
  (29 shorter events, 3.2 us)
Async XLA Ops:
  0.0 0.7 copy-start.7
  3.4 26.0 %collective-permute-start = (bf16[528,512]{1,0:T(8,128)(2,1)}, bf16[528,512]{1,0:T(8,128)(2,1)S(1)}, u32[]{:S(2)}, u32[]{:S(2)}) collective-permute-start(bf16[528,512]{1,0:T(8,128)(2,1)} %get-tuple-element.29.refs_0_), channel_id=1, source_target_pairs={{0,1},{1,2},{2,3},{3,0},{4,5},{5,6},{6,7},{7,4},{8,9},{9,10},{10,1... | collective-permute-start | bytes 1622024 | tf_op jit(solution)/shard_map/ppermute | solution.py:357
  5.0 25.1 %collective-permute-start.1 = (bf16[528,512]{1,0:T(8,128)(2,1)}, bf16[528,512]{1,0:T(8,128)(2,1)S(1)}, u32[]{:S(2)}, u32[]{:S(2)}) collective-permute-start(bf16[528,512]{1,0:T(8,128)(2,1)} %get-tuple-element.29.refs_0_), channel_id=1, source_target_pairs={{0,3},{1,0},{2,1},{3,2},{4,7},{5,4},{6,5},{7,6},{8,11},{9,8},{10,9... | collective-permute-start | bytes 1622024 | tf_op jit(solution)/shard_map/ppermute | solution.py:357
  29.3 0.8 copy-start.3
  30.2 0.8 copy-start.5
  31.0 1.8 %collective-permute-start.2 = (bf16[1024,128]{1,0:T(8,128)(2,1)S(1)}, bf16[1024,128]{1,0:T(8,128)(2,1)S(1)}, u32[]{:S(2)}, u32[]{:S(2)}) collective-permute-start(bf16[1024,128]{1,0:T(8,128)(2,1)S(1)} %bitcast.9), channel_id=1, source_target_pairs={{0,4},{4,0},{1,5},{5,1},{2,6},{6,2},{3,7},{7,3},{8,12},{12,8},{9,1... | collective-permute-start | bytes 786440 | tf_op jit(solution)/shard_map/ppermute | solution.py:369
  31.0 16.5 %collective-permute-start.3 = (bf16[528,512]{1,0:T(8,128)(2,1)}, bf16[528,512]{1,0:T(8,128)(2,1)}, u32[]{:S(2)}, u32[]{:S(2)}) collective-permute-start(bf16[528,512]{1,0:T(8,128)(2,1)} %get-tuple-element.29.refs_0_), channel_id=1, source_target_pairs={{0,2},{1,3},{2,0},{3,1},{4,6},{5,7},{6,4},{7,5},{8,10},{9,11},{10,... | collective-permute-start | bytes 1622024 | tf_op jit(solution)/shard_map/ppermute | solution.py:357
  32.8 18.3 %copy-start.8 = (f32[1024]{0:T(1024)S(1)}, f32[1024]{0:T(1024)}, u32[]{:S(2)}) copy-start(f32[1024]{0:T(1024)} %param.8) | copy-start | bytes 12292
  33.6 17.5 %all-to-all-start.1 = ((bf16[32,32,128]{2,1,0:T(8,128)(2,1)}), bf16[32,32,128]{2,1,0:T(8,128)(2,1)S(1)}, u32[]{:S(2)}, u32[]{:S(2)}) async-start(bf16[32,32,128]{2,1,0:T(8,128)(2,1)} %bitcast.5), calls=%async_computation.1 | async-start | bytes 524288 | tf_op jit(solution)/shard_map/all_to_all | solution.py:371
  51.6 15.9 %copy-start.2 = (bf16[528,512]{1,0:T(8,128)(2,1)S(1)}, bf16[528,512]{1,0:T(8,128)(2,1)}, u32[]{:S(2)}) copy-start(bf16[528,512]{1,0:T(8,128)(2,1)} %get-tuple-element.29.refs_0_) | copy-start | bytes 1622020
  51.6 15.9 %copy-start.4 = (bf16[528,512]{1,0:T(8,128)(2,1)S(1)}, bf16[528,512]{1,0:T(8,128)(2,1)}, u32[]{:S(2)}) copy-start(bf16[528,512]{1,0:T(8,128)(2,1)} %copy-done.3) | copy-start | bytes 1622020
  51.6 15.9 %copy-start.6 = (bf16[528,512]{1,0:T(8,128)(2,1)S(1)}, bf16[528,512]{1,0:T(8,128)(2,1)}, u32[]{:S(2)}) copy-start(bf16[528,512]{1,0:T(8,128)(2,1)} %copy-done.5) | copy-start | bytes 1622020
  51.7 15.6 %collective-permute-start.6 = (bf16[640,384]{1,0:T(8,128)(2,1)S(1)}, bf16[640,384]{1,0:T(8,128)(2,1)}, u32[]{:S(2)}, u32[]{:S(2)}) collective-permute-start(bf16[640,384]{1,0:T(8,128)(2,1)S(1)} %finish_heads.3.refs_3_.refs_0_), channel_id=1, source_target_pairs={{0,1},{1,2},{2,3},{3,0},{4,5},{5,6},{6,7},{7,4},{8,9},{9,10},{10,1... | collective-permute-start | bytes 1474568 | tf_op jit(solution)/shard_map/ppermute | solution.py:357
  52.4 14.8 %collective-permute-start.7 = (bf16[640,384]{1,0:T(8,128)(2,1)S(1)}, bf16[640,384]{1,0:T(8,128)(2,1)S(1)}, u32[]{:S(2)}, u32[]{:S(2)}) collective-permute-start(bf16[640,384]{1,0:T(8,128)(2,1)S(1)} %finish_heads.3.refs_3_.refs_0_), channel_id=1, source_target_pairs={{0,3},{1,0},{2,1},{3,2},{4,7},{5,4},{6,5},{7,6},{8,11},{9,8},{10,9... | collective-permute-start | bytes 1474568 | tf_op jit(solution)/shard_map/ppermute | solution.py:357
  55.4 20.1 %collective-permute-start.4 = (bf16[512,384]{1,0:T(8,128)(2,1)S(1)}, bf16[512,384]{1,0:T(8,128)(2,1)S(1)}, u32[]{:S(2)}, u32[]{:S(2)}) collective-permute-start(bf16[512,384]{1,0:T(8,128)(2,1)S(1)} %finish_heads.2.refs_1_), channel_id=1, source_target_pairs={{0,1},{1,2},{2,3},{3,0},{4,5},{5,6},{6,7},{7,4},{8,9},{9,10},{10,1... | collective-permute-start | bytes 1179656 | tf_op jit(solution)/shard_map/ppermute | solution.py:357
  55.5 20.0 %collective-permute-start.5 = (bf16[512,384]{1,0:T(8,128)(2,1)S(1)}, bf16[512,384]{1,0:T(8,128)(2,1)S(1)}, u32[]{:S(2)}, u32[]{:S(2)}) collective-permute-start(bf16[512,384]{1,0:T(8,128)(2,1)S(1)} %finish_heads.2.refs_1_), channel_id=1, source_target_pairs={{0,3},{1,0},{2,1},{3,2},{4,7},{5,4},{6,5},{7,6},{8,11},{9,8},{10,9... | collective-permute-start | bytes 1179656 | tf_op jit(solution)/shard_map/ppermute | solution.py:357
  67.2 16.4 %collective-permute-start.9 = (bf16[640,384]{1,0:T(8,128)(2,1)}, bf16[640,384]{1,0:T(8,128)(2,1)S(1)}, u32[]{:S(2)}, u32[]{:S(2)}) collective-permute-start(bf16[640,384]{1,0:T(8,128)(2,1)} %collective-permute-done.6.refs_4_.refs_0_), channel_id=1, source_target_pairs={{0,1},{1,2},{2,3},{3,0},{4,5},{5,6},{6,7},{7,4},{8,9},{9,10},{10,1... | collective-permute-start | bytes 1474568 | tf_op jit(solution)/shard_map/ppermute | solution.py:357
  70.0 0.8 copy-start
  75.5 10.6 %collective-permute-start.8 = (bf16[512,384]{1,0:T(8,128)(2,1)S(1)}, bf16[512,384]{1,0:T(8,128)(2,1)S(1)}, u32[]{:S(2)}, u32[]{:S(2)}) collective-permute-start(bf16[512,384]{1,0:T(8,128)(2,1)S(1)} %collective-permute-done.5.refs_1_), channel_id=1, source_target_pairs={{0,3},{1,0},{2,1},{3,2},{4,7},{5,4},{6,5},{7,6},{8,11},{9,8},{10,9... | collective-permute-start | bytes 1179656 | tf_op jit(solution)/shard_map/ppermute | solution.py:357
  76.0 3.6 %copy-start.1 = (bf16[640,384]{1,0:T(8,128)(2,1)S(1)}, bf16[640,384]{1,0:T(8,128)(2,1)}, u32[]{:S(2)}) copy-start(bf16[640,384]{1,0:T(8,128)(2,1)} %copy-done) | copy-start | bytes 1474564

commit v8 on v7

--- a/solution.py
+++ b/solution.py
@@ -66,7 +66,9 @@
     return (att * lax.rsqrt(mean_square + 1e-6) * gain).astype(BF16)
 
 
-def state_kernel(q_hbm, k_hbm, v_hbm, gain_ref, out_ref, early_hbm, q_ref, k_ref, v_ref, early_ref, sems):
+def state_kernel(
+    q_hbm, k_hbm, v_hbm, gain_hbm, out_ref, early_hbm, q_ref, k_ref, v_ref, gain_ref, early_ref, sems
+):
     early = slice(LATE * DH, HEADS * DH)
     late = slice(0, LATE * DH)
     copies = [
@@ -81,8 +83,10 @@
         )
     ]
     copies.append(pltpu.make_async_copy(q_hbm.at[:, early], q_ref, sems.at[4]))
-    for at in (4, 0, 1, 2, 3):
+    copies.append(pltpu.make_async_copy(gain_hbm, gain_ref, sems.at[5]))
+    for at in (5, 4, 0, 1, 2, 3):
         copies[at].start()
+    copies[5].wait()
     gain = gain_ref[:, early]
     high = gain.astype(BF16)
     rest = gain - high.astype(F32)
@@ -106,7 +110,7 @@
         cols = slice((EARLY + h - LATE) * DH, (EARLY + h - LATE + 1) * DH)
         early_ref[:HALF, cols] = top.astype(BF16)
         early_ref[HALF:BLK, cols] = bottom.astype(BF16)
-    out = pltpu.make_async_copy(early_ref, early_hbm, sems.at[5])
+    out = pltpu.make_async_copy(early_ref, early_hbm, sems.at[6])
     out.start()
     for h in range(LATE, HEADS):
         state(h)
@@ -123,19 +127,20 @@
     return pl.pallas_call(
         state_kernel,
         name="block_states",
-        in_specs=[HBM, HBM, HBM, VMEM],
+        in_specs=[HBM] * 4,
         out_specs=[VMEM, HBM],
         out_shape=[pltpu.VMEM((width, DH), BF16), pltpu.HBM(early, BF16)],
         scratch_shapes=[
             pltpu.VMEM((BLK, EARLY * DH), BF16),
             pltpu.VMEM(k.shape, BF16),
             pltpu.VMEM(v.shape, BF16),
+            pltpu.VMEM(gain.shape, F32),
             pltpu.VMEM(early, BF16),
-            pltpu.SemaphoreType.DMA((6,)),
+            pltpu.SemaphoreType.DMA((7,)),
         ],
         compiler_params=PARAMS,
         cost_estimate=cost(2 * BLK * DH * width, 2 * BLK * width * 2),
-    )(in_hbm(q), in_hbm(k), in_hbm(v), gain)
+    )(in_hbm(q), in_hbm(k), in_hbm(v), in_hbm(gain))
 
 
 def scan_kernel(core_ref, own_ref, other_ref, out_ref, *, chips):
@@ -364,9 +369,10 @@
     gain_row = gain.reshape(1, -1)
     states, early = block_states(q, k, v, gain_row)
     own = lax.all_to_all(states, "chip", 0, 0, tiled=True)
-    own, *near_e = lax.optimization_barrier((own, along(early, 1, ways), along(early, -1, ways)))
+    near_e = along(early, 1, ways), along(early, -1, ways)
+    other = lax.ppermute(own, "core", [(0, 1), (1, 0)])
     across_e = along(early, ways // 2, ways)
-    other = lax.ppermute(own, "core", [(0, 1), (1, 0)])
+    own, other, *near_e = lax.optimization_barrier((own, other, *near_e))
     sums = exclusive_sums(core, own, other, chips)
     carried = lax.all_to_all(sums, "chip", 0, 0, tiled=True)
     q_late, within = within_late(q, k, v)
@@ -379,8 +385,9 @@
     far_a = along(left_a, 1, ways)
     mine_b = finish_heads(q_late, within, carried, gain_row, b0, b1)
     mine_e, left_e, right_e = early_heads([early, *near_e], [mine_a, left_a, right_a])
-    left_b, right_b, mine_e, left_e, right_e = lax.optimization_barrier(
-        (along(mine_b, 1, ways), along(mine_b, -1, ways), mine_e, left_e, right_e)
+    left_b = along(mine_b, 1, ways)
+    right_b, mine_e, left_e, right_e = lax.optimization_barrier(
+        (along(mine_b, -1, ways), mine_e, left_e, right_e)
     )
     far_b = along(right_b, -1, ways)
     total, w = own_mix(column, w, [mine_a, mine_b, mine_e])

time: 89.2 us -> 97.6 us (1.094)
  starting transfers between devices: 17.2 us -> 47.2 us
  blocking collectives: 22.7 us -> 0 us
  waiting for transfers between devices: 22.9 us -> 26.1 us
  local copies, waits for them, and re-layouts: 3.11 us -> 0.88 us
    all_to_all x1 -> x0, blocking collectives: 22.7 us -> none  [shards(): own = lax.all_to_all(states, 'chip', 0, 0, tiled=True)]
    all_to_all x1, starting transfers between devices: 4.67 us -> 20.3 us  [shards(): carried = lax.all_to_all(sums, 'chip', 0, 0, tiled=True)]
    all_to_all x0 -> x1, starting transfers between devices: none -> 11.2 us  [shards(): own = lax.all_to_all(states, 'chip', 0, 0, tiled=True)]
    ppermute x9, waiting for transfers between devices: 19.2 us -> 9.66 us  [along(): lax.ppermute(value, 'fsdp', [(i, (i + shift) % count) for i in range(coun...]
    all_to_all x0 -> x1, waiting for transfers between devices: none -> 8.85 us  [shards(): own = lax.all_to_all(states, 'chip', 0, 0, tiled=True)]
    all_to_all x1, waiting for transfers between devices: 3.67 us -> 7.58 us  [shards(): carried = lax.all_to_all(sums, 'chip', 0, 0, tiled=True)]
    ppermute x9, starting transfers between devices: 12.5 us -> 15.7 us  [along(): lax.ppermute(value, 'fsdp', [(i, (i + shift) % count) for i in range(coun...]
    unnamed x18 -> x16, local copies, waits for them, and re-layouts: 3.11 us -> 0.88 us
  transfers between devices with their start and end apart: 11 -> 12, of which waited for: 4 -> 4; matrix products, arithmetic and copies ran while one was open for 0% -> 0% of each run, Pallas kernels for 19% -> 18%
where the time goes in v8:
time: 97.6 us; the launch traced here: 97.1 us
  starting transfers between devices  47.2 us (48%)
  waiting for transfers between devices  26.1 us (27%)
  Pallas kernels  22.6 us (23%)
    all_to_all x1, starting transfers between devices, shards(): carried = lax.all_to_all(sums, 'chip', 0, 0, tiled=True)  20.3 us
    ppermute x9, starting transfers between devices, along(): lax.ppermute(value, 'fsdp', [(i, (i + shift) % count) for i in range(coun...  15.7 us
    all_to_all x1, starting transfers between devices, shards(): own = lax.all_to_all(states, 'chip', 0, 0, tiled=True)  11.2 us
    ppermute x9, waiting for transfers between devices, along(): lax.ppermute(value, 'fsdp', [(i, (i + shift) % count) for i in range(coun...  9.66 us
    all_to_all x1, waiting for transfers between devices, shards(): own = lax.all_to_all(states, 'chip', 0, 0, tiled=True)  8.85 us
    all_to_all x1, waiting for transfers between devices, shards(): carried = lax.all_to_all(sums, 'chip', 0, 0, tiled=True)  7.58 us
    pallas_call x4, Pallas kernels, mix(): pl.pallas_call(functools.partial(mix_kernel, plan=tuple(plan), first=tota...  6.7 us
    pallas_call x2, Pallas kernels, early_heads(): pl.pallas_call(functools.partial(early_kernel, count=count), name='early_...  3.88 us
  transfers between devices with their start and end apart: 12, of which 4 were waited for; matrix products, arithmetic and copies ran while one was open for 0% of the time, Pallas kernels for 18%

profile of v8, /device:TPU:32, one launch (start us, length us, event | category | flops | bytes accessed | tf_op | source)
XLA Modules:
  0.0 97.1 jit_solution(9289941753591757413)
XLA Ops:
  0.0 3.4 %block_states.1 = (bf16[1024,128]{1,0:T(8,128)(2,1)}, bf16[528,512]{1,0:T(8,128)(2,1)}) custom-call(bf16[512,1024]{1,0:T(8,128)(2,1)} %q_hbm.3, bf16[512,1024]{1,0:T(8,128)(2,1)} %k_hbm.3, bf16[512,1024]{1,0:T(8,128)(2,1)} %v_hbm.3, f32[1,1024]{1,0:T(1,128)} %bitcast.11), custom_call_target="tpu_custom_call" | custom-call | flops 134217728 | bytes 2097152 | tf_op jit(solution)/shard_map/block_states/pallas_call | solution.py:127
  3.4 11.2 %all-to-all-start = ((bf16[32,32,128]{2,1,0:T(8,128)(2,1)}), bf16[32,32,128]{2,1,0:T(8,128)(2,1)S(1)}, u32[]{:S(2)}, u32[]{:S(2)}) async-start(bf16[32,32,128]{2,1,0:T(8,128)(2,1)} %bitcast.3), calls=%async_computation | async-start | bytes 524288 | tf_op jit(solution)/shard_map/all_to_all | solution.py:371
  14.6 1.7 %collective-permute-start.1 = (bf16[528,512]{1,0:T(8,128)(2,1)}, bf16[528,512]{1,0:T(8,128)(2,1)S(1)}, u32[]{:S(2)}, u32[]{:S(2)}) collective-permute-start(bf16[528,512]{1,0:T(8,128)(2,1)} %get-tuple-element.29.refs_0_), channel_id=1, source_target_pairs={{0,1},{1,2},{2,3},{3,0},{4,5},{5,6},{6,7},{7,4},{8,9},{9,10},{10,1... | collective-permute-start | bytes 1622024 | tf_op jit(solution)/shard_map/ppermute | solution.py:362
  16.3 1.7 %collective-permute-start.2 = (bf16[528,512]{1,0:T(8,128)(2,1)}, bf16[528,512]{1,0:T(8,128)(2,1)S(1)}, u32[]{:S(2)}, u32[]{:S(2)}) collective-permute-start(bf16[528,512]{1,0:T(8,128)(2,1)} %get-tuple-element.29.refs_0_), channel_id=1, source_target_pairs={{0,3},{1,0},{2,1},{3,2},{4,7},{5,4},{6,5},{7,6},{8,11},{9,8},{10,9... | collective-permute-start | bytes 1622024 | tf_op jit(solution)/shard_map/ppermute | solution.py:362
  17.9 8.8 %all-to-all-done = bf16[32,32,128]{2,1,0:T(8,128)(2,1)S(1)} async-done(((bf16[32,32,128]{2,1,0:T(8,128)(2,1)}), bf16[32,32,128]{2,1,0:T(8,128)(2,1)S(1)}, u32[]{:S(2)}, u32[]{:S(2)}) %all-to-all-start) | async-done | bytes 262176 | tf_op jit(solution)/shard_map/all_to_all | solution.py:371
  26.8 3.2 %collective-permute-start.3 = (bf16[528,512]{1,0:T(8,128)(2,1)}, bf16[528,512]{1,0:T(8,128)(2,1)}, u32[]{:S(2)}, u32[]{:S(2)}) collective-permute-start(bf16[528,512]{1,0:T(8,128)(2,1)} %get-tuple-element.29.refs_0_), channel_id=1, source_target_pairs={{0,2},{1,3},{2,0},{3,1},{4,6},{5,7},{6,4},{7,5},{8,10},{9,11},{10,... | collective-permute-start | bytes 1622024 | tf_op jit(solution)/shard_map/ppermute | solution.py:362
  30.0 1.0 %exclusive_sums.1 = bf16[1024,128]{1,0:T(8,128)(2,1)} custom-call(s32[1]{0:T(128)} %bitcast.1.core_ref, bf16[1024,128]{1,0:T(8,128)(2,1)S(1)} %bitcast.10, bf16[1024,128]{1,0:T(8,128)(2,1)S(1)} %collective-permute-done.other_ref), custom_call_target="tpu_custom_call" | custom-call | flops 524288 | bytes 786432 | tf_op jit(solution)/shard_map/exclusive_sums/pallas_call | solution.py:158
  31.1 20.3 %all-to-all-start.1 = ((bf16[32,32,128]{2,1,0:T(8,128)(2,1)}), bf16[32,32,128]{2,1,0:T(8,128)(2,1)S(1)}, u32[]{:S(2)}, u32[]{:S(2)}) async-start(bf16[32,32,128]{2,1,0:T(8,128)(2,1)} %bitcast.5), calls=%async_computation.1 | async-start | bytes 524288 | tf_op jit(solution)/shard_map/all_to_all | solution.py:377
  51.4 3.2 %within_late.1 = (bf16[512,768]{1,0:T(8,128)(2,1)S(1)}, f32[512,768]{1,0:T(8,128)S(1)}) custom-call(bf16[512,1024]{1,0:T(8,128)(2,1)} %q_hbm.3, bf16[512,1024]{1,0:T(8,128)(2,1)} %k_hbm.3, bf16[512,1024]{1,0:T(8,128)(2,1)} %v_hbm.3), custom_call_target="tpu_custom_call" | custom-call | flops 805306368 | bytes 3932160 | tf_op jit(solution)/shard_map/within_late/pallas_call | solution.py:191
  54.6 7.6 %all-to-all-done.1 = bf16[32,32,128]{2,1,0:T(8,128)(2,1)S(1)} async-done(((bf16[32,32,128]{2,1,0:T(8,128)(2,1)}), bf16[32,32,128]{2,1,0:T(8,128)(2,1)S(1)}, u32[]{:S(2)}, u32[]{:S(2)}) %all-to-all-start.1) | async-done | bytes 262176 | tf_op jit(solution)/shard_map/all_to_all | solution.py:377
  62.7 3.6 %collective-permute-start.6 = (bf16[640,384]{1,0:T(8,128)(2,1)S(1)}, bf16[640,384]{1,0:T(8,128)(2,1)S(1)}, u32[]{:S(2)}, u32[]{:S(2)}) collective-permute-start(bf16[640,384]{1,0:T(8,128)(2,1)S(1)} %finish_heads.3.refs_3_.refs_0_), channel_id=1, source_target_pairs={{0,3},{1,0},{2,1},{3,2},{4,7},{5,4},{6,5},{7,6},{8,11},{9,8},{10,9... | collective-permute-start | bytes 1474568 | tf_op jit(solution)/shard_map/ppermute | solution.py:362
  66.8 2.0 %collective-permute-start.4 = (bf16[512,384]{1,0:T(8,128)(2,1)S(1)}, bf16[512,384]{1,0:T(8,128)(2,1)S(1)}, u32[]{:S(2)}, u32[]{:S(2)}) collective-permute-start(bf16[512,384]{1,0:T(8,128)(2,1)S(1)} %finish_heads.2.refs_1_), channel_id=1, source_target_pairs={{0,3},{1,0},{2,1},{3,2},{4,7},{5,4},{6,5},{7,6},{8,11},{9,8},{10,9... | collective-permute-start | bytes 1179656 | tf_op jit(solution)/shard_map/ppermute | solution.py:362
  68.9 8.3 %collective-permute-done.5.refs_4_.refs_0_ = bf16[640,384]{1,0:T(8,128)(2,1)} collective-permute-done((bf16[640,384]{1,0:T(8,128)(2,1)S(1)}, bf16[640,384]{1,0:T(8,128)(2,1)}, u32[]{:S(2)}, u32[]{:S(2)}) %collective-permute-start.5) | collective-permute-done | bytes 491552 | tf_op jit(solution)/shard_map/ppermute | solution.py:362
  77.4 1.3 %collective-permute-start.9 = (bf16[512,384]{1,0:T(8,128)(2,1)S(1)}, bf16[512,384]{1,0:T(8,128)(2,1)S(1)}, u32[]{:S(2)}, u32[]{:S(2)}) collective-permute-start(bf16[512,384]{1,0:T(8,128)(2,1)S(1)} %finish_heads.2.refs_1_), channel_id=1, source_target_pairs={{0,1},{1,2},{2,3},{3,0},{4,5},{5,6},{6,7},{7,4},{8,9},{9,10},{10,1... | collective-permute-start | bytes 1179656 | tf_op jit(solution)/shard_map/ppermute | solution.py:362
  78.8 2.4 %early_heads.2 = (bf16[512,256]{1,0:T(8,128)(2,1)S(1)}, bf16[512,256]{1,0:T(8,128)(2,1)S(1)}, bf16[512,256]{1,0:T(8,128)(2,1)S(1)}) custom-call(bf16[528,512]{1,0:T(8,128)(2,1)S(1)} %copy-done.2, bf16[528,512]{1,0:T(8,128)(2,1)S(1)} %copy-done.4, bf16[528,512]{1,0:T(8,128)(2,1)S(1)} %copy-done.6, bf16[640,384]{1,0:T(8,128)(2,1)S(1)} %finish_heads.3.refs_3_.refs_0_, ...), custom_call_target="tpu_custom_call" | custom-call | flops 201326592 | bytes 2359296 | tf_op jit(solution)/shard_map/early_heads/pallas_call | solution.py:254
  81.2 0.8 copy-done
  82.0 1.9 %collective-permute-start.7 = (bf16[512,384]{1,0:T(8,128)(2,1)S(1)}, bf16[512,384]{1,0:T(8,128)(2,1)S(1)}, u32[]{:S(2)}, u32[]{:S(2)}) collective-permute-start(bf16[512,384]{1,0:T(8,128)(2,1)S(1)} %collective-permute-done.4.refs_1_), channel_id=1, source_target_pairs={{0,3},{1,0},{2,1},{3,2},{4,7},{5,4},{6,5},{7,6},{8,11},{9,8},{10,9... | collective-permute-start | bytes 1179656 | tf_op jit(solution)/shard_map/ppermute | solution.py:362
  83.9 3.5 %own_mix.1 = (f32[512,1024]{1,0:T(8,128)S(1)}, bf16[4096,1024]{1,0:T(8,128)(2,1)S(1)}) custom-call(s32[1]{0:T(128)} %bitcast.column_ref, bf16[640,384]{1,0:T(8,128)(2,1)S(1)} %finish_heads.3.refs_3_.refs_0_, bf16[512,384]{1,0:T(8,128)(2,1)S(1)} %finish_heads.2.refs_1_, bf16[512,256]{1,0:T(8,128)(2,1)S(1)} %get-tuple-element.45.refs_2_, ...), custom_call_target="tpu_custom_call" | custom-call | flops 1073741824 | bytes 8388608 | tf_op jit(solution)/shard_map/own_mix/pallas_call | solution.py:300
  87.4 2.8 %mix.4.refs_3_ = f32[512,1024]{1,0:T(8,128)S(1)} custom-call(s32[1]{0:T(128)} %bitcast.column_ref, bf16[640,384]{1,0:T(8,128)(2,1)} %collective-permute-done.5.refs_4_.refs_0_, bf16[512,256]{1,0:T(8,128)(2,1)S(1)} %get-tuple-element.48.refs_1_, bf16[640,384]{1,0:T(8,128)(2,1)S(1)} %copy-done.1, bf16[512,256]{1,0:T(8,128)(2,1)S(1)} %get-tuple-element.49.refs_3_, ...), custom_call_target="tpu_custom_call" | custom-call | flops 1342177280 | bytes 2621440 | tf_op jit(solution)/shard_map/mix/pallas_call | solution.py:349
  90.3 1.4 %collective-permute-done.9.refs_0_ = bf16[512,384]{1,0:T(8,128)(2,1)S(1)} collective-permute-done((bf16[512,384]{1,0:T(8,128)(2,1)S(1)}, bf16[512,384]{1,0:T(8,128)(2,1)S(1)}, u32[]{:S(2)}, u32[]{:S(2)}) %collective-permute-start.9) | collective-permute-done | bytes 393248 | tf_op jit(solution)/shard_map/ppermute | solution.py:362
  91.6 1.3 %mix.5.refs_3_ = f32[512,1024]{1,0:T(8,128)S(1)} custom-call(s32[1]{0:T(128)} %bitcast.column_ref, bf16[512,384]{1,0:T(8,128)(2,1)S(1)} %collective-permute-done.9.refs_0_, bf16[512,384]{1,0:T(8,128)(2,1)S(1)} %collective-permute-done.4.refs_1_, bf16[4096,1024]{1,0:T(8,128)(2,1)S(1)} %get-tuple-element.46.refs_4_.refs_2_.refs_1_, f32[512,1024]{1,0:T(8,128)S(1)} %mix.4.refs_3_), custom_call_target="tpu_custom_call" | custom-call | flops 805306368 | bytes 1572864 | tf_op jit(solution)/shard_map/mix/pallas_call | solution.py:349
  92.9 1.5 %early_heads.3.refs_1_ = bf16[512,256]{1,0:T(8,128)(2,1)S(1)} custom-call(bf16[528,512]{1,0:T(8,128)(2,1)} %collective-permute-done.3.refs_0_, bf16[640,384]{1,0:T(8,128)(2,1)S(1)} %collective-permute-done.8.refs_1_.refs_0_), custom_call_target="tpu_custom_call" | custom-call | flops 67108864 | bytes 786432 | tf_op jit(solution)/shard_map/early_heads/pallas_call | solution.py:254
  94.4 1.0 %mix.6.refs_2_ = f32[512,1024]{1,0:T(8,128)S(1)} custom-call(s32[1]{0:T(128)} %bitcast.column_ref, bf16[640,384]{1,0:T(8,128)(2,1)S(1)} %collective-permute-done.8.refs_1_.refs_0_, bf16[512,256]{1,0:T(8,128)(2,1)S(1)} %early_heads.3.refs_1_, bf16[4096,1024]{1,0:T(8,128)(2,1)S(1)} %get-tuple-element.46.refs_4_.refs_2_.refs_1_, f32[512,1024]{1,0:T(8,128)S(1)} %mix.5.refs_3_), custom_call_target="tpu_custom_call" | custom-call | flops 671088640 | bytes 1310720 | tf_op jit(solution)/shard_map/mix/pallas_call | solution.py:349
  95.4 1.6 %mix.7 = bf16[512,1024]{1,0:T(8,128)(2,1)} custom-call(s32[1]{0:T(128)} %bitcast.column_ref, bf16[512,384]{1,0:T(8,128)(2,1)S(1)} %collective-permute-done.7.refs_0_, bf16[4096,1024]{1,0:T(8,128)(2,1)S(1)} %get-tuple-element.46.refs_4_.refs_2_.refs_1_, f32[512,1024]{1,0:T(8,128)S(1)} %mix.6.refs_2_), custom_call_target="tpu_custom_call" | custom-call | flops 402653184 | bytes 786432 | tf_op jit(solution)/shard_map/mix/pallas_call | solution.py:349
  (28 shorter events, 1.4 us)
Async XLA Ops:
  3.4 23.4 %all-to-all-start = ((bf16[32,32,128]{2,1,0:T(8,128)(2,1)}), bf16[32,32,128]{2,1,0:T(8,128)(2,1)S(1)}, u32[]{:S(2)}, u32[]{:S(2)}) async-start(bf16[32,32,128]{2,1,0:T(8,128)(2,1)} %bitcast.3), calls=%async_computation | async-start | bytes 524288 | tf_op jit(solution)/shard_map/all_to_all | solution.py:371
  14.6 15.4 %collective-permute-start.1 = (bf16[528,512]{1,0:T(8,128)(2,1)}, bf16[528,512]{1,0:T(8,128)(2,1)S(1)}, u32[]{:S(2)}, u32[]{:S(2)}) collective-permute-start(bf16[528,512]{1,0:T(8,128)(2,1)} %get-tuple-element.29.refs_0_), channel_id=1, source_target_pairs={{0,1},{1,2},{2,3},{3,0},{4,5},{5,6},{6,7},{7,4},{8,9},{9,10},{10,1... | collective-permute-start | bytes 1622024 | tf_op jit(solution)/shard_map/ppermute | solution.py:362
  16.3 13.7 %collective-permute-start.2 = (bf16[528,512]{1,0:T(8,128)(2,1)}, bf16[528,512]{1,0:T(8,128)(2,1)S(1)}, u32[]{:S(2)}, u32[]{:S(2)}) collective-permute-start(bf16[528,512]{1,0:T(8,128)(2,1)} %get-tuple-element.29.refs_0_), channel_id=1, source_target_pairs={{0,3},{1,0},{2,1},{3,2},{4,7},{5,4},{6,5},{7,6},{8,11},{9,8},{10,9... | collective-permute-start | bytes 1622024 | tf_op jit(solution)/shard_map/ppermute | solution.py:362
  26.8 3.2 %collective-permute-start = (bf16[1024,128]{1,0:T(8,128)(2,1)S(1)}, bf16[1024,128]{1,0:T(8,128)(2,1)S(1)}, u32[]{:S(2)}, u32[]{:S(2)}) collective-permute-start(bf16[1024,128]{1,0:T(8,128)(2,1)S(1)} %bitcast.9), channel_id=1, source_target_pairs={{0,4},{4,0},{1,5},{5,1},{2,6},{6,2},{3,7},{7,3},{8,12},{12,8},{9,1... | collective-permute-start | bytes 786440 | tf_op jit(solution)/shard_map/ppermute | solution.py:373
  26.8 27.8 %collective-permute-start.3 = (bf16[528,512]{1,0:T(8,128)(2,1)}, bf16[528,512]{1,0:T(8,128)(2,1)}, u32[]{:S(2)}, u32[]{:S(2)}) collective-permute-start(bf16[528,512]{1,0:T(8,128)(2,1)} %get-tuple-element.29.refs_0_), channel_id=1, source_target_pairs={{0,2},{1,3},{2,0},{3,1},{4,6},{5,7},{6,4},{7,5},{8,10},{9,11},{10,... | collective-permute-start | bytes 1622024 | tf_op jit(solution)/shard_map/ppermute | solution.py:362
  30.0 1.0 %copy-start.3 = (bf16[528,512]{1,0:T(8,128)(2,1)}, bf16[528,512]{1,0:T(8,128)(2,1)S(1)}, u32[]{:S(2)}) copy-start(bf16[528,512]{1,0:T(8,128)(2,1)S(1)} %collective-permute-done.1.refs_1_) | copy-start | bytes 1622020
  30.0 1.1 %copy-start.5 = (bf16[528,512]{1,0:T(8,128)(2,1)}, bf16[528,512]{1,0:T(8,128)(2,1)S(1)}, u32[]{:S(2)}) copy-start(bf16[528,512]{1,0:T(8,128)(2,1)S(1)} %collective-permute-done.2.refs_2_) | copy-start | bytes 1622020
  30.0 32.2 %copy-start.7 = (f32[1024]{0:T(1024)S(1)}, f32[1024]{0:T(1024)}, u32[]{:S(2)}) copy-start(f32[1024]{0:T(1024)} %param.8) | copy-start | bytes 12292
  31.1 31.1 %all-to-all-start.1 = ((bf16[32,32,128]{2,1,0:T(8,128)(2,1)}), bf16[32,32,128]{2,1,0:T(8,128)(2,1)S(1)}, u32[]{:S(2)}, u32[]{:S(2)}) async-start(bf16[32,32,128]{2,1,0:T(8,128)(2,1)} %bitcast.5), calls=%async_computation.1 | async-start | bytes 524288 | tf_op jit(solution)/shard_map/all_to_all | solution.py:377
  62.6 16.1 %copy-start.2 = (bf16[528,512]{1,0:T(8,128)(2,1)S(1)}, bf16[528,512]{1,0:T(8,128)(2,1)}, u32[]{:S(2)}) copy-start(bf16[528,512]{1,0:T(8,128)(2,1)} %get-tuple-element.29.refs_0_) | copy-start | bytes 1622020
  62.6 16.1 %copy-start.4 = (bf16[528,512]{1,0:T(8,128)(2,1)S(1)}, bf16[528,512]{1,0:T(8,128)(2,1)}, u32[]{:S(2)}) copy-start(bf16[528,512]{1,0:T(8,128)(2,1)} %copy-done.3) | copy-start | bytes 1622020
  62.6 16.1 %copy-start.6 = (bf16[528,512]{1,0:T(8,128)(2,1)S(1)}, bf16[528,512]{1,0:T(8,128)(2,1)}, u32[]{:S(2)}) copy-start(bf16[528,512]{1,0:T(8,128)(2,1)} %copy-done.5) | copy-start | bytes 1622020
  62.7 14.5 %collective-permute-start.5 = (bf16[640,384]{1,0:T(8,128)(2,1)S(1)}, bf16[640,384]{1,0:T(8,128)(2,1)}, u32[]{:S(2)}, u32[]{:S(2)}) collective-permute-start(bf16[640,384]{1,0:T(8,128)(2,1)S(1)} %finish_heads.3.refs_3_.refs_0_), channel_id=1, source_target_pairs={{0,1},{1,2},{2,3},{3,0},{4,5},{5,6},{6,7},{7,4},{8,9},{9,10},{10,1... | collective-permute-start | bytes 1474568 | tf_op jit(solution)/shard_map/ppermute | solution.py:362
  62.7 14.4 %collective-permute-start.6 = (bf16[640,384]{1,0:T(8,128)(2,1)S(1)}, bf16[640,384]{1,0:T(8,128)(2,1)S(1)}, u32[]{:S(2)}, u32[]{:S(2)}) collective-permute-start(bf16[640,384]{1,0:T(8,128)(2,1)S(1)} %finish_heads.3.refs_3_.refs_0_), channel_id=1, source_target_pairs={{0,3},{1,0},{2,1},{3,2},{4,7},{5,4},{6,5},{7,6},{8,11},{9,8},{10,9... | collective-permute-start | bytes 1474568 | tf_op jit(solution)/shard_map/ppermute | solution.py:362
  66.8 15.1 %collective-permute-start.4 = (bf16[512,384]{1,0:T(8,128)(2,1)S(1)}, bf16[512,384]{1,0:T(8,128)(2,1)S(1)}, u32[]{:S(2)}, u32[]{:S(2)}) collective-permute-start(bf16[512,384]{1,0:T(8,128)(2,1)S(1)} %finish_heads.2.refs_1_), channel_id=1, source_target_pairs={{0,3},{1,0},{2,1},{3,2},{4,7},{5,4},{6,5},{7,6},{8,11},{9,8},{10,9... | collective-permute-start | bytes 1179656 | tf_op jit(solution)/shard_map/ppermute | solution.py:362
  77.2 15.7 %collective-permute-start.8 = (bf16[640,384]{1,0:T(8,128)(2,1)}, bf16[640,384]{1,0:T(8,128)(2,1)S(1)}, u32[]{:S(2)}, u32[]{:S(2)}) collective-permute-start(bf16[640,384]{1,0:T(8,128)(2,1)} %collective-permute-done.5.refs_4_.refs_0_), channel_id=1, source_target_pairs={{0,1},{1,2},{2,3},{3,0},{4,5},{5,6},{6,7},{7,4},{8,9},{9,10},{10,1... | collective-permute-start | bytes 1474568 | tf_op jit(solution)/shard_map/ppermute | solution.py:362
  77.4 14.2 %collective-permute-start.9 = (bf16[512,384]{1,0:T(8,128)(2,1)S(1)}, bf16[512,384]{1,0:T(8,128)(2,1)S(1)}, u32[]{:S(2)}, u32[]{:S(2)}) collective-permute-start(bf16[512,384]{1,0:T(8,128)(2,1)S(1)} %finish_heads.2.refs_1_), channel_id=1, source_target_pairs={{0,1},{1,2},{2,3},{3,0},{4,5},{5,6},{6,7},{7,4},{8,9},{9,10},{10,1... | collective-permute-start | bytes 1179656 | tf_op jit(solution)/shard_map/ppermute | solution.py:362
  81.2 0.8 copy-start
  82.0 13.4 %collective-permute-start.7 = (bf16[512,384]{1,0:T(8,128)(2,1)S(1)}, bf16[512,384]{1,0:T(8,128)(2,1)S(1)}, u32[]{:S(2)}, u32[]{:S(2)}) collective-permute-start(bf16[512,384]{1,0:T(8,128)(2,1)S(1)} %collective-permute-done.4.refs_1_), channel_id=1, source_target_pairs={{0,3},{1,0},{2,1},{3,2},{4,7},{5,4},{6,5},{7,6},{8,11},{9,8},{10,9... | collective-permute-start | bytes 1179656 | tf_op jit(solution)/shard_map/ppermute | solution.py:362
  83.9 3.6 %copy-start.1 = (bf16[640,384]{1,0:T(8,128)(2,1)S(1)}, bf16[640,384]{1,0:T(8,128)(2,1)}, u32[]{:S(2)}) copy-start(bf16[640,384]{1,0:T(8,128)(2,1)} %copy-done) | copy-start | bytes 1474564

commit v9 on v7

v9 whole, which is shorter than its diff:
```python
import functools

import jax
import jax.numpy as jnp
from jax import lax
from jax.experimental import pallas as pl
from jax.experimental.pallas import tpu as pltpu
from jax.sharding import Mesh
from jax.sharding import PartitionSpec as P

DH = 128
BLK = 512
HALF = BLK // 2
CORES = 2
HEADS = 8
LATE = 6
EARLY = HEADS - LATE
GAIN_ROWS = 16
CALLS = ((0, 3), (3, 6))
F32 = jnp.float32
BF16 = jnp.bfloat16
NN, NT, TN = ((1,), (0,)), ((1,), (1,)), ((0,), (0,))
SMEM = pl.BlockSpec(memory_space=pltpu.SMEM)
VMEM = pl.BlockSpec(memory_space=pltpu.VMEM)
HBM = pl.BlockSpec(memory_space=pltpu.HBM)
PARAMS = pltpu.CompilerParams(vmem_limit_bytes=20 * 2**20)


def dot(a, b, dims):
    return lax.dot_general(a, b, (dims, ((), ())), preferred_element_type=F32)


def in_vmem(value):
    return pltpu.with_memory_space_constraint(value, pltpu.VMEM)


def in_hbm(value):
    return pltpu.with_memory_space_constraint(value, pltpu.HBM)


def cost(flops, size):
    return pl.CostEstimate(flops=flops, bytes_accessed=size, transcendentals=0)


def within_block(q_ref, k_ref, v_ref, h, causal):
    cols = slice(h * DH, (h + 1) * DH)
    q0, q1 = q_ref[:HALF, cols], q_ref[HALF:, cols]
    k0, k1 = k_ref[:HALF, cols], k_ref[HALF:, cols]
    v0, v1 = v_ref[:HALF, cols], v_ref[HALF:, cols]
    s00 = jnp.where(causal, dot(q0, k0, NT), 0.0).astype(BF16)
    s10 = dot(q1, k0, NT).astype(BF16)
    s11 = jnp.where(causal, dot(q1, k1, NT), 0.0).astype(BF16)
    return dot(s00, v0, NN), dot(s10, v0, NN) + dot(s11, v1, NN)


def causal_mask():
    row = lax.broadcasted_iota(jnp.int32, (HALF, HALF), 0)
    col = lax.broadcasted_iota(jnp.int32, (HALF, HALF), 1)
    return col <= row


def finish(queries, within, state, gain):
    att = within + dot(queries, state, NN)
    mean = jnp.full((DH, DH), 1.0 / DH, BF16)
    mean_square = dot((att * att).astype(BF16), mean, NN)
    return (att * lax.rsqrt(mean_square + 1e-6) * gain).astype(BF16)


PARTS = 2


def state_kernel(k_hbm, v_hbm, out_ref, k_ref, v_ref, sems):
    width = k_ref.shape[1] // PARTS
    copies = []
    for part in range(PARTS):
        cols = slice(part * width, (part + 1) * width)
        for at, (hbm, ref) in enumerate(((k_hbm, k_ref), (v_hbm, v_ref))):
            copy = pltpu.make_async_copy(hbm.at[:, cols], ref.at[:, cols], sems.at[part, at])
            copy.start()
            copies.append(copy)
    for part in range(PARTS):
        copies[2 * part].wait()
        copies[2 * part + 1].wait()
        for h in range(part * width // DH, (part + 1) * width // DH):
            cols = slice(h * DH, (h + 1) * DH)
            out_ref[cols, :] = dot(k_ref[:, cols], v_ref[:, cols], TN).astype(BF16)


def block_states(k, v):
    width = k.shape[1]
    return pl.pallas_call(
        state_kernel,
        name="block_states",
        in_specs=[HBM, HBM],
        out_specs=VMEM,
        out_shape=jax.ShapeDtypeStruct((width, DH), BF16),
        scratch_shapes=[
            pltpu.VMEM(k.shape, BF16),
            pltpu.VMEM(v.shape, BF16),
            pltpu.SemaphoreType.DMA((PARTS, 2)),
        ],
        compiler_params=PARAMS,
        cost_estimate=cost(2 * BLK * DH * width, 2 * BLK * width * 2),
    )(in_hbm(k), in_hbm(v))


def within_early_kernel(q_hbm, k_hbm, v_hbm, gain_hbm, *refs):
    out_hbm, (q_ref, k_ref, v_ref, gain_ref, early_ref, sems) = refs[:EARLY], refs[EARLY:]
    early = slice(LATE * DH, HEADS * DH)
    sources = (q_hbm.at[:, early], k_hbm.at[:, early], v_hbm.at[:, early], gain_hbm)
    targets = (q_ref, k_ref, v_ref, gain_ref)
    copies = [
        pltpu.make_async_copy(source, target, sems.at[at])
        for at, (source, target) in enumerate(zip(sources, targets))
    ]
    for copy in copies:
        copy.start()
    for copy in copies:
        copy.wait()
    causal = causal_mask()
    blank = jnp.zeros((GAIN_ROWS - 3, DH), BF16)
    outs = []
    for h in range(EARLY):
        cols = slice(h * DH, (h + 1) * DH)
        gain = gain_ref[:, (LATE + h) * DH : (LATE + h + 1) * DH]
        high = gain.astype(BF16)
        rest = gain - high.astype(F32)
        middle = rest.astype(BF16)
        low = (rest - middle.astype(F32)).astype(BF16)
        top, bottom = within_block(q_ref, k_ref, v_ref, h, causal)
        early_ref[h, :BLK, :DH] = q_ref[:, cols]
        early_ref[h, :HALF, DH:] = top.astype(BF16)
        early_ref[h, HALF:BLK, DH:] = bottom.astype(BF16)
        early_ref[h, BLK:, :DH] = jnp.concatenate([high, middle, low, blank])
        early_ref[h, BLK:, DH:] = jnp.zeros((GAIN_ROWS, DH), BF16)
        outs.append(pltpu.make_async_copy(early_ref.at[h], out_hbm[h], sems.at[4 + h]))
        outs[-1].start()
    for copy in outs:
        copy.wait()


def within_early(q, k, v, gain):
    shape, block = (BLK, EARLY * DH), (BLK + GAIN_ROWS, 2 * DH)
    return pl.pallas_call(
        within_early_kernel,
        name="within_early",
        in_specs=[HBM] * 4,
        out_specs=[HBM] * EARLY,
        out_shape=[jax.ShapeDtypeStruct(block, BF16)] * EARLY,
        scratch_shapes=[
            pltpu.VMEM(shape, BF16),
            pltpu.VMEM(shape, BF16),
            pltpu.VMEM(shape, BF16),
            pltpu.VMEM(gain.shape, F32),
            pltpu.VMEM((EARLY, *block), BF16),
            pltpu.SemaphoreType.DMA((4 + EARLY,)),
        ],
        compiler_params=PARAMS,
        cost_estimate=cost(4 * BLK * BLK * DH * EARLY, BLK * DH * EARLY * 10),
    )(in_hbm(q), in_hbm(k), in_hbm(v), in_hbm(gain))


def scan_kernel(core_ref, own_ref, other_ref, out_ref, *, chips):
    rows = own_ref.shape[0] // chips
    second = (core_ref[0] == 1).astype(F32)
    before = jnp.zeros((rows, DH), F32)
    for chip in range(chips):
        at = slice(chip * rows, (chip + 1) * rows)
        other = other_ref[at, :].astype(F32)
        out_ref[at, :] = (before + second * other).astype(BF16)
        before = before + (own_ref[at, :].astype(F32) + other)


def exclusive_sums(core, own, other, chips):
    return pl.pallas_call(
        functools.partial(scan_kernel, chips=chips),
        name="exclusive_sums",
        in_specs=[SMEM, VMEM, VMEM],
        out_specs=VMEM,
        out_shape=jax.ShapeDtypeStruct(own.shape, BF16),
        compiler_params=PARAMS,
        cost_estimate=cost(own.size * 4, own.size * 6),
    )(core, own, other)


def within_kernel(q_hbm, k_hbm, v_hbm, q_ref, out_ref, k_ref, v_ref, sems):
    copies, split = [], CALLS[0][1] * DH
    parts = (slice(0, split), slice(split, LATE * DH))
    for part, cols in enumerate(parts):
        for at, (hbm, ref) in enumerate(((q_hbm, q_ref), (k_hbm, k_ref), (v_hbm, v_ref))):
            copies.append(
                pltpu.make_async_copy(hbm.at[:, cols], ref.at[:, cols], sems.at[part, at])
            )
            copies[-1].start()
    causal = causal_mask()
    for part, (first, last) in enumerate(CALLS):
        for copy in copies[3 * part : 3 * part + 3]:
            copy.wait()
        for h in range(first, last):
            cols = slice(h * DH, (h + 1) * DH)
            top, bottom = within_block(q_ref, k_ref, v_ref, h, causal)
            out_ref[:HALF, cols] = top
            out_ref[HALF:, cols] = bottom


def within_late(q, k, v):
    shape = (BLK, LATE * DH)
    return pl.pallas_call(
        within_kernel,
        name="within_late",
        in_specs=[HBM] * 3,
        out_specs=[VMEM, VMEM],
        out_shape=[pltpu.VMEM(shape, BF16), pltpu.VMEM(shape, F32)],
        scratch_shapes=[
            pltpu.VMEM(shape, BF16),
            pltpu.VMEM(shape, BF16),
            pltpu.SemaphoreType.DMA((2, 3)),
        ],
        compiler_params=PARAMS,
        cost_estimate=cost(4 * BLK * BLK * DH * LATE, BLK * DH * LATE * 10),
    )(in_hbm(q), in_hbm(k), in_hbm(v))


def finish_kernel(q_ref, within_ref, carried_ref, gain_ref, out_ref, *, first, last):
    for h in range(first, last):
        cols = slice(h * DH, (h + 1) * DH)
        out_cols = slice((h - first) * DH, (h - first + 1) * DH)
        out_ref[:BLK, out_cols] = finish(
            q_ref[:, cols], within_ref[:, cols], carried_ref[cols, :], gain_ref[:, cols]
        )
    if out_ref.shape[0] > BLK:
        out_ref[BLK:, EARLY * DH :] = jnp.zeros((DH, out_ref.shape[1] - EARLY * DH), BF16)
        for h in range(EARLY):
            state = carried_ref[(LATE + h) * DH : (LATE + h + 1) * DH, :]
            out_ref[BLK:, h * DH : (h + 1) * DH] = state


def finish_heads(q, within, carried, gain, first, last, states=False):
    heads = last - first
    return pl.pallas_call(
        functools.partial(finish_kernel, first=first, last=last),
        name="finish_heads",
        in_specs=[VMEM] * 4,
        out_specs=VMEM,
        out_shape=jax.ShapeDtypeStruct((BLK + DH if states else BLK, heads * DH), BF16),
        compiler_params=PARAMS,
        cost_estimate=cost(4 * BLK * DH * DH * heads, BLK * DH * heads * 8),
    )(q, within, carried, gain)


def early_kernel(*refs, count):
    hbm_refs, rest = refs[: count * EARLY], refs[count * EARLY :]
    a_refs, out_refs, (e_ref, sems) = rest[:count], rest[count : 2 * count], rest[2 * count :]
    copies = [
        pltpu.make_async_copy(hbm, e_ref.at[at], sems.at[at]) for at, hbm in enumerate(hbm_refs)
    ]
    for copy in copies:
        copy.start()
    for source, (a_ref, out_ref) in enumerate(zip(a_refs, out_refs)):
        for h in range(EARLY):
            at = source * EARLY + h
            copies[at].wait()
            cols = slice(h * DH, (h + 1) * DH)
            terms = e_ref[at, BLK:, :DH].astype(F32)
            gain = terms[0:1] + terms[1:2] + terms[2:3]
            within = e_ref[at, :BLK, DH:].astype(F32)
            out_ref[:, cols] = finish(e_ref[at, :BLK, :DH], within, a_ref[BLK:, cols], gain)


def early_heads(early, chunks):
    count = len(chunks)
    early = [value for pair in early for value in pair]
    return pl.pallas_call(
        functools.partial(early_kernel, count=count),
        name="early_heads",
        in_specs=[pl.BlockSpec(memory_space=pl.ANY)] * len(early) + [VMEM] * count,
        out_specs=[VMEM] * count,
        out_shape=[jax.ShapeDtypeStruct((BLK, EARLY * DH), BF16)] * count,
        scratch_shapes=[
            pltpu.VMEM((len(early), *early[0].shape), BF16),
            pltpu.SemaphoreType.DMA((len(early),)),
        ],
        compiler_params=PARAMS,
        cost_estimate=cost(4 * BLK * DH * DH * EARLY * count, BLK * DH * EARLY * count * 6),
    )(*early, *chunks)


TILE = 256


def weight_rows(w_hbm, column_ref, shift):
    depth = HEADS * DH
    ways = w_hbm.shape[0] // depth
    source = lax.rem(column_ref[0] + (shift + ways), ways)
    return w_hbm.at[pl.ds(pl.multiple_of(source * depth, depth), depth)]


def own_kernel(column_ref, *refs):
    *a_refs, w_hbm, total_ref, w_ref, sems = refs
    source = weight_rows(w_hbm, column_ref, 0)
    copies, rows, at = [], [], 0
    for piece, a_ref in enumerate(a_refs):
        rows.append(slice(at, at + a_ref.shape[1]))
        at += a_ref.shape[1]
        copies.append(
            pltpu.make_async_copy(source.at[rows[-1]], w_ref.at[rows[-1]], sems.at[piece])
        )
        copies[-1].start()
    for piece, a_ref in enumerate(a_refs):
        copies[piece].wait()
        for tile in range(total_ref.shape[1] // TILE):
            cols = slice(tile * TILE, (tile + 1) * TILE)
            term = dot(a_ref[:BLK, :], w_ref[rows[piece], cols], NN)
            total_ref[:, cols] = term if piece == 0 else total_ref[:, cols] + term


def own_mix(column, w, arrays):
    width, depth = w.shape[1], HEADS * DH
    return pl.pallas_call(
        own_kernel,
        name="own_mix",
        in_specs=[SMEM] + [VMEM] * len(arrays) + [HBM],
        out_specs=VMEM,
        out_shape=pltpu.VMEM((BLK, width), F32),
        scratch_shapes=[
            pltpu.VMEM((depth, width), BF16),
            pltpu.SemaphoreType.DMA((len(arrays),)),
        ],
        compiler_params=PARAMS,
        cost_estimate=cost(2 * BLK * depth * width, 2 * depth * width),
    )(column, *arrays, in_hbm(w))


def add_products(total_ref, out_ref, a_refs, w_ref, starts, cols):
    total = total_ref[:, cols]
    for a_ref, start in zip(a_refs, starts):
        total = total + dot(a_ref[:BLK, :], w_ref[start : start + a_ref.shape[1], cols], NN)
    out_ref[:, cols] = total.astype(out_ref.dtype)


SIDES = (-1, 1, 2)


def side_kernel(column_ref, *refs, starts):
    *a_refs, w_hbm, total_ref, out_ref, w_ref, sems = refs
    depth = HEADS * DH
    copies = []
    for at, shift in enumerate(SIDES):
        rows = slice(at * depth, (at + 1) * depth)
        copies.append(
            pltpu.make_async_copy(
                weight_rows(w_hbm, column_ref, shift), w_ref.at[rows], sems.at[at]
            )
        )
        copies[-1].start()
    half = len(a_refs) // 2
    for side in range(2):
        copies[side].wait()
        mine = slice(side * half, (side + 1) * half)
        for tile in range(out_ref.shape[1] // TILE):
            cols = slice(tile * TILE, (tile + 1) * TILE)
            source = out_ref if side else total_ref
            add_products(source, out_ref, a_refs[mine], w_ref, starts[mine], cols)
    copies[2].wait()


def side_mix(column, w, starts, arrays, total):
    width, depth = w.shape[1], len(SIDES) * HEADS * DH
    return pl.pallas_call(
        functools.partial(side_kernel, starts=starts),
        name="side_mix",
        in_specs=[SMEM] + [VMEM] * len(arrays) + [HBM, VMEM],
        out_specs=[VMEM, VMEM],
        out_shape=[pltpu.VMEM((BLK, width), F32), pltpu.VMEM((depth, width), BF16)],
        scratch_shapes=[pltpu.SemaphoreType.DMA((len(SIDES),))],
        compiler_params=PARAMS,
        cost_estimate=cost(2 * BLK * depth * width, 2 * depth * width),
    )(column, *arrays, in_hbm(w), total)


def mix_kernel(*refs, count, starts, last):
    a_refs, (w_ref, total_ref), rest = refs[:count], refs[count : count + 2], refs[count + 2 :]
    if last:
        out_hbm, out_ref, sems = rest
    else:
        (out_ref,) = rest
    copies = []
    for tile in range(out_ref.shape[1] // TILE):
        cols = slice(tile * TILE, (tile + 1) * TILE)
        add_products(total_ref, out_ref, a_refs, w_ref, starts, cols)
        if last:
            copy = pltpu.make_async_copy(out_ref.at[:, cols], out_hbm.at[:, cols], sems.at[tile])
            copy.start()
            copies.append(copy)
    for copy in copies:
        copy.wait()


def mix(w, starts, arrays, total, last=False):
    width = w.shape[1]
    depth = sum(a.shape[1] for a in arrays)
    if last:
        out_shape = jax.ShapeDtypeStruct((BLK, width), BF16)
        scratch = [pltpu.VMEM((BLK, width), BF16), pltpu.SemaphoreType.DMA((width // TILE,))]
    else:
        out_shape, scratch = pltpu.VMEM((BLK, width), F32), []
    return pl.pallas_call(
        functools.partial(mix_kernel, count=len(arrays), starts=starts, last=last),
        name="mix",
        in_specs=[VMEM] * (len(arrays) + 2),
        out_specs=HBM if last else VMEM,
        out_shape=out_shape,
        scratch_shapes=scratch,
        compiler_params=PARAMS,
        cost_estimate=cost(2 * BLK * depth * width, 2 * depth * width),
    )(*arrays, w, total)


def along(value, shift, count):
    return lax.ppermute(value, "fsdp", [(i, (i + shift) % count) for i in range(count)])


def shards(q, k, v, gain, w):
    chips, ways = lax.axis_size("chip"), lax.axis_size("fsdp")
    core = lax.axis_index("core").reshape(1)
    column = lax.axis_index("fsdp").reshape(1)
    gain_row = gain.reshape(1, -1)
    states = block_states(k, v)
    own = lax.all_to_all(states, "chip", 0, 0, tiled=True)
    early = within_early(q, k, v, gain_row)
    left_q = [along(value, 1, ways) for value in early]
    right_q = [along(value, -1, ways) for value in early]
    other = lax.ppermute(own, "core", [(0, 1), (1, 0)])
    own, other, left_q, right_q = lax.optimization_barrier((own, other, left_q, right_q))
    far_q = [along(left_q[0], 1, ways), along(right_q[1], -1, ways)]
    sums = exclusive_sums(core, own, other, chips)
    carried = lax.all_to_all(sums, "chip", 0, 0, tiled=True)
    q_late, within = within_late(q, k, v)
    carried, far_q, q_late, within = lax.optimization_barrier((carried, far_q, q_late, within))
    (a0, a1), (b0, b1) = CALLS
    mine_a = finish_heads(q_late, within, carried, gain_row, a0, a1, True)
    mine_b = finish_heads(q_late, within, carried, gain_row, b0, b1)
    (mine_e,) = early_heads([early], [mine_a])
    total = own_mix(column, w, [mine_a, mine_b, mine_e])
    left_a, right_a, total = lax.optimization_barrier(
        (along(mine_a, 1, ways), along(mine_a, -1, ways), total)
    )
    far_a = along(left_a, 1, ways)
    left_e, right_e = early_heads([left_q, right_q], [left_a, right_a])
    left_b = along(mine_b, 1, ways)
    right_b, left_e, right_e = lax.optimization_barrier(
        (along(mine_b, -1, ways), left_e, right_e)
    )
    far_b = along(right_b, -1, ways)
    depth = HEADS * DH
    at_a, at_b, at_e = a0 * DH, b0 * DH, LATE * DH
    starts = (at_a, at_e, depth + at_a, depth + at_e)
    total, w = side_mix(column, w, starts, [left_a, left_e, right_a, right_e], total)
    (far_e,) = early_heads([far_q], [far_a])
    total = mix(w, (2 * depth + at_a, 2 * depth + at_e), [far_a, far_e], total)
    total = mix(w, (at_b, depth + at_b), [left_b, right_b], total)
    return mix(w, (2 * depth + at_b,), [far_b], total, True)


def solution(mesh):
    seq, fsdp = mesh.devices.shape
    fine = Mesh(mesh.devices.reshape(seq // CORES, CORES, fsdp), ("chip", "core", "fsdp"))
    rows = ("chip", "core")
    placed = (P(rows, "fsdp"), P(rows, "fsdp"), P(rows, "fsdp"), P("fsdp"), P(None, "fsdp"))
    return jax.shard_map(
        shards, mesh=fine, in_specs=placed, out_specs=P(rows, "fsdp"), check_vma=False
    )
```

time: 89.2 us -> 87.4 us (0.980)
  blocking collectives: 22.7 us -> 0 us
  starting transfers between devices: 17.2 us -> 39.9 us
  waiting for transfers between devices: 22.9 us -> 17.4 us
  Pallas kernels: 21.7 us -> 25.3 us
  local copies, waits for them, and re-layouts: 3.11 us -> 4.08 us
    all_to_all x1 -> x0, blocking collectives: 22.7 us -> none  [shards(): own = lax.all_to_all(states, 'chip', 0, 0, tiled=True)]
    all_to_all x0 -> x1, starting transfers between devices: none -> 11.2 us  [shards(): own = lax.all_to_all(states, 'chip', 0, 0, tiled=True)]
    ppermute x9 -> x12, waiting for transfers between devices: 19.2 us -> 11 us  [along(): lax.ppermute(value, 'fsdp', [(i, (i + shift) % count) for i in range(coun...]
    ppermute x9 -> x12, starting transfers between devices: 12.5 us -> 18.9 us  [along(): lax.ppermute(value, 'fsdp', [(i, (i + shift) % count) for i in range(coun...]
    all_to_all x1, starting transfers between devices: 4.67 us -> 9.76 us  [shards(): carried = lax.all_to_all(sums, 'chip', 0, 0, tiled=True)]
    all_to_all x0 -> x1, waiting for transfers between devices: none -> 4.71 us  [shards(): own = lax.all_to_all(states, 'chip', 0, 0, tiled=True)]
    pallas_call x5 -> x6, Pallas kernels: 9.37 us -> 13.4 us  [the longest x1 4.79 us: side_mix(): pl.pallas_call(functools.partial(side_kernel, starts=starts), name='side_...]
    all_to_all x1, waiting for transfers between devices: 3.67 us -> 1.64 us  [shards(): carried = lax.all_to_all(sums, 'chip', 0, 0, tiled=True)]
  transfers between devices with their start and end apart: 11 -> 15, of which waited for: 4 -> 9; matrix products, arithmetic and copies ran while one was open for 0% -> 0% of each run, Pallas kernels for 19% -> 23%
where the time goes in v9:
time: 87.4 us; the launch traced here: 87 us
  starting transfers between devices  39.9 us (46%)
  Pallas kernels  25.3 us (29%)
  waiting for transfers between devices  17.4 us (20%)
  local copies, waits for them, and re-layouts  4.08 us (5%)
    ppermute x12, starting transfers between devices, along(): lax.ppermute(value, 'fsdp', [(i, (i + shift) % count) for i in range(coun...  18.9 us
    all_to_all x1, starting transfers between devices, shards(): own = lax.all_to_all(states, 'chip', 0, 0, tiled=True)  11.2 us
    ppermute x12, waiting for transfers between devices, along(): lax.ppermute(value, 'fsdp', [(i, (i + shift) % count) for i in range(coun...  11 us
    all_to_all x1, starting transfers between devices, shards(): carried = lax.all_to_all(sums, 'chip', 0, 0, tiled=True)  9.76 us
    pallas_call x1, Pallas kernels, side_mix(): pl.pallas_call(functools.partial(side_kernel, starts=starts), name='side_...  4.79 us
    all_to_all x1, waiting for transfers between devices, shards(): own = lax.all_to_all(states, 'chip', 0, 0, tiled=True)  4.71 us
    pallas_call x3, Pallas kernels, early_heads(): pl.pallas_call(functools.partial(early_kernel, count=count), name='early_...  4.1 us
    unnamed x30, local copies, waits for them, and re-layouts  4.08 us
  transfers between devices with their start and end apart: 15, of which 9 were waited for; matrix products, arithmetic and copies ran while one was open for 0% of the time, Pallas kernels for 23%

profile of v9, /device:TPU:32, one launch (start us, length us, event | category | flops | bytes accessed | tf_op | source)
XLA Modules:
  0.0 87.0 jit_solution(3562266511985423418)
XLA Ops:
  0.0 2.7 %block_states.1 = bf16[1024,128]{1,0:T(8,128)(2,1)} custom-call(bf16[512,1024]{1,0:T(8,128)(2,1)} %k_hbm.5, bf16[512,1024]{1,0:T(8,128)(2,1)} %v_hbm.5), custom_call_target="tpu_custom_call" | custom-call | flops 134217728 | bytes 2097152 | tf_op jit(solution)/shard_map/block_states/pallas_call | solution.py:91
  2.7 11.2 %all-to-all-start = ((bf16[32,32,128]{2,1,0:T(8,128)(2,1)}), bf16[32,32,128]{2,1,0:T(8,128)(2,1)S(1)}, u32[]{:S(2)}, u32[]{:S(2)}) async-start(bf16[32,32,128]{2,1,0:T(8,128)(2,1)} %bitcast.1), calls=%async_computation | async-start | bytes 524288 | tf_op jit(solution)/shard_map/all_to_all | solution.py:429
  13.9 2.1 %within_early.1 = (bf16[528,256]{1,0:T(8,128)(2,1)S(1)}, bf16[528,256]{1,0:T(8,128)(2,1)S(1)}) custom-call(bf16[512,1024]{1,0:T(8,128)(2,1)} %q_hbm.3, bf16[512,1024]{1,0:T(8,128)(2,1)} %k_hbm.5, bf16[512,1024]{1,0:T(8,128)(2,1)} %v_hbm.5, f32[1,1024]{1,0:T(1,128)} %bitcast.11), custom_call_target="tpu_custom_call" | custom-call | flops 268435456 | bytes 1310720 | tf_op jit(solution)/shard_map/within_early/pallas_call | solution.py:144
  16.0 1.6 %collective-permute-start.1 = (bf16[528,256]{1,0:T(8,128)(2,1)S(1)}, bf16[528,256]{1,0:T(8,128)(2,1)S(1)}, u32[]{:S(2)}, u32[]{:S(2)}) collective-permute-start(bf16[528,256]{1,0:T(8,128)(2,1)S(1)} %get-tuple-element.30.refs_0_), channel_id=1, source_target_pairs={{0,1},{1,2},{2,3},{3,0},{4,5},{5,6},{6,7},{7,4},{8,9},{9,10},{10,1... | collective-permute-start | bytes 811016 | tf_op jit(solution)/shard_map/ppermute | solution.py:420
  17.7 1.6 %collective-permute-start.2 = (bf16[528,256]{1,0:T(8,128)(2,1)S(1)}, bf16[528,256]{1,0:T(8,128)(2,1)S(1)}, u32[]{:S(2)}, u32[]{:S(2)}) collective-permute-start(bf16[528,256]{1,0:T(8,128)(2,1)S(1)} %get-tuple-element.31.refs_1_), channel_id=1, source_target_pairs={{0,1},{1,2},{2,3},{3,0},{4,5},{5,6},{6,7},{7,4},{8,9},{9,10},{10,1... | collective-permute-start | bytes 811016 | tf_op jit(solution)/shard_map/ppermute | solution.py:420
  19.3 1.7 %collective-permute-start.3 = (bf16[528,256]{1,0:T(8,128)(2,1)S(1)}, bf16[528,256]{1,0:T(8,128)(2,1)S(1)}, u32[]{:S(2)}, u32[]{:S(2)}) collective-permute-start(bf16[528,256]{1,0:T(8,128)(2,1)S(1)} %get-tuple-element.30.refs_0_), channel_id=1, source_target_pairs={{0,3},{1,0},{2,1},{3,2},{4,7},{5,4},{6,5},{7,6},{8,11},{9,8},{10,9... | collective-permute-start | bytes 811016 | tf_op jit(solution)/shard_map/ppermute | solution.py:420
  21.4 4.7 %all-to-all-done = bf16[32,32,128]{2,1,0:T(8,128)(2,1)S(1)} async-done(((bf16[32,32,128]{2,1,0:T(8,128)(2,1)}), bf16[32,32,128]{2,1,0:T(8,128)(2,1)S(1)}, u32[]{:S(2)}, u32[]{:S(2)}) %all-to-all-start) | async-done | bytes 262176 | tf_op jit(solution)/shard_map/all_to_all | solution.py:429
  26.7 4.1 %collective-permute-done.2.refs_1_ = bf16[528,256]{1,0:T(8,128)(2,1)S(1)} collective-permute-done((bf16[528,256]{1,0:T(8,128)(2,1)S(1)}, bf16[528,256]{1,0:T(8,128)(2,1)S(1)}, u32[]{:S(2)}, u32[]{:S(2)}) %collective-permute-start.2) | collective-permute-done | bytes 270368 | tf_op jit(solution)/shard_map/ppermute | solution.py:420
  33.1 9.8 %all-to-all-start.1 = ((bf16[32,32,128]{2,1,0:T(8,128)(2,1)}), bf16[32,32,128]{2,1,0:T(8,128)(2,1)S(1)}, u32[]{:S(2)}, u32[]{:S(2)}) async-start(bf16[32,32,128]{2,1,0:T(8,128)(2,1)} %bitcast.4), calls=%async_computation.1 | async-start | bytes 524288 | tf_op jit(solution)/shard_map/all_to_all | solution.py:437
  42.8 1.4 %collective-permute-start.5 = (bf16[528,256]{1,0:T(8,128)(2,1)S(1)}, bf16[528,256]{1,0:T(8,128)(2,1)S(1)}, u32[]{:S(2)}, u32[]{:S(2)}) collective-permute-start(bf16[528,256]{1,0:T(8,128)(2,1)S(1)} %collective-permute-done.1.refs_0_), channel_id=1, source_target_pairs={{0,1},{1,2},{2,3},{3,0},{4,5},{5,6},{6,7},{7,4},{8,9},{9,10},{10,1... | collective-permute-start | bytes 811016 | tf_op jit(solution)/shard_map/ppermute | solution.py:420
  44.2 2.0 %collective-permute-start.6 = (bf16[528,256]{1,0:T(8,128)(2,1)}, bf16[528,256]{1,0:T(8,128)(2,1)S(1)}, u32[]{:S(2)}, u32[]{:S(2)}) collective-permute-start(bf16[528,256]{1,0:T(8,128)(2,1)} %collective-permute-done.4.refs_3_), channel_id=1, source_target_pairs={{0,3},{1,0},{2,1},{3,2},{4,7},{5,4},{6,5},{7,6},{8,11},{9,8},{10,9... | collective-permute-start | bytes 811016 | tf_op jit(solution)/shard_map/ppermute | solution.py:420
  46.2 3.2 %within_late.1 = (bf16[512,768]{1,0:T(8,128)(2,1)S(1)}, f32[512,768]{1,0:T(8,128)S(1)}) custom-call(bf16[512,1024]{1,0:T(8,128)(2,1)} %q_hbm.3, bf16[512,1024]{1,0:T(8,128)(2,1)} %k_hbm.5, bf16[512,1024]{1,0:T(8,128)(2,1)} %v_hbm.5), custom_call_target="tpu_custom_call" | custom-call | flops 805306368 | bytes 3932160 | tf_op jit(solution)/shard_map/within_late/pallas_call | solution.py:208
  52.0 1.6 %all-to-all-done.1 = bf16[32,32,128]{2,1,0:T(8,128)(2,1)S(1)} async-done(((bf16[32,32,128]{2,1,0:T(8,128)(2,1)}), bf16[32,32,128]{2,1,0:T(8,128)(2,1)S(1)}, u32[]{:S(2)}, u32[]{:S(2)}) %all-to-all-start.1) | async-done | bytes 262176 | tf_op jit(solution)/shard_map/all_to_all | solution.py:437
  54.1 1.4 %collective-permute-start.8 = (bf16[640,384]{1,0:T(8,128)(2,1)S(1)}, bf16[640,384]{1,0:T(8,128)(2,1)}, u32[]{:S(2)}, u32[]{:S(2)}) collective-permute-start(bf16[640,384]{1,0:T(8,128)(2,1)S(1)} %finish_heads.3.refs_2_.refs_0_), channel_id=1, source_target_pairs={{0,1},{1,2},{2,3},{3,0},{4,5},{5,6},{6,7},{7,4},{8,9},{9,10},{10,1... | collective-permute-start | bytes 1474568 | tf_op jit(solution)/shard_map/ppermute | solution.py:420
  55.5 2.0 %collective-permute-start.9 = (bf16[640,384]{1,0:T(8,128)(2,1)S(1)}, bf16[640,384]{1,0:T(8,128)(2,1)}, u32[]{:S(2)}, u32[]{:S(2)}) collective-permute-start(bf16[640,384]{1,0:T(8,128)(2,1)S(1)} %finish_heads.3.refs_2_.refs_0_), channel_id=1, source_target_pairs={{0,3},{1,0},{2,1},{3,2},{4,7},{5,4},{6,5},{7,6},{8,11},{9,8},{10,9... | collective-permute-start | bytes 1474568 | tf_op jit(solution)/shard_map/ppermute | solution.py:420
  57.9 1.9 %collective-permute-start.7 = (bf16[512,384]{1,0:T(8,128)(2,1)S(1)}, bf16[512,384]{1,0:T(8,128)(2,1)S(1)}, u32[]{:S(2)}, u32[]{:S(2)}) collective-permute-start(bf16[512,384]{1,0:T(8,128)(2,1)S(1)} %finish_heads.2.refs_1_), channel_id=1, source_target_pairs={{0,3},{1,0},{2,1},{3,2},{4,7},{5,4},{6,5},{7,6},{8,11},{9,8},{10,9... | collective-permute-start | bytes 1179656 | tf_op jit(solution)/shard_map/ppermute | solution.py:420
  62.5 2.9 %own_mix.1.refs_5_ = f32[512,1024]{1,0:T(8,128)S(1)} custom-call(s32[1]{0:T(128)} %bitcast.6.column_ref, bf16[640,384]{1,0:T(8,128)(2,1)S(1)} %finish_heads.3.refs_2_.refs_0_, bf16[512,384]{1,0:T(8,128)(2,1)S(1)} %finish_heads.2.refs_1_, bf16[512,256]{1,0:T(8,128)(2,1)S(1)} %early_heads.3.refs_2_, bf16[4096,1024]{1,0:T(8,128)(2,1)} %refs_4_.1), custom_call_target="tpu_custom_call" | custom-call | flops 1073741824 | bytes 2097152 | tf_op jit(solution)/shard_map/own_mix/pallas_call | solution.py:319
  65.4 3.6 %collective-permute-done.9.refs_5_.refs_2_ = bf16[640,384]{1,0:T(8,128)(2,1)} collective-permute-done((bf16[640,384]{1,0:T(8,128)(2,1)S(1)}, bf16[640,384]{1,0:T(8,128)(2,1)}, u32[]{:S(2)}, u32[]{:S(2)}) %collective-permute-start.9) | collective-permute-done | bytes 491552 | tf_op jit(solution)/shard_map/ppermute | solution.py:420
  69.0 1.3 %collective-permute-start.12 = (bf16[640,384]{1,0:T(8,128)(2,1)}, bf16[640,384]{1,0:T(8,128)(2,1)S(1)}, u32[]{:S(2)}, u32[]{:S(2)}) collective-permute-start(bf16[640,384]{1,0:T(8,128)(2,1)} %collective-permute-done.8.refs_4_.refs_0_), channel_id=1, source_target_pairs={{0,1},{1,2},{2,3},{3,0},{4,5},{5,6},{6,7},{7,4},{8,9},{9,10},{10,1... | collective-permute-start | bytes 1474568 | tf_op jit(solution)/shard_map/ppermute | solution.py:420
  70.3 1.7 %collective-permute-start.11 = (bf16[512,384]{1,0:T(8,128)(2,1)S(1)}, bf16[512,384]{1,0:T(8,128)(2,1)S(1)}, u32[]{:S(2)}, u32[]{:S(2)}) collective-permute-start(bf16[512,384]{1,0:T(8,128)(2,1)S(1)} %finish_heads.2.refs_1_), channel_id=1, source_target_pairs={{0,1},{1,2},{2,3},{3,0},{4,5},{5,6},{6,7},{7,4},{8,9},{9,10},{10,1... | collective-permute-start | bytes 1179656 | tf_op jit(solution)/shard_map/ppermute | solution.py:420
  72.0 2.6 %early_heads.4 = (bf16[512,256]{1,0:T(8,128)(2,1)S(1)}, bf16[512,256]{1,0:T(8,128)(2,1)S(1)}) custom-call(bf16[528,256]{1,0:T(8,128)(2,1)S(1)} %copy-done.9, bf16[528,256]{1,0:T(8,128)(2,1)S(1)} %copy-done.11, bf16[528,256]{1,0:T(8,128)(2,1)S(1)} %copy-done.13, bf16[528,256]{1,0:T(8,128)(2,1)} %collective-permute-done.4.refs_3_, ...), custom_call_target="tpu_custom_call" | custom-call | flops 134217728 | bytes 1572864 | tf_op jit(solution)/shard_map/early_heads/pallas_call | solution.py:273
  75.2 2.0 %collective-permute-start.10 = (bf16[512,384]{1,0:T(8,128)(2,1)S(1)}, bf16[512,384]{1,0:T(8,128)(2,1)S(1)}, u32[]{:S(2)}, u32[]{:S(2)}) collective-permute-start(bf16[512,384]{1,0:T(8,128)(2,1)S(1)} %collective-permute-done.7.refs_1_), channel_id=1, source_target_pairs={{0,3},{1,0},{2,1},{3,2},{4,7},{5,4},{6,5},{7,6},{8,11},{9,8},{10,9... | collective-permute-start | bytes 1179656 | tf_op jit(solution)/shard_map/ppermute | solution.py:420
  77.1 4.8 %side_mix.1 = (f32[512,1024]{1,0:T(8,128)S(1)}, bf16[3072,1024]{1,0:T(8,128)(2,1)S(1)}) custom-call(s32[1]{0:T(128)} %bitcast.6.column_ref, bf16[640,384]{1,0:T(8,128)(2,1)} %collective-permute-done.8.refs_4_.refs_0_, bf16[512,256]{1,0:T(8,128)(2,1)S(1)} %get-tuple-element.48.refs_1_, bf16[640,384]{1,0:T(8,128)(2,1)} %collective-permute-done.9.refs_5_.refs_2_, ...), custom_call_target="tpu_custom_call" | custom-call | flops 3221225472 | bytes 6291456 | tf_op jit(solution)/shard_map/side_mix/pallas_call | solution.py:369
  85.2 1.6 %mix.5 = bf16[512,1024]{1,0:T(8,128)(2,1)} custom-call(bf16[512,384]{1,0:T(8,128)(2,1)S(1)} %collective-permute-done.10.refs_0_, bf16[3072,1024]{1,0:T(8,128)(2,1)S(1)} %get-tuple-element.51.refs_2_.refs_1_, f32[512,1024]{1,0:T(8,128)S(1)} %mix.4.refs_2_), custom_call_target="tpu_custom_call" | custom-call | flops 402653184 | bytes 786432 | tf_op jit(solution)/shard_map/mix/pallas_call | solution.py:407
  (50 shorter events, 13.3 us)
Async XLA Ops:
  2.7 23.4 %all-to-all-start = ((bf16[32,32,128]{2,1,0:T(8,128)(2,1)}), bf16[32,32,128]{2,1,0:T(8,128)(2,1)S(1)}, u32[]{:S(2)}, u32[]{:S(2)}) async-start(bf16[32,32,128]{2,1,0:T(8,128)(2,1)} %bitcast.1), calls=%async_computation | async-start | bytes 524288 | tf_op jit(solution)/shard_map/all_to_all | solution.py:429
  16.0 28.2 %copy-start = (bf16[528,256]{1,0:T(8,128)(2,1)}, bf16[528,256]{1,0:T(8,128)(2,1)S(1)}, u32[]{:S(2)}) copy-start(bf16[528,256]{1,0:T(8,128)(2,1)S(1)} %get-tuple-element.30.refs_0_) | copy-start | bytes 811012
  16.0 28.2 %copy-start.2 = (bf16[528,256]{1,0:T(8,128)(2,1)}, bf16[528,256]{1,0:T(8,128)(2,1)S(1)}, u32[]{:S(2)}) copy-start(bf16[528,256]{1,0:T(8,128)(2,1)S(1)} %get-tuple-element.31.refs_1_) | copy-start | bytes 811012
  16.0 10.7 %collective-permute-start.1 = (bf16[528,256]{1,0:T(8,128)(2,1)S(1)}, bf16[528,256]{1,0:T(8,128)(2,1)S(1)}, u32[]{:S(2)}, u32[]{:S(2)}) collective-permute-start(bf16[528,256]{1,0:T(8,128)(2,1)S(1)} %get-tuple-element.30.refs_0_), channel_id=1, source_target_pairs={{0,1},{1,2},{2,3},{3,0},{4,5},{5,6},{6,7},{7,4},{8,9},{9,10},{10,1... | collective-permute-start | bytes 811016 | tf_op jit(solution)/shard_map/ppermute | solution.py:420
  17.7 13.2 %collective-permute-start.2 = (bf16[528,256]{1,0:T(8,128)(2,1)S(1)}, bf16[528,256]{1,0:T(8,128)(2,1)S(1)}, u32[]{:S(2)}, u32[]{:S(2)}) collective-permute-start(bf16[528,256]{1,0:T(8,128)(2,1)S(1)} %get-tuple-element.31.refs_1_), channel_id=1, source_target_pairs={{0,1},{1,2},{2,3},{3,0},{4,5},{5,6},{6,7},{7,4},{8,9},{9,10},{10,1... | collective-permute-start | bytes 811016 | tf_op jit(solution)/shard_map/ppermute | solution.py:420
  19.3 11.6 %collective-permute-start.3 = (bf16[528,256]{1,0:T(8,128)(2,1)S(1)}, bf16[528,256]{1,0:T(8,128)(2,1)S(1)}, u32[]{:S(2)}, u32[]{:S(2)}) collective-permute-start(bf16[528,256]{1,0:T(8,128)(2,1)S(1)} %get-tuple-element.30.refs_0_), channel_id=1, source_target_pairs={{0,3},{1,0},{2,1},{3,2},{4,7},{5,4},{6,5},{7,6},{8,11},{9,8},{10,9... | collective-permute-start | bytes 811016 | tf_op jit(solution)/shard_map/ppermute | solution.py:420
  20.9 11.4 %collective-permute-start.4 = (bf16[528,256]{1,0:T(8,128)(2,1)S(1)}, bf16[528,256]{1,0:T(8,128)(2,1)}, u32[]{:S(2)}, u32[]{:S(2)}) collective-permute-start(bf16[528,256]{1,0:T(8,128)(2,1)S(1)} %get-tuple-element.31.refs_1_), channel_id=1, source_target_pairs={{0,3},{1,0},{2,1},{3,2},{4,7},{5,4},{6,5},{7,6},{8,11},{9,8},{10,9... | collective-permute-start | bytes 811016 | tf_op jit(solution)/shard_map/ppermute | solution.py:420
  26.1 6.2 %collective-permute-start = (bf16[1024,128]{1,0:T(8,128)(2,1)S(1)}, bf16[1024,128]{1,0:T(8,128)(2,1)S(1)}, u32[]{:S(2)}, u32[]{:S(2)}) collective-permute-start(bf16[1024,128]{1,0:T(8,128)(2,1)S(1)} %bitcast.9), channel_id=1, source_target_pairs={{0,4},{4,0},{1,5},{5,1},{2,6},{6,2},{3,7},{7,3},{8,12},{12,8},{9,1... | collective-permute-start | bytes 786440 | tf_op jit(solution)/shard_map/ppermute | solution.py:433
  26.7 22.7 %copy-start.8 = (bf16[528,256]{1,0:T(8,128)(2,1)}, bf16[528,256]{1,0:T(8,128)(2,1)S(1)}, u32[]{:S(2)}) copy-start(bf16[528,256]{1,0:T(8,128)(2,1)S(1)} %collective-permute-done.1.refs_0_) | copy-start | bytes 811012
  30.8 13.4 %copy-start.10 = (bf16[528,256]{1,0:T(8,128)(2,1)}, bf16[528,256]{1,0:T(8,128)(2,1)S(1)}, u32[]{:S(2)}) copy-start(bf16[528,256]{1,0:T(8,128)(2,1)S(1)} %collective-permute-done.2.refs_1_) | copy-start | bytes 811012
  32.3 21.4 %copy-start.14 = (f32[1024]{0:T(1024)S(1)}, f32[1024]{0:T(1024)}, u32[]{:S(2)}) copy-start(f32[1024]{0:T(1024)} %param.8) | copy-start | bytes 12292
  33.1 20.6 %all-to-all-start.1 = ((bf16[32,32,128]{2,1,0:T(8,128)(2,1)}), bf16[32,32,128]{2,1,0:T(8,128)(2,1)S(1)}, u32[]{:S(2)}, u32[]{:S(2)}) async-start(bf16[32,32,128]{2,1,0:T(8,128)(2,1)} %bitcast.4), calls=%async_computation.1 | async-start | bytes 524288 | tf_op jit(solution)/shard_map/all_to_all | solution.py:437
  42.8 7.7 %collective-permute-start.5 = (bf16[528,256]{1,0:T(8,128)(2,1)S(1)}, bf16[528,256]{1,0:T(8,128)(2,1)S(1)}, u32[]{:S(2)}, u32[]{:S(2)}) collective-permute-start(bf16[528,256]{1,0:T(8,128)(2,1)S(1)} %collective-permute-done.1.refs_0_), channel_id=1, source_target_pairs={{0,1},{1,2},{2,3},{3,0},{4,5},{5,6},{6,7},{7,4},{8,9},{9,10},{10,1... | collective-permute-start | bytes 811016 | tf_op jit(solution)/shard_map/ppermute | solution.py:420
  44.2 7.1 %collective-permute-start.6 = (bf16[528,256]{1,0:T(8,128)(2,1)}, bf16[528,256]{1,0:T(8,128)(2,1)S(1)}, u32[]{:S(2)}, u32[]{:S(2)}) collective-permute-start(bf16[528,256]{1,0:T(8,128)(2,1)} %collective-permute-done.4.refs_3_), channel_id=1, source_target_pairs={{0,3},{1,0},{2,1},{3,2},{4,7},{5,4},{6,5},{7,6},{8,11},{9,8},{10,9... | collective-permute-start | bytes 811016 | tf_op jit(solution)/shard_map/ppermute | solution.py:420
  54.1 11.2 %collective-permute-start.8 = (bf16[640,384]{1,0:T(8,128)(2,1)S(1)}, bf16[640,384]{1,0:T(8,128)(2,1)}, u32[]{:S(2)}, u32[]{:S(2)}) collective-permute-start(bf16[640,384]{1,0:T(8,128)(2,1)S(1)} %finish_heads.3.refs_2_.refs_0_), channel_id=1, source_target_pairs={{0,1},{1,2},{2,3},{3,0},{4,5},{5,6},{6,7},{7,4},{8,9},{9,10},{10,1... | collective-permute-start | bytes 1474568 | tf_op jit(solution)/shard_map/ppermute | solution.py:420
  55.5 13.5 %collective-permute-start.9 = (bf16[640,384]{1,0:T(8,128)(2,1)S(1)}, bf16[640,384]{1,0:T(8,128)(2,1)}, u32[]{:S(2)}, u32[]{:S(2)}) collective-permute-start(bf16[640,384]{1,0:T(8,128)(2,1)S(1)} %finish_heads.3.refs_2_.refs_0_), channel_id=1, source_target_pairs={{0,3},{1,0},{2,1},{3,2},{4,7},{5,4},{6,5},{7,6},{8,11},{9,8},{10,9... | collective-permute-start | bytes 1474568 | tf_op jit(solution)/shard_map/ppermute | solution.py:420
  57.9 17.3 %collective-permute-start.7 = (bf16[512,384]{1,0:T(8,128)(2,1)S(1)}, bf16[512,384]{1,0:T(8,128)(2,1)S(1)}, u32[]{:S(2)}, u32[]{:S(2)}) collective-permute-start(bf16[512,384]{1,0:T(8,128)(2,1)S(1)} %finish_heads.2.refs_1_), channel_id=1, source_target_pairs={{0,3},{1,0},{2,1},{3,2},{4,7},{5,4},{6,5},{7,6},{8,11},{9,8},{10,9... | collective-permute-start | bytes 1179656 | tf_op jit(solution)/shard_map/ppermute | solution.py:420
  62.5 9.5 %copy-start.9 = (bf16[528,256]{1,0:T(8,128)(2,1)S(1)}, bf16[528,256]{1,0:T(8,128)(2,1)}, u32[]{:S(2)}) copy-start(bf16[528,256]{1,0:T(8,128)(2,1)} %copy-done.8) | copy-start | bytes 811012
  62.5 9.5 %copy-start.11 = (bf16[528,256]{1,0:T(8,128)(2,1)S(1)}, bf16[528,256]{1,0:T(8,128)(2,1)}, u32[]{:S(2)}) copy-start(bf16[528,256]{1,0:T(8,128)(2,1)} %copy-done.10) | copy-start | bytes 811012
  62.5 9.5 %copy-start.13 = (bf16[528,256]{1,0:T(8,128)(2,1)S(1)}, bf16[528,256]{1,0:T(8,128)(2,1)}, u32[]{:S(2)}) copy-start(bf16[528,256]{1,0:T(8,128)(2,1)} %copy-done.12) | copy-start | bytes 811012
  69.0 12.9 %collective-permute-start.12 = (bf16[640,384]{1,0:T(8,128)(2,1)}, bf16[640,384]{1,0:T(8,128)(2,1)S(1)}, u32[]{:S(2)}, u32[]{:S(2)}) collective-permute-start(bf16[640,384]{1,0:T(8,128)(2,1)} %collective-permute-done.8.refs_4_.refs_0_), channel_id=1, source_target_pairs={{0,1},{1,2},{2,3},{3,0},{4,5},{5,6},{6,7},{7,4},{8,9},{9,10},{10,1... | collective-permute-start | bytes 1474568 | tf_op jit(solution)/shard_map/ppermute | solution.py:420
  70.3 13.7 %collective-permute-start.11 = (bf16[512,384]{1,0:T(8,128)(2,1)S(1)}, bf16[512,384]{1,0:T(8,128)(2,1)S(1)}, u32[]{:S(2)}, u32[]{:S(2)}) collective-permute-start(bf16[512,384]{1,0:T(8,128)(2,1)S(1)} %finish_heads.2.refs_1_), channel_id=1, source_target_pairs={{0,1},{1,2},{2,3},{3,0},{4,5},{5,6},{6,7},{7,4},{8,9},{9,10},{10,1... | collective-permute-start | bytes 1179656 | tf_op jit(solution)/shard_map/ppermute | solution.py:420
  75.2 6.8 %copy-start.7 = (bf16[528,256]{1,0:T(8,128)(2,1)S(1)}, bf16[528,256]{1,0:T(8,128)(2,1)}, u32[]{:S(2)}) copy-start(bf16[528,256]{1,0:T(8,128)(2,1)} %copy-done.6) | copy-start | bytes 811012
  75.2 10.0 %collective-permute-start.10 = (bf16[512,384]{1,0:T(8,128)(2,1)S(1)}, bf16[512,384]{1,0:T(8,128)(2,1)S(1)}, u32[]{:S(2)}, u32[]{:S(2)}) collective-permute-start(bf16[512,384]{1,0:T(8,128)(2,1)S(1)} %collective-permute-done.7.refs_1_), channel_id=1, source_target_pairs={{0,3},{1,0},{2,1},{3,2},{4,7},{5,4},{6,5},{7,6},{8,11},{9,8},{10,9... | collective-permute-start | bytes 1179656 | tf_op jit(solution)/shard_map/ppermute | solution.py:420
  (6 other events, 10.8 us)

commit v10 on v9

--- a/solution.py
+++ b/solution.py
@@ -430,8 +430,9 @@
     early = within_early(q, k, v, gain_row)
     left_q = [along(value, 1, ways) for value in early]
     right_q = [along(value, -1, ways) for value in early]
+    own, *early = lax.optimization_barrier((own, *early))
     other = lax.ppermute(own, "core", [(0, 1), (1, 0)])
-    own, other, left_q, right_q = lax.optimization_barrier((own, other, left_q, right_q))
+    left_q, right_q = lax.optimization_barrier((left_q, right_q))
     far_q = [along(left_q[0], 1, ways), along(right_q[1], -1, ways)]
     sums = exclusive_sums(core, own, other, chips)
     carried = lax.all_to_all(sums, "chip", 0, 0, tiled=True)

time: 87.4 us -> 92.7 us (1.061)
  waiting for transfers between devices: 17.4 us -> 25.7 us
  starting transfers between devices: 39.9 us -> 36.1 us
    all_to_all x1, waiting for transfers between devices: 4.71 us -> 10.1 us  [shards(): own = lax.all_to_all(states, 'chip', 0, 0, tiled=True)]
    all_to_all x1, starting transfers between devices: 9.76 us -> 4.62 us  [shards(): carried = lax.all_to_all(sums, 'chip', 0, 0, tiled=True)]
    ppermute x12, waiting for transfers between devices: 11 us -> 15.7 us  [along(): lax.ppermute(value, 'fsdp', [(i, (i + shift) % count) for i in range(coun...]
    all_to_all x1, waiting for transfers between devices: 1.64 us -> 0.01 us  [shards(): carried = lax.all_to_all(sums, 'chip', 0, 0, tiled=True)]
    ppermute x12, starting transfers between devices: 18.9 us -> 20.2 us  [along(): lax.ppermute(value, 'fsdp', [(i, (i + shift) % count) for i in range(coun...]
  transfers between devices with their start and end apart: 15 -> 15, of which waited for: 9 -> 8; matrix products, arithmetic and copies ran while one was open for 0% -> 0% of each run, Pallas kernels for 23% -> 22%
where the time goes in v10:
time: 92.7 us; the launch traced here: 92.2 us
  starting transfers between devices  36.1 us (39%)
  waiting for transfers between devices  25.7 us (28%)
  Pallas kernels  25.2 us (27%)
  local copies, waits for them, and re-layouts  4.8 us (5%)
    ppermute x12, starting transfers between devices, along(): lax.ppermute(value, 'fsdp', [(i, (i + shift) % count) for i in range(coun...  20.2 us
    ppermute x12, waiting for transfers between devices, along(): lax.ppermute(value, 'fsdp', [(i, (i + shift) % count) for i in range(coun...  15.7 us
    all_to_all x1, starting transfers between devices, shards(): own = lax.all_to_all(states, 'chip', 0, 0, tiled=True)  11.2 us
    all_to_all x1, waiting for transfers between devices, shards(): own = lax.all_to_all(states, 'chip', 0, 0, tiled=True)  10.1 us
    unnamed x30, local copies, waits for them, and re-layouts  4.8 us
    pallas_call x1, Pallas kernels, side_mix(): pl.pallas_call(functools.partial(side_kernel, starts=starts), name='side_...  4.79 us
    all_to_all x1, starting transfers between devices, shards(): carried = lax.all_to_all(sums, 'chip', 0, 0, tiled=True)  4.62 us
    pallas_call x3, Pallas kernels, early_heads(): pl.pallas_call(functools.partial(early_kernel, count=count), name='early_...  4.09 us
  transfers between devices with their start and end apart: 15, of which 8 were waited for; matrix products, arithmetic and copies ran while one was open for 0% of the time, Pallas kernels for 22%

profile of v10, /device:TPU:32, one launch (start us, length us, event | category | flops | bytes accessed | tf_op | source)
XLA Modules:
  0.0 92.2 jit_solution(17879497899522194382)
XLA Ops:
  0.0 2.7 %block_states.1 = bf16[1024,128]{1,0:T(8,128)(2,1)} custom-call(bf16[512,1024]{1,0:T(8,128)(2,1)} %k_hbm.5, bf16[512,1024]{1,0:T(8,128)(2,1)} %v_hbm.5), custom_call_target="tpu_custom_call" | custom-call | flops 134217728 | bytes 2097152 | tf_op jit(solution)/shard_map/block_states/pallas_call | solution.py:91
  2.7 11.2 %all-to-all-start = ((bf16[32,32,128]{2,1,0:T(8,128)(2,1)}), bf16[32,32,128]{2,1,0:T(8,128)(2,1)S(1)}, u32[]{:S(2)}, u32[]{:S(2)}) async-start(bf16[32,32,128]{2,1,0:T(8,128)(2,1)} %bitcast.1), calls=%async_computation | async-start | bytes 524288 | tf_op jit(solution)/shard_map/all_to_all | solution.py:429
  13.9 2.1 %within_early.1 = (bf16[528,256]{1,0:T(8,128)(2,1)S(1)}, bf16[528,256]{1,0:T(8,128)(2,1)S(1)}) custom-call(bf16[512,1024]{1,0:T(8,128)(2,1)} %q_hbm.3, bf16[512,1024]{1,0:T(8,128)(2,1)} %k_hbm.5, bf16[512,1024]{1,0:T(8,128)(2,1)} %v_hbm.5, f32[1,1024]{1,0:T(1,128)} %bitcast.11), custom_call_target="tpu_custom_call" | custom-call | flops 268435456 | bytes 1310720 | tf_op jit(solution)/shard_map/within_early/pallas_call | solution.py:144
  16.0 10.1 %all-to-all-done = bf16[32,32,128]{2,1,0:T(8,128)(2,1)S(1)} async-done(((bf16[32,32,128]{2,1,0:T(8,128)(2,1)}), bf16[32,32,128]{2,1,0:T(8,128)(2,1)S(1)}, u32[]{:S(2)}, u32[]{:S(2)}) %all-to-all-start) | async-done | bytes 262176 | tf_op jit(solution)/shard_map/all_to_all | solution.py:429
  26.1 1.6 %collective-permute-start.1 = (bf16[528,256]{1,0:T(8,128)(2,1)S(1)}, bf16[528,256]{1,0:T(8,128)(2,1)S(1)}, u32[]{:S(2)}, u32[]{:S(2)}) collective-permute-start(bf16[528,256]{1,0:T(8,128)(2,1)S(1)} %get-tuple-element.43.refs_0_), channel_id=1, source_target_pairs={{0,1},{1,2},{2,3},{3,0},{4,5},{5,6},{6,7},{7,4},{8,9},{9,10},{10,1... | collective-permute-start | bytes 811016 | tf_op jit(solution)/shard_map/ppermute | solution.py:420
  27.7 1.6 %collective-permute-start.2 = (bf16[528,256]{1,0:T(8,128)(2,1)S(1)}, bf16[528,256]{1,0:T(8,128)(2,1)S(1)}, u32[]{:S(2)}, u32[]{:S(2)}) collective-permute-start(bf16[528,256]{1,0:T(8,128)(2,1)S(1)} %get-tuple-element.44.refs_1_), channel_id=1, source_target_pairs={{0,1},{1,2},{2,3},{3,0},{4,5},{5,6},{6,7},{7,4},{8,9},{9,10},{10,1... | collective-permute-start | bytes 811016 | tf_op jit(solution)/shard_map/ppermute | solution.py:420
  29.2 1.7 %collective-permute-start.3 = (bf16[528,256]{1,0:T(8,128)(2,1)S(1)}, bf16[528,256]{1,0:T(8,128)(2,1)S(1)}, u32[]{:S(2)}, u32[]{:S(2)}) collective-permute-start(bf16[528,256]{1,0:T(8,128)(2,1)S(1)} %get-tuple-element.43.refs_0_), channel_id=1, source_target_pairs={{0,3},{1,0},{2,1},{3,2},{4,7},{5,4},{6,5},{7,6},{8,11},{9,8},{10,9... | collective-permute-start | bytes 811016 | tf_op jit(solution)/shard_map/ppermute | solution.py:420
  32.2 4.6 %all-to-all-start.1 = ((bf16[32,32,128]{2,1,0:T(8,128)(2,1)}), bf16[32,32,128]{2,1,0:T(8,128)(2,1)S(1)}, u32[]{:S(2)}, u32[]{:S(2)}) async-start(bf16[32,32,128]{2,1,0:T(8,128)(2,1)} %bitcast.4), calls=%async_computation.1 | async-start | bytes 524288 | tf_op jit(solution)/shard_map/all_to_all | solution.py:438
  36.8 5.2 %collective-permute-done.2.refs_1_ = bf16[528,256]{1,0:T(8,128)(2,1)S(1)} collective-permute-done((bf16[528,256]{1,0:T(8,128)(2,1)S(1)}, bf16[528,256]{1,0:T(8,128)(2,1)S(1)}, u32[]{:S(2)}, u32[]{:S(2)}) %collective-permute-start.2) | collective-permute-done | bytes 270368 | tf_op jit(solution)/shard_map/ppermute | solution.py:420
  43.5 1.3 %collective-permute-start.5 = (bf16[528,256]{1,0:T(8,128)(2,1)S(1)}, bf16[528,256]{1,0:T(8,128)(2,1)S(1)}, u32[]{:S(2)}, u32[]{:S(2)}) collective-permute-start(bf16[528,256]{1,0:T(8,128)(2,1)S(1)} %collective-permute-done.1.refs_0_), channel_id=1, source_target_pairs={{0,1},{1,2},{2,3},{3,0},{4,5},{5,6},{6,7},{7,4},{8,9},{9,10},{10,1... | collective-permute-start | bytes 811016 | tf_op jit(solution)/shard_map/ppermute | solution.py:420
  44.8 2.0 %collective-permute-start.6 = (bf16[528,256]{1,0:T(8,128)(2,1)}, bf16[528,256]{1,0:T(8,128)(2,1)S(1)}, u32[]{:S(2)}, u32[]{:S(2)}) collective-permute-start(bf16[528,256]{1,0:T(8,128)(2,1)} %collective-permute-done.4.refs_3_), channel_id=1, source_target_pairs={{0,3},{1,0},{2,1},{3,2},{4,7},{5,4},{6,5},{7,6},{8,11},{9,8},{10,9... | collective-permute-start | bytes 811016 | tf_op jit(solution)/shard_map/ppermute | solution.py:420
  46.7 3.2 %within_late.1 = (bf16[512,768]{1,0:T(8,128)(2,1)S(1)}, f32[512,768]{1,0:T(8,128)S(1)}) custom-call(bf16[512,1024]{1,0:T(8,128)(2,1)} %q_hbm.3, bf16[512,1024]{1,0:T(8,128)(2,1)} %k_hbm.5, bf16[512,1024]{1,0:T(8,128)(2,1)} %v_hbm.5), custom_call_target="tpu_custom_call" | custom-call | flops 805306368 | bytes 3932160 | tf_op jit(solution)/shard_map/within_late/pallas_call | solution.py:208
  49.9 3.0 %collective-permute-done.5.refs_0_ = bf16[528,256]{1,0:T(8,128)(2,1)S(1)} collective-permute-done((bf16[528,256]{1,0:T(8,128)(2,1)S(1)}, bf16[528,256]{1,0:T(8,128)(2,1)S(1)}, u32[]{:S(2)}, u32[]{:S(2)}) %collective-permute-start.5) | collective-permute-done | bytes 270368 | tf_op jit(solution)/shard_map/ppermute | solution.py:420
  54.9 3.2 %collective-permute-start.9 = (bf16[640,384]{1,0:T(8,128)(2,1)S(1)}, bf16[640,384]{1,0:T(8,128)(2,1)}, u32[]{:S(2)}, u32[]{:S(2)}) collective-permute-start(bf16[640,384]{1,0:T(8,128)(2,1)S(1)} %finish_heads.3.refs_2_.refs_0_), channel_id=1, source_target_pairs={{0,3},{1,0},{2,1},{3,2},{4,7},{5,4},{6,5},{7,6},{8,11},{9,8},{10,9... | collective-permute-start | bytes 1474568 | tf_op jit(solution)/shard_map/ppermute | solution.py:420
  58.6 1.5 %collective-permute-start.7 = (bf16[512,384]{1,0:T(8,128)(2,1)S(1)}, bf16[512,384]{1,0:T(8,128)(2,1)S(1)}, u32[]{:S(2)}, u32[]{:S(2)}) collective-permute-start(bf16[512,384]{1,0:T(8,128)(2,1)S(1)} %finish_heads.2.refs_1_), channel_id=1, source_target_pairs={{0,3},{1,0},{2,1},{3,2},{4,7},{5,4},{6,5},{7,6},{8,11},{9,8},{10,9... | collective-permute-start | bytes 1179656 | tf_op jit(solution)/shard_map/ppermute | solution.py:420
  62.8 2.9 %own_mix.1.refs_5_ = f32[512,1024]{1,0:T(8,128)S(1)} custom-call(s32[1]{0:T(128)} %bitcast.6.column_ref, bf16[640,384]{1,0:T(8,128)(2,1)S(1)} %finish_heads.3.refs_2_.refs_0_, bf16[512,384]{1,0:T(8,128)(2,1)S(1)} %finish_heads.2.refs_1_, bf16[512,256]{1,0:T(8,128)(2,1)S(1)} %early_heads.3.refs_2_, bf16[4096,1024]{1,0:T(8,128)(2,1)} %refs_4_.1), custom_call_target="tpu_custom_call" | custom-call | flops 1073741824 | bytes 2097152 | tf_op jit(solution)/shard_map/own_mix/pallas_call | solution.py:319
  65.6 2.6 %collective-permute-done.8.refs_4_.refs_0_ = bf16[640,384]{1,0:T(8,128)(2,1)} collective-permute-done((bf16[640,384]{1,0:T(8,128)(2,1)S(1)}, bf16[640,384]{1,0:T(8,128)(2,1)}, u32[]{:S(2)}, u32[]{:S(2)}) %collective-permute-start.8) | collective-permute-done | bytes 491552 | tf_op jit(solution)/shard_map/ppermute | solution.py:420
  68.2 1.6 %collective-permute-done.9.refs_5_.refs_2_ = bf16[640,384]{1,0:T(8,128)(2,1)} collective-permute-done((bf16[640,384]{1,0:T(8,128)(2,1)S(1)}, bf16[640,384]{1,0:T(8,128)(2,1)}, u32[]{:S(2)}, u32[]{:S(2)}) %collective-permute-start.9) | collective-permute-done | bytes 491552 | tf_op jit(solution)/shard_map/ppermute | solution.py:420
  71.0 2.0 %collective-permute-start.11 = (bf16[512,384]{1,0:T(8,128)(2,1)S(1)}, bf16[512,384]{1,0:T(8,128)(2,1)S(1)}, u32[]{:S(2)}, u32[]{:S(2)}) collective-permute-start(bf16[512,384]{1,0:T(8,128)(2,1)S(1)} %finish_heads.2.refs_1_), channel_id=1, source_target_pairs={{0,1},{1,2},{2,3},{3,0},{4,5},{5,6},{6,7},{7,4},{8,9},{9,10},{10,1... | collective-permute-start | bytes 1179656 | tf_op jit(solution)/shard_map/ppermute | solution.py:420
  73.0 2.6 %early_heads.4 = (bf16[512,256]{1,0:T(8,128)(2,1)S(1)}, bf16[512,256]{1,0:T(8,128)(2,1)S(1)}) custom-call(bf16[528,256]{1,0:T(8,128)(2,1)S(1)} %copy-done.9, bf16[528,256]{1,0:T(8,128)(2,1)S(1)} %copy-done.11, bf16[528,256]{1,0:T(8,128)(2,1)S(1)} %copy-done.13, bf16[528,256]{1,0:T(8,128)(2,1)} %collective-permute-done.4.refs_3_, ...), custom_call_target="tpu_custom_call" | custom-call | flops 134217728 | bytes 1572864 | tf_op jit(solution)/shard_map/early_heads/pallas_call | solution.py:273
  75.8 3.7 %collective-permute-start.10 = (bf16[512,384]{1,0:T(8,128)(2,1)S(1)}, bf16[512,384]{1,0:T(8,128)(2,1)S(1)}, u32[]{:S(2)}, u32[]{:S(2)}) collective-permute-start(bf16[512,384]{1,0:T(8,128)(2,1)S(1)} %collective-permute-done.7.refs_1_), channel_id=1, source_target_pairs={{0,3},{1,0},{2,1},{3,2},{4,7},{5,4},{6,5},{7,6},{8,11},{9,8},{10,9... | collective-permute-start | bytes 1179656 | tf_op jit(solution)/shard_map/ppermute | solution.py:420
  79.5 4.8 %side_mix.1 = (f32[512,1024]{1,0:T(8,128)S(1)}, bf16[3072,1024]{1,0:T(8,128)(2,1)S(1)}) custom-call(s32[1]{0:T(128)} %bitcast.6.column_ref, bf16[640,384]{1,0:T(8,128)(2,1)} %collective-permute-done.8.refs_4_.refs_0_, bf16[512,256]{1,0:T(8,128)(2,1)S(1)} %get-tuple-element.50.refs_1_, bf16[640,384]{1,0:T(8,128)(2,1)} %collective-permute-done.9.refs_5_.refs_2_, ...), custom_call_target="tpu_custom_call" | custom-call | flops 3221225472 | bytes 6291456 | tf_op jit(solution)/shard_map/side_mix/pallas_call | solution.py:369
  86.7 2.5 %collective-permute-done.11.refs_0_ = bf16[512,384]{1,0:T(8,128)(2,1)S(1)} collective-permute-done((bf16[512,384]{1,0:T(8,128)(2,1)S(1)}, bf16[512,384]{1,0:T(8,128)(2,1)S(1)}, u32[]{:S(2)}, u32[]{:S(2)}) %collective-permute-start.11) | collective-permute-done | bytes 393248 | tf_op jit(solution)/shard_map/ppermute | solution.py:420
  90.5 1.6 %mix.5 = bf16[512,1024]{1,0:T(8,128)(2,1)} custom-call(bf16[512,384]{1,0:T(8,128)(2,1)S(1)} %collective-permute-done.10.refs_0_, bf16[3072,1024]{1,0:T(8,128)(2,1)S(1)} %get-tuple-element.53.refs_2_.refs_1_, f32[512,1024]{1,0:T(8,128)S(1)} %mix.4.refs_2_), custom_call_target="tpu_custom_call" | custom-call | flops 402653184 | bytes 786432 | tf_op jit(solution)/shard_map/mix/pallas_call | solution.py:407
  (50 shorter events, 12.8 us)
Async XLA Ops:
  2.7 23.4 %all-to-all-start = ((bf16[32,32,128]{2,1,0:T(8,128)(2,1)}), bf16[32,32,128]{2,1,0:T(8,128)(2,1)S(1)}, u32[]{:S(2)}, u32[]{:S(2)}) async-start(bf16[32,32,128]{2,1,0:T(8,128)(2,1)} %bitcast.1), calls=%async_computation | async-start | bytes 524288 | tf_op jit(solution)/shard_map/all_to_all | solution.py:429
  16.0 28.7 %copy-start = (bf16[528,256]{1,0:T(8,128)(2,1)}, bf16[528,256]{1,0:T(8,128)(2,1)S(1)}, u32[]{:S(2)}) copy-start(bf16[528,256]{1,0:T(8,128)(2,1)S(1)} %get-tuple-element.43.refs_0_) | copy-start | bytes 811012
  16.0 28.7 %copy-start.2 = (bf16[528,256]{1,0:T(8,128)(2,1)}, bf16[528,256]{1,0:T(8,128)(2,1)S(1)}, u32[]{:S(2)}) copy-start(bf16[528,256]{1,0:T(8,128)(2,1)S(1)} %get-tuple-element.44.refs_1_) | copy-start | bytes 811012
  26.1 5.3 %collective-permute-start = (bf16[1024,128]{1,0:T(8,128)(2,1)S(1)}, bf16[1024,128]{1,0:T(8,128)(2,1)S(1)}, u32[]{:S(2)}, u32[]{:S(2)}) collective-permute-start(bf16[1024,128]{1,0:T(8,128)(2,1)S(1)} %bitcast.9), channel_id=1, source_target_pairs={{0,4},{4,0},{1,5},{5,1},{2,6},{6,2},{3,7},{7,3},{8,12},{12,8},{9,1... | collective-permute-start | bytes 786440 | tf_op jit(solution)/shard_map/ppermute | solution.py:434
  26.1 10.7 %collective-permute-start.1 = (bf16[528,256]{1,0:T(8,128)(2,1)S(1)}, bf16[528,256]{1,0:T(8,128)(2,1)S(1)}, u32[]{:S(2)}, u32[]{:S(2)}) collective-permute-start(bf16[528,256]{1,0:T(8,128)(2,1)S(1)} %get-tuple-element.43.refs_0_), channel_id=1, source_target_pairs={{0,1},{1,2},{2,3},{3,0},{4,5},{5,6},{6,7},{7,4},{8,9},{9,10},{10,1... | collective-permute-start | bytes 811016 | tf_op jit(solution)/shard_map/ppermute | solution.py:420
  27.7 14.4 %collective-permute-start.2 = (bf16[528,256]{1,0:T(8,128)(2,1)S(1)}, bf16[528,256]{1,0:T(8,128)(2,1)S(1)}, u32[]{:S(2)}, u32[]{:S(2)}) collective-permute-start(bf16[528,256]{1,0:T(8,128)(2,1)S(1)} %get-tuple-element.44.refs_1_), channel_id=1, source_target_pairs={{0,1},{1,2},{2,3},{3,0},{4,5},{5,6},{6,7},{7,4},{8,9},{9,10},{10,1... | collective-permute-start | bytes 811016 | tf_op jit(solution)/shard_map/ppermute | solution.py:420
  29.2 13.5 %collective-permute-start.3 = (bf16[528,256]{1,0:T(8,128)(2,1)S(1)}, bf16[528,256]{1,0:T(8,128)(2,1)S(1)}, u32[]{:S(2)}, u32[]{:S(2)}) collective-permute-start(bf16[528,256]{1,0:T(8,128)(2,1)S(1)} %get-tuple-element.43.refs_0_), channel_id=1, source_target_pairs={{0,3},{1,0},{2,1},{3,2},{4,7},{5,4},{6,5},{7,6},{8,11},{9,8},{10,9... | collective-permute-start | bytes 811016 | tf_op jit(solution)/shard_map/ppermute | solution.py:420
  30.9 12.6 %collective-permute-start.4 = (bf16[528,256]{1,0:T(8,128)(2,1)S(1)}, bf16[528,256]{1,0:T(8,128)(2,1)}, u32[]{:S(2)}, u32[]{:S(2)}) collective-permute-start(bf16[528,256]{1,0:T(8,128)(2,1)S(1)} %get-tuple-element.44.refs_1_), channel_id=1, source_target_pairs={{0,3},{1,0},{2,1},{3,2},{4,7},{5,4},{6,5},{7,6},{8,11},{9,8},{10,9... | collective-permute-start | bytes 811016 | tf_op jit(solution)/shard_map/ppermute | solution.py:420
  31.4 23.0 %copy-start.14 = (f32[1024]{0:T(1024)S(1)}, f32[1024]{0:T(1024)}, u32[]{:S(2)}) copy-start(f32[1024]{0:T(1024)} %param.8) | copy-start | bytes 12292
  32.2 22.2 %all-to-all-start.1 = ((bf16[32,32,128]{2,1,0:T(8,128)(2,1)}), bf16[32,32,128]{2,1,0:T(8,128)(2,1)S(1)}, u32[]{:S(2)}, u32[]{:S(2)}) async-start(bf16[32,32,128]{2,1,0:T(8,128)(2,1)} %bitcast.4), calls=%async_computation.1 | async-start | bytes 524288 | tf_op jit(solution)/shard_map/all_to_all | solution.py:438
  36.8 18.0 %copy-start.8 = (bf16[528,256]{1,0:T(8,128)(2,1)}, bf16[528,256]{1,0:T(8,128)(2,1)S(1)}, u32[]{:S(2)}) copy-start(bf16[528,256]{1,0:T(8,128)(2,1)S(1)} %collective-permute-done.1.refs_0_) | copy-start | bytes 811012
  43.5 9.4 %collective-permute-start.5 = (bf16[528,256]{1,0:T(8,128)(2,1)S(1)}, bf16[528,256]{1,0:T(8,128)(2,1)S(1)}, u32[]{:S(2)}, u32[]{:S(2)}) collective-permute-start(bf16[528,256]{1,0:T(8,128)(2,1)S(1)} %collective-permute-done.1.refs_0_), channel_id=1, source_target_pairs={{0,1},{1,2},{2,3},{3,0},{4,5},{5,6},{6,7},{7,4},{8,9},{9,10},{10,1... | collective-permute-start | bytes 811016 | tf_op jit(solution)/shard_map/ppermute | solution.py:420
  44.8 8.8 %collective-permute-start.6 = (bf16[528,256]{1,0:T(8,128)(2,1)}, bf16[528,256]{1,0:T(8,128)(2,1)S(1)}, u32[]{:S(2)}, u32[]{:S(2)}) collective-permute-start(bf16[528,256]{1,0:T(8,128)(2,1)} %collective-permute-done.4.refs_3_), channel_id=1, source_target_pairs={{0,3},{1,0},{2,1},{3,2},{4,7},{5,4},{6,5},{7,6},{8,11},{9,8},{10,9... | collective-permute-start | bytes 811016 | tf_op jit(solution)/shard_map/ppermute | solution.py:420
  54.8 13.4 %collective-permute-start.8 = (bf16[640,384]{1,0:T(8,128)(2,1)S(1)}, bf16[640,384]{1,0:T(8,128)(2,1)}, u32[]{:S(2)}, u32[]{:S(2)}) collective-permute-start(bf16[640,384]{1,0:T(8,128)(2,1)S(1)} %finish_heads.3.refs_2_.refs_0_), channel_id=1, source_target_pairs={{0,1},{1,2},{2,3},{3,0},{4,5},{5,6},{6,7},{7,4},{8,9},{9,10},{10,1... | collective-permute-start | bytes 1474568 | tf_op jit(solution)/shard_map/ppermute | solution.py:420
  54.9 14.9 %collective-permute-start.9 = (bf16[640,384]{1,0:T(8,128)(2,1)S(1)}, bf16[640,384]{1,0:T(8,128)(2,1)}, u32[]{:S(2)}, u32[]{:S(2)}) collective-permute-start(bf16[640,384]{1,0:T(8,128)(2,1)S(1)} %finish_heads.3.refs_2_.refs_0_), channel_id=1, source_target_pairs={{0,3},{1,0},{2,1},{3,2},{4,7},{5,4},{6,5},{7,6},{8,11},{9,8},{10,9... | collective-permute-start | bytes 1474568 | tf_op jit(solution)/shard_map/ppermute | solution.py:420
  58.6 17.2 %collective-permute-start.7 = (bf16[512,384]{1,0:T(8,128)(2,1)S(1)}, bf16[512,384]{1,0:T(8,128)(2,1)S(1)}, u32[]{:S(2)}, u32[]{:S(2)}) collective-permute-start(bf16[512,384]{1,0:T(8,128)(2,1)S(1)} %finish_heads.2.refs_1_), channel_id=1, source_target_pairs={{0,3},{1,0},{2,1},{3,2},{4,7},{5,4},{6,5},{7,6},{8,11},{9,8},{10,9... | collective-permute-start | bytes 1179656 | tf_op jit(solution)/shard_map/ppermute | solution.py:420
  62.7 10.3 %copy-start.9 = (bf16[528,256]{1,0:T(8,128)(2,1)S(1)}, bf16[528,256]{1,0:T(8,128)(2,1)}, u32[]{:S(2)}) copy-start(bf16[528,256]{1,0:T(8,128)(2,1)} %copy-done.8) | copy-start | bytes 811012
  62.8 10.3 %copy-start.11 = (bf16[528,256]{1,0:T(8,128)(2,1)S(1)}, bf16[528,256]{1,0:T(8,128)(2,1)}, u32[]{:S(2)}) copy-start(bf16[528,256]{1,0:T(8,128)(2,1)} %copy-done.10) | copy-start | bytes 811012
  62.8 10.3 %copy-start.13 = (bf16[528,256]{1,0:T(8,128)(2,1)S(1)}, bf16[528,256]{1,0:T(8,128)(2,1)}, u32[]{:S(2)}) copy-start(bf16[528,256]{1,0:T(8,128)(2,1)} %copy-done.12) | copy-start | bytes 811012
  69.8 15.2 %collective-permute-start.12 = (bf16[640,384]{1,0:T(8,128)(2,1)}, bf16[640,384]{1,0:T(8,128)(2,1)S(1)}, u32[]{:S(2)}, u32[]{:S(2)}) collective-permute-start(bf16[640,384]{1,0:T(8,128)(2,1)} %collective-permute-done.8.refs_4_.refs_0_), channel_id=1, source_target_pairs={{0,1},{1,2},{2,3},{3,0},{4,5},{5,6},{6,7},{7,4},{8,9},{9,10},{10,1... | collective-permute-start | bytes 1474568 | tf_op jit(solution)/shard_map/ppermute | solution.py:420
  71.0 18.2 %collective-permute-start.11 = (bf16[512,384]{1,0:T(8,128)(2,1)S(1)}, bf16[512,384]{1,0:T(8,128)(2,1)S(1)}, u32[]{:S(2)}, u32[]{:S(2)}) collective-permute-start(bf16[512,384]{1,0:T(8,128)(2,1)S(1)} %finish_heads.2.refs_1_), channel_id=1, source_target_pairs={{0,1},{1,2},{2,3},{3,0},{4,5},{5,6},{6,7},{7,4},{8,9},{9,10},{10,1... | collective-permute-start | bytes 1179656 | tf_op jit(solution)/shard_map/ppermute | solution.py:420
  75.8 9.2 %copy-start.5 = (bf16[528,256]{1,0:T(8,128)(2,1)S(1)}, bf16[528,256]{1,0:T(8,128)(2,1)}, u32[]{:S(2)}) copy-start(bf16[528,256]{1,0:T(8,128)(2,1)} %copy-done.4) | copy-start | bytes 811012
  75.8 9.2 %copy-start.7 = (bf16[528,256]{1,0:T(8,128)(2,1)S(1)}, bf16[528,256]{1,0:T(8,128)(2,1)}, u32[]{:S(2)}) copy-start(bf16[528,256]{1,0:T(8,128)(2,1)} %copy-done.6) | copy-start | bytes 811012
  75.8 14.6 %collective-permute-start.10 = (bf16[512,384]{1,0:T(8,128)(2,1)S(1)}, bf16[512,384]{1,0:T(8,128)(2,1)S(1)}, u32[]{:S(2)}, u32[]{:S(2)}) collective-permute-start(bf16[512,384]{1,0:T(8,128)(2,1)S(1)} %collective-permute-done.7.refs_1_), channel_id=1, source_target_pairs={{0,3},{1,0},{2,1},{3,2},{4,7},{5,4},{6,5},{7,6},{8,11},{9,8},{10,9... | collective-permute-start | bytes 1179656 | tf_op jit(solution)/shard_map/ppermute | solution.py:420
  (6 other events, 4.8 us)

commit v11 on v9

--- a/solution.py
+++ b/solution.py
@@ -13,10 +13,7 @@
 HALF = BLK // 2
 CORES = 2
 HEADS = 8
-LATE = 6
-EARLY = HEADS - LATE
-GAIN_ROWS = 16
-CALLS = ((0, 3), (3, 6))
+CALLS = ((0, 4), (4, 8))
 F32 = jnp.float32
 BF16 = jnp.bfloat16
 NN, NT, TN = ((1,), (0,)), ((1,), (1,)), ((0,), (0,))
@@ -104,62 +101,6 @@
     )(in_hbm(k), in_hbm(v))
 
 
-def within_early_kernel(q_hbm, k_hbm, v_hbm, gain_hbm, *refs):
-    out_hbm, (q_ref, k_ref, v_ref, gain_ref, early_ref, sems) = refs[:EARLY], refs[EARLY:]
-    early = slice(LATE * DH, HEADS * DH)
-    sources = (q_hbm.at[:, early], k_hbm.at[:, early], v_hbm.at[:, early], gain_hbm)
-    targets = (q_ref, k_ref, v_ref, gain_ref)
-    copies = [
-        pltpu.make_async_copy(source, target, sems.at[at])
-        for at, (source, target) in enumerate(zip(sources, targets))
-    ]
-    for copy in copies:
-        copy.start()
-    for copy in copies:
-        copy.wait()
-    causal = causal_mask()
-    blank = jnp.zeros((GAIN_ROWS - 3, DH), BF16)
-    outs = []
-    for h in range(EARLY):
-        cols = slice(h * DH, (h + 1) * DH)
-        gain = gain_ref[:, (LATE + h) * DH : (LATE + h + 1) * DH]
-        high = gain.astype(BF16)
-        rest = gain - high.astype(F32)
-        middle = rest.astype(BF16)
-        low = (rest - middle.astype(F32)).astype(BF16)
-        top, bottom = within_block(q_ref, k_ref, v_ref, h, causal)
-        early_ref[h, :BLK, :DH] = q_ref[:, cols]
-        early_ref[h, :HALF, DH:] = top.astype(BF16)
-        early_ref[h, HALF:BLK, DH:] = bottom.astype(BF16)
-        early_ref[h, BLK:, :DH] = jnp.concatenate([high, middle, low, blank])
-        early_ref[h, BLK:, DH:] = jnp.zeros((GAIN_ROWS, DH), BF16)
-        outs.append(pltpu.make_async_copy(early_ref.at[h], out_hbm[h], sems.at[4 + h]))
-        outs[-1].start()
-    for copy in outs:
-        copy.wait()
-
-
-def within_early(q, k, v, gain):
-    shape, block = (BLK, EARLY * DH), (BLK + GAIN_ROWS, 2 * DH)
-    return pl.pallas_call(
-        within_early_kernel,
-        name="within_early",
-        in_specs=[HBM] * 4,
-        out_specs=[HBM] * EARLY,
-        out_shape=[jax.ShapeDtypeStruct(block, BF16)] * EARLY,
-        scratch_shapes=[
-            pltpu.VMEM(shape, BF16),
-            pltpu.VMEM(shape, BF16),
-            pltpu.VMEM(shape, BF16),
-            pltpu.VMEM(gain.shape, F32),
-            pltpu.VMEM((EARLY, *block), BF16),
-            pltpu.SemaphoreType.DMA((4 + EARLY,)),
-        ],
-        compiler_params=PARAMS,
-        cost_estimate=cost(4 * BLK * BLK * DH * EARLY, BLK * DH * EARLY * 10),
-    )(in_hbm(q), in_hbm(k), in_hbm(v), in_hbm(gain))
-
-
 def scan_kernel(core_ref, own_ref, other_ref, out_ref, *, chips):
     rows = own_ref.shape[0] // chips
     second = (core_ref[0] == 1).astype(F32)
@@ -185,7 +126,7 @@
 
 def within_kernel(q_hbm, k_hbm, v_hbm, q_ref, out_ref, k_ref, v_ref, sems):
     copies, split = [], CALLS[0][1] * DH
-    parts = (slice(0, split), slice(split, LATE * DH))
+    parts = (slice(0, split), slice(split, HEADS * DH))
     for part, cols in enumerate(parts):
         for at, (hbm, ref) in enumerate(((q_hbm, q_ref), (k_hbm, k_ref), (v_hbm, v_ref))):
             copies.append(
@@ -203,11 +144,11 @@
             out_ref[HALF:, cols] = bottom
 
 
-def within_late(q, k, v):
-    shape = (BLK, LATE * DH)
+def within_all(q, k, v):
+    shape = (BLK, HEADS * DH)
     return pl.pallas_call(
         within_kernel,
-        name="within_late",
+        name="within_all",
         in_specs=[HBM] * 3,
         out_specs=[VMEM, VMEM],
         out_shape=[pltpu.VMEM(shape, BF16), pltpu.VMEM(shape, F32)],
@@ -217,7 +158,7 @@
             pltpu.SemaphoreType.DMA((2, 3)),
         ],
         compiler_params=PARAMS,
-        cost_estimate=cost(4 * BLK * BLK * DH * LATE, BLK * DH * LATE * 10),
+        cost_estimate=cost(4 * BLK * BLK * DH * HEADS, BLK * DH * HEADS * 10),
     )(in_hbm(q), in_hbm(k), in_hbm(v))
 
 
@@ -225,64 +166,22 @@
     for h in range(first, last):
         cols = slice(h * DH, (h + 1) * DH)
         out_cols = slice((h - first) * DH, (h - first + 1) * DH)
-        out_ref[:BLK, out_cols] = finish(
+        out_ref[:, out_cols] = finish(
             q_ref[:, cols], within_ref[:, cols], carried_ref[cols, :], gain_ref[:, cols]
         )
-    if out_ref.shape[0] > BLK:
-        out_ref[BLK:, EARLY * DH :] = jnp.zeros((DH, out_ref.shape[1] - EARLY * DH), BF16)
-        for h in range(EARLY):
-            state = carried_ref[(LATE + h) * DH : (LATE + h + 1) * DH, :]
-            out_ref[BLK:, h * DH : (h + 1) * DH] = state
-
-
-def finish_heads(q, within, carried, gain, first, last, states=False):
+
+
+def finish_heads(q, within, carried, gain, first, last):
     heads = last - first
     return pl.pallas_call(
         functools.partial(finish_kernel, first=first, last=last),
         name="finish_heads",
         in_specs=[VMEM] * 4,
         out_specs=VMEM,
-        out_shape=jax.ShapeDtypeStruct((BLK + DH if states else BLK, heads * DH), BF16),
+        out_shape=jax.ShapeDtypeStruct((BLK, heads * DH), BF16),
         compiler_params=PARAMS,
         cost_estimate=cost(4 * BLK * DH * DH * heads, BLK * DH * heads * 8),
     )(q, within, carried, gain)
-
-
-def early_kernel(*refs, count):
-    hbm_refs, rest = refs[: count * EARLY], refs[count * EARLY :]
-    a_refs, out_refs, (e_ref, sems) = rest[:count], rest[count : 2 * count], rest[2 * count :]
-    copies = [
-        pltpu.make_async_copy(hbm, e_ref.at[at], sems.at[at]) for at, hbm in enumerate(hbm_refs)
-    ]
-    for copy in copies:
-        copy.start()
-    for source, (a_ref, out_ref) in enumerate(zip(a_refs, out_refs)):
-        for h in range(EARLY):
-            at = source * EARLY + h
-            copies[at].wait()
-            cols = slice(h * DH, (h + 1) * DH)
-            terms = e_ref[at, BLK:, :DH].astype(F32)
-            gain = terms[0:1] + terms[1:2] + terms[2:3]
-            within = e_ref[at, :BLK, DH:].astype(F32)
-            out_ref[:, cols] = finish(e_ref[at, :BLK, :DH], within, a_ref[BLK:, cols], gain)
-
-
-def early_heads(early, chunks):
-    count = len(chunks)
-    early = [value for pair in early for value in pair]
-    return pl.pallas_call(
-        functools.partial(early_kernel, count=count),
-        name="early_heads",
-        in_specs=[pl.BlockSpec(memory_space=pl.ANY)] * len(early) + [VMEM] * count,
-        out_specs=[VMEM] * count,
-        out_shape=[jax.ShapeDtypeStruct((BLK, EARLY * DH), BF16)] * count,
-        scratch_shapes=[
-            pltpu.VMEM((len(early), *early[0].shape), BF16),
-            pltpu.SemaphoreType.DMA((len(early),)),
-        ],
-        compiler_params=PARAMS,
-        cost_estimate=cost(4 * BLK * DH * DH * EARLY * count, BLK * DH * EARLY * count * 6),
-    )(*early, *chunks)
 
 
 TILE = 256
@@ -310,7 +209,7 @@
         copies[piece].wait()
         for tile in range(total_ref.shape[1] // TILE):
             cols = slice(tile * TILE, (tile + 1) * TILE)
-            term = dot(a_ref[:BLK, :], w_ref[rows[piece], cols], NN)
+            term = dot(a_ref[...], w_ref[rows[piece], cols], NN)
             total_ref[:, cols] = term if piece == 0 else total_ref[:, cols] + term
 
 
@@ -334,7 +233,7 @@
 def add_products(total_ref, out_ref, a_refs, w_ref, starts, cols):
     total = total_ref[:, cols]
     for a_ref, start in zip(a_refs, starts):
-        total = total + dot(a_ref[:BLK, :], w_ref[start : start + a_ref.shape[1], cols], NN)
+        total = total + dot(a_ref[...], w_ref[start : start + a_ref.shape[1], cols], NN)
     out_ref[:, cols] = total.astype(out_ref.dtype)
 
 
@@ -427,38 +326,27 @@
     gain_row = gain.reshape(1, -1)
     states = block_states(k, v)
     own = lax.all_to_all(states, "chip", 0, 0, tiled=True)
-    early = within_early(q, k, v, gain_row)
-    left_q = [along(value, 1, ways) for value in early]
-    right_q = [along(value, -1, ways) for value in early]
     other = lax.ppermute(own, "core", [(0, 1), (1, 0)])
-    own, other, left_q, right_q = lax.optimization_barrier((own, other, left_q, right_q))
-    far_q = [along(left_q[0], 1, ways), along(right_q[1], -1, ways)]
     sums = exclusive_sums(core, own, other, chips)
     carried = lax.all_to_all(sums, "chip", 0, 0, tiled=True)
-    q_late, within = within_late(q, k, v)
-    carried, far_q, q_late, within = lax.optimization_barrier((carried, far_q, q_late, within))
+    q, within = within_all(q, k, v)
+    carried, q, within = lax.optimization_barrier((carried, q, within))
     (a0, a1), (b0, b1) = CALLS
-    mine_a = finish_heads(q_late, within, carried, gain_row, a0, a1, True)
-    mine_b = finish_heads(q_late, within, carried, gain_row, b0, b1)
-    (mine_e,) = early_heads([early], [mine_a])
-    total = own_mix(column, w, [mine_a, mine_b, mine_e])
+    mine_a = finish_heads(q, within, carried, gain_row, a0, a1)
+    mine_b = finish_heads(q, within, carried, gain_row, b0, b1)
+    total = own_mix(column, w, [mine_a, mine_b])
     left_a, right_a, total = lax.optimization_barrier(
         (along(mine_a, 1, ways), along(mine_a, -1, ways), total)
     )
     far_a = along(left_a, 1, ways)
-    left_e, right_e = early_heads([left_q, right_q], [left_a, right_a])
     left_b = along(mine_b, 1, ways)
-    right_b, left_e, right_e = lax.optimization_barrier(
-        (along(mine_b, -1, ways), left_e, right_e)
-    )
+    right_b = along(mine_b, -1, ways)
     far_b = along(right_b, -1, ways)
     depth = HEADS * DH
-    at_a, at_b, at_e = a0 * DH, b0 * DH, LATE * DH
-    starts = (at_a, at_e, depth + at_a, depth + at_e)
-    total, w = side_mix(column, w, starts, [left_a, left_e, right_a, right_e], total)
-    (far_e,) = early_heads([far_q], [far_a])
-    total = mix(w, (2 * depth + at_a, 2 * depth + at_e), [far_a, far_e], total)
+    at_a, at_b = a0 * DH, b0 * DH
+    total, w = side_mix(column, w, (at_a, depth + at_a), [left_a, right_a], total)
     total = mix(w, (at_b, depth + at_b), [left_b, right_b], total)
+    total = mix(w, (2 * depth + at_a,), [far_a], total)
     return mix(w, (2 * depth + at_b,), [far_b], total, True)
 
 

time: 87.4 us -> 85.7 us (0.981)
  starting transfers between devices: 39.9 us -> 14.2 us
  blocking collectives: 0 us -> 23.2 us
  waiting for transfers between devices: 17.4 us -> 26 us
  Pallas kernels: 25.3 us -> 21 us
  local copies, waits for them, and re-layouts: 4.08 us -> 0.01 us
    all_to_all x0 -> x1, blocking collectives: none -> 23.2 us  [shards(): own = lax.all_to_all(states, 'chip', 0, 0, tiled=True)]
    all_to_all x1 -> x0, starting transfers between devices: 11.2 us -> none  [shards(): own = lax.all_to_all(states, 'chip', 0, 0, tiled=True)]
    ppermute x12 -> x6, starting transfers between devices: 18.9 us -> 9.54 us  [along(): lax.ppermute(value, 'fsdp', [(i, (i + shift) % count) for i in range(coun...]
    all_to_all x1, waiting for transfers between devices: 1.64 us -> 8.7 us  [shards(): carried = lax.all_to_all(sums, 'chip', 0, 0, tiled=True)]
    pallas_call x5 -> x1, Pallas kernels: 9.36 us -> 3.83 us  [within_all(): pl.pallas_call(within_kernel, name='within_all', in_specs=[HBM] * 3, out_...]
    all_to_all x1, starting transfers between devices: 9.76 us -> 4.61 us  [shards(): carried = lax.all_to_all(sums, 'chip', 0, 0, tiled=True)]
    ppermute x12 -> x6, waiting for transfers between devices: 11 us -> 15.8 us  [along(): lax.ppermute(value, 'fsdp', [(i, (i + shift) % count) for i in range(coun...]
    all_to_all x1 -> x0, waiting for transfers between devices: 4.71 us -> none  [shards(): own = lax.all_to_all(states, 'chip', 0, 0, tiled=True)]
  transfers between devices with their start and end apart: 15 -> 8, of which waited for: 9 -> 6; matrix products, arithmetic and copies ran while one was open for 0% -> 0% of each run, Pallas kernels for 23% -> 18%
where the time goes in v11:
time: 85.7 us; the launch traced here: 84.6 us
  waiting for transfers between devices  26 us (30%)
  blocking collectives  23.2 us (27%)
  Pallas kernels  21 us (25%)
  starting transfers between devices  14.2 us (17%)
    all_to_all x1, blocking collectives, shards(): own = lax.all_to_all(states, 'chip', 0, 0, tiled=True)  23.2 us
    ppermute x6, waiting for transfers between devices, along(): lax.ppermute(value, 'fsdp', [(i, (i + shift) % count) for i in range(coun...  15.8 us
    ppermute x6, starting transfers between devices, along(): lax.ppermute(value, 'fsdp', [(i, (i + shift) % count) for i in range(coun...  9.54 us
    all_to_all x1, waiting for transfers between devices, shards(): carried = lax.all_to_all(sums, 'chip', 0, 0, tiled=True)  8.7 us
    all_to_all x1, starting transfers between devices, shards(): carried = lax.all_to_all(sums, 'chip', 0, 0, tiled=True)  4.61 us
    pallas_call x1, Pallas kernels, side_mix(): pl.pallas_call(functools.partial(side_kernel, starts=starts), name='side_...  4.37 us
    pallas_call x1, Pallas kernels, within_all(): pl.pallas_call(within_kernel, name='within_all', in_specs=[HBM] * 3, out_...  3.83 us
    pallas_call x1, Pallas kernels, own_mix(): pl.pallas_call(own_kernel, name='own_mix', in_specs=[SMEM] + [VMEM] * len...  3.75 us
  transfers between devices with their start and end apart: 8, of which 6 were waited for; matrix products, arithmetic and copies ran while one was open for 0% of the time, Pallas kernels for 18%

profile of v11, /device:TPU:32, one launch (start us, length us, event | category | flops | bytes accessed | tf_op | source)
XLA Modules:
  0.0 84.6 jit_solution(15677216055746530959)
XLA Ops:
  0.0 2.0 %block_states.1 = bf16[1024,128]{1,0:T(8,128)(2,1)S(1)} custom-call(bf16[512,1024]{1,0:T(8,128)(2,1)} %k_hbm.3, bf16[512,1024]{1,0:T(8,128)(2,1)} %v_hbm.3), custom_call_target="tpu_custom_call" | custom-call | flops 134217728 | bytes 2097152 | tf_op jit(solution)/shard_map/block_states/pallas_call | solution.py:88
  2.0 23.2 %all_to_all.23 = bf16[32,32,128]{2,1,0:T(8,128)(2,1)S(1)} all-to-all(bf16[32,32,128]{2,1,0:T(8,128)(2,1)S(1)} %bitcast.9), channel_id=1, replica_groups=mesh['chip'=32,'core'=2,'fsdp'=4] {'chip'}, dimensions={0} | all-to-all | bytes 524288 | tf_op jit(solution)/shard_map/all_to_all | solution.py:328
  25.2 1.5 %collective-permute-done.other_ref = bf16[1024,128]{1,0:T(8,128)(2,1)S(1)} collective-permute-done((bf16[1024,128]{1,0:T(8,128)(2,1)S(1)}, bf16[1024,128]{1,0:T(8,128)(2,1)S(1)}, u32[]{:S(2)}, u32[]{:S(2)}) %collective-permute-start) | collective-permute-done | bytes 262176 | tf_op jit(solution)/shard_map/ppermute | solution.py:329
  26.7 0.8 exclusive_sums.1
  27.5 4.6 %all-to-all-start.1 = ((bf16[32,32,128]{2,1,0:T(8,128)(2,1)}), bf16[32,32,128]{2,1,0:T(8,128)(2,1)S(1)}, u32[]{:S(2)}, u32[]{:S(2)}) async-start(bf16[32,32,128]{2,1,0:T(8,128)(2,1)} %bitcast.3), calls=%async_computation.1 | async-start | bytes 524288 | tf_op jit(solution)/shard_map/all_to_all | solution.py:331
  32.1 3.8 %within_all.1 = (bf16[512,1024]{1,0:T(8,128)(2,1)S(1)}, f32[512,1024]{1,0:T(8,128)S(1)}) custom-call(bf16[512,1024]{1,0:T(8,128)(2,1)} %q_hbm.1, bf16[512,1024]{1,0:T(8,128)(2,1)} %k_hbm.3, bf16[512,1024]{1,0:T(8,128)(2,1)} %v_hbm.3), custom_call_target="tpu_custom_call" | custom-call | flops 1073741824 | bytes 5242880 | tf_op jit(solution)/shard_map/within_all/pallas_call | solution.py:149
  36.0 8.7 %all-to-all-done.1 = bf16[32,32,128]{2,1,0:T(8,128)(2,1)S(1)} async-done(((bf16[32,32,128]{2,1,0:T(8,128)(2,1)}), bf16[32,32,128]{2,1,0:T(8,128)(2,1)S(1)}, u32[]{:S(2)}, u32[]{:S(2)}) %all-to-all-start.1) | async-done | bytes 262176 | tf_op jit(solution)/shard_map/all_to_all | solution.py:331
  44.7 1.3 %finish_heads.3.refs_0_ = bf16[512,512]{1,0:T(8,128)(2,1)} custom-call(bf16[512,1024]{1,0:T(8,128)(2,1)S(1)} %get-tuple-element.17.q_ref, f32[512,1024]{1,0:T(8,128)S(1)} %get-tuple-element.18.within_ref, bf16[1024,128]{1,0:T(8,128)(2,1)S(1)} %bitcast.7, f32[1,1024]{1,0:T(1,128)S(1)} %bitcast.12), custom_call_target="tpu_custom_call" | custom-call | flops 134217728 | bytes 2097152 | tf_op jit(solution)/shard_map/finish_heads/pallas_call | solution.py:176
  46.0 1.6 %collective-permute-start.3 = (bf16[512,512]{1,0:T(8,128)(2,1)}, bf16[512,512]{1,0:T(8,128)(2,1)}, u32[]{:S(2)}, u32[]{:S(2)}) collective-permute-start(bf16[512,512]{1,0:T(8,128)(2,1)} %finish_heads.3.refs_0_), channel_id=1, source_target_pairs={{0,1},{1,2},{2,3},{3,0},{4,5},{5,6},{6,7},{7,4},{8,9},{9,10},{10,1... | collective-permute-start | bytes 1572872 | tf_op jit(solution)/shard_map/ppermute | solution.py:319
  47.6 1.7 %collective-permute-start.4 = (bf16[512,512]{1,0:T(8,128)(2,1)}, bf16[512,512]{1,0:T(8,128)(2,1)}, u32[]{:S(2)}, u32[]{:S(2)}) collective-permute-start(bf16[512,512]{1,0:T(8,128)(2,1)} %finish_heads.3.refs_0_), channel_id=1, source_target_pairs={{0,3},{1,0},{2,1},{3,2},{4,7},{5,4},{6,5},{7,6},{8,11},{9,8},{10,9... | collective-permute-start | bytes 1572872 | tf_op jit(solution)/shard_map/ppermute | solution.py:319
  49.2 1.3 %finish_heads.2.refs_1_ = bf16[512,512]{1,0:T(8,128)(2,1)} custom-call(bf16[512,1024]{1,0:T(8,128)(2,1)S(1)} %get-tuple-element.17.q_ref, f32[512,1024]{1,0:T(8,128)S(1)} %get-tuple-element.18.within_ref, bf16[1024,128]{1,0:T(8,128)(2,1)S(1)} %bitcast.8, f32[1,1024]{1,0:T(1,128)S(1)} %bitcast.13), custom_call_target="tpu_custom_call" | custom-call | flops 134217728 | bytes 2097152 | tf_op jit(solution)/shard_map/finish_heads/pallas_call | solution.py:176
  50.6 1.8 %collective-permute-start.1 = (bf16[512,512]{1,0:T(8,128)(2,1)}, bf16[512,512]{1,0:T(8,128)(2,1)S(1)}, u32[]{:S(2)}, u32[]{:S(2)}) collective-permute-start(bf16[512,512]{1,0:T(8,128)(2,1)} %finish_heads.2.refs_1_), channel_id=1, source_target_pairs={{0,3},{1,0},{2,1},{3,2},{4,7},{5,4},{6,5},{7,6},{8,11},{9,8},{10,9... | collective-permute-start | bytes 1572872 | tf_op jit(solution)/shard_map/ppermute | solution.py:319
  52.4 0.2 collective-permute-start.6
  52.6 3.7 %own_mix.1.refs_3_ = f32[512,1024]{1,0:T(8,128)S(1)} custom-call(s32[1]{0:T(128)} %bitcast.6.column_ref, bf16[512,512]{1,0:T(8,128)(2,1)} %finish_heads.3.refs_0_, bf16[512,512]{1,0:T(8,128)(2,1)} %finish_heads.2.refs_1_, bf16[4096,1024]{1,0:T(8,128)(2,1)} %refs_2_.3), custom_call_target="tpu_custom_call" | custom-call | flops 1073741824 | bytes 2097152 | tf_op jit(solution)/shard_map/own_mix/pallas_call | solution.py:218
  56.4 6.0 %collective-permute-done.3.refs_0_ = bf16[512,512]{1,0:T(8,128)(2,1)} collective-permute-done((bf16[512,512]{1,0:T(8,128)(2,1)}, bf16[512,512]{1,0:T(8,128)(2,1)}, u32[]{:S(2)}, u32[]{:S(2)}) %collective-permute-start.3) | collective-permute-done | bytes 524320 | tf_op jit(solution)/shard_map/ppermute | solution.py:319
  62.4 0.4 collective-permute-done.4.refs_1_
  62.8 1.6 %collective-permute-start.5 = (bf16[512,512]{1,0:T(8,128)(2,1)}, bf16[512,512]{1,0:T(8,128)(2,1)S(1)}, u32[]{:S(2)}, u32[]{:S(2)}) collective-permute-start(bf16[512,512]{1,0:T(8,128)(2,1)} %collective-permute-done.3.refs_0_), channel_id=1, source_target_pairs={{0,1},{1,2},{2,3},{3,0},{4,5},{5,6},{6,7},{7,4},{8,9},{9,10},{10,1... | collective-permute-start | bytes 1572872 | tf_op jit(solution)/shard_map/ppermute | solution.py:319
  64.3 6.8 %collective-permute-done.1.refs_1_ = bf16[512,512]{1,0:T(8,128)(2,1)S(1)} collective-permute-done((bf16[512,512]{1,0:T(8,128)(2,1)}, bf16[512,512]{1,0:T(8,128)(2,1)S(1)}, u32[]{:S(2)}, u32[]{:S(2)}) %collective-permute-start.1) | collective-permute-done | bytes 524320 | tf_op jit(solution)/shard_map/ppermute | solution.py:319
  71.1 2.7 %collective-permute-start.2 = (bf16[512,512]{1,0:T(8,128)(2,1)S(1)}, bf16[512,512]{1,0:T(8,128)(2,1)S(1)}, u32[]{:S(2)}, u32[]{:S(2)}) collective-permute-start(bf16[512,512]{1,0:T(8,128)(2,1)S(1)} %collective-permute-done.1.refs_1_), channel_id=1, source_target_pairs={{0,3},{1,0},{2,1},{3,2},{4,7},{5,4},{6,5},{7,6},{8,11},{9,8},{10,9... | collective-permute-start | bytes 1572872 | tf_op jit(solution)/shard_map/ppermute | solution.py:319
  73.8 4.4 %side_mix.1 = (f32[512,1024]{1,0:T(8,128)S(1)}, bf16[3072,1024]{1,0:T(8,128)(2,1)S(1)}) custom-call(s32[1]{0:T(128)} %bitcast.6.column_ref, bf16[512,512]{1,0:T(8,128)(2,1)} %collective-permute-done.3.refs_0_, bf16[512,512]{1,0:T(8,128)(2,1)} %collective-permute-done.4.refs_1_, bf16[4096,1024]{1,0:T(8,128)(2,1)} %refs_2_.3, f32[512,1024]{1,0:T(8,128)S(1)} %own_mix.1.refs_3_), custom_call_target="tpu_custom_call" | custom-call | flops 3221225472 | bytes 6291456 | tf_op jit(solution)/shard_map/side_mix/pallas_call | solution.py:268
  78.2 1.2 %mix.3.refs_2_ = f32[512,1024]{1,0:T(8,128)S(1)} custom-call(bf16[512,512]{1,0:T(8,128)(2,1)S(1)} %collective-permute-done.6.refs_0_, bf16[512,512]{1,0:T(8,128)(2,1)S(1)} %collective-permute-done.1.refs_1_, bf16[3072,1024]{1,0:T(8,128)(2,1)S(1)} %get-tuple-element.23.refs_2_.refs_1_, f32[512,1024]{1,0:T(8,128)S(1)} %get-tuple-element.24.refs_3_), custom_call_target="tpu_custom_call" | custom-call | flops 1073741824 | bytes 2097152 | tf_op jit(solution)/shard_map/mix/pallas_call | solution.py:306
  79.5 2.6 %collective-permute-done.5.refs_0_ = bf16[512,512]{1,0:T(8,128)(2,1)S(1)} collective-permute-done((bf16[512,512]{1,0:T(8,128)(2,1)}, bf16[512,512]{1,0:T(8,128)(2,1)S(1)}, u32[]{:S(2)}, u32[]{:S(2)}) %collective-permute-start.5) | collective-permute-done | bytes 524320 | tf_op jit(solution)/shard_map/ppermute | solution.py:319
  82.1 0.7 mix.4.refs_2_
  82.8 1.6 %mix.5 = bf16[512,1024]{1,0:T(8,128)(2,1)} custom-call(bf16[512,512]{1,0:T(8,128)(2,1)S(1)} %collective-permute-done.2.refs_0_, bf16[3072,1024]{1,0:T(8,128)(2,1)S(1)} %get-tuple-element.23.refs_2_.refs_1_, f32[512,1024]{1,0:T(8,128)S(1)} %mix.4.refs_2_), custom_call_target="tpu_custom_call" | custom-call | flops 536870912 | bytes 1048576 | tf_op jit(solution)/shard_map/mix/pallas_call | solution.py:306
  (5 shorter events, 0.0 us)
Async XLA Ops:
  25.2 1.5 %collective-permute-start = (bf16[1024,128]{1,0:T(8,128)(2,1)S(1)}, bf16[1024,128]{1,0:T(8,128)(2,1)S(1)}, u32[]{:S(2)}, u32[]{:S(2)}) collective-permute-start(bf16[1024,128]{1,0:T(8,128)(2,1)S(1)} %bitcast.10), channel_id=1, source_target_pairs={{0,4},{4,0},{1,5},{5,1},{2,6},{6,2},{3,7},{7,3},{8,12},{12,8},{9,1... | collective-permute-start | bytes 786440 | tf_op jit(solution)/shard_map/ppermute | solution.py:329
  27.5 17.2 %all-to-all-start.1 = ((bf16[32,32,128]{2,1,0:T(8,128)(2,1)}), bf16[32,32,128]{2,1,0:T(8,128)(2,1)S(1)}, u32[]{:S(2)}, u32[]{:S(2)}) async-start(bf16[32,32,128]{2,1,0:T(8,128)(2,1)} %bitcast.3), calls=%async_computation.1 | async-start | bytes 524288 | tf_op jit(solution)/shard_map/all_to_all | solution.py:331
  32.1 12.5 %copy-start = (f32[1024]{0:T(1024)S(1)}, f32[1024]{0:T(1024)}, u32[]{:S(2)}) copy-start(f32[1024]{0:T(1024)} %param.8) | copy-start | bytes 12292
  46.0 16.4 %collective-permute-start.3 = (bf16[512,512]{1,0:T(8,128)(2,1)}, bf16[512,512]{1,0:T(8,128)(2,1)}, u32[]{:S(2)}, u32[]{:S(2)}) collective-permute-start(bf16[512,512]{1,0:T(8,128)(2,1)} %finish_heads.3.refs_0_), channel_id=1, source_target_pairs={{0,1},{1,2},{2,3},{3,0},{4,5},{5,6},{6,7},{7,4},{8,9},{9,10},{10,1... | collective-permute-start | bytes 1572872 | tf_op jit(solution)/shard_map/ppermute | solution.py:319
  47.6 15.2 %collective-permute-start.4 = (bf16[512,512]{1,0:T(8,128)(2,1)}, bf16[512,512]{1,0:T(8,128)(2,1)}, u32[]{:S(2)}, u32[]{:S(2)}) collective-permute-start(bf16[512,512]{1,0:T(8,128)(2,1)} %finish_heads.3.refs_0_), channel_id=1, source_target_pairs={{0,3},{1,0},{2,1},{3,2},{4,7},{5,4},{6,5},{7,6},{8,11},{9,8},{10,9... | collective-permute-start | bytes 1572872 | tf_op jit(solution)/shard_map/ppermute | solution.py:319
  50.6 20.5 %collective-permute-start.1 = (bf16[512,512]{1,0:T(8,128)(2,1)}, bf16[512,512]{1,0:T(8,128)(2,1)S(1)}, u32[]{:S(2)}, u32[]{:S(2)}) collective-permute-start(bf16[512,512]{1,0:T(8,128)(2,1)} %finish_heads.2.refs_1_), channel_id=1, source_target_pairs={{0,3},{1,0},{2,1},{3,2},{4,7},{5,4},{6,5},{7,6},{8,11},{9,8},{10,9... | collective-permute-start | bytes 1572872 | tf_op jit(solution)/shard_map/ppermute | solution.py:319
  52.4 25.8 %collective-permute-start.6 = (bf16[512,512]{1,0:T(8,128)(2,1)}, bf16[512,512]{1,0:T(8,128)(2,1)S(1)}, u32[]{:S(2)}, u32[]{:S(2)}) collective-permute-start(bf16[512,512]{1,0:T(8,128)(2,1)} %finish_heads.2.refs_1_), channel_id=1, source_target_pairs={{0,1},{1,2},{2,3},{3,0},{4,5},{5,6},{6,7},{7,4},{8,9},{9,10},{10,1... | collective-permute-start | bytes 1572872 | tf_op jit(solution)/shard_map/ppermute | solution.py:319
  62.8 19.3 %collective-permute-start.5 = (bf16[512,512]{1,0:T(8,128)(2,1)}, bf16[512,512]{1,0:T(8,128)(2,1)S(1)}, u32[]{:S(2)}, u32[]{:S(2)}) collective-permute-start(bf16[512,512]{1,0:T(8,128)(2,1)} %collective-permute-done.3.refs_0_), channel_id=1, source_target_pairs={{0,1},{1,2},{2,3},{3,0},{4,5},{5,6},{6,7},{7,4},{8,9},{9,10},{10,1... | collective-permute-start | bytes 1572872 | tf_op jit(solution)/shard_map/ppermute | solution.py:319
  71.1 11.7 %collective-permute-start.2 = (bf16[512,512]{1,0:T(8,128)(2,1)S(1)}, bf16[512,512]{1,0:T(8,128)(2,1)S(1)}, u32[]{:S(2)}, u32[]{:S(2)}) collective-permute-start(bf16[512,512]{1,0:T(8,128)(2,1)S(1)} %collective-permute-done.1.refs_1_), channel_id=1, source_target_pairs={{0,3},{1,0},{2,1},{3,2},{4,7},{5,4},{6,5},{7,6},{8,11},{9,8},{10,9... | collective-permute-start | bytes 1572872 | tf_op jit(solution)/shard_map/ppermute | solution.py:319

commit v12 on v11

--- a/solution.py
+++ b/solution.py
@@ -331,23 +331,26 @@
     carried = lax.all_to_all(sums, "chip", 0, 0, tiled=True)
     q, within = within_all(q, k, v)
     carried, q, within = lax.optimization_barrier((carried, q, within))
-    (a0, a1), (b0, b1) = CALLS
-    mine_a = finish_heads(q, within, carried, gain_row, a0, a1)
-    mine_b = finish_heads(q, within, carried, gain_row, b0, b1)
-    total = own_mix(column, w, [mine_a, mine_b])
-    left_a, right_a, total = lax.optimization_barrier(
-        (along(mine_a, 1, ways), along(mine_a, -1, ways), total)
-    )
-    far_a = along(left_a, 1, ways)
-    left_b = along(mine_b, 1, ways)
-    right_b = along(mine_b, -1, ways)
-    far_b = along(right_b, -1, ways)
+    heads = (0, 2, 4, 6)
+    mine = [finish_heads(q, within, carried, gain_row, h, h + 2) for h in heads]
+    left = [along(value, 1, ways) for value in mine]
+    right = [along(value, -1, ways) for value in mine]
+    total = own_mix(column, w, mine)
+    left[0], right[1], total = lax.optimization_barrier((left[0], right[1], total))
+    far = [
+        along(left[0], 1, ways),
+        along(right[1], -1, ways),
+        along(left[2], 1, ways),
+        along(right[3], -1, ways),
+    ]
     depth = HEADS * DH
-    at_a, at_b = a0 * DH, b0 * DH
-    total, w = side_mix(column, w, (at_a, depth + at_a), [left_a, right_a], total)
-    total = mix(w, (at_b, depth + at_b), [left_b, right_b], total)
-    total = mix(w, (2 * depth + at_a,), [far_a], total)
-    return mix(w, (2 * depth + at_b,), [far_b], total, True)
+    at = [h * DH for h in heads]
+    side = [depth + start for start in at]
+    across = [2 * depth + start for start in at]
+    total, w = side_mix(column, w, (*at[:2], *side[:2]), left[:2] + right[:2], total)
+    total = mix(w, (*at[2:], *side[2:]), left[2:] + right[2:], total)
+    total = mix(w, tuple(across[:2]), far[:2], total)
+    return mix(w, tuple(across[2:]), far[2:], total, True)
 
 
 def solution(mesh):

time: 85.7 us -> 87.7 us (1.023)
  waiting for transfers between devices: 26 us -> 22.2 us
  starting transfers between devices: 14.2 us -> 17 us
  Pallas kernels: 21 us -> 23.4 us
  local copies, waits for them, and re-layouts: 0.01 us -> 1.38 us
    ppermute x6 -> x12, waiting for transfers between devices: 15.8 us -> 12 us  [along(): lax.ppermute(value, 'fsdp', [(i, (i + shift) % count) for i in range(coun...]
    ppermute x6 -> x12, starting transfers between devices: 9.54 us -> 12.4 us  [along(): lax.ppermute(value, 'fsdp', [(i, (i + shift) % count) for i in range(coun...]
    pallas_call x2 -> x4, Pallas kernels: 2.65 us -> 4.39 us  [finish_heads(): pl.pallas_call(functools.partial(finish_kernel, first=first, last=last),...]
    unnamed x2 -> x10, local copies, waits for them, and re-layouts: 0.01 us -> 1.38 us
    pallas_call x3, Pallas kernels: 3.56 us -> 4.49 us  [mix(): pl.pallas_call(functools.partial(mix_kernel, count=len(arrays), starts=st...]
  transfers between devices with their start and end apart: 8 -> 14, of which waited for: 6 -> 7; matrix products, arithmetic and copies ran while one was open for 0% -> 0% of each run, Pallas kernels for 18% -> 20%
where the time goes in v12:
time: 87.7 us; the launch traced here: 87.4 us
  Pallas kernels  23.4 us (27%)
  blocking collectives  23.2 us (26%)
  waiting for transfers between devices  22.2 us (25%)
  starting transfers between devices  17 us (19%)
  local copies, waits for them, and re-layouts  1.38 us (2%)
    all_to_all x1, blocking collectives, shards(): own = lax.all_to_all(states, 'chip', 0, 0, tiled=True)  23.2 us
    ppermute x12, starting transfers between devices, along(): lax.ppermute(value, 'fsdp', [(i, (i + shift) % count) for i in range(coun...  12.4 us
    ppermute x12, waiting for transfers between devices, along(): lax.ppermute(value, 'fsdp', [(i, (i + shift) % count) for i in range(coun...  12 us
    all_to_all x1, waiting for transfers between devices, shards(): carried = lax.all_to_all(sums, 'chip', 0, 0, tiled=True)  8.7 us
    all_to_all x1, starting transfers between devices, shards(): carried = lax.all_to_all(sums, 'chip', 0, 0, tiled=True)  4.61 us
    pallas_call x3, Pallas kernels, mix(): pl.pallas_call(functools.partial(mix_kernel, count=len(arrays), starts=st...  4.49 us
    pallas_call x4, Pallas kernels, finish_heads(): pl.pallas_call(functools.partial(finish_kernel, first=first, last=last),...  4.39 us
    pallas_call x1, Pallas kernels, side_mix(): pl.pallas_call(functools.partial(side_kernel, starts=starts), name='side_...  4.11 us
  transfers between devices with their start and end apart: 14, of which 7 were waited for; matrix products, arithmetic and copies ran while one was open for 0% of the time, Pallas kernels for 20%

profile of v12, /device:TPU:32, one launch (start us, length us, event | category | flops | bytes accessed | tf_op | source)
XLA Modules:
  0.0 87.4 jit_solution(15643063121979621283)
XLA Ops:
  0.0 2.0 %block_states.1 = bf16[1024,128]{1,0:T(8,128)(2,1)S(1)} custom-call(bf16[512,1024]{1,0:T(8,128)(2,1)} %k_hbm.3, bf16[512,1024]{1,0:T(8,128)(2,1)} %v_hbm.3), custom_call_target="tpu_custom_call" | custom-call | flops 134217728 | bytes 2097152 | tf_op jit(solution)/shard_map/block_states/pallas_call | solution.py:88
  2.0 23.2 %all_to_all.23 = bf16[32,32,128]{2,1,0:T(8,128)(2,1)S(1)} all-to-all(bf16[32,32,128]{2,1,0:T(8,128)(2,1)S(1)} %bitcast.11), channel_id=1, replica_groups=mesh['chip'=32,'core'=2,'fsdp'=4] {'chip'}, dimensions={0} | all-to-all | bytes 524288 | tf_op jit(solution)/shard_map/all_to_all | solution.py:328
  25.2 1.5 %collective-permute-done.other_ref = bf16[1024,128]{1,0:T(8,128)(2,1)S(1)} collective-permute-done((bf16[1024,128]{1,0:T(8,128)(2,1)S(1)}, bf16[1024,128]{1,0:T(8,128)(2,1)S(1)}, u32[]{:S(2)}, u32[]{:S(2)}) %collective-permute-start) | collective-permute-done | bytes 262176 | tf_op jit(solution)/shard_map/ppermute | solution.py:329
  27.5 4.6 %all-to-all-start.1 = ((bf16[32,32,128]{2,1,0:T(8,128)(2,1)}), bf16[32,32,128]{2,1,0:T(8,128)(2,1)S(1)}, u32[]{:S(2)}, u32[]{:S(2)}) async-start(bf16[32,32,128]{2,1,0:T(8,128)(2,1)} %bitcast.3), calls=%async_computation.1 | async-start | bytes 524288 | tf_op jit(solution)/shard_map/all_to_all | solution.py:331
  32.1 3.8 %within_all.1 = (bf16[512,1024]{1,0:T(8,128)(2,1)S(1)}, f32[512,1024]{1,0:T(8,128)S(1)}) custom-call(bf16[512,1024]{1,0:T(8,128)(2,1)} %q_hbm.1, bf16[512,1024]{1,0:T(8,128)(2,1)} %k_hbm.3, bf16[512,1024]{1,0:T(8,128)(2,1)} %v_hbm.3), custom_call_target="tpu_custom_call" | custom-call | flops 1073741824 | bytes 5242880 | tf_op jit(solution)/shard_map/within_all/pallas_call | solution.py:149
  36.0 8.7 %all-to-all-done.1 = bf16[32,32,128]{2,1,0:T(8,128)(2,1)S(1)} async-done(((bf16[32,32,128]{2,1,0:T(8,128)(2,1)}), bf16[32,32,128]{2,1,0:T(8,128)(2,1)S(1)}, u32[]{:S(2)}, u32[]{:S(2)}) %all-to-all-start.1) | async-done | bytes 262176 | tf_op jit(solution)/shard_map/all_to_all | solution.py:331
  44.7 1.1 %finish_heads.7.refs_1_ = bf16[512,256]{1,0:T(8,128)(2,1)} custom-call(bf16[512,1024]{1,0:T(8,128)(2,1)S(1)} %get-tuple-element.17.q_ref, f32[512,1024]{1,0:T(8,128)S(1)} %get-tuple-element.18.within_ref, bf16[1024,128]{1,0:T(8,128)(2,1)S(1)} %bitcast.7, f32[1,1024]{1,0:T(1,128)S(1)} %bitcast.14), custom_call_target="tpu_custom_call" | custom-call | flops 67108864 | bytes 1048576 | tf_op jit(solution)/shard_map/finish_heads/pallas_call | solution.py:176
  45.8 3.0 %collective-permute-start.6 = (bf16[512,256]{1,0:T(8,128)(2,1)}, bf16[512,256]{1,0:T(8,128)(2,1)S(1)}, u32[]{:S(2)}, u32[]{:S(2)}) collective-permute-start(bf16[512,256]{1,0:T(8,128)(2,1)} %finish_heads.7.refs_1_), channel_id=1, source_target_pairs={{0,3},{1,0},{2,1},{3,2},{4,7},{5,4},{6,5},{7,6},{8,11},{9,8},{10,9... | collective-permute-start | bytes 786440 | tf_op jit(solution)/shard_map/ppermute | solution.py:319
  48.8 1.1 %finish_heads.6.refs_0_ = bf16[512,256]{1,0:T(8,128)(2,1)} custom-call(bf16[512,1024]{1,0:T(8,128)(2,1)S(1)} %get-tuple-element.17.q_ref, f32[512,1024]{1,0:T(8,128)S(1)} %get-tuple-element.18.within_ref, bf16[1024,128]{1,0:T(8,128)(2,1)S(1)} %bitcast.8, f32[1,1024]{1,0:T(1,128)S(1)} %bitcast.15), custom_call_target="tpu_custom_call" | custom-call | flops 67108864 | bytes 1048576 | tf_op jit(solution)/shard_map/finish_heads/pallas_call | solution.py:176
  50.5 2.7 %collective-permute-start.8 = (bf16[512,256]{1,0:T(8,128)(2,1)}, bf16[512,256]{1,0:T(8,128)(2,1)}, u32[]{:S(2)}, u32[]{:S(2)}) collective-permute-start(bf16[512,256]{1,0:T(8,128)(2,1)} %finish_heads.6.refs_0_), channel_id=1, source_target_pairs={{0,3},{1,0},{2,1},{3,2},{4,7},{5,4},{6,5},{7,6},{8,11},{9,8},{10,9... | collective-permute-start | bytes 786440 | tf_op jit(solution)/shard_map/ppermute | solution.py:319
  53.2 1.1 %finish_heads.5.refs_3_ = bf16[512,256]{1,0:T(8,128)(2,1)} custom-call(bf16[512,1024]{1,0:T(8,128)(2,1)S(1)} %get-tuple-element.17.q_ref, f32[512,1024]{1,0:T(8,128)S(1)} %get-tuple-element.18.within_ref, bf16[1024,128]{1,0:T(8,128)(2,1)S(1)} %bitcast.9, f32[1,1024]{1,0:T(1,128)S(1)} %bitcast.16), custom_call_target="tpu_custom_call" | custom-call | flops 67108864 | bytes 1048576 | tf_op jit(solution)/shard_map/finish_heads/pallas_call | solution.py:176
  54.3 2.0 %collective-permute-start.3 = (bf16[512,256]{1,0:T(8,128)(2,1)}, bf16[512,256]{1,0:T(8,128)(2,1)}, u32[]{:S(2)}, u32[]{:S(2)}) collective-permute-start(bf16[512,256]{1,0:T(8,128)(2,1)} %finish_heads.5.refs_3_), channel_id=1, source_target_pairs={{0,3},{1,0},{2,1},{3,2},{4,7},{5,4},{6,5},{7,6},{8,11},{9,8},{10,9... | collective-permute-start | bytes 786440 | tf_op jit(solution)/shard_map/ppermute | solution.py:319
  56.2 1.1 %finish_heads.4.refs_2_ = bf16[512,256]{1,0:T(8,128)(2,1)} custom-call(bf16[512,1024]{1,0:T(8,128)(2,1)S(1)} %get-tuple-element.17.q_ref, f32[512,1024]{1,0:T(8,128)S(1)} %get-tuple-element.18.within_ref, bf16[1024,128]{1,0:T(8,128)(2,1)S(1)} %bitcast.10, f32[1,1024]{1,0:T(1,128)S(1)} %bitcast.17), custom_call_target="tpu_custom_call" | custom-call | flops 67108864 | bytes 1048576 | tf_op jit(solution)/shard_map/finish_heads/pallas_call | solution.py:176
  58.1 2.5 %collective-permute-done.5.refs_0_ = bf16[512,256]{1,0:T(8,128)(2,1)S(1)} collective-permute-done((bf16[512,256]{1,0:T(8,128)(2,1)}, bf16[512,256]{1,0:T(8,128)(2,1)S(1)}, u32[]{:S(2)}, u32[]{:S(2)}) %collective-permute-start.5) | collective-permute-done | bytes 262176 | tf_op jit(solution)/shard_map/ppermute | solution.py:319
  61.3 3.7 %own_mix.1.refs_5_ = f32[512,1024]{1,0:T(8,128)S(1)} custom-call(s32[1]{0:T(128)} %bitcast.6.column_ref, bf16[512,256]{1,0:T(8,128)(2,1)} %finish_heads.6.refs_0_, bf16[512,256]{1,0:T(8,128)(2,1)} %finish_heads.7.refs_1_, bf16[512,256]{1,0:T(8,128)(2,1)} %finish_heads.4.refs_2_, bf16[512,256]{1,0:T(8,128)(2,1)} %finish_heads.5.refs_3_, ...), custom_call_target="tpu_custom_call" | custom-call | flops 1073741824 | bytes 2097152 | tf_op jit(solution)/shard_map/own_mix/pallas_call | solution.py:218
  65.0 1.3 %collective-permute-done.7.refs_1_ = bf16[512,256]{1,0:T(8,128)(2,1)} collective-permute-done((bf16[512,256]{1,0:T(8,128)(2,1)}, bf16[512,256]{1,0:T(8,128)(2,1)}, u32[]{:S(2)}, u32[]{:S(2)}) %collective-permute-start.7) | collective-permute-done | bytes 262176 | tf_op jit(solution)/shard_map/ppermute | solution.py:319
  66.3 2.0 %collective-permute-start.12 = (bf16[512,256]{1,0:T(8,128)(2,1)}, bf16[512,256]{1,0:T(8,128)(2,1)S(1)}, u32[]{:S(2)}, u32[]{:S(2)}) collective-permute-start(bf16[512,256]{1,0:T(8,128)(2,1)} %finish_heads.4.refs_2_), channel_id=1, source_target_pairs={{0,3},{1,0},{2,1},{3,2},{4,7},{5,4},{6,5},{7,6},{8,11},{9,8},{10,9... | collective-permute-start | bytes 786440 | tf_op jit(solution)/shard_map/ppermute | solution.py:319
  68.4 1.9 %collective-permute-start.9 = (bf16[512,256]{1,0:T(8,128)(2,1)S(1)}, bf16[512,256]{1,0:T(8,128)(2,1)S(1)}, u32[]{:S(2)}, u32[]{:S(2)}) collective-permute-start(bf16[512,256]{1,0:T(8,128)(2,1)S(1)} %copy-done.4), channel_id=1, source_target_pairs={{0,1},{1,2},{2,3},{3,0},{4,5},{5,6},{6,7},{7,4},{8,9},{9,10},{10,1... | collective-permute-start | bytes 786440 | tf_op jit(solution)/shard_map/ppermute | solution.py:319
  70.4 1.4 %collective-permute-done.1.refs_0_ = bf16[512,256]{1,0:T(8,128)(2,1)S(1)} collective-permute-done((bf16[512,256]{1,0:T(8,128)(2,1)}, bf16[512,256]{1,0:T(8,128)(2,1)S(1)}, u32[]{:S(2)}, u32[]{:S(2)}) %collective-permute-start.1) | collective-permute-done | bytes 262176 | tf_op jit(solution)/shard_map/ppermute | solution.py:319
  71.8 5.6 %collective-permute-done.11.refs_1_ = bf16[512,256]{1,0:T(8,128)(2,1)S(1)} collective-permute-done((bf16[512,256]{1,0:T(8,128)(2,1)}, bf16[512,256]{1,0:T(8,128)(2,1)S(1)}, u32[]{:S(2)}, u32[]{:S(2)}) %collective-permute-start.11) | collective-permute-done | bytes 262176 | tf_op jit(solution)/shard_map/ppermute | solution.py:319
  77.4 4.1 %side_mix.1 = (f32[512,1024]{1,0:T(8,128)S(1)}, bf16[3072,1024]{1,0:T(8,128)(2,1)S(1)}) custom-call(s32[1]{0:T(128)} %bitcast.6.column_ref, bf16[512,256]{1,0:T(8,128)(2,1)S(1)} %copy-done.4, bf16[512,256]{1,0:T(8,128)(2,1)} %collective-permute-done.7.refs_1_, bf16[512,256]{1,0:T(8,128)(2,1)} %collective-permute-done.8.refs_2_, ...), custom_call_target="tpu_custom_call" | custom-call | flops 3221225472 | bytes 6291456 | tf_op jit(solution)/shard_map/side_mix/pallas_call | solution.py:268
  81.5 2.2 %mix.3.refs_3_ = f32[512,1024]{1,0:T(8,128)S(1)} custom-call(bf16[512,256]{1,0:T(8,128)(2,1)S(1)} %collective-permute-done.1.refs_0_, bf16[512,256]{1,0:T(8,128)(2,1)S(1)} %collective-permute-done.11.refs_1_, bf16[512,256]{1,0:T(8,128)(2,1)S(1)} %collective-permute-done.12.refs_2_, bf16[512,256]{1,0:T(8,128)(2,1)} %collective-permute-done.3.refs_3_, ...), custom_call_target="tpu_custom_call" | custom-call | flops 1073741824 | bytes 2097152 | tf_op jit(solution)/shard_map/mix/pallas_call | solution.py:306
  84.5 1.1 %collective-permute-done.2.refs_0_ = bf16[512,256]{1,0:T(8,128)(2,1)S(1)} collective-permute-done((bf16[512,256]{1,0:T(8,128)(2,1)S(1)}, bf16[512,256]{1,0:T(8,128)(2,1)S(1)}, u32[]{:S(2)}, u32[]{:S(2)}) %collective-permute-start.2) | collective-permute-done | bytes 262176 | tf_op jit(solution)/shard_map/ppermute | solution.py:319
  85.6 1.6 %mix.5 = bf16[512,1024]{1,0:T(8,128)(2,1)} custom-call(bf16[512,256]{1,0:T(8,128)(2,1)S(1)} %collective-permute-done.2.refs_0_, bf16[512,256]{1,0:T(8,128)(2,1)S(1)} %collective-permute-done.4.refs_1_, bf16[3072,1024]{1,0:T(8,128)(2,1)S(1)} %get-tuple-element.23.refs_4_.refs_2_, f32[512,1024]{1,0:T(8,128)S(1)} %mix.4.refs_3_), custom_call_target="tpu_custom_call" | custom-call | flops 536870912 | bytes 1048576 | tf_op jit(solution)/shard_map/mix/pallas_call | solution.py:306
  (27 shorter events, 3.7 us)
Async XLA Ops:
  25.2 1.5 %collective-permute-start = (bf16[1024,128]{1,0:T(8,128)(2,1)S(1)}, bf16[1024,128]{1,0:T(8,128)(2,1)S(1)}, u32[]{:S(2)}, u32[]{:S(2)}) collective-permute-start(bf16[1024,128]{1,0:T(8,128)(2,1)S(1)} %bitcast.12), channel_id=1, source_target_pairs={{0,4},{4,0},{1,5},{5,1},{2,6},{6,2},{3,7},{7,3},{8,12},{12,8},{9,1... | collective-permute-start | bytes 786440 | tf_op jit(solution)/shard_map/ppermute | solution.py:329
  27.5 17.2 %all-to-all-start.1 = ((bf16[32,32,128]{2,1,0:T(8,128)(2,1)}), bf16[32,32,128]{2,1,0:T(8,128)(2,1)S(1)}, u32[]{:S(2)}, u32[]{:S(2)}) async-start(bf16[32,32,128]{2,1,0:T(8,128)(2,1)} %bitcast.3), calls=%async_computation.1 | async-start | bytes 524288 | tf_op jit(solution)/shard_map/all_to_all | solution.py:331
  32.1 12.5 %copy-start = (f32[1024]{0:T(1024)S(1)}, f32[1024]{0:T(1024)}, u32[]{:S(2)}) copy-start(f32[1024]{0:T(1024)} %param.8) | copy-start | bytes 12292
  45.8 11.6 %collective-permute-start.6 = (bf16[512,256]{1,0:T(8,128)(2,1)}, bf16[512,256]{1,0:T(8,128)(2,1)S(1)}, u32[]{:S(2)}, u32[]{:S(2)}) collective-permute-start(bf16[512,256]{1,0:T(8,128)(2,1)} %finish_heads.7.refs_1_), channel_id=1, source_target_pairs={{0,3},{1,0},{2,1},{3,2},{4,7},{5,4},{6,5},{7,6},{8,11},{9,8},{10,9... | collective-permute-start | bytes 786440 | tf_op jit(solution)/shard_map/ppermute | solution.py:319
  49.9 10.7 %collective-permute-start.5 = (bf16[512,256]{1,0:T(8,128)(2,1)}, bf16[512,256]{1,0:T(8,128)(2,1)S(1)}, u32[]{:S(2)}, u32[]{:S(2)}) collective-permute-start(bf16[512,256]{1,0:T(8,128)(2,1)} %finish_heads.6.refs_0_), channel_id=1, source_target_pairs={{0,1},{1,2},{2,3},{3,0},{4,5},{5,6},{6,7},{7,4},{8,9},{9,10},{10,1... | collective-permute-start | bytes 786440 | tf_op jit(solution)/shard_map/ppermute | solution.py:319
  49.9 16.4 %collective-permute-start.7 = (bf16[512,256]{1,0:T(8,128)(2,1)}, bf16[512,256]{1,0:T(8,128)(2,1)}, u32[]{:S(2)}, u32[]{:S(2)}) collective-permute-start(bf16[512,256]{1,0:T(8,128)(2,1)} %finish_heads.7.refs_1_), channel_id=1, source_target_pairs={{0,1},{1,2},{2,3},{3,0},{4,5},{5,6},{6,7},{7,4},{8,9},{9,10},{10,1... | collective-permute-start | bytes 786440 | tf_op jit(solution)/shard_map/ppermute | solution.py:319
  50.5 17.8 %collective-permute-start.8 = (bf16[512,256]{1,0:T(8,128)(2,1)}, bf16[512,256]{1,0:T(8,128)(2,1)}, u32[]{:S(2)}, u32[]{:S(2)}) collective-permute-start(bf16[512,256]{1,0:T(8,128)(2,1)} %finish_heads.6.refs_0_), channel_id=1, source_target_pairs={{0,3},{1,0},{2,1},{3,2},{4,7},{5,4},{6,5},{7,6},{8,11},{9,8},{10,9... | collective-permute-start | bytes 786440 | tf_op jit(solution)/shard_map/ppermute | solution.py:319
  54.3 14.2 %collective-permute-start.3 = (bf16[512,256]{1,0:T(8,128)(2,1)}, bf16[512,256]{1,0:T(8,128)(2,1)}, u32[]{:S(2)}, u32[]{:S(2)}) collective-permute-start(bf16[512,256]{1,0:T(8,128)(2,1)} %finish_heads.5.refs_3_), channel_id=1, source_target_pairs={{0,3},{1,0},{2,1},{3,2},{4,7},{5,4},{6,5},{7,6},{8,11},{9,8},{10,9... | collective-permute-start | bytes 786440 | tf_op jit(solution)/shard_map/ppermute | solution.py:319
  57.4 0.7 copy-start.1
  57.4 14.4 %collective-permute-start.1 = (bf16[512,256]{1,0:T(8,128)(2,1)}, bf16[512,256]{1,0:T(8,128)(2,1)S(1)}, u32[]{:S(2)}, u32[]{:S(2)}) collective-permute-start(bf16[512,256]{1,0:T(8,128)(2,1)} %finish_heads.4.refs_2_), channel_id=1, source_target_pairs={{0,1},{1,2},{2,3},{3,0},{4,5},{5,6},{6,7},{7,4},{8,9},{9,10},{10,1... | collective-permute-start | bytes 786440 | tf_op jit(solution)/shard_map/ppermute | solution.py:319
  60.6 0.7 copy-start.3
  61.2 16.2 %collective-permute-start.11 = (bf16[512,256]{1,0:T(8,128)(2,1)}, bf16[512,256]{1,0:T(8,128)(2,1)S(1)}, u32[]{:S(2)}, u32[]{:S(2)}) collective-permute-start(bf16[512,256]{1,0:T(8,128)(2,1)} %finish_heads.5.refs_3_), channel_id=1, source_target_pairs={{0,1},{1,2},{2,3},{3,0},{4,5},{5,6},{6,7},{7,4},{8,9},{9,10},{10,1... | collective-permute-start | bytes 786440 | tf_op jit(solution)/shard_map/ppermute | solution.py:319
  61.3 7.1 %copy-start.2 = (bf16[512,256]{1,0:T(8,128)(2,1)S(1)}, bf16[512,256]{1,0:T(8,128)(2,1)}, u32[]{:S(2)}) copy-start(bf16[512,256]{1,0:T(8,128)(2,1)} %copy-done.1) | copy-start | bytes 786436
  61.3 7.2 %copy-start.4 = (bf16[512,256]{1,0:T(8,128)(2,1)S(1)}, bf16[512,256]{1,0:T(8,128)(2,1)}, u32[]{:S(2)}) copy-start(bf16[512,256]{1,0:T(8,128)(2,1)} %copy-done.3) | copy-start | bytes 786436
  66.3 15.3 %collective-permute-start.12 = (bf16[512,256]{1,0:T(8,128)(2,1)}, bf16[512,256]{1,0:T(8,128)(2,1)S(1)}, u32[]{:S(2)}, u32[]{:S(2)}) collective-permute-start(bf16[512,256]{1,0:T(8,128)(2,1)} %finish_heads.4.refs_2_), channel_id=1, source_target_pairs={{0,3},{1,0},{2,1},{3,2},{4,7},{5,4},{6,5},{7,6},{8,11},{9,8},{10,9... | collective-permute-start | bytes 786440 | tf_op jit(solution)/shard_map/ppermute | solution.py:319
  68.3 15.4 %collective-permute-start.10 = (bf16[512,256]{1,0:T(8,128)(2,1)S(1)}, bf16[512,256]{1,0:T(8,128)(2,1)S(1)}, u32[]{:S(2)}, u32[]{:S(2)}) collective-permute-start(bf16[512,256]{1,0:T(8,128)(2,1)S(1)} %copy-done.2), channel_id=1, source_target_pairs={{0,3},{1,0},{2,1},{3,2},{4,7},{5,4},{6,5},{7,6},{8,11},{9,8},{10,9... | collective-permute-start | bytes 786440 | tf_op jit(solution)/shard_map/ppermute | solution.py:319
  68.4 15.3 %collective-permute-start.9 = (bf16[512,256]{1,0:T(8,128)(2,1)S(1)}, bf16[512,256]{1,0:T(8,128)(2,1)S(1)}, u32[]{:S(2)}, u32[]{:S(2)}) collective-permute-start(bf16[512,256]{1,0:T(8,128)(2,1)S(1)} %copy-done.4), channel_id=1, source_target_pairs={{0,1},{1,2},{2,3},{3,0},{4,5},{5,6},{6,7},{7,4},{8,9},{9,10},{10,1... | collective-permute-start | bytes 786440 | tf_op jit(solution)/shard_map/ppermute | solution.py:319
  71.8 12.7 %collective-permute-start.4 = (bf16[512,256]{1,0:T(8,128)(2,1)}, bf16[512,256]{1,0:T(8,128)(2,1)S(1)}, u32[]{:S(2)}, u32[]{:S(2)}) collective-permute-start(bf16[512,256]{1,0:T(8,128)(2,1)} %collective-permute-done.3.refs_3_), channel_id=1, source_target_pairs={{0,3},{1,0},{2,1},{3,2},{4,7},{5,4},{6,5},{7,6},{8,11},{9,8},{10,9... | collective-permute-start | bytes 786440 | tf_op jit(solution)/shard_map/ppermute | solution.py:319
  77.4 8.2 %collective-permute-start.2 = (bf16[512,256]{1,0:T(8,128)(2,1)S(1)}, bf16[512,256]{1,0:T(8,128)(2,1)S(1)}, u32[]{:S(2)}, u32[]{:S(2)}) collective-permute-start(bf16[512,256]{1,0:T(8,128)(2,1)S(1)} %collective-permute-done.1.refs_0_), channel_id=1, source_target_pairs={{0,1},{1,2},{2,3},{3,0},{4,5},{5,6},{6,7},{7,4},{8,9},{9,10},{10,1... | collective-permute-start | bytes 786440 | tf_op jit(solution)/shard_map/ppermute | solution.py:319

commit v13 on v11

--- a/solution.py
+++ b/solution.py
@@ -124,37 +124,48 @@
     )(core, own, other)
 
 
-def within_kernel(q_hbm, k_hbm, v_hbm, q_ref, out_ref, k_ref, v_ref, sems):
+def within_kernel(q_hbm, k_hbm, v_hbm, qa_ref, a_ref, b_hbm, q_ref, k_ref, v_ref, b_ref, sems):
     copies, split = [], CALLS[0][1] * DH
     parts = (slice(0, split), slice(split, HEADS * DH))
     for part, cols in enumerate(parts):
-        for at, (hbm, ref) in enumerate(((q_hbm, q_ref), (k_hbm, k_ref), (v_hbm, v_ref))):
-            copies.append(
-                pltpu.make_async_copy(hbm.at[:, cols], ref.at[:, cols], sems.at[part, at])
-            )
+        q_part = qa_ref if part == 0 else q_ref
+        sources = (q_hbm.at[:, cols], k_hbm.at[:, cols], v_hbm.at[:, cols])
+        targets = (q_part, k_ref.at[part], v_ref.at[part])
+        for at, (source, target) in enumerate(zip(sources, targets)):
+            copies.append(pltpu.make_async_copy(source, target, sems.at[part, at]))
             copies[-1].start()
     causal = causal_mask()
     for part, (first, last) in enumerate(CALLS):
         for copy in copies[3 * part : 3 * part + 3]:
             copy.wait()
-        for h in range(first, last):
+        q_part, out_ref = (qa_ref, a_ref) if part == 0 else (q_ref, b_ref)
+        for h in range(last - first):
             cols = slice(h * DH, (h + 1) * DH)
-            top, bottom = within_block(q_ref, k_ref, v_ref, h, causal)
+            top, bottom = within_block(q_part, k_ref.at[part], v_ref.at[part], h, causal)
             out_ref[:HALF, cols] = top
             out_ref[HALF:, cols] = bottom
+    copy = pltpu.make_async_copy(b_ref, b_hbm, sems.at[0, 0])
+    copy.start()
+    copy.wait()
 
 
 def within_all(q, k, v):
-    shape = (BLK, HEADS * DH)
+    shape = (BLK, HEADS // 2 * DH)
     return pl.pallas_call(
         within_kernel,
         name="within_all",
         in_specs=[HBM] * 3,
-        out_specs=[VMEM, VMEM],
-        out_shape=[pltpu.VMEM(shape, BF16), pltpu.VMEM(shape, F32)],
+        out_specs=[VMEM, VMEM, HBM],
+        out_shape=[
+            pltpu.VMEM(shape, BF16),
+            pltpu.VMEM(shape, F32),
+            jax.ShapeDtypeStruct(shape, F32),
+        ],
         scratch_shapes=[
             pltpu.VMEM(shape, BF16),
-            pltpu.VMEM(shape, BF16),
+            pltpu.VMEM((2, *shape), BF16),
+            pltpu.VMEM((2, *shape), BF16),
+            pltpu.VMEM(shape, F32),
             pltpu.SemaphoreType.DMA((2, 3)),
         ],
         compiler_params=PARAMS,
@@ -162,23 +173,39 @@
     )(in_hbm(q), in_hbm(k), in_hbm(v))
 
 
-def finish_kernel(q_ref, within_ref, carried_ref, gain_ref, out_ref, *, first, last):
+def finish_kernel(q_ref, within_ref, carried_ref, gain_ref, out_ref, *scratch, first, last):
+    if scratch:
+        q_hbm, within_hbm = q_ref.at[:, first * DH : last * DH], within_ref
+        q_ref, within_ref, sems = scratch
+        copies = [
+            pltpu.make_async_copy(q_hbm, q_ref, sems.at[0]),
+            pltpu.make_async_copy(within_hbm, within_ref, sems.at[1]),
+        ]
+        for copy in copies:
+            copy.start()
+        for copy in copies:
+            copy.wait()
     for h in range(first, last):
         cols = slice(h * DH, (h + 1) * DH)
         out_cols = slice((h - first) * DH, (h - first + 1) * DH)
         out_ref[:, out_cols] = finish(
-            q_ref[:, cols], within_ref[:, cols], carried_ref[cols, :], gain_ref[:, cols]
+            q_ref[:, out_cols], within_ref[:, out_cols], carried_ref[cols, :], gain_ref[:, cols]
         )
 
 
-def finish_heads(q, within, carried, gain, first, last):
+def finish_heads(q, within, carried, gain, first, last, fetch=False):
     heads = last - first
+    shape = (BLK, heads * DH)
+    scratch = [pltpu.VMEM(shape, BF16), pltpu.VMEM(shape, F32), pltpu.SemaphoreType.DMA((2,))]
+    if fetch:
+        q, within = in_hbm(q), in_hbm(within)
     return pl.pallas_call(
         functools.partial(finish_kernel, first=first, last=last),
         name="finish_heads",
-        in_specs=[VMEM] * 4,
+        in_specs=[HBM if fetch else VMEM] * 2 + [VMEM] * 2,
         out_specs=VMEM,
-        out_shape=jax.ShapeDtypeStruct((BLK, heads * DH), BF16),
+        out_shape=jax.ShapeDtypeStruct(shape, BF16),
+        scratch_shapes=scratch if fetch else [],
         compiler_params=PARAMS,
         cost_estimate=cost(4 * BLK * DH * DH * heads, BLK * DH * heads * 8),
     )(q, within, carried, gain)
@@ -329,11 +356,13 @@
     other = lax.ppermute(own, "core", [(0, 1), (1, 0)])
     sums = exclusive_sums(core, own, other, chips)
     carried = lax.all_to_all(sums, "chip", 0, 0, tiled=True)
-    q, within = within_all(q, k, v)
-    carried, q, within = lax.optimization_barrier((carried, q, within))
+    q_a, within_a, within_b = within_all(q, k, v)
+    carried, q_a, within_a, within_b = lax.optimization_barrier(
+        (carried, q_a, within_a, within_b)
+    )
     (a0, a1), (b0, b1) = CALLS
-    mine_a = finish_heads(q, within, carried, gain_row, a0, a1)
-    mine_b = finish_heads(q, within, carried, gain_row, b0, b1)
+    mine_a = finish_heads(q_a, within_a, carried, gain_row, a0, a1)
+    mine_b = finish_heads(q, within_b, carried, gain_row, b0, b1, True)
     total = own_mix(column, w, [mine_a, mine_b])
     left_a, right_a, total = lax.optimization_barrier(
         (along(mine_a, 1, ways), along(mine_a, -1, ways), total)

time: 85.7 us -> 84.9 us (level)
  Pallas kernels: 21 us -> 18.5 us
  local copies, waits for them, and re-layouts: 0.01 us -> 0.97 us
    ppermute x6, waiting for transfers between devices: 15.8 us -> 17.2 us  [along(): lax.ppermute(value, 'fsdp', [(i, (i + shift) % count) for i in range(coun...]
    pallas_call x1, Pallas kernels: 3.75 us -> 2.55 us  [own_mix(): pl.pallas_call(own_kernel, name='own_mix', in_specs=[SMEM] + [VMEM] * len...]
    pallas_call x1, Pallas kernels: 4.37 us -> 3.19 us  [side_mix(): pl.pallas_call(functools.partial(side_kernel, starts=starts), name='side_...]
    all_to_all x1, waiting for transfers between devices: 8.7 us -> 7.66 us  [shards(): carried = lax.all_to_all(sums, 'chip', 0, 0, tiled=True)]
    unnamed x2 -> x4, local copies, waits for them, and re-layouts: 0.01 us -> 0.97 us
  transfers between devices with their start and end apart: 8 -> 8, of which waited for: 6 -> 6; matrix products, arithmetic and copies ran while one was open for 0% -> 0% of each run, Pallas kernels for 18% -> 16%
where the time goes in v13:
time: 84.9 us; the launch traced here: 83.7 us
  waiting for transfers between devices  26.4 us (31%)
  blocking collectives  23.2 us (27%)
  Pallas kernels  18.5 us (22%)
  starting transfers between devices  14.4 us (17%)
  local copies, waits for them, and re-layouts  0.97 us (1%)
    all_to_all x1, blocking collectives, shards(): own = lax.all_to_all(states, 'chip', 0, 0, tiled=True)  23.2 us
    ppermute x6, waiting for transfers between devices, along(): lax.ppermute(value, 'fsdp', [(i, (i + shift) % count) for i in range(coun...  17.2 us
    ppermute x6, starting transfers between devices, along(): lax.ppermute(value, 'fsdp', [(i, (i + shift) % count) for i in range(coun...  9.76 us
    all_to_all x1, waiting for transfers between devices, shards(): carried = lax.all_to_all(sums, 'chip', 0, 0, tiled=True)  7.66 us
    all_to_all x1, starting transfers between devices, shards(): carried = lax.all_to_all(sums, 'chip', 0, 0, tiled=True)  4.61 us
    pallas_call x1, Pallas kernels, within_all(): pl.pallas_call(within_kernel, name='within_all', in_specs=[HBM] * 3, out_...  3.89 us
    pallas_call x3, Pallas kernels, mix(): pl.pallas_call(functools.partial(mix_kernel, count=len(arrays), starts=st...  3.57 us
    pallas_call x1, Pallas kernels, side_mix(): pl.pallas_call(functools.partial(side_kernel, starts=starts), name='side_...  3.19 us
  transfers between devices with their start and end apart: 8, of which 6 were waited for; matrix products, arithmetic and copies ran while one was open for 0% of the time, Pallas kernels for 16%

profile of v13, /device:TPU:32, one launch (start us, length us, event | category | flops | bytes accessed | tf_op | source)
XLA Modules:
  0.0 83.7 jit_solution(13127802111085280447)
XLA Ops:
  0.0 2.0 %block_states.1 = bf16[1024,128]{1,0:T(8,128)(2,1)S(1)} custom-call(bf16[512,1024]{1,0:T(8,128)(2,1)} %k_hbm.3, bf16[512,1024]{1,0:T(8,128)(2,1)} %v_hbm.3), custom_call_target="tpu_custom_call" | custom-call | flops 134217728 | bytes 2097152 | tf_op jit(solution)/shard_map/block_states/pallas_call | solution.py:88
  2.0 23.2 %all_to_all.23 = bf16[32,32,128]{2,1,0:T(8,128)(2,1)S(1)} all-to-all(bf16[32,32,128]{2,1,0:T(8,128)(2,1)S(1)} %bitcast.9), channel_id=1, replica_groups=mesh['chip'=32,'core'=2,'fsdp'=4] {'chip'}, dimensions={0} | all-to-all | bytes 524288 | tf_op jit(solution)/shard_map/all_to_all | solution.py:355
  25.2 1.5 %collective-permute-done.other_ref = bf16[1024,128]{1,0:T(8,128)(2,1)S(1)} collective-permute-done((bf16[1024,128]{1,0:T(8,128)(2,1)S(1)}, bf16[1024,128]{1,0:T(8,128)(2,1)S(1)}, u32[]{:S(2)}, u32[]{:S(2)}) %collective-permute-start) | collective-permute-done | bytes 262176 | tf_op jit(solution)/shard_map/ppermute | solution.py:356
  26.7 0.8 exclusive_sums.1
  27.5 4.6 %all-to-all-start.1 = ((bf16[32,32,128]{2,1,0:T(8,128)(2,1)}), bf16[32,32,128]{2,1,0:T(8,128)(2,1)S(1)}, u32[]{:S(2)}, u32[]{:S(2)}) async-start(bf16[32,32,128]{2,1,0:T(8,128)(2,1)} %bitcast.3), calls=%async_computation.1 | async-start | bytes 524288 | tf_op jit(solution)/shard_map/all_to_all | solution.py:358
  32.1 3.9 %within_all.1 = (bf16[512,512]{1,0:T(8,128)(2,1)S(1)}, f32[512,512]{1,0:T(8,128)S(1)}, f32[512,512]{1,0:T(8,128)S(1)}) custom-call(bf16[512,1024]{1,0:T(8,128)(2,1)} %q_ref.1, bf16[512,1024]{1,0:T(8,128)(2,1)} %k_hbm.3, bf16[512,1024]{1,0:T(8,128)(2,1)} %v_hbm.3), custom_call_target="tpu_custom_call" | custom-call | flops 1073741824 | bytes 5242880 | tf_op jit(solution)/shard_map/within_all/pallas_call | solution.py:154
  36.1 1.0 %copy-done = f32[512,512]{1,0:T(8,128)} copy-done((f32[512,512]{1,0:T(8,128)}, f32[512,512]{1,0:T(8,128)S(1)}, u32[]{:S(2)}) %copy-start) | copy-done | bytes 1048600
  37.0 7.7 %all-to-all-done.1 = bf16[32,32,128]{2,1,0:T(8,128)(2,1)S(1)} async-done(((bf16[32,32,128]{2,1,0:T(8,128)(2,1)}), bf16[32,32,128]{2,1,0:T(8,128)(2,1)S(1)}, u32[]{:S(2)}, u32[]{:S(2)}) %all-to-all-start.1) | async-done | bytes 262176 | tf_op jit(solution)/shard_map/all_to_all | solution.py:358
  44.7 0.5 finish_heads.3.refs_0_
  45.2 1.7 %collective-permute-start.3 = (bf16[512,512]{1,0:T(8,128)(2,1)S(1)}, bf16[512,512]{1,0:T(8,128)(2,1)S(1)}, u32[]{:S(2)}, u32[]{:S(2)}) collective-permute-start(bf16[512,512]{1,0:T(8,128)(2,1)S(1)} %finish_heads.3.refs_0_), channel_id=1, source_target_pairs={{0,1},{1,2},{2,3},{3,0},{4,5},{5,6},{6,7},{7,4},{8,9},{9,10},{10,1... | collective-permute-start | bytes 1572872 | tf_op jit(solution)/shard_map/ppermute | solution.py:346
  46.9 1.7 %collective-permute-start.4 = (bf16[512,512]{1,0:T(8,128)(2,1)S(1)}, bf16[512,512]{1,0:T(8,128)(2,1)S(1)}, u32[]{:S(2)}, u32[]{:S(2)}) collective-permute-start(bf16[512,512]{1,0:T(8,128)(2,1)S(1)} %finish_heads.3.refs_0_), channel_id=1, source_target_pairs={{0,3},{1,0},{2,1},{3,2},{4,7},{5,4},{6,5},{7,6},{8,11},{9,8},{10,9... | collective-permute-start | bytes 1572872 | tf_op jit(solution)/shard_map/ppermute | solution.py:346
  48.5 1.9 %finish_heads.2.refs_1_ = bf16[512,512]{1,0:T(8,128)(2,1)S(1)} custom-call(bf16[512,1024]{1,0:T(8,128)(2,1)} %q_ref.1, f32[512,512]{1,0:T(8,128)} %copy-done, bf16[1024,128]{1,0:T(8,128)(2,1)S(1)} %bitcast.8, f32[1,1024]{1,0:T(1,128)S(1)} %bitcast.13), custom_call_target="tpu_custom_call" | custom-call | flops 134217728 | bytes 2097152 | tf_op jit(solution)/shard_map/finish_heads/pallas_call | solution.py:202
  50.5 1.9 %collective-permute-start.1 = (bf16[512,512]{1,0:T(8,128)(2,1)S(1)}, bf16[512,512]{1,0:T(8,128)(2,1)S(1)}, u32[]{:S(2)}, u32[]{:S(2)}) collective-permute-start(bf16[512,512]{1,0:T(8,128)(2,1)S(1)} %finish_heads.2.refs_1_), channel_id=1, source_target_pairs={{0,3},{1,0},{2,1},{3,2},{4,7},{5,4},{6,5},{7,6},{8,11},{9,8},{10,9... | collective-permute-start | bytes 1572872 | tf_op jit(solution)/shard_map/ppermute | solution.py:346
  52.6 2.5 %own_mix.1.refs_3_ = f32[512,1024]{1,0:T(8,128)S(1)} custom-call(s32[1]{0:T(128)} %bitcast.6.column_ref, bf16[512,512]{1,0:T(8,128)(2,1)S(1)} %finish_heads.3.refs_0_, bf16[512,512]{1,0:T(8,128)(2,1)S(1)} %finish_heads.2.refs_1_, bf16[4096,1024]{1,0:T(8,128)(2,1)} %refs_2_.3), custom_call_target="tpu_custom_call" | custom-call | flops 1073741824 | bytes 2097152 | tf_op jit(solution)/shard_map/own_mix/pallas_call | solution.py:245
  55.1 6.2 %collective-permute-done.3.refs_0_ = bf16[512,512]{1,0:T(8,128)(2,1)S(1)} collective-permute-done((bf16[512,512]{1,0:T(8,128)(2,1)S(1)}, bf16[512,512]{1,0:T(8,128)(2,1)S(1)}, u32[]{:S(2)}, u32[]{:S(2)}) %collective-permute-start.3) | collective-permute-done | bytes 524320 | tf_op jit(solution)/shard_map/ppermute | solution.py:346
  61.4 0.4 collective-permute-done.4.refs_1_
  61.7 1.6 %collective-permute-start.5 = (bf16[512,512]{1,0:T(8,128)(2,1)S(1)}, bf16[512,512]{1,0:T(8,128)(2,1)S(1)}, u32[]{:S(2)}, u32[]{:S(2)}) collective-permute-start(bf16[512,512]{1,0:T(8,128)(2,1)S(1)} %collective-permute-done.3.refs_0_), channel_id=1, source_target_pairs={{0,1},{1,2},{2,3},{3,0},{4,5},{5,6},{6,7},{7,4},{8,9},{9,10},{10,1... | collective-permute-start | bytes 1572872 | tf_op jit(solution)/shard_map/ppermute | solution.py:346
  63.3 6.9 %collective-permute-done.1.refs_1_ = bf16[512,512]{1,0:T(8,128)(2,1)S(1)} collective-permute-done((bf16[512,512]{1,0:T(8,128)(2,1)S(1)}, bf16[512,512]{1,0:T(8,128)(2,1)S(1)}, u32[]{:S(2)}, u32[]{:S(2)}) %collective-permute-start.1) | collective-permute-done | bytes 524320 | tf_op jit(solution)/shard_map/ppermute | solution.py:346
  70.2 2.8 %collective-permute-start.2 = (bf16[512,512]{1,0:T(8,128)(2,1)S(1)}, bf16[512,512]{1,0:T(8,128)(2,1)S(1)}, u32[]{:S(2)}, u32[]{:S(2)}) collective-permute-start(bf16[512,512]{1,0:T(8,128)(2,1)S(1)} %collective-permute-done.1.refs_1_), channel_id=1, source_target_pairs={{0,3},{1,0},{2,1},{3,2},{4,7},{5,4},{6,5},{7,6},{8,11},{9,8},{10,9... | collective-permute-start | bytes 1572872 | tf_op jit(solution)/shard_map/ppermute | solution.py:346
  73.0 3.2 %side_mix.1 = (f32[512,1024]{1,0:T(8,128)S(1)}, bf16[3072,1024]{1,0:T(8,128)(2,1)S(1)}) custom-call(s32[1]{0:T(128)} %bitcast.6.column_ref, bf16[512,512]{1,0:T(8,128)(2,1)S(1)} %collective-permute-done.3.refs_0_, bf16[512,512]{1,0:T(8,128)(2,1)S(1)} %collective-permute-done.4.refs_1_, bf16[4096,1024]{1,0:T(8,128)(2,1)} %refs_2_.3, ...), custom_call_target="tpu_custom_call" | custom-call | flops 3221225472 | bytes 6291456 | tf_op jit(solution)/shard_map/side_mix/pallas_call | solution.py:295
  76.2 1.2 %mix.3.refs_2_ = f32[512,1024]{1,0:T(8,128)S(1)} custom-call(bf16[512,512]{1,0:T(8,128)(2,1)S(1)} %collective-permute-done.6.refs_0_, bf16[512,512]{1,0:T(8,128)(2,1)S(1)} %collective-permute-done.1.refs_1_, bf16[3072,1024]{1,0:T(8,128)(2,1)S(1)} %get-tuple-element.27.refs_2_.refs_1_, f32[512,1024]{1,0:T(8,128)S(1)} %get-tuple-element.28.refs_3_), custom_call_target="tpu_custom_call" | custom-call | flops 1073741824 | bytes 2097152 | tf_op jit(solution)/shard_map/mix/pallas_call | solution.py:333
  77.4 3.7 %collective-permute-done.5.refs_0_ = bf16[512,512]{1,0:T(8,128)(2,1)S(1)} collective-permute-done((bf16[512,512]{1,0:T(8,128)(2,1)S(1)}, bf16[512,512]{1,0:T(8,128)(2,1)S(1)}, u32[]{:S(2)}, u32[]{:S(2)}) %collective-permute-start.5) | collective-permute-done | bytes 524320 | tf_op jit(solution)/shard_map/ppermute | solution.py:346
  81.2 0.7 mix.4.refs_2_
  81.9 1.6 %mix.5 = bf16[512,1024]{1,0:T(8,128)(2,1)} custom-call(bf16[512,512]{1,0:T(8,128)(2,1)S(1)} %collective-permute-done.2.refs_0_, bf16[3072,1024]{1,0:T(8,128)(2,1)S(1)} %get-tuple-element.27.refs_2_.refs_1_, f32[512,1024]{1,0:T(8,128)S(1)} %mix.4.refs_2_), custom_call_target="tpu_custom_call" | custom-call | flops 536870912 | bytes 1048576 | tf_op jit(solution)/shard_map/mix/pallas_call | solution.py:333
  (7 shorter events, 0.2 us)
Async XLA Ops:
  25.2 1.5 %collective-permute-start = (bf16[1024,128]{1,0:T(8,128)(2,1)S(1)}, bf16[1024,128]{1,0:T(8,128)(2,1)S(1)}, u32[]{:S(2)}, u32[]{:S(2)}) collective-permute-start(bf16[1024,128]{1,0:T(8,128)(2,1)S(1)} %bitcast.10), channel_id=1, source_target_pairs={{0,4},{4,0},{1,5},{5,1},{2,6},{6,2},{3,7},{7,3},{8,12},{12,8},{9,1... | collective-permute-start | bytes 786440 | tf_op jit(solution)/shard_map/ppermute | solution.py:356
  27.5 17.2 %all-to-all-start.1 = ((bf16[32,32,128]{2,1,0:T(8,128)(2,1)}), bf16[32,32,128]{2,1,0:T(8,128)(2,1)S(1)}, u32[]{:S(2)}, u32[]{:S(2)}) async-start(bf16[32,32,128]{2,1,0:T(8,128)(2,1)} %bitcast.3), calls=%async_computation.1 | async-start | bytes 524288 | tf_op jit(solution)/shard_map/all_to_all | solution.py:358
  32.1 12.5 %copy-start.1 = (f32[1024]{0:T(1024)S(1)}, f32[1024]{0:T(1024)}, u32[]{:S(2)}) copy-start(f32[1024]{0:T(1024)} %param.8) | copy-start | bytes 12292
  36.0 1.0 %copy-start = (f32[512,512]{1,0:T(8,128)}, f32[512,512]{1,0:T(8,128)S(1)}, u32[]{:S(2)}) copy-start(f32[512,512]{1,0:T(8,128)S(1)} %get-tuple-element.20.within_ref) | copy-start | bytes 3145732
  45.2 16.1 %collective-permute-start.3 = (bf16[512,512]{1,0:T(8,128)(2,1)S(1)}, bf16[512,512]{1,0:T(8,128)(2,1)S(1)}, u32[]{:S(2)}, u32[]{:S(2)}) collective-permute-start(bf16[512,512]{1,0:T(8,128)(2,1)S(1)} %finish_heads.3.refs_0_), channel_id=1, source_target_pairs={{0,1},{1,2},{2,3},{3,0},{4,5},{5,6},{6,7},{7,4},{8,9},{9,10},{10,1... | collective-permute-start | bytes 1572872 | tf_op jit(solution)/shard_map/ppermute | solution.py:346
  46.9 14.9 %collective-permute-start.4 = (bf16[512,512]{1,0:T(8,128)(2,1)S(1)}, bf16[512,512]{1,0:T(8,128)(2,1)S(1)}, u32[]{:S(2)}, u32[]{:S(2)}) collective-permute-start(bf16[512,512]{1,0:T(8,128)(2,1)S(1)} %finish_heads.3.refs_0_), channel_id=1, source_target_pairs={{0,3},{1,0},{2,1},{3,2},{4,7},{5,4},{6,5},{7,6},{8,11},{9,8},{10,9... | collective-permute-start | bytes 1572872 | tf_op jit(solution)/shard_map/ppermute | solution.py:346
  50.5 19.7 %collective-permute-start.1 = (bf16[512,512]{1,0:T(8,128)(2,1)S(1)}, bf16[512,512]{1,0:T(8,128)(2,1)S(1)}, u32[]{:S(2)}, u32[]{:S(2)}) collective-permute-start(bf16[512,512]{1,0:T(8,128)(2,1)S(1)} %finish_heads.2.refs_1_), channel_id=1, source_target_pairs={{0,3},{1,0},{2,1},{3,2},{4,7},{5,4},{6,5},{7,6},{8,11},{9,8},{10,9... | collective-permute-start | bytes 1572872 | tf_op jit(solution)/shard_map/ppermute | solution.py:346
  52.4 23.8 %collective-permute-start.6 = (bf16[512,512]{1,0:T(8,128)(2,1)S(1)}, bf16[512,512]{1,0:T(8,128)(2,1)S(1)}, u32[]{:S(2)}, u32[]{:S(2)}) collective-permute-start(bf16[512,512]{1,0:T(8,128)(2,1)S(1)} %finish_heads.2.refs_1_), channel_id=1, source_target_pairs={{0,1},{1,2},{2,3},{3,0},{4,5},{5,6},{6,7},{7,4},{8,9},{9,10},{10,1... | collective-permute-start | bytes 1572872 | tf_op jit(solution)/shard_map/ppermute | solution.py:346
  61.7 19.4 %collective-permute-start.5 = (bf16[512,512]{1,0:T(8,128)(2,1)S(1)}, bf16[512,512]{1,0:T(8,128)(2,1)S(1)}, u32[]{:S(2)}, u32[]{:S(2)}) collective-permute-start(bf16[512,512]{1,0:T(8,128)(2,1)S(1)} %collective-permute-done.3.refs_0_), channel_id=1, source_target_pairs={{0,1},{1,2},{2,3},{3,0},{4,5},{5,6},{6,7},{7,4},{8,9},{9,10},{10,1... | collective-permute-start | bytes 1572872 | tf_op jit(solution)/shard_map/ppermute | solution.py:346
  70.2 11.7 %collective-permute-start.2 = (bf16[512,512]{1,0:T(8,128)(2,1)S(1)}, bf16[512,512]{1,0:T(8,128)(2,1)S(1)}, u32[]{:S(2)}, u32[]{:S(2)}) collective-permute-start(bf16[512,512]{1,0:T(8,128)(2,1)S(1)} %collective-permute-done.1.refs_1_), channel_id=1, source_target_pairs={{0,3},{1,0},{2,1},{3,2},{4,7},{5,4},{6,5},{7,6},{8,11},{9,8},{10,9... | collective-permute-start | bytes 1572872 | tf_op jit(solution)/shard_map/ppermute | solution.py:346

commit v14 on v13

--- a/solution.py
+++ b/solution.py
@@ -63,7 +63,7 @@
     return (att * lax.rsqrt(mean_square + 1e-6) * gain).astype(BF16)
 
 
-PARTS = 2
+PARTS = 4
 
 
 def state_kernel(k_hbm, v_hbm, out_ref, k_ref, v_ref, sems):

time: 84.9 us -> 85.2 us (level)
  no operation moved by 1% of the time
where the time goes in v14:
time: 85.2 us; the launch traced here: 84 us
  waiting for transfers between devices  26.4 us (31%)
  blocking collectives  23.2 us (27%)
  Pallas kernels  18.8 us (22%)
  starting transfers between devices  14.4 us (17%)
  local copies, waits for them, and re-layouts  0.97 us (1%)
    all_to_all x1, blocking collectives, shards(): own = lax.all_to_all(states, 'chip', 0, 0, tiled=True)  23.2 us
    ppermute x6, waiting for transfers between devices, along(): lax.ppermute(value, 'fsdp', [(i, (i + shift) % count) for i in range(coun...  17.2 us
    ppermute x6, starting transfers between devices, along(): lax.ppermute(value, 'fsdp', [(i, (i + shift) % count) for i in range(coun...  9.75 us
    all_to_all x1, waiting for transfers between devices, shards(): carried = lax.all_to_all(sums, 'chip', 0, 0, tiled=True)  7.66 us
    all_to_all x1, starting transfers between devices, shards(): carried = lax.all_to_all(sums, 'chip', 0, 0, tiled=True)  4.61 us
    pallas_call x1, Pallas kernels, within_all(): pl.pallas_call(within_kernel, name='within_all', in_specs=[HBM] * 3, out_...  3.89 us
    pallas_call x3, Pallas kernels, mix(): pl.pallas_call(functools.partial(mix_kernel, count=len(arrays), starts=st...  3.57 us
    pallas_call x1, Pallas kernels, side_mix(): pl.pallas_call(functools.partial(side_kernel, starts=starts), name='side_...  3.19 us
  transfers between devices with their start and end apart: 8, of which 6 were waited for; matrix products, arithmetic and copies ran while one was open for 0% of the time, Pallas kernels for 16%

profile of v14, /device:TPU:32, one launch (start us, length us, event | category | flops | bytes accessed | tf_op | source)
XLA Modules:
  0.0 84.0 jit_solution(16946897245128151812)
XLA Ops:
  0.0 2.3 %block_states.1 = bf16[1024,128]{1,0:T(8,128)(2,1)S(1)} custom-call(bf16[512,1024]{1,0:T(8,128)(2,1)} %k_hbm.3, bf16[512,1024]{1,0:T(8,128)(2,1)} %v_hbm.3), custom_call_target="tpu_custom_call" | custom-call | flops 134217728 | bytes 2097152 | tf_op jit(solution)/shard_map/block_states/pallas_call | solution.py:88
  2.3 23.2 %all_to_all.23 = bf16[32,32,128]{2,1,0:T(8,128)(2,1)S(1)} all-to-all(bf16[32,32,128]{2,1,0:T(8,128)(2,1)S(1)} %bitcast.9), channel_id=1, replica_groups=mesh['chip'=32,'core'=2,'fsdp'=4] {'chip'}, dimensions={0} | all-to-all | bytes 524288 | tf_op jit(solution)/shard_map/all_to_all | solution.py:355
  25.5 1.5 %collective-permute-done.other_ref = bf16[1024,128]{1,0:T(8,128)(2,1)S(1)} collective-permute-done((bf16[1024,128]{1,0:T(8,128)(2,1)S(1)}, bf16[1024,128]{1,0:T(8,128)(2,1)S(1)}, u32[]{:S(2)}, u32[]{:S(2)}) %collective-permute-start) | collective-permute-done | bytes 262176 | tf_op jit(solution)/shard_map/ppermute | solution.py:356
  27.0 0.8 exclusive_sums.1
  27.8 4.6 %all-to-all-start.1 = ((bf16[32,32,128]{2,1,0:T(8,128)(2,1)}), bf16[32,32,128]{2,1,0:T(8,128)(2,1)S(1)}, u32[]{:S(2)}, u32[]{:S(2)}) async-start(bf16[32,32,128]{2,1,0:T(8,128)(2,1)} %bitcast.3), calls=%async_computation.1 | async-start | bytes 524288 | tf_op jit(solution)/shard_map/all_to_all | solution.py:358
  32.5 3.9 %within_all.1 = (bf16[512,512]{1,0:T(8,128)(2,1)S(1)}, f32[512,512]{1,0:T(8,128)S(1)}, f32[512,512]{1,0:T(8,128)S(1)}) custom-call(bf16[512,1024]{1,0:T(8,128)(2,1)} %q_ref.1, bf16[512,1024]{1,0:T(8,128)(2,1)} %k_hbm.3, bf16[512,1024]{1,0:T(8,128)(2,1)} %v_hbm.3), custom_call_target="tpu_custom_call" | custom-call | flops 1073741824 | bytes 5242880 | tf_op jit(solution)/shard_map/within_all/pallas_call | solution.py:154
  36.4 1.0 %copy-done = f32[512,512]{1,0:T(8,128)} copy-done((f32[512,512]{1,0:T(8,128)}, f32[512,512]{1,0:T(8,128)S(1)}, u32[]{:S(2)}) %copy-start) | copy-done | bytes 1048600
  37.3 7.7 %all-to-all-done.1 = bf16[32,32,128]{2,1,0:T(8,128)(2,1)S(1)} async-done(((bf16[32,32,128]{2,1,0:T(8,128)(2,1)}), bf16[32,32,128]{2,1,0:T(8,128)(2,1)S(1)}, u32[]{:S(2)}, u32[]{:S(2)}) %all-to-all-start.1) | async-done | bytes 262176 | tf_op jit(solution)/shard_map/all_to_all | solution.py:358
  45.0 0.5 finish_heads.3.refs_0_
  45.5 1.7 %collective-permute-start.3 = (bf16[512,512]{1,0:T(8,128)(2,1)S(1)}, bf16[512,512]{1,0:T(8,128)(2,1)S(1)}, u32[]{:S(2)}, u32[]{:S(2)}) collective-permute-start(bf16[512,512]{1,0:T(8,128)(2,1)S(1)} %finish_heads.3.refs_0_), channel_id=1, source_target_pairs={{0,1},{1,2},{2,3},{3,0},{4,5},{5,6},{6,7},{7,4},{8,9},{9,10},{10,1... | collective-permute-start | bytes 1572872 | tf_op jit(solution)/shard_map/ppermute | solution.py:346
  47.2 1.7 %collective-permute-start.4 = (bf16[512,512]{1,0:T(8,128)(2,1)S(1)}, bf16[512,512]{1,0:T(8,128)(2,1)S(1)}, u32[]{:S(2)}, u32[]{:S(2)}) collective-permute-start(bf16[512,512]{1,0:T(8,128)(2,1)S(1)} %finish_heads.3.refs_0_), channel_id=1, source_target_pairs={{0,3},{1,0},{2,1},{3,2},{4,7},{5,4},{6,5},{7,6},{8,11},{9,8},{10,9... | collective-permute-start | bytes 1572872 | tf_op jit(solution)/shard_map/ppermute | solution.py:346
  48.9 1.9 %finish_heads.2.refs_1_ = bf16[512,512]{1,0:T(8,128)(2,1)S(1)} custom-call(bf16[512,1024]{1,0:T(8,128)(2,1)} %q_ref.1, f32[512,512]{1,0:T(8,128)} %copy-done, bf16[1024,128]{1,0:T(8,128)(2,1)S(1)} %bitcast.8, f32[1,1024]{1,0:T(1,128)S(1)} %bitcast.13), custom_call_target="tpu_custom_call" | custom-call | flops 134217728 | bytes 2097152 | tf_op jit(solution)/shard_map/finish_heads/pallas_call | solution.py:202
  50.8 1.9 %collective-permute-start.1 = (bf16[512,512]{1,0:T(8,128)(2,1)S(1)}, bf16[512,512]{1,0:T(8,128)(2,1)S(1)}, u32[]{:S(2)}, u32[]{:S(2)}) collective-permute-start(bf16[512,512]{1,0:T(8,128)(2,1)S(1)} %finish_heads.2.refs_1_), channel_id=1, source_target_pairs={{0,3},{1,0},{2,1},{3,2},{4,7},{5,4},{6,5},{7,6},{8,11},{9,8},{10,9... | collective-permute-start | bytes 1572872 | tf_op jit(solution)/shard_map/ppermute | solution.py:346
  52.9 2.5 %own_mix.1.refs_3_ = f32[512,1024]{1,0:T(8,128)S(1)} custom-call(s32[1]{0:T(128)} %bitcast.6.column_ref, bf16[512,512]{1,0:T(8,128)(2,1)S(1)} %finish_heads.3.refs_0_, bf16[512,512]{1,0:T(8,128)(2,1)S(1)} %finish_heads.2.refs_1_, bf16[4096,1024]{1,0:T(8,128)(2,1)} %refs_2_.3), custom_call_target="tpu_custom_call" | custom-call | flops 1073741824 | bytes 2097152 | tf_op jit(solution)/shard_map/own_mix/pallas_call | solution.py:245
  55.5 6.2 %collective-permute-done.3.refs_0_ = bf16[512,512]{1,0:T(8,128)(2,1)S(1)} collective-permute-done((bf16[512,512]{1,0:T(8,128)(2,1)S(1)}, bf16[512,512]{1,0:T(8,128)(2,1)S(1)}, u32[]{:S(2)}, u32[]{:S(2)}) %collective-permute-start.3) | collective-permute-done | bytes 524320 | tf_op jit(solution)/shard_map/ppermute | solution.py:346
  61.7 0.4 collective-permute-done.4.refs_1_
  62.1 1.6 %collective-permute-start.5 = (bf16[512,512]{1,0:T(8,128)(2,1)S(1)}, bf16[512,512]{1,0:T(8,128)(2,1)S(1)}, u32[]{:S(2)}, u32[]{:S(2)}) collective-permute-start(bf16[512,512]{1,0:T(8,128)(2,1)S(1)} %collective-permute-done.3.refs_0_), channel_id=1, source_target_pairs={{0,1},{1,2},{2,3},{3,0},{4,5},{5,6},{6,7},{7,4},{8,9},{9,10},{10,1... | collective-permute-start | bytes 1572872 | tf_op jit(solution)/shard_map/ppermute | solution.py:346
  63.6 6.9 %collective-permute-done.1.refs_1_ = bf16[512,512]{1,0:T(8,128)(2,1)S(1)} collective-permute-done((bf16[512,512]{1,0:T(8,128)(2,1)S(1)}, bf16[512,512]{1,0:T(8,128)(2,1)S(1)}, u32[]{:S(2)}, u32[]{:S(2)}) %collective-permute-start.1) | collective-permute-done | bytes 524320 | tf_op jit(solution)/shard_map/ppermute | solution.py:346
  70.5 2.8 %collective-permute-start.2 = (bf16[512,512]{1,0:T(8,128)(2,1)S(1)}, bf16[512,512]{1,0:T(8,128)(2,1)S(1)}, u32[]{:S(2)}, u32[]{:S(2)}) collective-permute-start(bf16[512,512]{1,0:T(8,128)(2,1)S(1)} %collective-permute-done.1.refs_1_), channel_id=1, source_target_pairs={{0,3},{1,0},{2,1},{3,2},{4,7},{5,4},{6,5},{7,6},{8,11},{9,8},{10,9... | collective-permute-start | bytes 1572872 | tf_op jit(solution)/shard_map/ppermute | solution.py:346
  73.3 3.2 %side_mix.1 = (f32[512,1024]{1,0:T(8,128)S(1)}, bf16[3072,1024]{1,0:T(8,128)(2,1)S(1)}) custom-call(s32[1]{0:T(128)} %bitcast.6.column_ref, bf16[512,512]{1,0:T(8,128)(2,1)S(1)} %collective-permute-done.3.refs_0_, bf16[512,512]{1,0:T(8,128)(2,1)S(1)} %collective-permute-done.4.refs_1_, bf16[4096,1024]{1,0:T(8,128)(2,1)} %refs_2_.3, ...), custom_call_target="tpu_custom_call" | custom-call | flops 3221225472 | bytes 6291456 | tf_op jit(solution)/shard_map/side_mix/pallas_call | solution.py:295
  76.5 1.2 %mix.3.refs_2_ = f32[512,1024]{1,0:T(8,128)S(1)} custom-call(bf16[512,512]{1,0:T(8,128)(2,1)S(1)} %collective-permute-done.6.refs_0_, bf16[512,512]{1,0:T(8,128)(2,1)S(1)} %collective-permute-done.1.refs_1_, bf16[3072,1024]{1,0:T(8,128)(2,1)S(1)} %get-tuple-element.27.refs_2_.refs_1_, f32[512,1024]{1,0:T(8,128)S(1)} %get-tuple-element.28.refs_3_), custom_call_target="tpu_custom_call" | custom-call | flops 1073741824 | bytes 2097152 | tf_op jit(solution)/shard_map/mix/pallas_call | solution.py:333
  77.7 3.7 %collective-permute-done.5.refs_0_ = bf16[512,512]{1,0:T(8,128)(2,1)S(1)} collective-permute-done((bf16[512,512]{1,0:T(8,128)(2,1)S(1)}, bf16[512,512]{1,0:T(8,128)(2,1)S(1)}, u32[]{:S(2)}, u32[]{:S(2)}) %collective-permute-start.5) | collective-permute-done | bytes 524320 | tf_op jit(solution)/shard_map/ppermute | solution.py:346
  81.5 0.7 mix.4.refs_2_
  82.2 1.6 %mix.5 = bf16[512,1024]{1,0:T(8,128)(2,1)} custom-call(bf16[512,512]{1,0:T(8,128)(2,1)S(1)} %collective-permute-done.2.refs_0_, bf16[3072,1024]{1,0:T(8,128)(2,1)S(1)} %get-tuple-element.27.refs_2_.refs_1_, f32[512,1024]{1,0:T(8,128)S(1)} %mix.4.refs_2_), custom_call_target="tpu_custom_call" | custom-call | flops 536870912 | bytes 1048576 | tf_op jit(solution)/shard_map/mix/pallas_call | solution.py:333
  (7 shorter events, 0.2 us)
Async XLA Ops:
  25.5 1.5 %collective-permute-start = (bf16[1024,128]{1,0:T(8,128)(2,1)S(1)}, bf16[1024,128]{1,0:T(8,128)(2,1)S(1)}, u32[]{:S(2)}, u32[]{:S(2)}) collective-permute-start(bf16[1024,128]{1,0:T(8,128)(2,1)S(1)} %bitcast.10), channel_id=1, source_target_pairs={{0,4},{4,0},{1,5},{5,1},{2,6},{6,2},{3,7},{7,3},{8,12},{12,8},{9,1... | collective-permute-start | bytes 786440 | tf_op jit(solution)/shard_map/ppermute | solution.py:356
  27.8 17.2 %all-to-all-start.1 = ((bf16[32,32,128]{2,1,0:T(8,128)(2,1)}), bf16[32,32,128]{2,1,0:T(8,128)(2,1)S(1)}, u32[]{:S(2)}, u32[]{:S(2)}) async-start(bf16[32,32,128]{2,1,0:T(8,128)(2,1)} %bitcast.3), calls=%async_computation.1 | async-start | bytes 524288 | tf_op jit(solution)/shard_map/all_to_all | solution.py:358
  32.5 12.5 %copy-start.1 = (f32[1024]{0:T(1024)S(1)}, f32[1024]{0:T(1024)}, u32[]{:S(2)}) copy-start(f32[1024]{0:T(1024)} %param.8) | copy-start | bytes 12292
  36.4 1.0 %copy-start = (f32[512,512]{1,0:T(8,128)}, f32[512,512]{1,0:T(8,128)S(1)}, u32[]{:S(2)}) copy-start(f32[512,512]{1,0:T(8,128)S(1)} %get-tuple-element.20.within_ref) | copy-start | bytes 3145732
  45.5 16.2 %collective-permute-start.3 = (bf16[512,512]{1,0:T(8,128)(2,1)S(1)}, bf16[512,512]{1,0:T(8,128)(2,1)S(1)}, u32[]{:S(2)}, u32[]{:S(2)}) collective-permute-start(bf16[512,512]{1,0:T(8,128)(2,1)S(1)} %finish_heads.3.refs_0_), channel_id=1, source_target_pairs={{0,1},{1,2},{2,3},{3,0},{4,5},{5,6},{6,7},{7,4},{8,9},{9,10},{10,1... | collective-permute-start | bytes 1572872 | tf_op jit(solution)/shard_map/ppermute | solution.py:346
  47.2 14.9 %collective-permute-start.4 = (bf16[512,512]{1,0:T(8,128)(2,1)S(1)}, bf16[512,512]{1,0:T(8,128)(2,1)S(1)}, u32[]{:S(2)}, u32[]{:S(2)}) collective-permute-start(bf16[512,512]{1,0:T(8,128)(2,1)S(1)} %finish_heads.3.refs_0_), channel_id=1, source_target_pairs={{0,3},{1,0},{2,1},{3,2},{4,7},{5,4},{6,5},{7,6},{8,11},{9,8},{10,9... | collective-permute-start | bytes 1572872 | tf_op jit(solution)/shard_map/ppermute | solution.py:346
  50.8 19.7 %collective-permute-start.1 = (bf16[512,512]{1,0:T(8,128)(2,1)S(1)}, bf16[512,512]{1,0:T(8,128)(2,1)S(1)}, u32[]{:S(2)}, u32[]{:S(2)}) collective-permute-start(bf16[512,512]{1,0:T(8,128)(2,1)S(1)} %finish_heads.2.refs_1_), channel_id=1, source_target_pairs={{0,3},{1,0},{2,1},{3,2},{4,7},{5,4},{6,5},{7,6},{8,11},{9,8},{10,9... | collective-permute-start | bytes 1572872 | tf_op jit(solution)/shard_map/ppermute | solution.py:346
  52.7 23.8 %collective-permute-start.6 = (bf16[512,512]{1,0:T(8,128)(2,1)S(1)}, bf16[512,512]{1,0:T(8,128)(2,1)S(1)}, u32[]{:S(2)}, u32[]{:S(2)}) collective-permute-start(bf16[512,512]{1,0:T(8,128)(2,1)S(1)} %finish_heads.2.refs_1_), channel_id=1, source_target_pairs={{0,1},{1,2},{2,3},{3,0},{4,5},{5,6},{6,7},{7,4},{8,9},{9,10},{10,1... | collective-permute-start | bytes 1572872 | tf_op jit(solution)/shard_map/ppermute | solution.py:346
  62.1 19.4 %collective-permute-start.5 = (bf16[512,512]{1,0:T(8,128)(2,1)S(1)}, bf16[512,512]{1,0:T(8,128)(2,1)S(1)}, u32[]{:S(2)}, u32[]{:S(2)}) collective-permute-start(bf16[512,512]{1,0:T(8,128)(2,1)S(1)} %collective-permute-done.3.refs_0_), channel_id=1, source_target_pairs={{0,1},{1,2},{2,3},{3,0},{4,5},{5,6},{6,7},{7,4},{8,9},{9,10},{10,1... | collective-permute-start | bytes 1572872 | tf_op jit(solution)/shard_map/ppermute | solution.py:346
  70.5 11.7 %collective-permute-start.2 = (bf16[512,512]{1,0:T(8,128)(2,1)S(1)}, bf16[512,512]{1,0:T(8,128)(2,1)S(1)}, u32[]{:S(2)}, u32[]{:S(2)}) collective-permute-start(bf16[512,512]{1,0:T(8,128)(2,1)S(1)} %collective-permute-done.1.refs_1_), channel_id=1, source_target_pairs={{0,3},{1,0},{2,1},{3,2},{4,7},{5,4},{6,5},{7,6},{8,11},{9,8},{10,9... | collective-permute-start | bytes 1572872 | tf_op jit(solution)/shard_map/ppermute | solution.py:346

commit v15 on v14

--- a/solution.py
+++ b/solution.py
@@ -63,7 +63,7 @@
     return (att * lax.rsqrt(mean_square + 1e-6) * gain).astype(BF16)
 
 
-PARTS = 4
+PARTS = 1
 
 
 def state_kernel(k_hbm, v_hbm, out_ref, k_ref, v_ref, sems):

time: 85.2 us -> 85 us (level)
  no operation moved by 1% of the time
where the time goes in v15:
time: 85 us; the launch traced here: 83.7 us
  waiting for transfers between devices  26.4 us (31%)
  blocking collectives  23.2 us (27%)
  Pallas kernels  18.6 us (22%)
  starting transfers between devices  14.4 us (17%)
  local copies, waits for them, and re-layouts  0.97 us (1%)
    all_to_all x1, blocking collectives, shards(): own = lax.all_to_all(states, 'chip', 0, 0, tiled=True)  23.2 us
    ppermute x6, waiting for transfers between devices, along(): lax.ppermute(value, 'fsdp', [(i, (i + shift) % count) for i in range(coun...  17.2 us
    ppermute x6, starting transfers between devices, along(): lax.ppermute(value, 'fsdp', [(i, (i + shift) % count) for i in range(coun...  9.76 us
    all_to_all x1, waiting for transfers between devices, shards(): carried = lax.all_to_all(sums, 'chip', 0, 0, tiled=True)  7.65 us
    all_to_all x1, starting transfers between devices, shards(): carried = lax.all_to_all(sums, 'chip', 0, 0, tiled=True)  4.61 us
    pallas_call x1, Pallas kernels, within_all(): pl.pallas_call(within_kernel, name='within_all', in_specs=[HBM] * 3, out_...  3.9 us
    pallas_call x3, Pallas kernels, mix(): pl.pallas_call(functools.partial(mix_kernel, count=len(arrays), starts=st...  3.57 us
    pallas_call x1, Pallas kernels, side_mix(): pl.pallas_call(functools.partial(side_kernel, starts=starts), name='side_...  3.19 us
  transfers between devices with their start and end apart: 8, of which 6 were waited for; matrix products, arithmetic and copies ran while one was open for 0% of the time, Pallas kernels for 16%

profile of v15, /device:TPU:32, one launch (start us, length us, event | category | flops | bytes accessed | tf_op | source)
XLA Modules:
  0.0 83.7 jit_solution(17255066632719436429)
XLA Ops:
  0.0 2.1 %block_states.1 = bf16[1024,128]{1,0:T(8,128)(2,1)S(1)} custom-call(bf16[512,1024]{1,0:T(8,128)(2,1)} %k_hbm.3, bf16[512,1024]{1,0:T(8,128)(2,1)} %v_hbm.3), custom_call_target="tpu_custom_call" | custom-call | flops 134217728 | bytes 2097152 | tf_op jit(solution)/shard_map/block_states/pallas_call | solution.py:88
  2.1 23.2 %all_to_all.23 = bf16[32,32,128]{2,1,0:T(8,128)(2,1)S(1)} all-to-all(bf16[32,32,128]{2,1,0:T(8,128)(2,1)S(1)} %bitcast.9), channel_id=1, replica_groups=mesh['chip'=32,'core'=2,'fsdp'=4] {'chip'}, dimensions={0} | all-to-all | bytes 524288 | tf_op jit(solution)/shard_map/all_to_all | solution.py:355
  25.2 1.5 %collective-permute-done.other_ref = bf16[1024,128]{1,0:T(8,128)(2,1)S(1)} collective-permute-done((bf16[1024,128]{1,0:T(8,128)(2,1)S(1)}, bf16[1024,128]{1,0:T(8,128)(2,1)S(1)}, u32[]{:S(2)}, u32[]{:S(2)}) %collective-permute-start) | collective-permute-done | bytes 262176 | tf_op jit(solution)/shard_map/ppermute | solution.py:356
  26.8 0.8 exclusive_sums.1
  27.6 4.6 %all-to-all-start.1 = ((bf16[32,32,128]{2,1,0:T(8,128)(2,1)}), bf16[32,32,128]{2,1,0:T(8,128)(2,1)S(1)}, u32[]{:S(2)}, u32[]{:S(2)}) async-start(bf16[32,32,128]{2,1,0:T(8,128)(2,1)} %bitcast.3), calls=%async_computation.1 | async-start | bytes 524288 | tf_op jit(solution)/shard_map/all_to_all | solution.py:358
  32.2 3.9 %within_all.1 = (bf16[512,512]{1,0:T(8,128)(2,1)S(1)}, f32[512,512]{1,0:T(8,128)S(1)}, f32[512,512]{1,0:T(8,128)S(1)}) custom-call(bf16[512,1024]{1,0:T(8,128)(2,1)} %q_ref.1, bf16[512,1024]{1,0:T(8,128)(2,1)} %k_hbm.3, bf16[512,1024]{1,0:T(8,128)(2,1)} %v_hbm.3), custom_call_target="tpu_custom_call" | custom-call | flops 1073741824 | bytes 5242880 | tf_op jit(solution)/shard_map/within_all/pallas_call | solution.py:154
  36.1 1.0 %copy-done = f32[512,512]{1,0:T(8,128)} copy-done((f32[512,512]{1,0:T(8,128)}, f32[512,512]{1,0:T(8,128)S(1)}, u32[]{:S(2)}) %copy-start) | copy-done | bytes 1048600
  37.1 7.6 %all-to-all-done.1 = bf16[32,32,128]{2,1,0:T(8,128)(2,1)S(1)} async-done(((bf16[32,32,128]{2,1,0:T(8,128)(2,1)}), bf16[32,32,128]{2,1,0:T(8,128)(2,1)S(1)}, u32[]{:S(2)}, u32[]{:S(2)}) %all-to-all-start.1) | async-done | bytes 262176 | tf_op jit(solution)/shard_map/all_to_all | solution.py:358
  44.8 0.5 finish_heads.3.refs_0_
  45.3 1.7 %collective-permute-start.3 = (bf16[512,512]{1,0:T(8,128)(2,1)S(1)}, bf16[512,512]{1,0:T(8,128)(2,1)S(1)}, u32[]{:S(2)}, u32[]{:S(2)}) collective-permute-start(bf16[512,512]{1,0:T(8,128)(2,1)S(1)} %finish_heads.3.refs_0_), channel_id=1, source_target_pairs={{0,1},{1,2},{2,3},{3,0},{4,5},{5,6},{6,7},{7,4},{8,9},{9,10},{10,1... | collective-permute-start | bytes 1572872 | tf_op jit(solution)/shard_map/ppermute | solution.py:346
  47.0 1.7 %collective-permute-start.4 = (bf16[512,512]{1,0:T(8,128)(2,1)S(1)}, bf16[512,512]{1,0:T(8,128)(2,1)S(1)}, u32[]{:S(2)}, u32[]{:S(2)}) collective-permute-start(bf16[512,512]{1,0:T(8,128)(2,1)S(1)} %finish_heads.3.refs_0_), channel_id=1, source_target_pairs={{0,3},{1,0},{2,1},{3,2},{4,7},{5,4},{6,5},{7,6},{8,11},{9,8},{10,9... | collective-permute-start | bytes 1572872 | tf_op jit(solution)/shard_map/ppermute | solution.py:346
  48.6 1.9 %finish_heads.2.refs_1_ = bf16[512,512]{1,0:T(8,128)(2,1)S(1)} custom-call(bf16[512,1024]{1,0:T(8,128)(2,1)} %q_ref.1, f32[512,512]{1,0:T(8,128)} %copy-done, bf16[1024,128]{1,0:T(8,128)(2,1)S(1)} %bitcast.8, f32[1,1024]{1,0:T(1,128)S(1)} %bitcast.13), custom_call_target="tpu_custom_call" | custom-call | flops 134217728 | bytes 2097152 | tf_op jit(solution)/shard_map/finish_heads/pallas_call | solution.py:202
  50.6 1.9 %collective-permute-start.1 = (bf16[512,512]{1,0:T(8,128)(2,1)S(1)}, bf16[512,512]{1,0:T(8,128)(2,1)S(1)}, u32[]{:S(2)}, u32[]{:S(2)}) collective-permute-start(bf16[512,512]{1,0:T(8,128)(2,1)S(1)} %finish_heads.2.refs_1_), channel_id=1, source_target_pairs={{0,3},{1,0},{2,1},{3,2},{4,7},{5,4},{6,5},{7,6},{8,11},{9,8},{10,9... | collective-permute-start | bytes 1572872 | tf_op jit(solution)/shard_map/ppermute | solution.py:346
  52.7 2.5 %own_mix.1.refs_3_ = f32[512,1024]{1,0:T(8,128)S(1)} custom-call(s32[1]{0:T(128)} %bitcast.6.column_ref, bf16[512,512]{1,0:T(8,128)(2,1)S(1)} %finish_heads.3.refs_0_, bf16[512,512]{1,0:T(8,128)(2,1)S(1)} %finish_heads.2.refs_1_, bf16[4096,1024]{1,0:T(8,128)(2,1)} %refs_2_.3), custom_call_target="tpu_custom_call" | custom-call | flops 1073741824 | bytes 2097152 | tf_op jit(solution)/shard_map/own_mix/pallas_call | solution.py:245
  55.2 6.2 %collective-permute-done.3.refs_0_ = bf16[512,512]{1,0:T(8,128)(2,1)S(1)} collective-permute-done((bf16[512,512]{1,0:T(8,128)(2,1)S(1)}, bf16[512,512]{1,0:T(8,128)(2,1)S(1)}, u32[]{:S(2)}, u32[]{:S(2)}) %collective-permute-start.3) | collective-permute-done | bytes 524320 | tf_op jit(solution)/shard_map/ppermute | solution.py:346
  61.5 0.4 collective-permute-done.4.refs_1_
  61.8 1.6 %collective-permute-start.5 = (bf16[512,512]{1,0:T(8,128)(2,1)S(1)}, bf16[512,512]{1,0:T(8,128)(2,1)S(1)}, u32[]{:S(2)}, u32[]{:S(2)}) collective-permute-start(bf16[512,512]{1,0:T(8,128)(2,1)S(1)} %collective-permute-done.3.refs_0_), channel_id=1, source_target_pairs={{0,1},{1,2},{2,3},{3,0},{4,5},{5,6},{6,7},{7,4},{8,9},{9,10},{10,1... | collective-permute-start | bytes 1572872 | tf_op jit(solution)/shard_map/ppermute | solution.py:346
  63.4 6.9 %collective-permute-done.1.refs_1_ = bf16[512,512]{1,0:T(8,128)(2,1)S(1)} collective-permute-done((bf16[512,512]{1,0:T(8,128)(2,1)S(1)}, bf16[512,512]{1,0:T(8,128)(2,1)S(1)}, u32[]{:S(2)}, u32[]{:S(2)}) %collective-permute-start.1) | collective-permute-done | bytes 524320 | tf_op jit(solution)/shard_map/ppermute | solution.py:346
  70.3 2.8 %collective-permute-start.2 = (bf16[512,512]{1,0:T(8,128)(2,1)S(1)}, bf16[512,512]{1,0:T(8,128)(2,1)S(1)}, u32[]{:S(2)}, u32[]{:S(2)}) collective-permute-start(bf16[512,512]{1,0:T(8,128)(2,1)S(1)} %collective-permute-done.1.refs_1_), channel_id=1, source_target_pairs={{0,3},{1,0},{2,1},{3,2},{4,7},{5,4},{6,5},{7,6},{8,11},{9,8},{10,9... | collective-permute-start | bytes 1572872 | tf_op jit(solution)/shard_map/ppermute | solution.py:346
  73.0 3.2 %side_mix.1 = (f32[512,1024]{1,0:T(8,128)S(1)}, bf16[3072,1024]{1,0:T(8,128)(2,1)S(1)}) custom-call(s32[1]{0:T(128)} %bitcast.6.column_ref, bf16[512,512]{1,0:T(8,128)(2,1)S(1)} %collective-permute-done.3.refs_0_, bf16[512,512]{1,0:T(8,128)(2,1)S(1)} %collective-permute-done.4.refs_1_, bf16[4096,1024]{1,0:T(8,128)(2,1)} %refs_2_.3, ...), custom_call_target="tpu_custom_call" | custom-call | flops 3221225472 | bytes 6291456 | tf_op jit(solution)/shard_map/side_mix/pallas_call | solution.py:295
  76.3 1.2 %mix.3.refs_2_ = f32[512,1024]{1,0:T(8,128)S(1)} custom-call(bf16[512,512]{1,0:T(8,128)(2,1)S(1)} %collective-permute-done.6.refs_0_, bf16[512,512]{1,0:T(8,128)(2,1)S(1)} %collective-permute-done.1.refs_1_, bf16[3072,1024]{1,0:T(8,128)(2,1)S(1)} %get-tuple-element.27.refs_2_.refs_1_, f32[512,1024]{1,0:T(8,128)S(1)} %get-tuple-element.28.refs_3_), custom_call_target="tpu_custom_call" | custom-call | flops 1073741824 | bytes 2097152 | tf_op jit(solution)/shard_map/mix/pallas_call | solution.py:333
  77.5 3.7 %collective-permute-done.5.refs_0_ = bf16[512,512]{1,0:T(8,128)(2,1)S(1)} collective-permute-done((bf16[512,512]{1,0:T(8,128)(2,1)S(1)}, bf16[512,512]{1,0:T(8,128)(2,1)S(1)}, u32[]{:S(2)}, u32[]{:S(2)}) %collective-permute-start.5) | collective-permute-done | bytes 524320 | tf_op jit(solution)/shard_map/ppermute | solution.py:346
  81.2 0.7 mix.4.refs_2_
  82.0 1.6 %mix.5 = bf16[512,1024]{1,0:T(8,128)(2,1)} custom-call(bf16[512,512]{1,0:T(8,128)(2,1)S(1)} %collective-permute-done.2.refs_0_, bf16[3072,1024]{1,0:T(8,128)(2,1)S(1)} %get-tuple-element.27.refs_2_.refs_1_, f32[512,1024]{1,0:T(8,128)S(1)} %mix.4.refs_2_), custom_call_target="tpu_custom_call" | custom-call | flops 536870912 | bytes 1048576 | tf_op jit(solution)/shard_map/mix/pallas_call | solution.py:333
  (7 shorter events, 0.2 us)
Async XLA Ops:
  25.2 1.5 %collective-permute-start = (bf16[1024,128]{1,0:T(8,128)(2,1)S(1)}, bf16[1024,128]{1,0:T(8,128)(2,1)S(1)}, u32[]{:S(2)}, u32[]{:S(2)}) collective-permute-start(bf16[1024,128]{1,0:T(8,128)(2,1)S(1)} %bitcast.10), channel_id=1, source_target_pairs={{0,4},{4,0},{1,5},{5,1},{2,6},{6,2},{3,7},{7,3},{8,12},{12,8},{9,1... | collective-permute-start | bytes 786440 | tf_op jit(solution)/shard_map/ppermute | solution.py:356
  27.6 17.2 %all-to-all-start.1 = ((bf16[32,32,128]{2,1,0:T(8,128)(2,1)}), bf16[32,32,128]{2,1,0:T(8,128)(2,1)S(1)}, u32[]{:S(2)}, u32[]{:S(2)}) async-start(bf16[32,32,128]{2,1,0:T(8,128)(2,1)} %bitcast.3), calls=%async_computation.1 | async-start | bytes 524288 | tf_op jit(solution)/shard_map/all_to_all | solution.py:358
  32.2 12.5 %copy-start.1 = (f32[1024]{0:T(1024)S(1)}, f32[1024]{0:T(1024)}, u32[]{:S(2)}) copy-start(f32[1024]{0:T(1024)} %param.8) | copy-start | bytes 12292
  36.1 1.0 %copy-start = (f32[512,512]{1,0:T(8,128)}, f32[512,512]{1,0:T(8,128)S(1)}, u32[]{:S(2)}) copy-start(f32[512,512]{1,0:T(8,128)S(1)} %get-tuple-element.20.within_ref) | copy-start | bytes 3145732
  45.3 16.2 %collective-permute-start.3 = (bf16[512,512]{1,0:T(8,128)(2,1)S(1)}, bf16[512,512]{1,0:T(8,128)(2,1)S(1)}, u32[]{:S(2)}, u32[]{:S(2)}) collective-permute-start(bf16[512,512]{1,0:T(8,128)(2,1)S(1)} %finish_heads.3.refs_0_), channel_id=1, source_target_pairs={{0,1},{1,2},{2,3},{3,0},{4,5},{5,6},{6,7},{7,4},{8,9},{9,10},{10,1... | collective-permute-start | bytes 1572872 | tf_op jit(solution)/shard_map/ppermute | solution.py:346
  47.0 14.9 %collective-permute-start.4 = (bf16[512,512]{1,0:T(8,128)(2,1)S(1)}, bf16[512,512]{1,0:T(8,128)(2,1)S(1)}, u32[]{:S(2)}, u32[]{:S(2)}) collective-permute-start(bf16[512,512]{1,0:T(8,128)(2,1)S(1)} %finish_heads.3.refs_0_), channel_id=1, source_target_pairs={{0,3},{1,0},{2,1},{3,2},{4,7},{5,4},{6,5},{7,6},{8,11},{9,8},{10,9... | collective-permute-start | bytes 1572872 | tf_op jit(solution)/shard_map/ppermute | solution.py:346
  50.6 19.7 %collective-permute-start.1 = (bf16[512,512]{1,0:T(8,128)(2,1)S(1)}, bf16[512,512]{1,0:T(8,128)(2,1)S(1)}, u32[]{:S(2)}, u32[]{:S(2)}) collective-permute-start(bf16[512,512]{1,0:T(8,128)(2,1)S(1)} %finish_heads.2.refs_1_), channel_id=1, source_target_pairs={{0,3},{1,0},{2,1},{3,2},{4,7},{5,4},{6,5},{7,6},{8,11},{9,8},{10,9... | collective-permute-start | bytes 1572872 | tf_op jit(solution)/shard_map/ppermute | solution.py:346
  52.4 23.8 %collective-permute-start.6 = (bf16[512,512]{1,0:T(8,128)(2,1)S(1)}, bf16[512,512]{1,0:T(8,128)(2,1)S(1)}, u32[]{:S(2)}, u32[]{:S(2)}) collective-permute-start(bf16[512,512]{1,0:T(8,128)(2,1)S(1)} %finish_heads.2.refs_1_), channel_id=1, source_target_pairs={{0,1},{1,2},{2,3},{3,0},{4,5},{5,6},{6,7},{7,4},{8,9},{9,10},{10,1... | collective-permute-start | bytes 1572872 | tf_op jit(solution)/shard_map/ppermute | solution.py:346
  61.8 19.4 %collective-permute-start.5 = (bf16[512,512]{1,0:T(8,128)(2,1)S(1)}, bf16[512,512]{1,0:T(8,128)(2,1)S(1)}, u32[]{:S(2)}, u32[]{:S(2)}) collective-permute-start(bf16[512,512]{1,0:T(8,128)(2,1)S(1)} %collective-permute-done.3.refs_0_), channel_id=1, source_target_pairs={{0,1},{1,2},{2,3},{3,0},{4,5},{5,6},{6,7},{7,4},{8,9},{9,10},{10,1... | collective-permute-start | bytes 1572872 | tf_op jit(solution)/shard_map/ppermute | solution.py:346
  70.3 11.7 %collective-permute-start.2 = (bf16[512,512]{1,0:T(8,128)(2,1)S(1)}, bf16[512,512]{1,0:T(8,128)(2,1)S(1)}, u32[]{:S(2)}, u32[]{:S(2)}) collective-permute-start(bf16[512,512]{1,0:T(8,128)(2,1)S(1)} %collective-permute-done.1.refs_1_), channel_id=1, source_target_pairs={{0,3},{1,0},{2,1},{3,2},{4,7},{5,4},{6,5},{7,6},{8,11},{9,8},{10,9... | collective-permute-start | bytes 1572872 | tf_op jit(solution)/shard_map/ppermute | solution.py:346
